TPU v7x, 128 devices: a whole 4x4x4 slice. The times are simulated.
128 devices in a mesh: dp: 8 (over y, core), expert: 16 (over x, z).
Axes of the slice: x: 4, y: 4, z: 4, core: 2. Of those that a mesh axis runs over, the one named last changes fastest.
Arguments:
- hidden_in: bfloat16 [8192, 7168], P(('dp', 'expert')), may hold values from -6 to 6
- norm_gain: float32 [7168], replicated, may hold values from 0.25 to 4
- route_logits: float32 [8192, 8], P(('dp', 'expert')), may hold values from -6 to 6
- expert_ids: int32 [8192, 8], P(('dp', 'expert')), may hold values from 0 to 255, as said below
- w_gate: bfloat16 [16, 7168, 2048], P('dp', None, 'expert'), may hold values from -0.0625 to 0.0625
- w_up: bfloat16 [16, 7168, 2048], P('dp', None, 'expert'), may hold values from -0.0625 to 0.0625
- w_down: bfloat16 [16, 2048, 7168], P('dp', 'expert'), may hold values from -0.125 to 0.125
- w_latent: bfloat16 [7168, 576], P(('dp', 'expert')), may hold values from -0.0625 to 0.0625
- kv_gain: float32 [512], replicated, may hold values from 0.25 to 4
- queries: bfloat16 [8192, 36864], P(('dp', 'expert')), may hold values from -240 to 240
- page_pool: bfloat16 [16384, 9216], P(('dp', 'expert')), may hold values from -6 to 6
- page_table: int32 [8192, 6], P(('dp', 'expert')), may hold values from 0 to 159
- kv_lengths: int32 [8192], P(('dp', 'expert')), may hold values from 1 to 96, 393216 in all
- migration: int32 [8, 16, 8, 4], P('dp', 'expert'), may hold values from 0 to 127
Outputs:
- hidden_out: bfloat16 [8192, 7168], P(('dp', 'expert'))
- attended: bfloat16 [8192, 32768], P(('dp', 'expert'))
Inputs may be any that keep to these rules, and one draw needn't show every extreme that they name: `expert_ids`: each row names 8 different experts, at most one of them below 16. The rows of one device name one window expert at most 4 times; in every draw one window expert is named exactly 4 times by the rows of every device.
All inputs are finite; a program needn't handle non-finite values. No bound on the sum of `kv_lengths` on one device may be relied on, other than what follows from the above.
Results may differ from a plain program's by a relative error of at most 0.038.
Values may be sent and summed in bfloat16 or wider, within the bound.
No kernel may reach another device: no remote copies, remote signals or barrier semaphores. Data moves between devices by JAX's collectives and lax.ppermute only.
A program may use at most 192 MiB of HBM per device.

v0:
```python
import functools

import jax
import jax.numpy as jnp
from jax import lax
from jax.experimental import pallas as pl
from jax.experimental.pallas import tpu as pltpu
from jax.sharding import PartitionSpec as P

HEADS = 64
LATENT = 512
PAGE = 16
MAXP = 6
CAP = 4
MCAP = 4
KVW = 576
SIDE = 4

softmax_scale = 192.0 ** (-0.5)
routed_scale = 2.5
norm_eps = 1e-06
MIB = 1 << 20


def rms_rows(values, gain):
    stat = jnp.mean(values * values, axis=-1, keepdims=True)
    return values * lax.rsqrt(stat + norm_eps) * gain


def shift(value, axis, step):
    pairs = []
    for x in range(SIDE):
        for z in range(SIDE):
            to_x = (x + step) % SIDE if axis == "x" else x
            to_z = (z + step) % SIDE if axis == "z" else z
            pairs.append((x * SIDE + z, to_x * SIDE + to_z))
    return lax.ppermute(value, "expert", pairs)


def ffn_kernel(expert, count, rows, parts, *refs):
    xs = refs[:count]
    gate_hbm, up_hbm, down_hbm = refs[count : count + 3]
    outs = refs[count + 3 : 2 * count + 3]
    x_buf, w_buf, d_buf, o_buf, acc, in_sem, d_sem, out_sem = refs[2 * count + 3 :]
    depth = gate_hbm.shape[1]
    piece = depth // parts

    def loads(c):
        cut = pl.ds(pl.multiple_of(c * piece, piece), piece)
        yield pltpu.make_async_copy(
            gate_hbm.at[expert, cut], w_buf.at[cut, pl.ds(0, 128)], in_sem.at[c, 0]
        )
        yield pltpu.make_async_copy(
            up_hbm.at[expert, cut], w_buf.at[cut, pl.ds(128, 128)], in_sem.at[c, 1]
        )
        at = 0
        for i in range(count):
            yield pltpu.make_async_copy(
                xs[i].at[:, cut], x_buf.at[pl.ds(at, rows[i]), cut], in_sem.at[c, 2 + i]
            )
            at += rows[i]

    def stores(c):
        cut = pl.ds(pl.multiple_of(c * piece, piece), piece)
        at = 0
        for i in range(count):
            yield pltpu.make_async_copy(
                o_buf.at[pl.ds(at, rows[i]), cut], outs[i].at[:, cut], out_sem.at[c, i]
            )
            at += rows[i]

    for c in range(parts):
        for copy in loads(c):
            copy.start()
    down = pltpu.make_async_copy(down_hbm.at[expert], d_buf, d_sem)
    down.start()
    acc[...] = jnp.zeros_like(acc)

    @pl.loop(0, parts)
    def _(c):
        for copy in loads(c):
            copy.wait()
        cut = pl.ds(pl.multiple_of(c * piece, piece), piece)
        acc[...] += jnp.dot(x_buf[:, cut], w_buf[cut, :], preferred_element_type=jnp.float32)

    gate = acc[:, :128]
    active = (gate / (1.0 + jnp.exp(-gate)) * acc[:, 128:]).astype(jnp.bfloat16)
    down.wait()

    @pl.loop(0, parts)
    def _(c):
        cut = pl.ds(pl.multiple_of(c * piece, piece), piece)
        o_buf[:, cut] = jnp.dot(active, d_buf[:, cut], preferred_element_type=jnp.float32).astype(
            jnp.bfloat16
        )
        for copy in stores(c):
            copy.start()

    @pl.loop(0, parts)
    def _(c):
        for copy in stores(c):
            copy.wait()


def ffn(blocks, expert, w_gate, w_up, w_down):
    rows = tuple(block.shape[0] for block in blocks)
    count, total, depth, parts = len(rows), sum(rows), w_gate.shape[1], 4
    return pl.pallas_call(
        functools.partial(ffn_kernel, expert, count, rows, parts),
        out_shape=[jax.ShapeDtypeStruct(block.shape, jnp.bfloat16) for block in blocks],
        in_specs=[pl.BlockSpec(memory_space=pl.ANY)] * (count + 3),
        out_specs=[pl.BlockSpec(memory_space=pl.ANY)] * count,
        scratch_shapes=[
            pltpu.VMEM((total, depth), jnp.bfloat16),
            pltpu.VMEM((depth, 256), jnp.bfloat16),
            pltpu.VMEM((128, depth), jnp.bfloat16),
            pltpu.VMEM((total, depth), jnp.bfloat16),
            pltpu.VMEM((total, 256), jnp.float32),
            pltpu.SemaphoreType.DMA((parts, 2 + count)),
            pltpu.SemaphoreType.DMA,
            pltpu.SemaphoreType.DMA((parts, count)),
        ],
        compiler_params=pltpu.CompilerParams(vmem_limit_bytes=58 * MIB),
        cost_estimate=pl.CostEstimate(
            flops=2 * total * depth * 384,
            bytes_accessed=2 * depth * (384 + 2 * total),
            transcendentals=total * 128,
        ),
        name="ffn",
    )(*blocks, w_gate, w_up, w_down)


def attend_kernel(
    step, table, lengths, q_ref, pool_ref, more_ref, out_ref, top_ref, total_ref, wide, pages, q_buf, o_buf
):
    pair = 2 * KVW

    def split(chunk):
        chunk = chunk.astype(jnp.float32)
        return chunk[:, :640], pltpu.roll(chunk[:, 512:], KVW, 1)

    def spread(target, value, start, stride):
        for i in range(5):
            target[i, pl.ds(start, value.shape[0], stride=stride), :] = value[
                :, 128 * i : 128 * (i + 1)
            ]

    def joined(source, rows):
        lanes = [source[i, rows, :] for i in range(4)] + [source[4, rows, : KVW - LATENT]]
        return jnp.concatenate(lanes, axis=1).astype(jnp.bfloat16)

    @pl.when(pl.program_id(0) == 0)
    def _():
        for source, base in ((pool_ref, 0), (more_ref, pool_ref.shape[0])):

            @pl.loop(0, source.shape[0] // 16)
            def _(b):
                rows = pl.ds(pl.multiple_of(b * 16, 16), 16)
                for u in range(PAGE // 2):
                    even, odd = split(source[rows, pair * u : pair * (u + 1)])
                    spread(wide, even, 2 * u, PAGE)
                    spread(wide, odd, 2 * u + 1, PAGE)
                pages[pl.ds(pl.multiple_of((base + b * 16) * PAGE, 256), 256), :] = joined(
                    wide, slice(None)
                )

    @pl.loop(0, HEADS // 2, unroll=4)
    def _(u):
        even, odd = split(q_ref[:, pl.ds(pl.multiple_of(u * pair, 128), pair)])
        spread(q_buf, even, 2 * u, HEADS)
        spread(q_buf, odd, 2 * u + 1, HEADS)

    first = pl.program_id(0) * step
    for r in range(step):
        row = first + r
        keys = jnp.concatenate(
            [
                pages[pl.ds(pl.multiple_of(table[row * MAXP + p] * PAGE, PAGE), PAGE), :]
                for p in range(MAXP)
            ],
            axis=0,
        )
        query = joined(q_buf, slice(r * HEADS, (r + 1) * HEADS))
        scores = (
            lax.dot_general(
                keys, query, (((1,), (1,)), ((), ())), preferred_element_type=jnp.float32
            )
            * softmax_scale
        )
        valid = lax.broadcasted_iota(jnp.int32, scores.shape, 0) < lengths[row]
        scores = jnp.where(valid, scores, -1e30)
        top = jnp.max(scores, axis=0, keepdims=True)
        expo = jnp.where(valid, jnp.exp(scores - top), 0.0)
        total = jnp.sum(expo, axis=0, keepdims=True)
        probs = (expo / total).astype(jnp.bfloat16)
        result = lax.dot_general(
            probs, keys[:, :LATENT], (((0,), (0,)), ((), ())), preferred_element_type=jnp.float32
        )
        for i in range(4):
            o_buf[i, r * HEADS : (r + 1) * HEADS, :] = result[:, 128 * i : 128 * (i + 1)]
        top_ref[r : r + 1, :] = top
        total_ref[r : r + 1, :] = total

    @pl.loop(0, HEADS, unroll=4)
    def _(h):
        for i in range(4):
            out_ref[:, pl.ds(pl.multiple_of(h * LATENT + 128 * i, 128), 128)] = o_buf[
                i, pl.ds(h, step, stride=HEADS), :
            ].astype(jnp.bfloat16)


def attend_cached(queries, pool, more, page_table, kv_lengths):
    rows, step = queries.shape[0], 16
    entries = (pool.shape[0] + more.shape[0]) * PAGE
    whole = lambda i, t, n: (0, 0)
    block = lambda i, t, n: (i, 0)
    return pl.pallas_call(
        functools.partial(attend_kernel, step),
        out_shape=[
            jax.ShapeDtypeStruct((rows, HEADS * LATENT), jnp.bfloat16),
            jax.ShapeDtypeStruct((rows, HEADS), jnp.float32),
            jax.ShapeDtypeStruct((rows, HEADS), jnp.float32),
        ],
        grid_spec=pltpu.PrefetchScalarGridSpec(
            num_scalar_prefetch=2,
            grid=(rows // step,),
            in_specs=[
                pl.BlockSpec((step, queries.shape[1]), block),
                pl.BlockSpec(pool.shape, whole),
                pl.BlockSpec(more.shape, whole),
            ],
            out_specs=[
                pl.BlockSpec((step, HEADS * LATENT), block),
                pl.BlockSpec((step, HEADS), block),
                pl.BlockSpec((step, HEADS), block),
            ],
            scratch_shapes=[
                pltpu.VMEM((5, 16 * PAGE, 128), jnp.float32),
                pltpu.VMEM((entries, KVW), jnp.bfloat16),
                pltpu.VMEM((5, step * HEADS, 128), jnp.float32),
                pltpu.VMEM((4, step * HEADS, 128), jnp.float32),
            ],
        ),
        compiler_params=pltpu.CompilerParams(vmem_limit_bytes=58 * MIB),
        cost_estimate=pl.CostEstimate(
            flops=2 * rows * HEADS * MAXP * PAGE * (KVW + LATENT),
            bytes_accessed=2 * (queries.size + entries * KVW + rows * HEADS * LATENT),
            transcendentals=rows * HEADS * MAXP * PAGE,
        ),
        name="attend_cached",
    )(page_table.reshape(rows * MAXP), kv_lengths, queries, pool, more)


def pack_kernel(own, below, above, far, low, high, sem):
    n = own.shape[0]
    copies = [
        pltpu.make_async_copy(source, target.at[pl.ds(at, n)], sem.at[i])
        for i, (source, target, at) in enumerate(
            ((own, low, 0), (below, low, n), (above, high, 0), (far, high, n))
        )
    ]
    for copy in copies:
        copy.start()
    for copy in copies:
        copy.wait()


def pack(own, below, above, far):
    shape = jax.ShapeDtypeStruct((2 * own.shape[0], own.shape[1]), own.dtype)
    hbm = pl.BlockSpec(memory_space=pl.ANY)
    return pl.pallas_call(
        pack_kernel,
        out_shape=[shape, shape],
        in_specs=[hbm] * 4,
        out_specs=[hbm] * 2,
        scratch_shapes=[pltpu.SemaphoreType.DMA((4,))],
        compiler_params=pltpu.CompilerParams(vmem_limit_bytes=58 * MIB),
        cost_estimate=pl.CostEstimate(
            flops=0, bytes_accessed=16 * own.size, transcendentals=0
        ),
        name="pack",
    )(own, below, above, far)


def tail_kernel(
    parts,
    hidden_ref,
    back_ref,
    gain_ref,
    cos_ref,
    sin_ref,
    top_ref,
    total_ref,
    place_ref,
    w_hbm,
    q_hbm,
    o_hbm,
    hidden_out_ref,
    out_ref,
    w_buf,
    q_buf,
    o_buf,
    key_buf,
    own_buf,
    keep_buf,
    w_sem,
    q_sem,
    o_sem,
):
    width = hidden_ref.shape[1]
    piece = width // parts
    q_piece = q_hbm.shape[1] // parts_q
    o_piece = o_hbm.shape[1] // parts_q
    w_loads, q_loads, o_loads = [], [], []
    for c in range(parts):
        cut = pl.ds(c * piece, piece)
        w_loads.append(pltpu.make_async_copy(w_hbm.at[cut], w_buf.at[cut], w_sem.at[c]))
    for c in range(parts_q):
        cut = pl.ds(c * q_piece, q_piece)
        q_loads.append(pltpu.make_async_copy(q_hbm.at[:, cut], q_buf.at[:, cut], q_sem.at[c]))
        cut = pl.ds(c * o_piece, o_piece)
        o_loads.append(pltpu.make_async_copy(o_hbm.at[:, cut], o_buf.at[:, cut], o_sem.at[c]))
    for copy in w_loads + q_loads + o_loads:
        copy.start()
    place = place_ref[...]
    pick = (place != 0.0).astype(jnp.bfloat16)
    weight = jnp.sum(place, axis=1, keepdims=True)
    projected = jnp.zeros((hidden_ref.shape[0], KVW), jnp.float32)
    for c in range(parts):
        cut = slice(c * piece, (c + 1) * piece)
        picked = jnp.dot(pick, back_ref[:, cut], preferred_element_type=jnp.float32)
        hidden = (hidden_ref[:, cut].astype(jnp.float32) + weight * picked).astype(jnp.bfloat16)
        hidden_out_ref[:, cut] = hidden
        w_loads[c].wait()
        projected += jnp.dot(hidden, w_buf[cut, :], preferred_element_type=jnp.float32)
    latent = rms_rows(projected[:, :LATENT], gain_ref[...])
    first = projected[:, LATENT : LATENT + 32]
    second = projected[:, LATENT + 32 :]
    cosine, sine = cos_ref[...], sin_ref[...]
    new_key = jnp.concatenate(
        [latent, first * cosine - second * sine, second * cosine + first * sine], axis=1
    )
    new_key = new_key.astype(jnp.bfloat16).astype(jnp.float32)
    key_buf[...] = jnp.concatenate([new_key, new_key], axis=1)
    lane = lax.broadcasted_iota(jnp.int32, (8, 128), 1)
    head = lax.broadcasted_iota(jnp.int32, (8, HEADS), 1)
    blocks = hidden_ref.shape[0] // 8
    own_buf[...] = jnp.zeros_like(own_buf)
    for copy in q_loads:
        copy.wait()

    @pl.loop(0, HEADS // 2)
    def _(j):
        for b in range(blocks):
            rows = slice(8 * b, 8 * b + 8)
            cut = pl.ds(pl.multiple_of(j * 2 * KVW, 2 * KVW), 2 * KVW)
            product = q_buf[rows, cut].astype(jnp.float32) * key_buf[rows, :]
            tiles = [product[:, 128 * i : 128 * (i + 1)] for i in range(9)]
            low = tiles[0] + tiles[1] + tiles[2] + tiles[3] + jnp.where(lane < 64, tiles[4], 0.0)
            high = tiles[5] + tiles[6] + tiles[7] + tiles[8] + jnp.where(lane < 64, 0.0, tiles[4])
            low = jnp.sum(low, axis=1, keepdims=True)
            high = jnp.sum(high, axis=1, keepdims=True)
            own_buf[rows, :] += jnp.where(head == 2 * j, low, 0.0) + jnp.where(
                head == 2 * j + 1, high, 0.0
            )

    own = own_buf[...] * softmax_scale
    top_old = top_ref[...]
    top = jnp.maximum(top_old, own)
    part = total_ref[...] * jnp.exp(top_old - top)
    part_own = jnp.exp(own - top)
    inverse = 1.0 / (part + part_own)
    keep_buf[...] = part * inverse
    own_buf[...] = (part_own * inverse).astype(jnp.bfloat16).astype(jnp.float32)
    for copy in o_loads:
        copy.wait()

    @pl.loop(0, HEADS)
    def _(h):
        for b in range(blocks):
            rows = slice(8 * b, 8 * b + 8)
            keep = jnp.sum(jnp.where(head == h, keep_buf[rows, :], 0.0), axis=1, keepdims=True)
            add = jnp.sum(jnp.where(head == h, own_buf[rows, :], 0.0), axis=1, keepdims=True)
            cut = pl.ds(pl.multiple_of(h * LATENT, LATENT), LATENT)
            out_ref[rows, cut] = (
                o_buf[rows, cut].astype(jnp.float32) * keep + add * key_buf[rows, :LATENT]
            ).astype(jnp.bfloat16)


parts_q = 4


def tail(hidden_in, back, kv_gain, cosine, sine, top, total, place_weight, w_all, queries, o):
    rows, width = hidden_in.shape
    parts = 7
    vmem = pl.BlockSpec(memory_space=pltpu.VMEM)
    hbm = pl.BlockSpec(memory_space=pl.ANY)
    return pl.pallas_call(
        functools.partial(tail_kernel, parts),
        out_shape=[
            jax.ShapeDtypeStruct((rows, width), jnp.bfloat16),
            jax.ShapeDtypeStruct((rows, HEADS * LATENT), jnp.bfloat16),
        ],
        in_specs=[vmem] * 8 + [hbm] * 3,
        out_specs=[vmem] * 2,
        scratch_shapes=[
            pltpu.VMEM(w_all.shape, jnp.bfloat16),
            pltpu.VMEM(queries.shape, jnp.bfloat16),
            pltpu.VMEM(o.shape, jnp.bfloat16),
            pltpu.VMEM((rows, 2 * KVW), jnp.float32),
            pltpu.VMEM((rows, HEADS), jnp.float32),
            pltpu.VMEM((rows, HEADS), jnp.float32),
            pltpu.SemaphoreType.DMA((parts,)),
            pltpu.SemaphoreType.DMA((parts_q,)),
            pltpu.SemaphoreType.DMA((parts_q,)),
        ],
        compiler_params=pltpu.CompilerParams(vmem_limit_bytes=48 * MIB),
        cost_estimate=pl.CostEstimate(
            flops=2 * rows * width * KVW,
            bytes_accessed=2 * (w_all.size + queries.size + 2 * o.size),
            transcendentals=rows * HEADS * 2,
        ),
        name="tail",
    )(
        hidden_in,
        back,
        kv_gain.reshape(1, LATENT),
        cosine,
        sine,
        top,
        total,
        place_weight,
        w_all,
        queries,
        o,
    )


def plus(*terms):
    total = terms[0].astype(jnp.float32)
    for term in terms[1:]:
        total = total + term.astype(jnp.float32)
    return total.astype(jnp.bfloat16)


def after(values, *others):
    return lax.optimization_barrier((values, others))[0]


def body(
    hidden_in,
    norm_gain,
    route_logits,
    expert_ids,
    w_gate,
    w_up,
    w_down,
    w_latent,
    kv_gain,
    queries,
    page_pool,
    page_table,
    kv_lengths,
    migration,
):
    dp_count = lax.axis_size("dp")
    ex_count = lax.axis_size("expert")
    row_count = hidden_in.shape[0]
    local_experts = w_gate.shape[0]
    window = local_experts * dp_count
    width = hidden_in.shape[1]
    x_wide = hidden_in.astype(jnp.float32)
    normed = rms_rows(x_wide, norm_gain).astype(jnp.bfloat16)
    in_window = expert_ids < window
    has = jnp.any(in_window, axis=1)
    chosen = jnp.sum(jnp.where(in_window, expert_ids, 0), axis=1)
    sigma = jax.nn.sigmoid(route_logits)
    weight = (
        routed_scale * jnp.sum(jnp.where(in_window, sigma, 0.0), axis=1) / jnp.sum(sigma, axis=1)
    )
    onehot = ((chosen[:, None] == jnp.arange(window)[None, :]) & has[:, None]).astype(jnp.int32)
    rank = jnp.cumsum(onehot, axis=0) - onehot
    slot = jnp.sum(rank * onehot, axis=1)
    slots = local_experts * CAP
    place = chosen * CAP + slot
    pick = (place[:, None] == jnp.arange(window * CAP)[None, :]) & has[:, None]
    packed = jnp.einsum(
        "rs,rd->sd", pick.astype(jnp.bfloat16), normed, preferred_element_type=jnp.float32
    ).astype(jnp.bfloat16)
    place_weight = jnp.where(pick, weight[:, None], 0.0)
    arrived = lax.all_to_all(
        packed.reshape(dp_count, slots, width), "dp", split_axis=0, concat_axis=0, tiled=True
    )
    outgoing = jnp.take(page_pool, migration.reshape(dp_count * MCAP), axis=0, mode="clip")
    arrived = after(arrived, outgoing)
    axes = (("z", "x"), ("x", "z"))
    both = range(local_experts)
    rows = [
        arrived[:, k * CAP : (k + 1) * CAP].reshape(dp_count * CAP, width) for k in both
    ]

    incoming = lax.all_to_all(
        outgoing.reshape(dp_count, MCAP, page_pool.shape[1]),
        "dp",
        split_axis=0,
        concat_axis=0,
        tiled=True,
    ).reshape(dp_count * MCAP, page_pool.shape[1])
    below = [shift(rows[k], axes[k][0], 1) for k in both]
    above = [shift(rows[k], axes[k][0], -1) for k in both]
    below, above = after((below, above))
    beyond = [shift(below[k], axes[k][0], 1) for k in both]
    beyond = after(beyond)
    low, high = zip(*(pack(rows[k], below[k], above[k], beyond[k]) for k in both))
    low, high = after((low, high))
    below_low = [shift(low[k], axes[k][1], 1) for k in both]
    above_high = [shift(high[k], axes[k][1], -1) for k in both]
    below_high = [shift(high[k], axes[k][1], 1) for k in both]
    above_low = [shift(low[k], axes[k][1], -1) for k in both]
    query, pool = after((queries, page_pool), low, high)
    cached, top, total = attend_cached(query, pool, incoming, page_table, kv_lengths)
    w_local = after(w_latent, cached)
    spread = lax.all_to_all(
        jnp.broadcast_to(w_local[None], (ex_count,) + w_latent.shape),
        "expert",
        split_axis=0,
        concat_axis=0,
        tiled=True,
    )
    below_low, above_high = after((below_low, above_high), cached)
    far_low = [shift(below_low[k], axes[k][1], 1) for k in both]
    far_high = [shift(above_high[k], axes[k][1], -1) for k in both]
    w_all = lax.all_gather(
        spread.reshape(ex_count * w_latent.shape[0], KVW), "dp", axis=0, tiled=True
    )
    weights = (w_gate, w_up, w_down)
    y_own = [ffn([low[k], high[k]], k, *weights) for k in both]
    below_high, above_low = after((below_high, above_low), y_own)
    y_side = [
        ffn([below_low[k], below_high[k], above_low[k], above_high[k]], k, *weights) for k in both
    ]
    early_up = [shift(y_side[k][3], axes[k][1], 1) for k in both]
    early_down = [shift(y_side[k][0], axes[k][1], -1) for k in both]
    far_low, far_high = after((far_low, far_high), y_side, spread)
    y_far = [ffn([far_low[k], far_high[k]], k, *weights) for k in both]
    relay_up = [shift(y_far[k][0], axes[k][1], 1) for k in both]
    relay_down = [shift(y_far[k][1], axes[k][1], -1) for k in both]
    early_up, early_down, relay_up, relay_down = after((early_up, early_down, relay_up, relay_down))
    late_up = [shift(plus(y_side[k][2], relay_up[k]), axes[k][1], 1) for k in both]
    late_down = [shift(plus(y_side[k][1], relay_down[k]), axes[k][1], -1) for k in both]
    late_up, late_down = after((late_up, late_down), w_all)
    n = rows[0].shape[0]
    terms_low = [(y_own[k][0], late_up[k], early_down[k]) for k in both]
    terms_high = [(y_own[k][1], early_up[k], late_down[k]) for k in both]
    for_far = [plus(*(term[n:] for term in terms_high[k])) for k in both]
    for_below = [plus(*(term[n:] for term in terms_low[k])) for k in both]
    relayed = [shift(for_far[k], axes[k][0], 1) for k in both]
    from_above = [shift(for_below[k], axes[k][0], -1) for k in both]
    relayed, from_above = after((relayed, from_above))
    from_below = [
        shift(plus(*(term[:n] for term in terms_high[k]), relayed[k]), axes[k][0], 1) for k in both
    ]
    from_below = after(from_below)
    finished = [
        plus(*(term[:n] for term in terms_low[k]), from_below[k], from_above[k]).reshape(
            dp_count, CAP, width
        )
        for k in both
    ]
    back = lax.all_to_all(
        jnp.concatenate(finished, axis=1), "dp", split_axis=0, concat_axis=0, tiled=True
    ).reshape(window * CAP, width)

    half = (KVW - LATENT) // 2
    freq = 10000.0 ** (-jnp.arange(half, dtype=jnp.float32) / half)
    angle = kv_lengths.astype(jnp.float32)[:, None] * freq[None, :]
    return tuple(
        tail(
            hidden_in,
            back,
            kv_gain,
            jnp.cos(angle),
            jnp.sin(angle),
            top,
            total,
            place_weight,
            w_all,
            queries,
            cached,
        )
    )


def solution(mesh):
    return jax.shard_map(
        body,
        mesh=mesh,
        in_specs=(
            P(("dp", "expert"), None),
            P(),
            P(("dp", "expert"), None),
            P(("dp", "expert"), None),
            P("dp", None, "expert"),
            P("dp", None, "expert"),
            P("dp", "expert", None),
            P(("dp", "expert"), None),
            P(),
            P(("dp", "expert"), None),
            P(("dp", "expert"), None),
            P(("dp", "expert"), None),
            P(("dp", "expert")),
            P("dp", "expert", None, None),
        ),
        out_specs=(P(("dp", "expert"), None), P(("dp", "expert"), None)),
        check_vma=False,
    )
```

profile of v0, /device:TPU:1, one launch (start us, length us, event | category | flops | bytes accessed | tf_op | source)
XLA Modules:
  0.0 469.0 jit_solution(6662176826465948536)
XLA Ops:
  10.5 2.8 fusion
  13.2 6.0 %all-to-all-start = ((bf16[8,8,7168]{2,1,0:T(8,128)(2,1)}), bf16[8,8,7168]{2,1,0:T(8,128)(2,1)S(1)}, u32[]{:S(2)}, u32[]{:S(2)}) async-start(bf16[8,8,7168]{2,1,0:T(8,128)(2,1)} %fusion), calls=%async_computation | async-start | bytes 1835008 | tf_op jit(solution)/shard_map/all_to_all | solution.py:491
  21.1 11.8 %all-to-all-done = bf16[8,8,7168]{2,1,0:T(8,128)(2,1)S(1)} async-done(((bf16[8,8,7168]{2,1,0:T(8,128)(2,1)}), bf16[8,8,7168]{2,1,0:T(8,128)(2,1)S(1)}, u32[]{:S(2)}, u32[]{:S(2)}) %all-to-all-start) | async-done | bytes 917536 | tf_op jit(solution)/shard_map/all_to_all | solution.py:491
  41.1 5.2 %all-to-all-start.1 = ((bf16[8,4,9216]{2,1,0:T(4,128)(2,1)}), bf16[8,4,9216]{2,1,0:T(4,128)(2,1)S(1)}, u32[]{:S(2)}, u32[]{:S(2)}) async-start(bf16[8,4,9216]{2,1,0:T(4,128)(2,1)} %reshape.74), calls=%async_computation.1 | async-start | bytes 1179648 | tf_op jit(solution)/shard_map/all_to_all | solution.py:502
  51.2 5.2 %all-to-all-done.1 = bf16[8,4,9216]{2,1,0:T(4,128)(2,1)S(1)} async-done(((bf16[8,4,9216]{2,1,0:T(4,128)(2,1)}), bf16[8,4,9216]{2,1,0:T(4,128)(2,1)S(1)}, u32[]{:S(2)}, u32[]{:S(2)}) %all-to-all-start.1) | async-done | bytes 589856 | tf_op jit(solution)/shard_map/all_to_all | solution.py:502
  57.4 2.7 collective-permute-done.4.far
  60.2 56.7 %pack.3 = (bf16[64,7168]{1,0:T(8,128)(2,1)}, bf16[64,7168]{1,0:T(8,128)(2,1)}) custom-call(bf16[32,7168]{1,0:T(8,128)(2,1)} %copy-done.8, bf16[32,7168]{1,0:T(8,128)(2,1)} %copy-done.35, bf16[32,7168]{1,0:T(8,128)(2,1)} %copy-done.36, bf16[32,7168]{1,0:T(8,128)(2,1)} %collective-permute-done.5.far), custom_call_target="tpu_custom_call" | custom-call | bytes 3670016 | tf_op jit(solution)/shard_map/pack/pallas_call | solution.py:271
  116.9 56.7 %pack.2 = (bf16[64,7168]{1,0:T(8,128)(2,1)}, bf16[64,7168]{1,0:T(8,128)(2,1)}) custom-call(bf16[32,7168]{1,0:T(8,128)(2,1)} %copy-done.7, bf16[32,7168]{1,0:T(8,128)(2,1)} %copy-done.33, bf16[32,7168]{1,0:T(8,128)(2,1)} %copy-done.34, bf16[32,7168]{1,0:T(8,128)(2,1)} %collective-permute-done.4.far), custom_call_target="tpu_custom_call" | custom-call | bytes 3670016 | tf_op jit(solution)/shard_map/pack/pallas_call | solution.py:271
  173.7 44.2 %attend_cached.1 = (bf16[64,32768]{1,0:T(8,128)(2,1)}, f32[64,64]{1,0:T(8,128)}, f32[64,64]{1,0:T(8,128)}) custom-call(s32[384]{0:T(512)} %reshape.73.table, s32[64]{0:T(128)} %lengths.1, bf16[64,36864]{1,0:T(8,128)(2,1)} %q_hbm.1, bf16[128,9216]{1,0:T(8,128)(2,1)} %pool_ref, bf16[32,9216]{1,0:T(8,128)(2,1)} %reshape.75.more_ref), custom_call_target="tpu_custom_call" | custom-call | flops 855638016 | bytes 11862016 | tf_op jit(solution)/shard_map/attend_cached/pallas_call | solution.py:217
  218.0 18.8 %all_to_all.20 = bf16[16,56,576]{2,1,0:T(8,128)(2,1)} all-to-all(bf16[16,56,576]{2,1,0:T(8,128)(2,1)S(1)} %broadcast_in_dim.28), channel_id=1, replica_groups=mesh['dp'=8,'expert'=16] {'expert'}, dimensions={0} | all-to-all | bytes 2064384 | tf_op jit(solution)/shard_map/all_to_all | solution.py:523
  242.3 12.4 %collective-permute-done.6.refs_0_ = bf16[64,7168]{1,0:T(8,128)(2,1)S(1)} collective-permute-done((bf16[64,7168]{1,0:T(8,128)(2,1)}, bf16[64,7168]{1,0:T(8,128)(2,1)S(1)}, u32[]{:S(2)}, u32[]{:S(2)}) %collective-permute-start.6) | collective-permute-done | bytes 917536 | tf_op jit(solution)/shard_map/ppermute | solution.py:37
  258.9 15.5 %collective-permute-done.10.refs_1_ = bf16[64,7168]{1,0:T(8,128)(2,1)S(1)} collective-permute-done((bf16[64,7168]{1,0:T(8,128)(2,1)}, bf16[64,7168]{1,0:T(8,128)(2,1)S(1)}, u32[]{:S(2)}, u32[]{:S(2)}) %collective-permute-start.10) | collective-permute-done | bytes 917536 | tf_op jit(solution)/shard_map/ppermute | solution.py:37
  275.0 5.5 %ffn.6 = (bf16[64,7168]{1,0:T(8,128)(2,1)}, bf16[64,7168]{1,0:T(8,128)(2,1)}) custom-call(bf16[64,7168]{1,0:T(8,128)(2,1)} %get-tuple-element.80.refs_0_, bf16[64,7168]{1,0:T(8,128)(2,1)} %get-tuple-element.81.refs_1_, bf16[2,7168,128]{2,1,0:T(8,128)(2,1)} %refs_2_.7, bf16[2,7168,128]{2,1,0:T(8,128)(2,1)} %refs_3_.7, bf16[2,128,7168]{2,1,0:T(8,128)(2,1)} %refs_4_.11), custom_call_target="tpu_custom_call" | custom-call | flops 704643072 | bytes 9175040 | tf_op jit(solution)/shard_map/ffn/pallas_call | solution.py:108
  280.5 5.3 %ffn.7 = (bf16[64,7168]{1,0:T(8,128)(2,1)}, bf16[64,7168]{1,0:T(8,128)(2,1)}) custom-call(bf16[64,7168]{1,0:T(8,128)(2,1)} %get-tuple-element.83.refs_0_, bf16[64,7168]{1,0:T(8,128)(2,1)} %get-tuple-element.84.refs_1_, bf16[2,7168,128]{2,1,0:T(8,128)(2,1)} %refs_2_.7, bf16[2,7168,128]{2,1,0:T(8,128)(2,1)} %refs_3_.7, bf16[2,128,7168]{2,1,0:T(8,128)(2,1)} %refs_4_.11), custom_call_target="tpu_custom_call" | custom-call | flops 704643072 | bytes 9175040 | tf_op jit(solution)/shard_map/ffn/pallas_call | solution.py:108
  288.6 6.6 %ffn.9 = (bf16[64,7168]{1,0:T(8,128)(2,1)}, bf16[64,7168]{1,0:T(8,128)(2,1)}, bf16[64,7168]{1,0:T(8,128)(2,1)}, bf16[64,7168]{1,0:T(8,128)(2,1)}) custom-call(bf16[64,7168]{1,0:T(8,128)(2,1)} %copy-done.11, bf16[64,7168]{1,0:T(8,128)(2,1)} %collective-permute-done.11.refs_1_, bf16[64,7168]{1,0:T(8,128)(2,1)} %collective-permute-done.13.refs_2_, ...), custom_call_target="tpu_custom_call" | custom-call | flops 1409286144 | bytes 12845056 | tf_op jit(solution)/shard_map/ffn/pallas_call | solution.py:108
  295.4 6.6 %ffn.8 = (bf16[64,7168]{1,0:T(8,128)(2,1)}, bf16[64,7168]{1,0:T(8,128)(2,1)}, bf16[64,7168]{1,0:T(8,128)(2,1)}, bf16[64,7168]{1,0:T(8,128)(2,1)}) custom-call(bf16[64,7168]{1,0:T(8,128)(2,1)} %copy-done.12, bf16[64,7168]{1,0:T(8,128)(2,1)} %copy-done.13, bf16[64,7168]{1,0:T(8,128)(2,1)} %copy-done.14, bf16[64,7168]{1,0:T(8,128)(2,1)} %copy-done.10, ...), custom_call_target="tpu_custom_call" | custom-call | flops 1409286144 | bytes 12845056 | tf_op jit(solution)/shard_map/ffn/pallas_call | solution.py:108
  302.0 2.7 collective-permute-start.17
  307.4 5.3 %ffn.11 = (bf16[64,7168]{1,0:T(8,128)(2,1)}, bf16[64,7168]{1,0:T(8,128)(2,1)}) custom-call(bf16[64,7168]{1,0:T(8,128)(2,1)} %collective-permute-done.19.refs_0_, bf16[64,7168]{1,0:T(8,128)(2,1)} %collective-permute-done.21.refs_1_, bf16[2,7168,128]{2,1,0:T(8,128)(2,1)} %refs_2_.7, bf16[2,7168,128]{2,1,0:T(8,128)(2,1)} %refs_3_.7, bf16[2,128,7168]{2,1,0:T(8,128)(2,1)} %refs_4_.11), custom_call_target="tpu_custom_call" | custom-call | flops 704643072 | bytes 9175040 | tf_op jit(solution)/shard_map/ffn/pallas_call | solution.py:108
  312.8 5.4 %ffn.10 = (bf16[64,7168]{1,0:T(8,128)(2,1)}, bf16[64,7168]{1,0:T(8,128)(2,1)}) custom-call(bf16[64,7168]{1,0:T(8,128)(2,1)} %collective-permute-done.18.refs_0_, bf16[64,7168]{1,0:T(8,128)(2,1)} %copy-done.16, bf16[2,7168,128]{2,1,0:T(8,128)(2,1)} %refs_2_.7, bf16[2,7168,128]{2,1,0:T(8,128)(2,1)} %refs_3_.7, bf16[2,128,7168]{2,1,0:T(8,128)(2,1)} %refs_4_.11), custom_call_target="tpu_custom_call" | custom-call | flops 704643072 | bytes 9175040 | tf_op jit(solution)/shard_map/ffn/pallas_call | solution.py:108
  320.9 3.4 collective-permute-done.17
  327.0 5.9 %collective-permute-done.23 = bf16[64,7168]{1,0:T(8,128)(2,1)S(1)} collective-permute-done((bf16[64,7168]{1,0:T(8,128)(2,1)}, bf16[64,7168]{1,0:T(8,128)(2,1)S(1)}, u32[]{:S(2)}, u32[]{:S(2)}) %collective-permute-start.23) | collective-permute-done | bytes 917536 | tf_op jit(solution)/shard_map/ppermute | solution.py:37
  333.0 11.0 %collective-permute-done.25 = bf16[64,7168]{1,0:T(8,128)(2,1)S(1)} collective-permute-done((bf16[64,7168]{1,0:T(8,128)(2,1)}, bf16[64,7168]{1,0:T(8,128)(2,1)S(1)}, u32[]{:S(2)}, u32[]{:S(2)}) %collective-permute-start.25) | collective-permute-done | bytes 917536 | tf_op jit(solution)/shard_map/ppermute | solution.py:37
  344.2 3.4 collective-permute-start.29
  351.0 9.8 %collective-permute-done.29 = bf16[64,7168]{1,0:T(8,128)(2,1)} collective-permute-done((bf16[64,7168]{1,0:T(8,128)(2,1)S(1)}, bf16[64,7168]{1,0:T(8,128)(2,1)}, u32[]{:S(2)}, u32[]{:S(2)}) %collective-permute-start.29) | collective-permute-done | bytes 917536 | tf_op jit(solution)/shard_map/ppermute | solution.py:37
  360.7 3.1 collective-permute-done.28
  368.6 3.4 collective-permute-start.32
  374.8 3.2 collective-permute-done.33
  380.0 7.2 %collective-permute-done.31 = bf16[32,7168]{1,0:T(8,128)(2,1)S(1)} collective-permute-done((bf16[32,7168]{1,0:T(8,128)(2,1)S(1)}, bf16[32,7168]{1,0:T(8,128)(2,1)S(1)}, u32[]{:S(2)}, u32[]{:S(2)}) %collective-permute-start.31) | collective-permute-done | bytes 458784 | tf_op jit(solution)/shard_map/ppermute | solution.py:37
  390.7 7.2 %collective-permute-done.35 = bf16[32,7168]{1,0:T(8,128)(2,1)S(1)} collective-permute-done((bf16[32,7168]{1,0:T(8,128)(2,1)S(1)}, bf16[32,7168]{1,0:T(8,128)(2,1)S(1)}, u32[]{:S(2)}, u32[]{:S(2)}) %collective-permute-start.35) | collective-permute-done | bytes 458784 | tf_op jit(solution)/shard_map/ppermute | solution.py:37
  402.7 25.9 %all-to-all-start.3 = ((bf16[8,8,7168]{2,1,0:T(8,128)(2,1)}), bf16[8,8,7168]{2,1,0:T(8,128)(2,1)S(1)}, u32[]{:S(2)}, u32[]{:S(2)}) async-start(bf16[8,8,7168]{2,1,0:T(8,128)(2,1)} %pad_maximum_fusion), calls=%async_computation.3 | async-start | bytes 1835008 | tf_op jit(solution)/shard_map/all_to_all | solution.py:570
  429.1 13.3 %all-to-all-done.3 = bf16[8,8,7168]{2,1,0:T(8,128)(2,1)S(1)} async-done(((bf16[8,8,7168]{2,1,0:T(8,128)(2,1)}), bf16[8,8,7168]{2,1,0:T(8,128)(2,1)S(1)}, u32[]{:S(2)}, u32[]{:S(2)}) %all-to-all-start.3) | async-done | bytes 917536 | tf_op jit(solution)/shard_map/all_to_all | solution.py:570
  444.6 17.6 %tail.1 = (bf16[64,7168]{1,0:T(8,128)(2,1)}, bf16[64,32768]{1,0:T(8,128)(2,1)}) custom-call(bf16[64,7168]{1,0:T(8,128)(2,1)S(1)} %copy-done, bf16[64,7168]{1,0:T(8,128)(2,1)S(1)} %bitcast.7, f32[1,512]{1,0:T(1,128)S(1)} %bitcast.8, f32[64,32]{1,0:T(8,128)S(1)} %get-tuple-element.141.cos_ref, f32[64,32]{1,0:T(8,128)S(1)} %get-tuple-element.140.sin_ref, ...), custom_call_target="tpu_custom_call" | custom-call | flops 528482304 | bytes 21364736 | tf_op jit(solution)/shard_map/tail/pallas_call | solution.py:398
  (187 shorter events, 64.3 us)
Async XLA Ops:
  13.2 19.7 %all-to-all-start = ((bf16[8,8,7168]{2,1,0:T(8,128)(2,1)}), bf16[8,8,7168]{2,1,0:T(8,128)(2,1)S(1)}, u32[]{:S(2)}, u32[]{:S(2)}) async-start(bf16[8,8,7168]{2,1,0:T(8,128)(2,1)} %fusion), calls=%async_computation | async-start | bytes 1835008 | tf_op jit(solution)/shard_map/all_to_all | solution.py:491
  33.3 13.8 %collective-permute-start = (bf16[32,7168]{1,0:T(8,128)(2,1)S(1)}, bf16[32,7168]{1,0:T(8,128)(2,1)S(1)}, u32[]{:S(2)}, u32[]{:S(2)}) collective-permute-start(bf16[32,7168]{1,0:T(8,128)(2,1)S(1)} %reshape.71.own), channel_id=1, source_target_pairs={{0,1},{1,2},{2,3},{3,0},{4,5},{5,6},{6,7},{7,4},{8,9},{9,10},{10,1... | collective-permute-start | bytes 1376264 | tf_op jit(solution)/shard_map/ppermute | solution.py:37
  41.1 15.4 %all-to-all-start.1 = ((bf16[8,4,9216]{2,1,0:T(4,128)(2,1)}), bf16[8,4,9216]{2,1,0:T(4,128)(2,1)S(1)}, u32[]{:S(2)}, u32[]{:S(2)}) async-start(bf16[8,4,9216]{2,1,0:T(4,128)(2,1)} %reshape.74), calls=%async_computation.1 | async-start | bytes 1179648 | tf_op jit(solution)/shard_map/all_to_all | solution.py:502
  46.2 317.6 %all-gather.2.cloned.1.call-start = ((), (), s32[]{:S(2)}) async-start(), calls=%async_computation.4 | async-start | bytes 10321920 | tf_op jit(solution)/shard_map/all_gather | solution.py:533
  236.8 17.9 %collective-permute-start.6 = (bf16[64,7168]{1,0:T(8,128)(2,1)}, bf16[64,7168]{1,0:T(8,128)(2,1)S(1)}, u32[]{:S(2)}, u32[]{:S(2)}) collective-permute-start(bf16[64,7168]{1,0:T(8,128)(2,1)} %get-tuple-element.80.refs_0_), channel_id=1, source_target_pairs={{0,4},{1,5},{2,6},{3,7},{4,8},{5,9},{6,10},{7,11},{8,12},{9,13},{1... | collective-permute-start | bytes 2752520 | tf_op jit(solution)/shard_map/ppermute | solution.py:37
  237.4 18.2 %collective-permute-start.7 = (bf16[64,7168]{1,0:T(8,128)(2,1)S(1)}, bf16[64,7168]{1,0:T(8,128)(2,1)S(1)}, u32[]{:S(2)}, u32[]{:S(2)}) collective-permute-start(bf16[64,7168]{1,0:T(8,128)(2,1)S(1)} %copy-done.15), channel_id=1, source_target_pairs={{0,1},{1,2},{2,3},{3,0},{4,5},{5,6},{6,7},{7,4},{8,9},{9,10},{10,1... | collective-permute-start | bytes 2752520 | tf_op jit(solution)/shard_map/ppermute | solution.py:37
  237.4 19.5 %collective-permute-start.8 = (bf16[64,7168]{1,0:T(8,128)(2,1)}, bf16[64,7168]{1,0:T(8,128)(2,1)S(1)}, u32[]{:S(2)}, u32[]{:S(2)}) collective-permute-start(bf16[64,7168]{1,0:T(8,128)(2,1)} %get-tuple-element.81.refs_1_), channel_id=1, source_target_pairs={{0,12},{1,13},{2,14},{3,15},{4,0},{5,1},{6,2},{7,3},{8,4},{9,5},{1... | collective-permute-start | bytes 2752520 | tf_op jit(solution)/shard_map/ppermute | solution.py:37
  239.9 18.0 %collective-permute-start.9 = (bf16[64,7168]{1,0:T(8,128)(2,1)}, bf16[64,7168]{1,0:T(8,128)(2,1)S(1)}, u32[]{:S(2)}, u32[]{:S(2)}) collective-permute-start(bf16[64,7168]{1,0:T(8,128)(2,1)} %get-tuple-element.84.refs_1_), channel_id=1, source_target_pairs={{0,3},{1,0},{2,1},{3,2},{4,7},{5,4},{6,5},{7,6},{8,11},{9,8},{10,9... | collective-permute-start | bytes 2752520 | tf_op jit(solution)/shard_map/ppermute | solution.py:37
  242.3 32.1 %collective-permute-start.10 = (bf16[64,7168]{1,0:T(8,128)(2,1)}, bf16[64,7168]{1,0:T(8,128)(2,1)S(1)}, u32[]{:S(2)}, u32[]{:S(2)}) collective-permute-start(bf16[64,7168]{1,0:T(8,128)(2,1)} %get-tuple-element.81.refs_1_), channel_id=1, source_target_pairs={{0,4},{1,5},{2,6},{3,7},{4,8},{5,9},{6,10},{7,11},{8,12},{9,13},{1... | collective-permute-start | bytes 2752520 | tf_op jit(solution)/shard_map/ppermute | solution.py:37
  254.7 31.1 %collective-permute-start.11 = (bf16[64,7168]{1,0:T(8,128)(2,1)}, bf16[64,7168]{1,0:T(8,128)(2,1)}, u32[]{:S(2)}, u32[]{:S(2)}) collective-permute-start(bf16[64,7168]{1,0:T(8,128)(2,1)} %get-tuple-element.84.refs_1_), channel_id=1, source_target_pairs={{0,1},{1,2},{2,3},{3,0},{4,5},{5,6},{6,7},{7,4},{8,9},{9,10},{10,1... | collective-permute-start | bytes 2752520 | tf_op jit(solution)/shard_map/ppermute | solution.py:37
  255.6 30.2 %collective-permute-start.12 = (bf16[64,7168]{1,0:T(8,128)(2,1)}, bf16[64,7168]{1,0:T(8,128)(2,1)S(1)}, u32[]{:S(2)}, u32[]{:S(2)}) collective-permute-start(bf16[64,7168]{1,0:T(8,128)(2,1)} %get-tuple-element.80.refs_0_), channel_id=1, source_target_pairs={{0,12},{1,13},{2,14},{3,15},{4,0},{5,1},{6,2},{7,3},{8,4},{9,5},{1... | collective-permute-start | bytes 2752520 | tf_op jit(solution)/shard_map/ppermute | solution.py:37
  256.9 29.0 %collective-permute-start.13 = (bf16[64,7168]{1,0:T(8,128)(2,1)}, bf16[64,7168]{1,0:T(8,128)(2,1)}, u32[]{:S(2)}, u32[]{:S(2)}) collective-permute-start(bf16[64,7168]{1,0:T(8,128)(2,1)} %get-tuple-element.83.refs_0_), channel_id=1, source_target_pairs={{0,3},{1,0},{2,1},{3,2},{4,7},{5,4},{6,5},{7,6},{8,11},{9,8},{10,9... | collective-permute-start | bytes 2752520 | tf_op jit(solution)/shard_map/ppermute | solution.py:37
  257.9 44.1 %collective-permute-start.18 = (bf16[64,7168]{1,0:T(8,128)(2,1)S(1)}, bf16[64,7168]{1,0:T(8,128)(2,1)}, u32[]{:S(2)}, u32[]{:S(2)}) collective-permute-start(bf16[64,7168]{1,0:T(8,128)(2,1)S(1)} %collective-permute-done.6.refs_0_), channel_id=1, source_target_pairs={{0,4},{1,5},{2,6},{3,7},{4,8},{5,9},{6,10},{7,11},{8,12},{9,13},{1... | collective-permute-start | bytes 2752520 | tf_op jit(solution)/shard_map/ppermute | solution.py:37
  274.4 30.4 %collective-permute-start.19 = (bf16[64,7168]{1,0:T(8,128)(2,1)S(1)}, bf16[64,7168]{1,0:T(8,128)(2,1)}, u32[]{:S(2)}, u32[]{:S(2)}) collective-permute-start(bf16[64,7168]{1,0:T(8,128)(2,1)S(1)} %collective-permute-done.7.refs_0_), channel_id=1, source_target_pairs={{0,1},{1,2},{2,3},{3,0},{4,5},{5,6},{6,7},{7,4},{8,9},{9,10},{10,1... | collective-permute-start | bytes 2752520 | tf_op jit(solution)/shard_map/ppermute | solution.py:37
  285.9 19.7 %collective-permute-start.20 = (bf16[64,7168]{1,0:T(8,128)(2,1)S(1)}, bf16[64,7168]{1,0:T(8,128)(2,1)S(1)}, u32[]{:S(2)}, u32[]{:S(2)}) collective-permute-start(bf16[64,7168]{1,0:T(8,128)(2,1)S(1)} %collective-permute-done.8.refs_3_), channel_id=1, source_target_pairs={{0,12},{1,13},{2,14},{3,15},{4,0},{5,1},{6,2},{7,3},{8,4},{9,5},{1... | collective-permute-start | bytes 2752520 | tf_op jit(solution)/shard_map/ppermute | solution.py:37
  286.3 21.2 %collective-permute-start.21 = (bf16[64,7168]{1,0:T(8,128)(2,1)S(1)}, bf16[64,7168]{1,0:T(8,128)(2,1)}, u32[]{:S(2)}, u32[]{:S(2)}) collective-permute-start(bf16[64,7168]{1,0:T(8,128)(2,1)S(1)} %collective-permute-done.9.refs_3_), channel_id=1, source_target_pairs={{0,3},{1,0},{2,1},{3,2},{4,7},{5,4},{6,5},{7,6},{8,11},{9,8},{10,9... | collective-permute-start | bytes 2752520 | tf_op jit(solution)/shard_map/ppermute | solution.py:37
  295.3 22.9 %collective-permute-start.15 = (bf16[64,7168]{1,0:T(8,128)(2,1)}, bf16[64,7168]{1,0:T(8,128)(2,1)S(1)}, u32[]{:S(2)}, u32[]{:S(2)}) collective-permute-start(bf16[64,7168]{1,0:T(8,128)(2,1)} %get-tuple-element.101), channel_id=1, source_target_pairs={{0,1},{1,2},{2,3},{3,0},{4,5},{5,6},{6,7},{7,4},{8,9},{9,10},{10,1... | collective-permute-start | bytes 2752520 | tf_op jit(solution)/shard_map/ppermute | solution.py:37
  302.0 22.3 %collective-permute-start.17 = (bf16[64,7168]{1,0:T(8,128)(2,1)}, bf16[64,7168]{1,0:T(8,128)(2,1)S(1)}, u32[]{:S(2)}, u32[]{:S(2)}) collective-permute-start(bf16[64,7168]{1,0:T(8,128)(2,1)} %get-tuple-element.103), channel_id=1, source_target_pairs={{0,3},{1,0},{2,1},{3,2},{4,7},{5,4},{6,5},{7,6},{8,11},{9,8},{10,9... | collective-permute-start | bytes 2752520 | tf_op jit(solution)/shard_map/ppermute | solution.py:37
  304.8 21.2 %collective-permute-start.14 = (bf16[64,7168]{1,0:T(8,128)(2,1)}, bf16[64,7168]{1,0:T(8,128)(2,1)S(1)}, u32[]{:S(2)}, u32[]{:S(2)}) collective-permute-start(bf16[64,7168]{1,0:T(8,128)(2,1)} %get-tuple-element.96), channel_id=1, source_target_pairs={{0,4},{1,5},{2,6},{3,7},{4,8},{5,9},{6,10},{7,11},{8,12},{9,13},{1... | collective-permute-start | bytes 2752520 | tf_op jit(solution)/shard_map/ppermute | solution.py:37
  305.6 21.4 %collective-permute-start.16 = (bf16[64,7168]{1,0:T(8,128)(2,1)}, bf16[64,7168]{1,0:T(8,128)(2,1)S(1)}, u32[]{:S(2)}, u32[]{:S(2)}) collective-permute-start(bf16[64,7168]{1,0:T(8,128)(2,1)} %get-tuple-element.102), channel_id=1, source_target_pairs={{0,12},{1,13},{2,14},{3,15},{4,0},{5,1},{6,2},{7,3},{8,4},{9,5},{1... | collective-permute-start | bytes 2752520 | tf_op jit(solution)/shard_map/ppermute | solution.py:37
  312.8 20.2 %collective-permute-start.23 = (bf16[64,7168]{1,0:T(8,128)(2,1)}, bf16[64,7168]{1,0:T(8,128)(2,1)S(1)}, u32[]{:S(2)}, u32[]{:S(2)}) collective-permute-start(bf16[64,7168]{1,0:T(8,128)(2,1)} %get-tuple-element.113), channel_id=1, source_target_pairs={{0,1},{1,2},{2,3},{3,0},{4,5},{5,6},{6,7},{7,4},{8,9},{9,10},{10,1... | collective-permute-start | bytes 2752520 | tf_op jit(solution)/shard_map/ppermute | solution.py:37
  318.3 25.7 %collective-permute-start.25 = (bf16[64,7168]{1,0:T(8,128)(2,1)}, bf16[64,7168]{1,0:T(8,128)(2,1)S(1)}, u32[]{:S(2)}, u32[]{:S(2)}) collective-permute-start(bf16[64,7168]{1,0:T(8,128)(2,1)} %get-tuple-element.115), channel_id=1, source_target_pairs={{0,3},{1,0},{2,1},{3,2},{4,7},{5,4},{6,5},{7,6},{8,11},{9,8},{10,9... | collective-permute-start | bytes 2752520 | tf_op jit(solution)/shard_map/ppermute | solution.py:37
  324.3 19.7 %collective-permute-start.22 = (bf16[64,7168]{1,0:T(8,128)(2,1)}, bf16[64,7168]{1,0:T(8,128)(2,1)S(1)}, u32[]{:S(2)}, u32[]{:S(2)}) collective-permute-start(bf16[64,7168]{1,0:T(8,128)(2,1)} %get-tuple-element.110), channel_id=1, source_target_pairs={{0,4},{1,5},{2,6},{3,7},{4,8},{5,9},{6,10},{7,11},{8,12},{9,13},{1... | collective-permute-start | bytes 2752520 | tf_op jit(solution)/shard_map/ppermute | solution.py:37
  326.0 18.0 %collective-permute-start.24 = (bf16[64,7168]{1,0:T(8,128)(2,1)}, bf16[64,7168]{1,0:T(8,128)(2,1)S(1)}, u32[]{:S(2)}, u32[]{:S(2)}) collective-permute-start(bf16[64,7168]{1,0:T(8,128)(2,1)} %get-tuple-element.114), channel_id=1, source_target_pairs={{0,12},{1,13},{2,14},{3,15},{4,0},{5,1},{6,2},{7,3},{8,4},{9,5},{1... | collective-permute-start | bytes 2752520 | tf_op jit(solution)/shard_map/ppermute | solution.py:37
  344.2 16.5 %collective-permute-start.29 = (bf16[64,7168]{1,0:T(8,128)(2,1)S(1)}, bf16[64,7168]{1,0:T(8,128)(2,1)}, u32[]{:S(2)}, u32[]{:S(2)}) collective-permute-start(bf16[64,7168]{1,0:T(8,128)(2,1)S(1)} %add_convert_fusion), channel_id=1, source_target_pairs={{0,3},{1,0},{2,1},{3,2},{4,7},{5,4},{6,5},{7,6},{8,11},{9,8},{10,9... | collective-permute-start | bytes 2752520 | tf_op jit(solution)/shard_map/ppermute | solution.py:37
  347.8 16.0 %collective-permute-start.28 = (bf16[64,7168]{1,0:T(8,128)(2,1)S(1)}, bf16[64,7168]{1,0:T(8,128)(2,1)}, u32[]{:S(2)}, u32[]{:S(2)}) collective-permute-start(bf16[64,7168]{1,0:T(8,128)(2,1)S(1)} %add_convert_fusion.1), channel_id=1, source_target_pairs={{0,12},{1,13},{2,14},{3,15},{4,0},{5,1},{6,2},{7,3},{8,4},{9,5},{1... | collective-permute-start | bytes 2752520 | tf_op jit(solution)/shard_map/ppermute | solution.py:37
  348.2 15.6 %collective-permute-start.27 = (bf16[64,7168]{1,0:T(8,128)(2,1)S(1)}, bf16[64,7168]{1,0:T(8,128)(2,1)}, u32[]{:S(2)}, u32[]{:S(2)}) collective-permute-start(bf16[64,7168]{1,0:T(8,128)(2,1)S(1)} %add_convert_fusion.2), channel_id=1, source_target_pairs={{0,1},{1,2},{2,3},{3,0},{4,5},{5,6},{6,7},{7,4},{8,9},{9,10},{10,1... | collective-permute-start | bytes 2752520 | tf_op jit(solution)/shard_map/ppermute | solution.py:37
  349.2 14.6 %collective-permute-start.26 = (bf16[64,7168]{1,0:T(8,128)(2,1)S(1)}, bf16[64,7168]{1,0:T(8,128)(2,1)}, u32[]{:S(2)}, u32[]{:S(2)}) collective-permute-start(bf16[64,7168]{1,0:T(8,128)(2,1)S(1)} %add_convert_fusion.3), channel_id=1, source_target_pairs={{0,4},{1,5},{2,6},{3,7},{4,8},{5,9},{6,10},{7,11},{8,12},{9,13},{1... | collective-permute-start | bytes 2752520 | tf_op jit(solution)/shard_map/ppermute | solution.py:37
  365.3 12.7 %collective-permute-start.33 = (bf16[32,7168]{1,0:T(8,128)(2,1)S(1)}, bf16[32,7168]{1,0:T(8,128)(2,1)S(1)}, u32[]{:S(2)}, u32[]{:S(2)}) collective-permute-start(bf16[32,7168]{1,0:T(8,128)(2,1)S(1)} %add_convert_fusion.8), channel_id=1, source_target_pairs={{0,12},{1,13},{2,14},{3,15},{4,0},{5,1},{6,2},{7,3},{8,4},{9,5},{1... | collective-permute-start | bytes 1376264 | tf_op jit(solution)/shard_map/ppermute | solution.py:37
  373.2 14.0 %collective-permute-start.31 = (bf16[32,7168]{1,0:T(8,128)(2,1)S(1)}, bf16[32,7168]{1,0:T(8,128)(2,1)S(1)}, u32[]{:S(2)}, u32[]{:S(2)}) collective-permute-start(bf16[32,7168]{1,0:T(8,128)(2,1)S(1)} %add_convert_fusion.10), channel_id=1, source_target_pairs={{0,4},{1,5},{2,6},{3,7},{4,8},{5,9},{6,10},{7,11},{8,12},{9,13},{1... | collective-permute-start | bytes 1376264 | tf_op jit(solution)/shard_map/ppermute | solution.py:37
  374.5 13.5 %collective-permute-start.30 = (bf16[32,7168]{1,0:T(8,128)(2,1)S(1)}, bf16[32,7168]{1,0:T(8,128)(2,1)S(1)}, u32[]{:S(2)}, u32[]{:S(2)}) collective-permute-start(bf16[32,7168]{1,0:T(8,128)(2,1)S(1)} %add_convert_fusion.11), channel_id=1, source_target_pairs={{0,1},{1,2},{2,3},{3,0},{4,5},{5,6},{6,7},{7,4},{8,9},{9,10},{10,1... | collective-permute-start | bytes 1376264 | tf_op jit(solution)/shard_map/ppermute | solution.py:37
  402.7 39.6 %all-to-all-start.3 = ((bf16[8,8,7168]{2,1,0:T(8,128)(2,1)}), bf16[8,8,7168]{2,1,0:T(8,128)(2,1)S(1)}, u32[]{:S(2)}, u32[]{:S(2)}) async-start(bf16[8,8,7168]{2,1,0:T(8,128)(2,1)} %pad_maximum_fusion), calls=%async_computation.3 | async-start | bytes 1835008 | tf_op jit(solution)/shard_map/all_to_all | solution.py:570
  (51 other events, 1086.0 us)
Sparse Core Ops, SparseCore 0:
  237.0 54.0 all-gather.1
where the time goes:
time: 470 us; the launch traced here: 469 us
  Pallas kernels  210 us (45%)
  waiting for transfers between devices  119 us (25%)
  starting transfers between devices  79.7 us (17%)
  blocking collectives  18.8 us (4%)
  other arithmetic  15.1 us (3%)
  between operations  14.8 us (3%)
  local copies, waits for them, and re-layouts  8.71 us (2%)
    pallas_call x2, Pallas kernels, pack(): pl.pallas_call(pack_kernel, out_shape=[shape, shape], in_specs=[hbm] * 4,...  113 us
    ppermute x36, waiting for transfers between devices, shift(): return lax.ppermute(value, 'expert', pairs)  88.8 us
    pallas_call x1, Pallas kernels, attend_cached(): pl.pallas_call(functools.partial(attend_kernel, step), out_shape=[jax.Sha...  44.2 us
    ppermute x36, starting transfers between devices, shift(): return lax.ppermute(value, 'expert', pairs)  42.6 us
    pallas_call x6, Pallas kernels, ffn(): pl.pallas_call(functools.partial(ffn_kernel, expert, count, rows, parts),...  34.7 us
    all_to_all x1, starting transfers between devices, body(): lax.all_to_all(jnp.concatenate(finished, axis=1), 'dp', split_axis=0, con...  25.9 us
    all_to_all x1, blocking collectives, body(): lax.all_to_all(jnp.broadcast_to(w_local[None], (ex_count,) + w_latent.sha...  18.8 us
    pallas_call x1, Pallas kernels, tail(): pl.pallas_call(functools.partial(tail_kernel, parts), out_shape=[jax.Shap...  17.6 us
  transfers between devices with their start and end apart: 40, of which 22 were waited for; matrix products, arithmetic and copies ran while one was open for 2% of the time, Pallas kernels for 7%

commit v1 on v0

--- a/solution.py
+++ b/solution.py
@@ -37,249 +37,241 @@
     return lax.ppermute(value, "expert", pairs)
 
 
-def ffn_kernel(expert, count, rows, parts, *refs):
-    xs = refs[:count]
-    gate_hbm, up_hbm, down_hbm = refs[count : count + 3]
-    outs = refs[count + 3 : 2 * count + 3]
-    x_buf, w_buf, d_buf, o_buf, acc, in_sem, d_sem, out_sem = refs[2 * count + 3 :]
+def ffn_kernel(count, rows, parts, *refs):
+    experts = 2
+    xs = refs[: experts * count]
+    gate_hbm, up_hbm, down_hbm = refs[experts * count : experts * count + 3]
+    outs = refs[experts * count + 3 : 2 * experts * count + 3]
+    x_buf, w_buf, d_buf, o_buf, acc, in_sem, d_sem, out_sem = refs[2 * experts * count + 3 :]
     depth = gate_hbm.shape[1]
     piece = depth // parts
 
-    def loads(c):
+    def loads(e, c):
         cut = pl.ds(pl.multiple_of(c * piece, piece), piece)
         yield pltpu.make_async_copy(
-            gate_hbm.at[expert, cut], w_buf.at[cut, pl.ds(0, 128)], in_sem.at[c, 0]
+            gate_hbm.at[e, cut], w_buf.at[e, cut, pl.ds(0, 128)], in_sem.at[e, c, 0]
         )
         yield pltpu.make_async_copy(
-            up_hbm.at[expert, cut], w_buf.at[cut, pl.ds(128, 128)], in_sem.at[c, 1]
+            up_hbm.at[e, cut], w_buf.at[e, cut, pl.ds(128, 128)], in_sem.at[e, c, 1]
         )
-        at = 0
         for i in range(count):
             yield pltpu.make_async_copy(
-                xs[i].at[:, cut], x_buf.at[pl.ds(at, rows[i]), cut], in_sem.at[c, 2 + i]
+                xs[e * count + i].at[:, cut],
+                x_buf.at[e, pl.ds(i * rows, rows), cut],
+                in_sem.at[e, c, 2 + i],
             )
-            at += rows[i]
-
-    def stores(c):
+
+    def stores(e, c):
         cut = pl.ds(pl.multiple_of(c * piece, piece), piece)
-        at = 0
         for i in range(count):
             yield pltpu.make_async_copy(
-                o_buf.at[pl.ds(at, rows[i]), cut], outs[i].at[:, cut], out_sem.at[c, i]
+                o_buf.at[e, pl.ds(i * rows, rows), cut],
+                outs[e * count + i].at[:, cut],
+                out_sem.at[e, c, i],
             )
-            at += rows[i]
-
-    for c in range(parts):
-        for copy in loads(c):
-            copy.start()
-    down = pltpu.make_async_copy(down_hbm.at[expert], d_buf, d_sem)
-    down.start()
-    acc[...] = jnp.zeros_like(acc)
-
-    @pl.loop(0, parts)
-    def _(c):
-        for copy in loads(c):
-            copy.wait()
-        cut = pl.ds(pl.multiple_of(c * piece, piece), piece)
-        acc[...] += jnp.dot(x_buf[:, cut], w_buf[cut, :], preferred_element_type=jnp.float32)
-
-    gate = acc[:, :128]
-    active = (gate / (1.0 + jnp.exp(-gate)) * acc[:, 128:]).astype(jnp.bfloat16)
-    down.wait()
-
-    @pl.loop(0, parts)
-    def _(c):
-        cut = pl.ds(pl.multiple_of(c * piece, piece), piece)
-        o_buf[:, cut] = jnp.dot(active, d_buf[:, cut], preferred_element_type=jnp.float32).astype(
-            jnp.bfloat16
-        )
-        for copy in stores(c):
-            copy.start()
-
-    @pl.loop(0, parts)
-    def _(c):
-        for copy in stores(c):
-            copy.wait()
-
-
-def ffn(blocks, expert, w_gate, w_up, w_down):
-    rows = tuple(block.shape[0] for block in blocks)
-    count, total, depth, parts = len(rows), sum(rows), w_gate.shape[1], 4
-    return pl.pallas_call(
-        functools.partial(ffn_kernel, expert, count, rows, parts),
-        out_shape=[jax.ShapeDtypeStruct(block.shape, jnp.bfloat16) for block in blocks],
-        in_specs=[pl.BlockSpec(memory_space=pl.ANY)] * (count + 3),
-        out_specs=[pl.BlockSpec(memory_space=pl.ANY)] * count,
+
+    down = []
+    for e in range(experts):
+        for c in range(parts):
+            for copy in loads(e, c):
+                copy.start()
+        down.append(pltpu.make_async_copy(down_hbm.at[e], d_buf.at[e], d_sem.at[e]))
+        down[e].start()
+    for e in range(experts):
+        acc[...] = jnp.zeros_like(acc)
+
+        @pl.loop(0, parts)
+        def _(c):
+            for copy in loads(e, c):
+                copy.wait()
+            cut = pl.ds(pl.multiple_of(c * piece, piece), piece)
+            acc[...] += jnp.dot(
+                x_buf[e, :, cut], w_buf[e, cut, :], preferred_element_type=jnp.float32
+            )
+
+        gate = acc[:, :128]
+        active = (gate / (1.0 + jnp.exp(-gate)) * acc[:, 128:]).astype(jnp.bfloat16)
+        down[e].wait()
+
+        @pl.loop(0, parts)
+        def _(c):
+            cut = pl.ds(pl.multiple_of(c * piece, piece), piece)
+            o_buf[e, :, cut] = jnp.dot(
+                active, d_buf[e, :, cut], preferred_element_type=jnp.float32
+            ).astype(jnp.bfloat16)
+            for copy in stores(e, c):
+                copy.start()
+
+    for e in range(experts):
+
+        @pl.loop(0, parts)
+        def _(c):
+            for copy in stores(e, c):
+                copy.wait()
+
+
+def ffn(blocks, w_gate, w_up, w_down):
+    experts, count = len(blocks), len(blocks[0])
+    flat = [block for part in blocks for block in part]
+    rows, depth, parts = flat[0].shape[0], w_gate.shape[1], 7
+    total = rows * count
+    done = pl.pallas_call(
+        functools.partial(ffn_kernel, count, rows, parts),
+        out_shape=[jax.ShapeDtypeStruct(block.shape, jnp.bfloat16) for block in flat],
+        in_specs=[pl.BlockSpec(memory_space=pl.ANY)] * (len(flat) + 3),
+        out_specs=[pl.BlockSpec(memory_space=pl.ANY)] * len(flat),
         scratch_shapes=[
-            pltpu.VMEM((total, depth), jnp.bfloat16),
-            pltpu.VMEM((depth, 256), jnp.bfloat16),
-            pltpu.VMEM((128, depth), jnp.bfloat16),
-            pltpu.VMEM((total, depth), jnp.bfloat16),
+            pltpu.VMEM((experts, total, depth), jnp.bfloat16),
+            pltpu.VMEM((experts, depth, 256), jnp.bfloat16),
+            pltpu.VMEM((experts, 128, depth), jnp.bfloat16),
+            pltpu.VMEM((experts, total, depth), jnp.bfloat16),
             pltpu.VMEM((total, 256), jnp.float32),
-            pltpu.SemaphoreType.DMA((parts, 2 + count)),
-            pltpu.SemaphoreType.DMA,
-            pltpu.SemaphoreType.DMA((parts, count)),
+            pltpu.SemaphoreType.DMA((experts, parts, 2 + count)),
+            pltpu.SemaphoreType.DMA((experts,)),
+            pltpu.SemaphoreType.DMA((experts, parts, count)),
         ],
         compiler_params=pltpu.CompilerParams(vmem_limit_bytes=58 * MIB),
         cost_estimate=pl.CostEstimate(
-            flops=2 * total * depth * 384,
-            bytes_accessed=2 * depth * (384 + 2 * total),
-            transcendentals=total * 128,
+            flops=2 * experts * total * depth * 384,
+            bytes_accessed=2 * experts * depth * (384 + 2 * total),
+            transcendentals=experts * total * 128,
         ),
         name="ffn",
-    )(*blocks, w_gate, w_up, w_down)
+    )(*flat, w_gate, w_up, w_down)
+    return [done[e * count : (e + 1) * count] for e in range(experts)]
 
 
 def attend_kernel(
-    step, table, lengths, q_ref, pool_ref, more_ref, out_ref, top_ref, total_ref, wide, pages, q_buf, o_buf
+    step, table, lengths, q_ref, pool_hbm, more_hbm, out_ref, top_ref, total_ref, pages, sem
 ):
-    pair = 2 * KVW
-
-    def split(chunk):
-        chunk = chunk.astype(jnp.float32)
-        return chunk[:, :640], pltpu.roll(chunk[:, 512:], KVW, 1)
-
-    def spread(target, value, start, stride):
-        for i in range(5):
-            target[i, pl.ds(start, value.shape[0], stride=stride), :] = value[
-                :, 128 * i : 128 * (i + 1)
-            ]
-
-    def joined(source, rows):
-        lanes = [source[i, rows, :] for i in range(4)] + [source[4, rows, : KVW - LATENT]]
-        return jnp.concatenate(lanes, axis=1).astype(jnp.bfloat16)
+    own_pages = pool_hbm.shape[0]
 
     @pl.when(pl.program_id(0) == 0)
     def _():
-        for source, base in ((pool_ref, 0), (more_ref, pool_ref.shape[0])):
-
-            @pl.loop(0, source.shape[0] // 16)
-            def _(b):
-                rows = pl.ds(pl.multiple_of(b * 16, 16), 16)
-                for u in range(PAGE // 2):
-                    even, odd = split(source[rows, pair * u : pair * (u + 1)])
-                    spread(wide, even, 2 * u, PAGE)
-                    spread(wide, odd, 2 * u + 1, PAGE)
-                pages[pl.ds(pl.multiple_of((base + b * 16) * PAGE, 256), 256), :] = joined(
-                    wide, slice(None)
-                )
-
-    @pl.loop(0, HEADS // 2, unroll=4)
-    def _(u):
-        even, odd = split(q_ref[:, pl.ds(pl.multiple_of(u * pair, 128), pair)])
-        spread(q_buf, even, 2 * u, HEADS)
-        spread(q_buf, odd, 2 * u + 1, HEADS)
+        copies = [
+            pltpu.make_async_copy(pool_hbm, pages.at[pl.ds(0, own_pages)], sem.at[0]),
+            pltpu.make_async_copy(
+                more_hbm, pages.at[pl.ds(own_pages, more_hbm.shape[0])], sem.at[1]
+            ),
+        ]
+        for copy in copies:
+            copy.start()
+        for copy in copies:
+            copy.wait()
 
     first = pl.program_id(0) * step
+    keys = [
+        jnp.concatenate([pages[table[(first + r) * MAXP + p]] for p in range(MAXP)], axis=0)
+        for r in range(step)
+    ]
+    scores = jnp.concatenate(
+        [
+            lax.dot_general(
+                keys[r], q_ref[r], (((1,), (1,)), ((), ())), preferred_element_type=jnp.float32
+            )
+            for r in range(step)
+        ],
+        axis=1,
+    )
+    scores = scores * softmax_scale
+    column = lax.broadcasted_iota(jnp.int32, (1, step * HEADS), 1) // HEADS
+    length = jnp.zeros_like(column)
     for r in range(step):
-        row = first + r
-        keys = jnp.concatenate(
-            [
-                pages[pl.ds(pl.multiple_of(table[row * MAXP + p] * PAGE, PAGE), PAGE), :]
-                for p in range(MAXP)
-            ],
-            axis=0,
-        )
-        query = joined(q_buf, slice(r * HEADS, (r + 1) * HEADS))
-        scores = (
-            lax.dot_general(
-                keys, query, (((1,), (1,)), ((), ())), preferred_element_type=jnp.float32
-            )
-            * softmax_scale
-        )
-        valid = lax.broadcasted_iota(jnp.int32, scores.shape, 0) < lengths[row]
-        scores = jnp.where(valid, scores, -1e30)
-        top = jnp.max(scores, axis=0, keepdims=True)
-        expo = jnp.where(valid, jnp.exp(scores - top), 0.0)
-        total = jnp.sum(expo, axis=0, keepdims=True)
-        probs = (expo / total).astype(jnp.bfloat16)
-        result = lax.dot_general(
-            probs, keys[:, :LATENT], (((0,), (0,)), ((), ())), preferred_element_type=jnp.float32
-        )
-        for i in range(4):
-            o_buf[i, r * HEADS : (r + 1) * HEADS, :] = result[:, 128 * i : 128 * (i + 1)]
-        top_ref[r : r + 1, :] = top
-        total_ref[r : r + 1, :] = total
-
-    @pl.loop(0, HEADS, unroll=4)
-    def _(h):
-        for i in range(4):
-            out_ref[:, pl.ds(pl.multiple_of(h * LATENT + 128 * i, 128), 128)] = o_buf[
-                i, pl.ds(h, step, stride=HEADS), :
-            ].astype(jnp.bfloat16)
-
-
-def attend_cached(queries, pool, more, page_table, kv_lengths):
-    rows, step = queries.shape[0], 16
-    entries = (pool.shape[0] + more.shape[0]) * PAGE
-    whole = lambda i, t, n: (0, 0)
-    block = lambda i, t, n: (i, 0)
+        length = jnp.where(column == r, lengths[first + r], length)
+    valid = lax.broadcasted_iota(jnp.int32, scores.shape, 0) < length
+    scores = jnp.where(valid, scores, -1e30)
+    top = jnp.max(scores, axis=0, keepdims=True)
+    expo = jnp.where(valid, jnp.exp(scores - top), 0.0)
+    total = jnp.sum(expo, axis=0, keepdims=True)
+    probs = (expo / total).astype(jnp.bfloat16)
+    for r in range(step):
+        cut = slice(r * HEADS, (r + 1) * HEADS)
+        out_ref[r] = lax.dot_general(
+            probs[:, cut],
+            keys[r][:, :LATENT],
+            (((0,), (0,)), ((), ())),
+            preferred_element_type=jnp.float32,
+        ).astype(jnp.bfloat16)
+        top_ref[r : r + 1, :] = top[:, cut]
+        total_ref[r : r + 1, :] = total[:, cut]
+
+
+def attend_cached(query, pool, more, page_table, kv_lengths):
+    rows, step = query.shape[0], 8
+    entries = pool.shape[0] + more.shape[0]
+    hbm = pl.BlockSpec(memory_space=pl.ANY)
     return pl.pallas_call(
         functools.partial(attend_kernel, step),
         out_shape=[
-            jax.ShapeDtypeStruct((rows, HEADS * LATENT), jnp.bfloat16),
+            jax.ShapeDtypeStruct((rows, HEADS, LATENT), jnp.bfloat16),
             jax.ShapeDtypeStruct((rows, HEADS), jnp.float32),
             jax.ShapeDtypeStruct((rows, HEADS), jnp.float32),
         ],
         grid_spec=pltpu.PrefetchScalarGridSpec(
             num_scalar_prefetch=2,
             grid=(rows // step,),
-            in_specs=[
-                pl.BlockSpec((step, queries.shape[1]), block),
-                pl.BlockSpec(pool.shape, whole),
-                pl.BlockSpec(more.shape, whole),
-            ],
+            in_specs=[pl.BlockSpec((step, HEADS, KVW), lambda i, t, n: (i, 0, 0)), hbm, hbm],
             out_specs=[
-                pl.BlockSpec((step, HEADS * LATENT), block),
-                pl.BlockSpec((step, HEADS), block),
-                pl.BlockSpec((step, HEADS), block),
+                pl.BlockSpec((step, HEADS, LATENT), lambda i, t, n: (i, 0, 0)),
+                pl.BlockSpec((step, HEADS), lambda i, t, n: (i, 0)),
+                pl.BlockSpec((step, HEADS), lambda i, t, n: (i, 0)),
             ],
             scratch_shapes=[
-                pltpu.VMEM((5, 16 * PAGE, 128), jnp.float32),
-                pltpu.VMEM((entries, KVW), jnp.bfloat16),
-                pltpu.VMEM((5, step * HEADS, 128), jnp.float32),
-                pltpu.VMEM((4, step * HEADS, 128), jnp.float32),
+                pltpu.VMEM((entries, PAGE, KVW), jnp.bfloat16),
+                pltpu.SemaphoreType.DMA((2,)),
             ],
         ),
         compiler_params=pltpu.CompilerParams(vmem_limit_bytes=58 * MIB),
         cost_estimate=pl.CostEstimate(
             flops=2 * rows * HEADS * MAXP * PAGE * (KVW + LATENT),
-            bytes_accessed=2 * (queries.size + entries * KVW + rows * HEADS * LATENT),
+            bytes_accessed=2 * (query.size + entries * PAGE * KVW + rows * HEADS * LATENT),
             transcendentals=rows * HEADS * MAXP * PAGE,
         ),
         name="attend_cached",
-    )(page_table.reshape(rows * MAXP), kv_lengths, queries, pool, more)
-
-
-def pack_kernel(own, below, above, far, low, high, sem):
-    n = own.shape[0]
-    copies = [
-        pltpu.make_async_copy(source, target.at[pl.ds(at, n)], sem.at[i])
-        for i, (source, target, at) in enumerate(
-            ((own, low, 0), (below, low, n), (above, high, 0), (far, high, n))
-        )
+    )(page_table.reshape(rows * MAXP), kv_lengths, query, pool, more)
+
+
+def pack_kernel(count, *refs):
+    blocks, halves = refs[: 4 * count], refs[4 * count : 6 * count]
+    buf, in_sem, out_sem = refs[6 * count :]
+    n = blocks[0].shape[0]
+    loads = [
+        pltpu.make_async_copy(blocks[i], buf.at[i // 2, pl.ds(i % 2 * n, n)], in_sem.at[i])
+        for i in range(4 * count)
     ]
-    for copy in copies:
+    stores = [
+        pltpu.make_async_copy(buf.at[i], halves[i], out_sem.at[i]) for i in range(2 * count)
+    ]
+    for copy in loads:
         copy.start()
-    for copy in copies:
+    for i in range(2 * count):
+        loads[2 * i].wait()
+        loads[2 * i + 1].wait()
+        stores[i].start()
+    for copy in stores:
         copy.wait()
 
 
-def pack(own, below, above, far):
-    shape = jax.ShapeDtypeStruct((2 * own.shape[0], own.shape[1]), own.dtype)
+def pack(groups):
+    count, (n, width) = len(groups), groups[0][0].shape
     hbm = pl.BlockSpec(memory_space=pl.ANY)
-    return pl.pallas_call(
-        pack_kernel,
-        out_shape=[shape, shape],
-        in_specs=[hbm] * 4,
-        out_specs=[hbm] * 2,
-        scratch_shapes=[pltpu.SemaphoreType.DMA((4,))],
+    done = pl.pallas_call(
+        functools.partial(pack_kernel, count),
+        out_shape=[jax.ShapeDtypeStruct((2 * n, width), jnp.bfloat16)] * (2 * count),
+        in_specs=[hbm] * (4 * count),
+        out_specs=[hbm] * (2 * count),
+        scratch_shapes=[
+            pltpu.VMEM((2 * count, 2 * n, width), jnp.bfloat16),
+            pltpu.SemaphoreType.DMA((4 * count,)),
+            pltpu.SemaphoreType.DMA((2 * count,)),
+        ],
         compiler_params=pltpu.CompilerParams(vmem_limit_bytes=58 * MIB),
         cost_estimate=pl.CostEstimate(
-            flops=0, bytes_accessed=16 * own.size, transcendentals=0
+            flops=0, bytes_accessed=16 * count * n * width, transcendentals=0
         ),
         name="pack",
-    )(own, below, above, far)
+    )(*(block for group in groups for block in group))
+    return done[0::2], done[1::2]
 
 
 def tail_kernel(
@@ -492,7 +484,9 @@
         packed.reshape(dp_count, slots, width), "dp", split_axis=0, concat_axis=0, tiled=True
     )
     outgoing = jnp.take(page_pool, migration.reshape(dp_count * MCAP), axis=0, mode="clip")
-    arrived = after(arrived, outgoing)
+    query = queries.reshape(row_count, HEADS, KVW)
+    arrived = after(arrived, outgoing, query)
+    w_all = lax.all_gather(w_latent, ("dp", "expert"), axis=0, tiled=True)
     axes = (("z", "x"), ("x", "z"))
     both = range(local_experts)
     rows = [
@@ -510,48 +504,41 @@
     above = [shift(rows[k], axes[k][0], -1) for k in both]
     below, above = after((below, above))
     beyond = [shift(below[k], axes[k][0], 1) for k in both]
-    beyond = after(beyond)
-    low, high = zip(*(pack(rows[k], below[k], above[k], beyond[k]) for k in both))
-    low, high = after((low, high))
+    pool = after(page_pool, rows).reshape(page_pool.shape[0], PAGE, KVW)
+    more = incoming.reshape(dp_count * MCAP, PAGE, KVW)
+    beyond = after(beyond, pool, more)
+    low, high = pack([(rows[k], below[k], above[k], beyond[k]) for k in both])
     below_low = [shift(low[k], axes[k][1], 1) for k in both]
     above_high = [shift(high[k], axes[k][1], -1) for k in both]
+    pool = after(pool, low, high)
+    cached, top, total = attend_cached(query, pool, more, page_table, kv_lengths)
+    low, high = after((low, high), cached)
     below_high = [shift(high[k], axes[k][1], 1) for k in both]
     above_low = [shift(low[k], axes[k][1], -1) for k in both]
-    query, pool = after((queries, page_pool), low, high)
-    cached, top, total = attend_cached(query, pool, incoming, page_table, kv_lengths)
-    w_local = after(w_latent, cached)
-    spread = lax.all_to_all(
-        jnp.broadcast_to(w_local[None], (ex_count,) + w_latent.shape),
-        "expert",
-        split_axis=0,
-        concat_axis=0,
-        tiled=True,
-    )
-    below_low, above_high = after((below_low, above_high), cached)
+    weights = (w_gate, w_up, w_down)
+    y_first = ffn([[low[k], high[k], below_low[k], above_high[k]] for k in both], *weights)
+    below_low, above_high, below_high, above_low = after(
+        (below_low, above_high, below_high, above_low), y_first
+    )
     far_low = [shift(below_low[k], axes[k][1], 1) for k in both]
     far_high = [shift(above_high[k], axes[k][1], -1) for k in both]
-    w_all = lax.all_gather(
-        spread.reshape(ex_count * w_latent.shape[0], KVW), "dp", axis=0, tiled=True
-    )
-    weights = (w_gate, w_up, w_down)
-    y_own = [ffn([low[k], high[k]], k, *weights) for k in both]
-    below_high, above_low = after((below_high, above_low), y_own)
-    y_side = [
-        ffn([below_low[k], below_high[k], above_low[k], above_high[k]], k, *weights) for k in both
-    ]
-    early_up = [shift(y_side[k][3], axes[k][1], 1) for k in both]
-    early_down = [shift(y_side[k][0], axes[k][1], -1) for k in both]
-    far_low, far_high = after((far_low, far_high), y_side, spread)
-    y_far = [ffn([far_low[k], far_high[k]], k, *weights) for k in both]
+    y_second = ffn([[below_high[k], above_low[k]] for k in both], *weights)
+    y_first = after(y_first, y_second)
+    early_down = [shift(y_first[k][2], axes[k][1], -1) for k in both]
+    early_up = [shift(y_first[k][3], axes[k][1], 1) for k in both]
+    far_low, far_high = after((far_low, far_high), y_second)
+    y_far = ffn([[far_low[k], far_high[k]] for k in both], *weights)
+    y_far, early_down, early_up = after((y_far, early_down, early_up))
     relay_up = [shift(y_far[k][0], axes[k][1], 1) for k in both]
     relay_down = [shift(y_far[k][1], axes[k][1], -1) for k in both]
-    early_up, early_down, relay_up, relay_down = after((early_up, early_down, relay_up, relay_down))
-    late_up = [shift(plus(y_side[k][2], relay_up[k]), axes[k][1], 1) for k in both]
-    late_down = [shift(plus(y_side[k][1], relay_down[k]), axes[k][1], -1) for k in both]
+    cached = after(cached, y_far).reshape(row_count, HEADS * LATENT)
+    relay_up, relay_down = after((relay_up, relay_down), cached)
+    late_up = [shift(plus(y_second[k][1], relay_up[k]), axes[k][1], 1) for k in both]
+    late_down = [shift(plus(y_second[k][0], relay_down[k]), axes[k][1], -1) for k in both]
     late_up, late_down = after((late_up, late_down), w_all)
     n = rows[0].shape[0]
-    terms_low = [(y_own[k][0], late_up[k], early_down[k]) for k in both]
-    terms_high = [(y_own[k][1], early_up[k], late_down[k]) for k in both]
+    terms_low = [(y_first[k][0], late_up[k], early_down[k]) for k in both]
+    terms_high = [(y_first[k][1], early_up[k], late_down[k]) for k in both]
     for_far = [plus(*(term[n:] for term in terms_high[k])) for k in both]
     for_below = [plus(*(term[n:] for term in terms_low[k])) for k in both]
     relayed = [shift(for_far[k], axes[k][0], 1) for k in both]

time: 470 us -> 301 us (0.64)
  Pallas kernels: 210 us -> 70.1 us
  local copies, waits for them, and re-layouts: 8.71 us -> 33.6 us
  waiting for transfers between devices: 119 us -> 95.7 us
  blocking collectives: 18.8 us -> 0 us
  starting transfers between devices: 79.7 us -> 67 us
    pallas_call x8 -> x4, Pallas kernels: 148 us -> 39.4 us  [the longest x3 36.1 us: ffn(): pl.pallas_call(functools.partial(ffn_kernel, count, rows, parts), out_sha...]
    pallas_call x1, Pallas kernels: 44.2 us -> 13.2 us  [attend_cached(): pl.pallas_call(functools.partial(attend_kernel, step), out_shape=[jax.Sha...]
    all_to_all x1 -> x0, blocking collectives: 18.8 us -> none  [body(): lax.all_to_all(jnp.broadcast_to(w_local[None], (ex_count,) + w_latent.sha...]
    ppermute x36, waiting for transfers between devices: 88.8 us -> 74 us  [shift(): return lax.ppermute(value, 'expert', pairs)]
    all_to_all x1, starting transfers between devices: 25.9 us -> 14.6 us  [body(): lax.all_to_all(jnp.concatenate(finished, axis=1), 'dp', split_axis=0, con...]
    all_to_all x1, waiting for transfers between devices: 11.8 us -> 2.03 us  [body(): lax.all_to_all(packed.reshape(dp_count, slots, width), 'dp', split_axis=0...]
    reshape x1, local copies, waits for them, and re-layouts: 0.98 us -> 10 us  [body(): query = queries.reshape(row_count, HEADS, KVW)]
    optimization_barrier x0 -> x2, local copies, waits for them, and re-layouts: none -> 5.86 us  [after(): return lax.optimization_barrier((values, others))[0]]
  transfers between devices with their start and end apart: 40 -> 40, of which waited for: 22 -> 27; matrix products, arithmetic and copies ran while one was open for 2% -> 14% of each run, Pallas kernels for 7% -> 18%
where the time goes in v1:
time: 301 us; the launch traced here: 300 us
  waiting for transfers between devices  95.7 us (32%)
  Pallas kernels  70.1 us (23%)
  starting transfers between devices  67 us (22%)
  local copies, waits for them, and re-layouts  33.6 us (11%)
  other arithmetic  15.9 us (5%)
  between operations  14.5 us (5%)
    ppermute x36, waiting for transfers between devices, shift(): return lax.ppermute(value, 'expert', pairs)  74 us
    ppermute x36, starting transfers between devices, shift(): return lax.ppermute(value, 'expert', pairs)  41.1 us
    pallas_call x3, Pallas kernels, ffn(): pl.pallas_call(functools.partial(ffn_kernel, count, rows, parts), out_sha...  36.1 us
    pallas_call x1, Pallas kernels, tail(): pl.pallas_call(functools.partial(tail_kernel, parts), out_shape=[jax.Shap...  17.6 us
    all_to_all x1, starting transfers between devices, body(): lax.all_to_all(jnp.concatenate(finished, axis=1), 'dp', split_axis=0, con...  14.6 us
    all_to_all x1, waiting for transfers between devices, body(): lax.all_to_all(jnp.concatenate(finished, axis=1), 'dp', split_axis=0, con...  13.3 us
    pallas_call x1, Pallas kernels, attend_cached(): pl.pallas_call(functools.partial(attend_kernel, step), out_shape=[jax.Sha...  13.2 us
    convert_element_type x11, other arithmetic, plus(): return total.astype(jnp.bfloat16)  11 us
  transfers between devices with their start and end apart: 40, of which 27 were waited for; matrix products, arithmetic and copies ran while one was open for 14% of the time, Pallas kernels for 18%

profile of v1, /device:TPU:1, one launch (start us, length us, event | category | flops | bytes accessed | tf_op | source)
XLA Modules:
  0.0 299.5 jit_solution(2161061210236156672)
XLA Ops:
  11.2 2.6 fusion
  13.8 6.0 %all-to-all-start = ((bf16[8,8,7168]{2,1,0:T(8,128)(2,1)}), bf16[8,8,7168]{2,1,0:T(8,128)(2,1)S(1)}, u32[]{:S(2)}, u32[]{:S(2)}) async-start(bf16[8,8,7168]{2,1,0:T(8,128)(2,1)} %fusion), calls=%async_computation | async-start | bytes 1835008 | tf_op jit(solution)/shard_map/all_to_all | solution.py:483
  19.8 10.0 %reshape.73.q_ref = bf16[64,64,576]{2,1,0:T(8,128)(2,1)} reshape(bf16[64,36864]{1,0:T(8,128)(2,1)} %q_hbm.1) | data formatting | bytes 9437184 | tf_op jit(solution)/shard_map/reshape | solution.py:487
  45.9 5.2 %all-to-all-start.1 = ((bf16[8,4,9216]{2,1,0:T(4,128)(2,1)}), bf16[8,4,9216]{2,1,0:T(4,128)(2,1)S(1)}, u32[]{:S(2)}, u32[]{:S(2)}) async-start(bf16[8,4,9216]{2,1,0:T(4,128)(2,1)} %reshape.77), calls=%async_computation.1 | async-start | bytes 1179648 | tf_op jit(solution)/shard_map/all_to_all | solution.py:496
  54.2 2.4 collective-permute-done.3.refs_6_
  57.6 5.7 %all-to-all-done.1 = bf16[8,4,9216]{2,1,0:T(4,128)(2,1)S(1)} async-done(((bf16[8,4,9216]{2,1,0:T(4,128)(2,1)}), bf16[8,4,9216]{2,1,0:T(4,128)(2,1)S(1)}, u32[]{:S(2)}, u32[]{:S(2)}) %all-to-all-start.1) | async-done | bytes 589856 | tf_op jit(solution)/shard_map/all_to_all | solution.py:496
  69.1 3.3 %pack.1 = (bf16[64,7168]{1,0:T(8,128)(2,1)}, bf16[64,7168]{1,0:T(8,128)(2,1)}, bf16[64,7168]{1,0:T(8,128)(2,1)}, bf16[64,7168]{1,0:T(8,128)(2,1)}) custom-call(bf16[32,7168]{1,0:T(8,128)(2,1)} %copy-done.9, bf16[32,7168]{1,0:T(8,128)(2,1)} %collective-permute-done.refs_1_, bf16[32,7168]{1,0:T(8,128)(2,1)} %collective-permute-done.2.refs_2_, ...), custom_call_target="tpu_custom_call" | custom-call | bytes 7340032 | tf_op jit(solution)/shard_map/pack/pallas_call | solution.py:258
  72.6 2.5 collective-permute-start.7
  75.1 2.7 collective-permute-start.9
  78.6 3.4 %copy.20.pool_hbm = bf16[128,16,576]{2,1,0:T(8,128)(2,1)} copy(bf16[128,16,576]{0,2,1:T(8,128)(2,1)S(1)} %bitcast.12) | data formatting | bytes 4718592 | tf_op jit(solution)/shard_map/optimization_barrier | solution.py:439
  82.0 13.2 %attend_cached.1 = (bf16[64,64,512]{2,1,0:T(8,128)(2,1)}, f32[64,64]{1,0:T(8,128)}, f32[64,64]{1,0:T(8,128)}) custom-call(s32[384]{0:T(512)} %reshape.78.table, s32[64]{0:T(128)} %lengths.1, bf16[64,64,576]{2,1,0:T(8,128)(2,1)} %reshape.73.q_ref, bf16[128,16,576]{2,1,0:T(8,128)(2,1)} %copy.20.pool_hbm, bf16[32,16,576]{2,1,0:T(8,128)(2,1)} %reshape_reshape.3.more_hbm), custom_call_target="tpu_custom_call" | custom-call | flops 855638016 | bytes 11862016 | tf_op jit(solution)/shard_map/attend_cached/pallas_call | solution.py:203
  95.3 7.6 %collective-permute-done.6.refs_2_ = bf16[64,7168]{1,0:T(8,128)(2,1)} collective-permute-done((bf16[64,7168]{1,0:T(8,128)(2,1)}, bf16[64,7168]{1,0:T(8,128)(2,1)}, u32[]{:S(2)}, u32[]{:S(2)}) %collective-permute-start.6) | collective-permute-done | bytes 917536 | tf_op jit(solution)/shard_map/ppermute | solution.py:37
  106.7 14.1 %ffn.3 = (bf16[64,7168]{1,0:T(8,128)(2,1)}, bf16[64,7168]{1,0:T(8,128)(2,1)}, bf16[64,7168]{1,0:T(8,128)(2,1)}, bf16[64,7168]{1,0:T(8,128)(2,1)}, bf16[64,7168]{...) custom-call(bf16[64,7168]{1,0:T(8,128)(2,1)} %get-tuple-element.95.refs_0_, ...), custom_call_target="tpu_custom_call" | custom-call | flops 2818572288 | bytes 25690112 | tf_op jit(solution)/shard_map/ffn/pallas_call | solution.py:118
  126.4 2.5 collective-permute-start.17
  128.9 11.0 %ffn.4 = (bf16[64,7168]{1,0:T(8,128)(2,1)}, bf16[64,7168]{1,0:T(8,128)(2,1)}, bf16[64,7168]{1,0:T(8,128)(2,1)}, bf16[64,7168]{1,0:T(8,128)(2,1)}) custom-call(bf16[64,7168]{1,0:T(8,128)(2,1)} %copy-done.10, bf16[64,7168]{1,0:T(8,128)(2,1)} %copy-done.12, bf16[64,7168]{1,0:T(8,128)(2,1)} %copy-done.11, bf16[64,7168]{1,0:T(8,128)(2,1)} %copy-done.15, ...), custom_call_target="tpu_custom_call" | custom-call | flops 1409286144 | bytes 18350080 | tf_op jit(solution)/shard_map/ffn/pallas_call | solution.py:118
  142.4 2.6 collective-permute-start.19
  145.9 11.1 %ffn.5 = (bf16[64,7168]{1,0:T(8,128)(2,1)}, bf16[64,7168]{1,0:T(8,128)(2,1)}, bf16[64,7168]{1,0:T(8,128)(2,1)}, bf16[64,7168]{1,0:T(8,128)(2,1)}) custom-call(bf16[64,7168]{1,0:T(8,128)(2,1)} %copy-done.13, bf16[64,7168]{1,0:T(8,128)(2,1)} %collective-permute-done.16.refs_1_, bf16[64,7168]{1,0:T(8,128)(2,1)} %copy-done.14, ...), custom_call_target="tpu_custom_call" | custom-call | flops 1409286144 | bytes 18350080 | tf_op jit(solution)/shard_map/ffn/pallas_call | solution.py:118
  157.0 5.7 %collective-permute-done.18 = bf16[64,7168]{1,0:T(8,128)(2,1)} collective-permute-done((bf16[64,7168]{1,0:T(8,128)(2,1)}, bf16[64,7168]{1,0:T(8,128)(2,1)}, u32[]{:S(2)}, u32[]{:S(2)}) %collective-permute-start.18) | collective-permute-done | bytes 917536 | tf_op jit(solution)/shard_map/ppermute | solution.py:37
  162.6 2.9 collective-permute-done.19
  165.6 2.6 collective-permute-start.24
  168.2 3.4 %collective-permute-start.25 = (bf16[64,7168]{1,0:T(8,128)(2,1)}, bf16[64,7168]{1,0:T(8,128)(2,1)S(1)}, u32[]{:S(2)}, u32[]{:S(2)}) collective-permute-start(bf16[64,7168]{1,0:T(8,128)(2,1)} %get-tuple-element.135), channel_id=1, source_target_pairs={{0,3},{1,0},{2,1},{3,2},{4,7},{5,4},{6,5},{7,6},{8,11},{9,8},{10,9... | collective-permute-start | bytes 2752520 | tf_op jit(solution)/shard_map/ppermute | solution.py:37
  171.6 4.5 %copy.21 = bf16[8,8,64,512]{3,1,2,0:T(8,128)(2,1)} copy(bf16[8,8,64,512]{3,2,1,0:T(8,128)(2,1)S(1)} %bitcast.13) | data formatting | bytes 8388608
  176.2 8.8 %collective-permute-done.22 = bf16[64,7168]{1,0:T(8,128)(2,1)S(1)} collective-permute-done((bf16[64,7168]{1,0:T(8,128)(2,1)}, bf16[64,7168]{1,0:T(8,128)(2,1)S(1)}, u32[]{:S(2)}, u32[]{:S(2)}) %collective-permute-start.22) | collective-permute-done | bytes 917536 | tf_op jit(solution)/shard_map/ppermute | solution.py:37
  187.4 3.4 %collective-permute-start.29 = (bf16[64,7168]{1,0:T(8,128)(2,1)S(1)}, bf16[64,7168]{1,0:T(8,128)(2,1)}, u32[]{:S(2)}, u32[]{:S(2)}) collective-permute-start(bf16[64,7168]{1,0:T(8,128)(2,1)S(1)} %add_convert_fusion), channel_id=1, source_target_pairs={{0,3},{1,0},{2,1},{3,2},{4,7},{5,4},{6,5},{7,6},{8,11},{9,8},{10,9... | collective-permute-start | bytes 2752520 | tf_op jit(solution)/shard_map/ppermute | solution.py:37
  193.4 12.5 %collective-permute-done.29 = bf16[64,7168]{1,0:T(8,128)(2,1)} collective-permute-done((bf16[64,7168]{1,0:T(8,128)(2,1)S(1)}, bf16[64,7168]{1,0:T(8,128)(2,1)}, u32[]{:S(2)}, u32[]{:S(2)}) %collective-permute-start.29) | collective-permute-done | bytes 917536 | tf_op jit(solution)/shard_map/ppermute | solution.py:37
  220.0 4.5 %collective-permute-done.31 = bf16[32,7168]{1,0:T(8,128)(2,1)S(1)} collective-permute-done((bf16[32,7168]{1,0:T(8,128)(2,1)S(1)}, bf16[32,7168]{1,0:T(8,128)(2,1)S(1)}, u32[]{:S(2)}, u32[]{:S(2)}) %collective-permute-start.31) | collective-permute-done | bytes 458784 | tf_op jit(solution)/shard_map/ppermute | solution.py:37
  224.6 2.8 collective-permute-done.30
  230.3 7.4 %collective-permute-done.35 = bf16[32,7168]{1,0:T(8,128)(2,1)S(1)} collective-permute-done((bf16[32,7168]{1,0:T(8,128)(2,1)S(1)}, bf16[32,7168]{1,0:T(8,128)(2,1)S(1)}, u32[]{:S(2)}, u32[]{:S(2)}) %collective-permute-start.35) | collective-permute-done | bytes 458784 | tf_op jit(solution)/shard_map/ppermute | solution.py:37
  237.7 3.0 %collective-permute-done.34 = bf16[32,7168]{1,0:T(8,128)(2,1)S(1)} collective-permute-done((bf16[32,7168]{1,0:T(8,128)(2,1)S(1)}, bf16[32,7168]{1,0:T(8,128)(2,1)S(1)}, u32[]{:S(2)}, u32[]{:S(2)}) %collective-permute-start.34) | collective-permute-done | bytes 458784 | tf_op jit(solution)/shard_map/ppermute | solution.py:37
  244.6 14.6 %all-to-all-start.2 = ((bf16[8,8,7168]{2,1,0:T(8,128)(2,1)}), bf16[8,8,7168]{2,1,0:T(8,128)(2,1)S(1)}, u32[]{:S(2)}, u32[]{:S(2)}) async-start(bf16[8,8,7168]{2,1,0:T(8,128)(2,1)} %pad_maximum_fusion), calls=%async_computation.2 | async-start | bytes 1835008 | tf_op jit(solution)/shard_map/all_to_all | solution.py:557
  259.5 13.3 %all-to-all-done.2 = bf16[8,8,7168]{2,1,0:T(8,128)(2,1)S(1)} async-done(((bf16[8,8,7168]{2,1,0:T(8,128)(2,1)}), bf16[8,8,7168]{2,1,0:T(8,128)(2,1)S(1)}, u32[]{:S(2)}, u32[]{:S(2)}) %all-to-all-start.2) | async-done | bytes 917536 | tf_op jit(solution)/shard_map/all_to_all | solution.py:557
  275.1 17.6 %tail.1 = (bf16[64,7168]{1,0:T(8,128)(2,1)}, bf16[64,32768]{1,0:T(8,128)(2,1)}) custom-call(bf16[64,7168]{1,0:T(8,128)(2,1)S(1)} %copy-done.1, bf16[64,7168]{1,0:T(8,128)(2,1)S(1)} %bitcast.10, f32[1,512]{1,0:T(1,128)S(1)} %bitcast.11, f32[64,32]{1,0:T(8,128)S(1)} %get-tuple-element.165.cos_ref, f32[64,32]{1,0:T(8,128)S(1)} %get-tuple-element.164.sin_ref, ...), custom_call_target="tpu_custom_call" | custom-call | flops 528482304 | bytes 21364736 | tf_op jit(solution)/shard_map/tail/pallas_call | solution.py:390
  (161 shorter events, 72.2 us)
Async XLA Ops:
  7.2 202.2 %all-gather.2.cloned.1.call-start = ((), (), s32[]{:S(2)}) async-start(), calls=%async_computation.3 | async-start | bytes 9246720 | tf_op jit(solution)/shard_map/all_gather | solution.py:489
  13.8 20.0 %all-to-all-start = ((bf16[8,8,7168]{2,1,0:T(8,128)(2,1)}), bf16[8,8,7168]{2,1,0:T(8,128)(2,1)S(1)}, u32[]{:S(2)}, u32[]{:S(2)}) async-start(bf16[8,8,7168]{2,1,0:T(8,128)(2,1)} %fusion), calls=%async_computation | async-start | bytes 1835008 | tf_op jit(solution)/shard_map/all_to_all | solution.py:483
  36.2 15.0 %collective-permute-start = (bf16[32,7168]{1,0:T(8,128)(2,1)S(1)}, bf16[32,7168]{1,0:T(8,128)(2,1)}, u32[]{:S(2)}, u32[]{:S(2)}) collective-permute-start(bf16[32,7168]{1,0:T(8,128)(2,1)S(1)} %reshape.74.refs_0_), channel_id=1, source_target_pairs={{0,1},{1,2},{2,3},{3,0},{4,5},{5,6},{6,7},{7,4},{8,9},{9,10},{10,1... | collective-permute-start | bytes 1376264 | tf_op jit(solution)/shard_map/ppermute | solution.py:37
  39.9 13.3 %collective-permute-start.1 = (bf16[32,7168]{1,0:T(8,128)(2,1)}, bf16[32,7168]{1,0:T(8,128)(2,1)}, u32[]{:S(2)}, u32[]{:S(2)}) collective-permute-start(bf16[32,7168]{1,0:T(8,128)(2,1)} %reshape.75.refs_4_), channel_id=1, source_target_pairs={{0,4},{1,5},{2,6},{3,7},{4,8},{5,9},{6,10},{7,11},{8,12},{9,13},{1... | collective-permute-start | bytes 1376264 | tf_op jit(solution)/shard_map/ppermute | solution.py:37
  41.2 12.9 %collective-permute-start.2 = (bf16[32,7168]{1,0:T(8,128)(2,1)S(1)}, bf16[32,7168]{1,0:T(8,128)(2,1)}, u32[]{:S(2)}, u32[]{:S(2)}) collective-permute-start(bf16[32,7168]{1,0:T(8,128)(2,1)S(1)} %reshape.74.refs_0_), channel_id=1, source_target_pairs={{0,3},{1,0},{2,1},{3,2},{4,7},{5,4},{6,5},{7,6},{8,11},{9,8},{10,9... | collective-permute-start | bytes 1376264 | tf_op jit(solution)/shard_map/ppermute | solution.py:37
  43.5 13.1 %collective-permute-start.3 = (bf16[32,7168]{1,0:T(8,128)(2,1)}, bf16[32,7168]{1,0:T(8,128)(2,1)}, u32[]{:S(2)}, u32[]{:S(2)}) collective-permute-start(bf16[32,7168]{1,0:T(8,128)(2,1)} %reshape.75.refs_4_), channel_id=1, source_target_pairs={{0,12},{1,13},{2,14},{3,15},{4,0},{5,1},{6,2},{7,3},{8,4},{9,5},{1... | collective-permute-start | bytes 1376264 | tf_op jit(solution)/shard_map/ppermute | solution.py:37
  45.9 17.4 %all-to-all-start.1 = ((bf16[8,4,9216]{2,1,0:T(4,128)(2,1)}), bf16[8,4,9216]{2,1,0:T(4,128)(2,1)S(1)}, u32[]{:S(2)}, u32[]{:S(2)}) async-start(bf16[8,4,9216]{2,1,0:T(4,128)(2,1)} %reshape.77), calls=%async_computation.1 | async-start | bytes 1179648 | tf_op jit(solution)/shard_map/all_to_all | solution.py:496
  72.4 30.5 %collective-permute-start.6 = (bf16[64,7168]{1,0:T(8,128)(2,1)}, bf16[64,7168]{1,0:T(8,128)(2,1)}, u32[]{:S(2)}, u32[]{:S(2)}) collective-permute-start(bf16[64,7168]{1,0:T(8,128)(2,1)} %get-tuple-element.95.refs_0_), channel_id=1, source_target_pairs={{0,4},{1,5},{2,6},{3,7},{4,8},{5,9},{6,10},{7,11},{8,12},{9,13},{1... | collective-permute-start | bytes 2752520 | tf_op jit(solution)/shard_map/ppermute | solution.py:37
  72.6 31.1 %collective-permute-start.7 = (bf16[64,7168]{1,0:T(8,128)(2,1)}, bf16[64,7168]{1,0:T(8,128)(2,1)S(1)}, u32[]{:S(2)}, u32[]{:S(2)}) collective-permute-start(bf16[64,7168]{1,0:T(8,128)(2,1)} %get-tuple-element.96.refs_1_), channel_id=1, source_target_pairs={{0,12},{1,13},{2,14},{3,15},{4,0},{5,1},{6,2},{7,3},{8,4},{9,5},{1... | collective-permute-start | bytes 2752520 | tf_op jit(solution)/shard_map/ppermute | solution.py:37
  75.1 29.4 %collective-permute-start.8 = (bf16[64,7168]{1,0:T(8,128)(2,1)}, bf16[64,7168]{1,0:T(8,128)(2,1)}, u32[]{:S(2)}, u32[]{:S(2)}) collective-permute-start(bf16[64,7168]{1,0:T(8,128)(2,1)} %get-tuple-element.97.refs_4_), channel_id=1, source_target_pairs={{0,1},{1,2},{2,3},{3,0},{4,5},{5,6},{6,7},{7,4},{8,9},{9,10},{10,1... | collective-permute-start | bytes 2752520 | tf_op jit(solution)/shard_map/ppermute | solution.py:37
  75.1 31.6 %collective-permute-start.9 = (bf16[64,7168]{1,0:T(8,128)(2,1)}, bf16[64,7168]{1,0:T(8,128)(2,1)}, u32[]{:S(2)}, u32[]{:S(2)}) collective-permute-start(bf16[64,7168]{1,0:T(8,128)(2,1)} %get-tuple-element.98.refs_5_), channel_id=1, source_target_pairs={{0,3},{1,0},{2,1},{3,2},{4,7},{5,4},{6,5},{7,6},{8,11},{9,8},{10,9... | collective-permute-start | bytes 2752520 | tf_op jit(solution)/shard_map/ppermute | solution.py:37
  95.2 27.3 %collective-permute-start.10 = (bf16[64,7168]{1,0:T(8,128)(2,1)}, bf16[64,7168]{1,0:T(8,128)(2,1)S(1)}, u32[]{:S(2)}, u32[]{:S(2)}) collective-permute-start(bf16[64,7168]{1,0:T(8,128)(2,1)} %get-tuple-element.96.refs_1_), channel_id=1, source_target_pairs={{0,4},{1,5},{2,6},{3,7},{4,8},{5,9},{6,10},{7,11},{8,12},{9,13},{1... | collective-permute-start | bytes 2752520 | tf_op jit(solution)/shard_map/ppermute | solution.py:37
  102.9 19.9 %collective-permute-start.11 = (bf16[64,7168]{1,0:T(8,128)(2,1)}, bf16[64,7168]{1,0:T(8,128)(2,1)S(1)}, u32[]{:S(2)}, u32[]{:S(2)}) collective-permute-start(bf16[64,7168]{1,0:T(8,128)(2,1)} %get-tuple-element.98.refs_5_), channel_id=1, source_target_pairs={{0,1},{1,2},{2,3},{3,0},{4,5},{5,6},{6,7},{7,4},{8,9},{9,10},{10,1... | collective-permute-start | bytes 2752520 | tf_op jit(solution)/shard_map/ppermute | solution.py:37
  103.7 19.0 %collective-permute-start.12 = (bf16[64,7168]{1,0:T(8,128)(2,1)}, bf16[64,7168]{1,0:T(8,128)(2,1)S(1)}, u32[]{:S(2)}, u32[]{:S(2)}) collective-permute-start(bf16[64,7168]{1,0:T(8,128)(2,1)} %get-tuple-element.95.refs_0_), channel_id=1, source_target_pairs={{0,12},{1,13},{2,14},{3,15},{4,0},{5,1},{6,2},{7,3},{8,4},{9,5},{1... | collective-permute-start | bytes 2752520 | tf_op jit(solution)/shard_map/ppermute | solution.py:37
  104.5 18.7 %collective-permute-start.13 = (bf16[64,7168]{1,0:T(8,128)(2,1)S(1)}, bf16[64,7168]{1,0:T(8,128)(2,1)S(1)}, u32[]{:S(2)}, u32[]{:S(2)}) collective-permute-start(bf16[64,7168]{1,0:T(8,128)(2,1)S(1)} %copy-done.25), channel_id=1, source_target_pairs={{0,3},{1,0},{2,1},{3,2},{4,7},{5,4},{6,5},{7,6},{8,11},{9,8},{10,9... | collective-permute-start | bytes 2752520 | tf_op jit(solution)/shard_map/ppermute | solution.py:37
  123.2 19.2 %collective-permute-start.14 = (bf16[64,7168]{1,0:T(8,128)(2,1)}, bf16[64,7168]{1,0:T(8,128)(2,1)S(1)}, u32[]{:S(2)}, u32[]{:S(2)}) collective-permute-start(bf16[64,7168]{1,0:T(8,128)(2,1)} %collective-permute-done.6.refs_2_), channel_id=1, source_target_pairs={{0,4},{1,5},{2,6},{3,7},{4,8},{5,9},{6,10},{7,11},{8,12},{9,13},{1... | collective-permute-start | bytes 2752520 | tf_op jit(solution)/shard_map/ppermute | solution.py:37
  123.6 21.4 %collective-permute-start.15 = (bf16[64,7168]{1,0:T(8,128)(2,1)}, bf16[64,7168]{1,0:T(8,128)(2,1)S(1)}, u32[]{:S(2)}, u32[]{:S(2)}) collective-permute-start(bf16[64,7168]{1,0:T(8,128)(2,1)} %collective-permute-done.8.refs_6_), channel_id=1, source_target_pairs={{0,1},{1,2},{2,3},{3,0},{4,5},{5,6},{6,7},{7,4},{8,9},{9,10},{10,1... | collective-permute-start | bytes 2752520 | tf_op jit(solution)/shard_map/ppermute | solution.py:37
  124.6 20.4 %collective-permute-start.16 = (bf16[64,7168]{1,0:T(8,128)(2,1)}, bf16[64,7168]{1,0:T(8,128)(2,1)}, u32[]{:S(2)}, u32[]{:S(2)}) collective-permute-start(bf16[64,7168]{1,0:T(8,128)(2,1)} %copy-done.20), channel_id=1, source_target_pairs={{0,12},{1,13},{2,14},{3,15},{4,0},{5,1},{6,2},{7,3},{8,4},{9,5},{1... | collective-permute-start | bytes 2752520 | tf_op jit(solution)/shard_map/ppermute | solution.py:37
  126.4 18.7 %collective-permute-start.17 = (bf16[64,7168]{1,0:T(8,128)(2,1)}, bf16[64,7168]{1,0:T(8,128)(2,1)}, u32[]{:S(2)}, u32[]{:S(2)}) collective-permute-start(bf16[64,7168]{1,0:T(8,128)(2,1)} %collective-permute-done.9.refs_7_), channel_id=1, source_target_pairs={{0,3},{1,0},{2,1},{3,2},{4,7},{5,4},{6,5},{7,6},{8,11},{9,8},{10,9... | collective-permute-start | bytes 2752520 | tf_op jit(solution)/shard_map/ppermute | solution.py:37
  139.8 22.8 %collective-permute-start.18 = (bf16[64,7168]{1,0:T(8,128)(2,1)}, bf16[64,7168]{1,0:T(8,128)(2,1)}, u32[]{:S(2)}, u32[]{:S(2)}) collective-permute-start(bf16[64,7168]{1,0:T(8,128)(2,1)} %get-tuple-element.128), channel_id=1, source_target_pairs={{0,12},{1,13},{2,14},{3,15},{4,0},{5,1},{6,2},{7,3},{8,4},{9,5},{1... | collective-permute-start | bytes 2752520 | tf_op jit(solution)/shard_map/ppermute | solution.py:37
  142.4 23.2 %collective-permute-start.19 = (bf16[64,7168]{1,0:T(8,128)(2,1)}, bf16[64,7168]{1,0:T(8,128)(2,1)}, u32[]{:S(2)}, u32[]{:S(2)}) collective-permute-start(bf16[64,7168]{1,0:T(8,128)(2,1)} %get-tuple-element.129), channel_id=1, source_target_pairs={{0,3},{1,0},{2,1},{3,2},{4,7},{5,4},{6,5},{7,6},{8,11},{9,8},{10,9... | collective-permute-start | bytes 2752520 | tf_op jit(solution)/shard_map/ppermute | solution.py:37
  145.0 20.5 %collective-permute-start.20 = (bf16[64,7168]{1,0:T(8,128)(2,1)}, bf16[64,7168]{1,0:T(8,128)(2,1)}, u32[]{:S(2)}, u32[]{:S(2)}) collective-permute-start(bf16[64,7168]{1,0:T(8,128)(2,1)} %get-tuple-element.130), channel_id=1, source_target_pairs={{0,4},{1,5},{2,6},{3,7},{4,8},{5,9},{6,10},{7,11},{8,12},{9,13},{1... | collective-permute-start | bytes 2752520 | tf_op jit(solution)/shard_map/ppermute | solution.py:37
  145.0 20.5 %collective-permute-start.21 = (bf16[64,7168]{1,0:T(8,128)(2,1)}, bf16[64,7168]{1,0:T(8,128)(2,1)}, u32[]{:S(2)}, u32[]{:S(2)}) collective-permute-start(bf16[64,7168]{1,0:T(8,128)(2,1)} %get-tuple-element.131), channel_id=1, source_target_pairs={{0,1},{1,2},{2,3},{3,0},{4,5},{5,6},{6,7},{7,4},{8,9},{9,10},{10,1... | collective-permute-start | bytes 2752520 | tf_op jit(solution)/shard_map/ppermute | solution.py:37
  165.5 19.4 %collective-permute-start.22 = (bf16[64,7168]{1,0:T(8,128)(2,1)}, bf16[64,7168]{1,0:T(8,128)(2,1)S(1)}, u32[]{:S(2)}, u32[]{:S(2)}) collective-permute-start(bf16[64,7168]{1,0:T(8,128)(2,1)} %get-tuple-element.132), channel_id=1, source_target_pairs={{0,4},{1,5},{2,6},{3,7},{4,8},{5,9},{6,10},{7,11},{8,12},{9,13},{1... | collective-permute-start | bytes 2752520 | tf_op jit(solution)/shard_map/ppermute | solution.py:37
  165.5 20.5 %collective-permute-start.23 = (bf16[64,7168]{1,0:T(8,128)(2,1)}, bf16[64,7168]{1,0:T(8,128)(2,1)S(1)}, u32[]{:S(2)}, u32[]{:S(2)}) collective-permute-start(bf16[64,7168]{1,0:T(8,128)(2,1)} %get-tuple-element.133), channel_id=1, source_target_pairs={{0,1},{1,2},{2,3},{3,0},{4,5},{5,6},{6,7},{7,4},{8,9},{9,10},{10,1... | collective-permute-start | bytes 2752520 | tf_op jit(solution)/shard_map/ppermute | solution.py:37
  165.6 20.4 %collective-permute-start.24 = (bf16[64,7168]{1,0:T(8,128)(2,1)}, bf16[64,7168]{1,0:T(8,128)(2,1)S(1)}, u32[]{:S(2)}, u32[]{:S(2)}) collective-permute-start(bf16[64,7168]{1,0:T(8,128)(2,1)} %get-tuple-element.134), channel_id=1, source_target_pairs={{0,12},{1,13},{2,14},{3,15},{4,0},{5,1},{6,2},{7,3},{8,4},{9,5},{1... | collective-permute-start | bytes 2752520 | tf_op jit(solution)/shard_map/ppermute | solution.py:37
  168.2 19.0 %collective-permute-start.25 = (bf16[64,7168]{1,0:T(8,128)(2,1)}, bf16[64,7168]{1,0:T(8,128)(2,1)S(1)}, u32[]{:S(2)}, u32[]{:S(2)}) collective-permute-start(bf16[64,7168]{1,0:T(8,128)(2,1)} %get-tuple-element.135), channel_id=1, source_target_pairs={{0,3},{1,0},{2,1},{3,2},{4,7},{5,4},{6,5},{7,6},{8,11},{9,8},{10,9... | collective-permute-start | bytes 2752520 | tf_op jit(solution)/shard_map/ppermute | solution.py:37
  187.4 18.5 %collective-permute-start.29 = (bf16[64,7168]{1,0:T(8,128)(2,1)S(1)}, bf16[64,7168]{1,0:T(8,128)(2,1)}, u32[]{:S(2)}, u32[]{:S(2)}) collective-permute-start(bf16[64,7168]{1,0:T(8,128)(2,1)S(1)} %add_convert_fusion), channel_id=1, source_target_pairs={{0,3},{1,0},{2,1},{3,2},{4,7},{5,4},{6,5},{7,6},{8,11},{9,8},{10,9... | collective-permute-start | bytes 2752520 | tf_op jit(solution)/shard_map/ppermute | solution.py:37
  191.0 15.7 %collective-permute-start.28 = (bf16[64,7168]{1,0:T(8,128)(2,1)S(1)}, bf16[64,7168]{1,0:T(8,128)(2,1)}, u32[]{:S(2)}, u32[]{:S(2)}) collective-permute-start(bf16[64,7168]{1,0:T(8,128)(2,1)S(1)} %add_convert_fusion.1), channel_id=1, source_target_pairs={{0,12},{1,13},{2,14},{3,15},{4,0},{5,1},{6,2},{7,3},{8,4},{9,5},{1... | collective-permute-start | bytes 2752520 | tf_op jit(solution)/shard_map/ppermute | solution.py:37
  191.6 17.4 %collective-permute-start.27 = (bf16[64,7168]{1,0:T(8,128)(2,1)S(1)}, bf16[64,7168]{1,0:T(8,128)(2,1)}, u32[]{:S(2)}, u32[]{:S(2)}) collective-permute-start(bf16[64,7168]{1,0:T(8,128)(2,1)S(1)} %add_convert_fusion.2), channel_id=1, source_target_pairs={{0,1},{1,2},{2,3},{3,0},{4,5},{5,6},{6,7},{7,4},{8,9},{9,10},{10,1... | collective-permute-start | bytes 2752520 | tf_op jit(solution)/shard_map/ppermute | solution.py:37
  192.4 17.0 %collective-permute-start.26 = (bf16[64,7168]{1,0:T(8,128)(2,1)S(1)}, bf16[64,7168]{1,0:T(8,128)(2,1)}, u32[]{:S(2)}, u32[]{:S(2)}) collective-permute-start(bf16[64,7168]{1,0:T(8,128)(2,1)S(1)} %add_convert_fusion.3), channel_id=1, source_target_pairs={{0,4},{1,5},{2,6},{3,7},{4,8},{5,9},{6,10},{7,11},{8,12},{9,13},{1... | collective-permute-start | bytes 2752520 | tf_op jit(solution)/shard_map/ppermute | solution.py:37
  244.6 28.3 %all-to-all-start.2 = ((bf16[8,8,7168]{2,1,0:T(8,128)(2,1)}), bf16[8,8,7168]{2,1,0:T(8,128)(2,1)S(1)}, u32[]{:S(2)}, u32[]{:S(2)}) async-start(bf16[8,8,7168]{2,1,0:T(8,128)(2,1)} %pad_maximum_fusion), calls=%async_computation.2 | async-start | bytes 1835008 | tf_op jit(solution)/shard_map/all_to_all | solution.py:557
  (39 other events, 503.4 us)
Sparse Core Ops, SparseCore 0:
  11.0 83.8 all-gather.1

commit v2 on v1

v2 whole, which is shorter than its diff:
```python
import functools

import jax
import jax.numpy as jnp
from jax import lax
from jax.experimental import pallas as pl
from jax.experimental.pallas import tpu as pltpu
from jax.sharding import PartitionSpec as P

HEADS = 64
LATENT = 512
PAGE = 16
MAXP = 6
CAP = 4
MCAP = 4
KVW = 576
SIDE = 4

softmax_scale = 192.0 ** (-0.5)
routed_scale = 2.5
norm_eps = 1e-06
MIB = 1 << 20


def rms_rows(values, gain):
    stat = jnp.mean(values * values, axis=-1, keepdims=True)
    return values * lax.rsqrt(stat + norm_eps) * gain


def shift(value, axis, step):
    pairs = []
    for x in range(SIDE):
        for z in range(SIDE):
            to_x = (x + step) % SIDE if axis == "x" else x
            to_z = (z + step) % SIDE if axis == "z" else z
            pairs.append((x * SIDE + z, to_x * SIDE + to_z))
    return lax.ppermute(value, "expert", pairs)


def ffn_kernel(count, rows, parts, *refs):
    xs = refs[:count]
    gate_hbm, up_hbm, down_hbm = refs[count : count + 3]
    outs = refs[count + 3 : 2 * count + 3]
    x_buf, w_buf, d_buf, o_buf, acc, in_sem, w_sem, d_sem, out_sem = refs[2 * count + 3 :]
    depth = gate_hbm.shape[1]
    piece = depth // parts

    def loads(c):
        cut = pl.ds(pl.multiple_of(c * piece, piece), piece)
        for e in range(2):
            for j, source in enumerate((gate_hbm, up_hbm)):
                yield pltpu.make_async_copy(
                    source.at[e, cut],
                    w_buf.at[cut, pl.ds(256 * e + 128 * j, 128)],
                    w_sem.at[c, 2 * e + j],
                )
        for i in range(count):
            yield pltpu.make_async_copy(
                xs[i].at[:, cut], x_buf.at[pl.ds(i * rows, rows), cut], in_sem.at[c, i]
            )

    def stores(c):
        cut = pl.ds(pl.multiple_of(c * piece, piece), piece)
        for i in range(count):
            yield pltpu.make_async_copy(
                o_buf.at[pl.ds(i * rows, rows), cut], outs[i].at[:, cut], out_sem.at[c, i]
            )

    @pl.loop(0, parts)
    def _(c):
        for copy in loads(c):
            copy.start()

    down = [
        pltpu.make_async_copy(down_hbm.at[e], d_buf.at[pl.ds(128 * e, 128)], d_sem.at[e])
        for e in range(2)
    ]
    for copy in down:
        copy.start()
    acc[...] = jnp.zeros_like(acc)

    @pl.loop(0, parts)
    def _(c):
        for copy in loads(c):
            copy.wait()
        cut = pl.ds(pl.multiple_of(c * piece, piece), piece)
        acc[...] += jnp.dot(x_buf[:, cut], w_buf[cut, :], preferred_element_type=jnp.float32)

    first = lax.broadcasted_iota(jnp.int32, (rows * count, 128), 0) % (2 * CAP) < CAP
    gate = jnp.where(first, acc[:, :128], acc[:, 256:384])
    up = jnp.where(first, acc[:, 128:256], acc[:, 384:])
    active = gate / (1.0 + jnp.exp(-gate)) * up
    active = jnp.concatenate(
        [jnp.where(first, active, 0.0), jnp.where(first, 0.0, active)], axis=1
    ).astype(jnp.bfloat16)
    for copy in down:
        copy.wait()

    @pl.loop(0, parts)
    def _(c):
        cut = pl.ds(pl.multiple_of(c * piece, piece), piece)
        o_buf[:, cut] = jnp.dot(active, d_buf[:, cut], preferred_element_type=jnp.float32).astype(
            jnp.bfloat16
        )
        for copy in stores(c):
            copy.start()

    @pl.loop(0, parts)
    def _(c):
        for copy in stores(c):
            copy.wait()


def ffn(blocks, w_gate, w_up, w_down):
    chains, per_chain = len(blocks), len(blocks[0])
    flat = [block for part in blocks for block in part]
    count, rows, depth, parts = len(flat), flat[0].shape[0], w_gate.shape[1], 4
    total = rows * count
    done = pl.pallas_call(
        functools.partial(ffn_kernel, count, rows, parts),
        out_shape=[jax.ShapeDtypeStruct(block.shape, jnp.bfloat16) for block in flat],
        in_specs=[pl.BlockSpec(memory_space=pl.ANY)] * (count + 3),
        out_specs=[pl.BlockSpec(memory_space=pl.ANY)] * count,
        scratch_shapes=[
            pltpu.VMEM((total, depth), jnp.bfloat16),
            pltpu.VMEM((depth, 512), jnp.bfloat16),
            pltpu.VMEM((256, depth), jnp.bfloat16),
            pltpu.VMEM((total, depth), jnp.bfloat16),
            pltpu.VMEM((total, 512), jnp.float32),
            pltpu.SemaphoreType.DMA((parts, count)),
            pltpu.SemaphoreType.DMA((parts, 4)),
            pltpu.SemaphoreType.DMA((2,)),
            pltpu.SemaphoreType.DMA((parts, count)),
        ],
        compiler_params=pltpu.CompilerParams(vmem_limit_bytes=58 * MIB),
        cost_estimate=pl.CostEstimate(
            flops=2 * total * depth * 768,
            bytes_accessed=2 * depth * (768 + 2 * total),
            transcendentals=total * 128,
        ),
        name="ffn",
    )(*flat, w_gate, w_up, w_down)
    return [done[k * per_chain : (k + 1) * per_chain] for k in range(chains)]


def attend_kernel(
    step, table, lengths, q_ref, pool_hbm, more_hbm, out_ref, top_ref, total_ref, pages, sem
):
    own_pages = pool_hbm.shape[0]

    @pl.when(pl.program_id(0) == 0)
    def _():
        copies = [
            pltpu.make_async_copy(pool_hbm, pages.at[pl.ds(0, own_pages)], sem.at[0]),
            pltpu.make_async_copy(
                more_hbm, pages.at[pl.ds(own_pages, more_hbm.shape[0])], sem.at[1]
            ),
        ]
        for copy in copies:
            copy.start()
        for copy in copies:
            copy.wait()

    first = pl.program_id(0) * step
    keys = [
        jnp.concatenate([pages[table[(first + r) * MAXP + p]] for p in range(MAXP)], axis=0)
        for r in range(step)
    ]
    scores = jnp.concatenate(
        [
            lax.dot_general(
                keys[r], q_ref[r], (((1,), (1,)), ((), ())), preferred_element_type=jnp.float32
            )
            for r in range(step)
        ],
        axis=1,
    )
    scores = scores * softmax_scale
    column = lax.broadcasted_iota(jnp.int32, (1, step * HEADS), 1) // HEADS
    length = jnp.zeros_like(column)
    for r in range(step):
        length = jnp.where(column == r, lengths[first + r], length)
    valid = lax.broadcasted_iota(jnp.int32, scores.shape, 0) < length
    scores = jnp.where(valid, scores, -1e30)
    top = jnp.max(scores, axis=0, keepdims=True)
    expo = jnp.where(valid, jnp.exp(scores - top), 0.0)
    total = jnp.sum(expo, axis=0, keepdims=True)
    probs = (expo / total).astype(jnp.bfloat16)
    for r in range(step):
        cut = slice(r * HEADS, (r + 1) * HEADS)
        out_ref[r] = lax.dot_general(
            probs[:, cut],
            keys[r][:, :LATENT],
            (((0,), (0,)), ((), ())),
            preferred_element_type=jnp.float32,
        ).astype(jnp.bfloat16)
        top_ref[r : r + 1, :] = top[:, cut]
        total_ref[r : r + 1, :] = total[:, cut]


def attend_cached(query, pool, more, page_table, kv_lengths):
    rows, step = query.shape[0], 8
    entries = pool.shape[0] + more.shape[0]
    hbm = pl.BlockSpec(memory_space=pl.ANY)
    return pl.pallas_call(
        functools.partial(attend_kernel, step),
        out_shape=[
            jax.ShapeDtypeStruct((rows, HEADS, LATENT), jnp.bfloat16),
            jax.ShapeDtypeStruct((rows, HEADS), jnp.float32),
            jax.ShapeDtypeStruct((rows, HEADS), jnp.float32),
        ],
        grid_spec=pltpu.PrefetchScalarGridSpec(
            num_scalar_prefetch=2,
            grid=(rows // step,),
            in_specs=[pl.BlockSpec((step, HEADS, KVW), lambda i, t, n: (i, 0, 0)), hbm, hbm],
            out_specs=[
                pl.BlockSpec((step, HEADS, LATENT), lambda i, t, n: (i, 0, 0)),
                pl.BlockSpec((step, HEADS), lambda i, t, n: (i, 0)),
                pl.BlockSpec((step, HEADS), lambda i, t, n: (i, 0)),
            ],
            scratch_shapes=[
                pltpu.VMEM((entries, PAGE, KVW), jnp.bfloat16),
                pltpu.SemaphoreType.DMA((2,)),
            ],
        ),
        compiler_params=pltpu.CompilerParams(vmem_limit_bytes=58 * MIB),
        cost_estimate=pl.CostEstimate(
            flops=2 * rows * HEADS * MAXP * PAGE * (KVW + LATENT),
            bytes_accessed=2 * (query.size + entries * PAGE * KVW + rows * HEADS * LATENT),
            transcendentals=rows * HEADS * MAXP * PAGE,
        ),
        name="attend_cached",
    )(page_table.reshape(rows * MAXP), kv_lengths, query, pool, more)


def pack_kernel(count, *refs):
    blocks, joined = refs[: 2 * count], refs[2 * count : 3 * count]
    buf, in_sem, out_sem = refs[3 * count :]
    n = blocks[0].shape[0]
    loads = [
        pltpu.make_async_copy(blocks[i], buf.at[i // 2, pl.ds(i % 2 * n, n)], in_sem.at[i])
        for i in range(2 * count)
    ]
    stores = [pltpu.make_async_copy(buf.at[i], joined[i], out_sem.at[i]) for i in range(count)]
    for copy in loads:
        copy.start()
    for i in range(count):
        loads[2 * i].wait()
        loads[2 * i + 1].wait()
        stores[i].start()
    for copy in stores:
        copy.wait()


def pack(pairs):
    count, (n, width) = len(pairs), pairs[0][0].shape
    hbm = pl.BlockSpec(memory_space=pl.ANY)
    return pl.pallas_call(
        functools.partial(pack_kernel, count),
        out_shape=[jax.ShapeDtypeStruct((2 * n, width), jnp.bfloat16)] * count,
        in_specs=[hbm] * (2 * count),
        out_specs=[hbm] * count,
        scratch_shapes=[
            pltpu.VMEM((count, 2 * n, width), jnp.bfloat16),
            pltpu.SemaphoreType.DMA((2 * count,)),
            pltpu.SemaphoreType.DMA((count,)),
        ],
        compiler_params=pltpu.CompilerParams(vmem_limit_bytes=58 * MIB),
        cost_estimate=pl.CostEstimate(
            flops=0, bytes_accessed=8 * count * n * width, transcendentals=0
        ),
        name="pack",
    )(*(block for pair in pairs for block in pair))


def tail_kernel(
    parts,
    groups,
    hidden_ref,
    back_ref,
    gain_ref,
    cos_ref,
    sin_ref,
    top_ref,
    total_ref,
    place_ref,
    w_hbm,
    q_hbm,
    o_hbm,
    hidden_out_hbm,
    out_hbm,
    w_ref,
    q_ref,
    o_ref,
    hidden_buf,
    key_buf,
    own_buf,
    keep_buf,
    w_sem,
    q_sem,
    o_sem,
    hidden_sem,
    out_sem,
):
    width = hidden_ref.shape[1]
    piece = width // parts
    per_group = HEADS // groups
    span, q_span = per_group * LATENT, per_group * KVW

    def w_load(c):
        cut = pl.ds(pl.multiple_of(c * piece, piece), piece)
        return pltpu.make_async_copy(w_hbm.at[cut], w_ref.at[cut], w_sem.at[c])

    def q_load(g):
        cut = pl.ds(pl.multiple_of(g * q_span, 128), q_span)
        return pltpu.make_async_copy(q_hbm.at[:, cut], q_ref.at[:, cut], q_sem.at[g])

    def o_load(g):
        cut = pl.ds(pl.multiple_of(g * span, span), span)
        return pltpu.make_async_copy(o_hbm.at[:, cut], o_ref.at[:, cut], o_sem.at[g])

    def store(g):
        cut = pl.ds(pl.multiple_of(g * span, span), span)
        return pltpu.make_async_copy(o_ref.at[:, cut], out_hbm.at[:, cut], out_sem.at[g])

    for c in range(parts):
        w_load(c).start()

    @pl.loop(0, groups)
    def _(g):
        q_load(g).start()

    @pl.loop(0, groups)
    def _(g):
        o_load(g).start()

    place = place_ref[...]
    pick = (place != 0.0).astype(jnp.bfloat16)
    weight = jnp.sum(place, axis=1, keepdims=True)
    projected = jnp.zeros((hidden_ref.shape[0], KVW), jnp.float32)
    for c in range(parts):
        cut = slice(c * piece, (c + 1) * piece)
        picked = jnp.dot(pick, back_ref[:, cut], preferred_element_type=jnp.float32)
        hidden = (hidden_ref[:, cut].astype(jnp.float32) + weight * picked).astype(jnp.bfloat16)
        hidden_buf[:, cut] = hidden
        w_load(c).wait()
        projected += jnp.dot(hidden, w_ref[cut, :], preferred_element_type=jnp.float32)
    hidden_copy = pltpu.make_async_copy(hidden_buf, hidden_out_hbm, hidden_sem)
    hidden_copy.start()
    latent = rms_rows(projected[:, :LATENT], gain_ref[...])
    first = projected[:, LATENT : LATENT + 32]
    second = projected[:, LATENT + 32 :]
    cosine, sine = cos_ref[...], sin_ref[...]
    new_key = jnp.concatenate(
        [latent, first * cosine - second * sine, second * cosine + first * sine], axis=1
    )
    new_key = new_key.astype(jnp.bfloat16).astype(jnp.float32)
    key_buf[...] = jnp.concatenate([new_key, new_key], axis=1)
    lane = lax.broadcasted_iota(jnp.int32, (8, 128), 1)
    head = lax.broadcasted_iota(jnp.int32, (8, HEADS), 1)
    blocks = hidden_ref.shape[0] // 8
    own_buf[...] = jnp.zeros_like(own_buf)

    @pl.loop(0, HEADS // 2)
    def _(j):
        @pl.when(j % (per_group // 2) == 0)
        def _():
            q_load(j // (per_group // 2)).wait()

        cut = pl.ds(pl.multiple_of(j * 2 * KVW, 128), 2 * KVW)
        for b in range(blocks):
            rows = slice(8 * b, 8 * b + 8)
            product = q_ref[rows, cut].astype(jnp.float32) * key_buf[rows, :]
            tiles = [product[:, 128 * i : 128 * (i + 1)] for i in range(9)]
            low = (tiles[0] + tiles[1]) + (tiles[2] + tiles[3]) + jnp.where(lane < 64, tiles[4], 0.0)
            high = (tiles[5] + tiles[6]) + (tiles[7] + tiles[8])
            high = high + jnp.where(lane < 64, 0.0, tiles[4])
            low = jnp.sum(low, axis=1, keepdims=True)
            high = jnp.sum(high, axis=1, keepdims=True)
            own_buf[rows, :] = jnp.where(
                head == 2 * j, low, jnp.where(head == 2 * j + 1, high, own_buf[rows, :])
            )

    own = own_buf[...] * softmax_scale
    top_old = top_ref[...]
    top = jnp.maximum(top_old, own)
    part = total_ref[...] * jnp.exp(top_old - top)
    part_own = jnp.exp(own - top)
    inverse = 1.0 / (part + part_own)
    keep_buf[...] = part * inverse
    own_buf[...] = (part_own * inverse).astype(jnp.bfloat16).astype(jnp.float32)

    @pl.loop(0, groups)
    def _(g):
        o_load(g).wait()
        for b in range(blocks):
            rows = slice(8 * b, 8 * b + 8)
            key_low = key_buf[rows, :LATENT]
            keeps, adds = keep_buf[rows, :], own_buf[rows, :]
            for i in range(per_group):
                h = g * per_group + i
                keep = jnp.sum(jnp.where(head == h, keeps, 0.0), axis=1, keepdims=True)
                add = jnp.sum(jnp.where(head == h, adds, 0.0), axis=1, keepdims=True)
                cut = pl.ds(pl.multiple_of(h * LATENT, LATENT), LATENT)
                o_ref[rows, cut] = (
                    o_ref[rows, cut].astype(jnp.float32) * keep + add * key_low
                ).astype(jnp.bfloat16)
        store(g).start()

    @pl.loop(0, groups)
    def _(g):
        store(g).wait()

    hidden_copy.wait()


def tail(hidden_in, back, kv_gain, cosine, sine, top, total, place_weight, w_all, queries, o):
    rows, width = hidden_in.shape
    parts, groups = 7, 8
    vmem = pl.BlockSpec(memory_space=pltpu.VMEM)
    hbm = pl.BlockSpec(memory_space=pl.ANY)
    return pl.pallas_call(
        functools.partial(tail_kernel, parts, groups),
        out_shape=[
            jax.ShapeDtypeStruct((rows, width), jnp.bfloat16),
            jax.ShapeDtypeStruct((rows, HEADS * LATENT), jnp.bfloat16),
        ],
        in_specs=[vmem] * 8 + [hbm] * 3,
        out_specs=[hbm] * 2,
        scratch_shapes=[
            pltpu.VMEM(w_all.shape, jnp.bfloat16),
            pltpu.VMEM(queries.shape, jnp.bfloat16),
            pltpu.VMEM(o.shape, jnp.bfloat16),
            pltpu.VMEM((rows, width), jnp.bfloat16),
            pltpu.VMEM((rows, 2 * KVW), jnp.float32),
            pltpu.VMEM((rows, HEADS), jnp.float32),
            pltpu.VMEM((rows, HEADS), jnp.float32),
            pltpu.SemaphoreType.DMA((parts,)),
            pltpu.SemaphoreType.DMA((groups,)),
            pltpu.SemaphoreType.DMA((groups,)),
            pltpu.SemaphoreType.DMA,
            pltpu.SemaphoreType.DMA((groups,)),
        ],
        compiler_params=pltpu.CompilerParams(vmem_limit_bytes=40 * MIB),
        cost_estimate=pl.CostEstimate(
            flops=2 * rows * width * KVW,
            bytes_accessed=2 * (w_all.size + queries.size + 2 * o.size),
            transcendentals=rows * HEADS * 2,
        ),
        name="tail",
    )(
        hidden_in,
        back,
        kv_gain.reshape(1, LATENT),
        cosine,
        sine,
        top,
        total,
        place_weight,
        w_all,
        queries,
        o,
    )


def plus(*terms):
    total = terms[0].astype(jnp.float32)
    for term in terms[1:]:
        total = total + term.astype(jnp.float32)
    return total.astype(jnp.bfloat16)


def after(values, *others):
    return lax.optimization_barrier((values, others))[0]


def body(
    hidden_in,
    norm_gain,
    route_logits,
    expert_ids,
    w_gate,
    w_up,
    w_down,
    w_latent,
    kv_gain,
    queries,
    page_pool,
    page_table,
    kv_lengths,
    migration,
):
    dp_count = lax.axis_size("dp")
    ex_count = lax.axis_size("expert")
    row_count = hidden_in.shape[0]
    local_experts = w_gate.shape[0]
    window = local_experts * dp_count
    width = hidden_in.shape[1]
    x_wide = hidden_in.astype(jnp.float32)
    normed = rms_rows(x_wide, norm_gain).astype(jnp.bfloat16)
    in_window = expert_ids < window
    has = jnp.any(in_window, axis=1)
    chosen = jnp.sum(jnp.where(in_window, expert_ids, 0), axis=1)
    sigma = jax.nn.sigmoid(route_logits)
    weight = (
        routed_scale * jnp.sum(jnp.where(in_window, sigma, 0.0), axis=1) / jnp.sum(sigma, axis=1)
    )
    onehot = ((chosen[:, None] == jnp.arange(window)[None, :]) & has[:, None]).astype(jnp.int32)
    rank = jnp.cumsum(onehot, axis=0) - onehot
    slot = jnp.sum(rank * onehot, axis=1)
    slots = local_experts * CAP
    place = chosen * CAP + slot
    pick = (place[:, None] == jnp.arange(window * CAP)[None, :]) & has[:, None]
    packed = jnp.einsum(
        "rs,rd->sd", pick.astype(jnp.bfloat16), normed, preferred_element_type=jnp.float32
    ).astype(jnp.bfloat16)
    place_weight = jnp.where(pick, weight[:, None], 0.0)
    arrived = lax.all_to_all(
        packed.reshape(dp_count, slots, width), "dp", split_axis=0, concat_axis=0, tiled=True
    )
    outgoing = jnp.take(page_pool, migration.reshape(dp_count * MCAP), axis=0, mode="clip")
    query = queries.reshape(row_count, HEADS, KVW)
    arrived = after(arrived, outgoing, query)
    arrived = arrived.reshape(window * CAP, width)
    axes = (("z", "x"), ("x", "z"))
    both = range(2)
    n = arrived.shape[0] // 2
    rows = [arrived[k * n : (k + 1) * n] for k in both]
    weights = (w_gate, w_up, w_down)

    below = [shift(rows[k], axes[k][0], 1) for k in both]
    above = [shift(rows[k], axes[k][0], -1) for k in both]
    incoming = lax.all_to_all(
        after(outgoing, arrived).reshape(dp_count, MCAP, page_pool.shape[1]),
        "dp",
        split_axis=0,
        concat_axis=0,
        tiled=True,
    ).reshape(dp_count * MCAP, page_pool.shape[1])
    below, above = after((below, above))
    beyond = [shift(above[k], axes[k][0], -1) for k in both]
    low = pack([(rows[k], below[k]) for k in both])
    below_low = [shift(low[k], axes[k][1], 1) for k in both]
    low_too, beyond = after((low, beyond))
    above_low = [shift(low_too[k], axes[k][1], -1) for k in both]
    w_local, pool = after((w_latent, page_pool), low, incoming)
    spread = lax.all_to_all(
        jnp.broadcast_to(w_local[None], (ex_count,) + w_latent.shape),
        "expert",
        split_axis=0,
        concat_axis=0,
        tiled=True,
    ).reshape(ex_count * w_latent.shape[0], KVW)
    pool = pool.reshape(page_pool.shape[0], PAGE, KVW)
    more = incoming.reshape(dp_count * MCAP, PAGE, KVW)
    high = pack([(above[k], beyond[k]) for k in both])
    high = after(high, pool, more)
    below_low, above_low = after((below_low, above_low), spread)
    w_all = lax.all_gather(spread, "dp", axis=0, tiled=True)
    below_high = [shift(high[k], axes[k][1], 1) for k in both]
    above_high = [shift(high[k], axes[k][1], -1) for k in both]
    y_first = ffn([[low[k], high[k], below_low[k], above_low[k]] for k in both], *weights)
    below_low, above_high, below_high, above_low = after(
        (below_low, above_high, below_high, above_low), y_first
    )
    far_low = [shift(below_low[k], axes[k][1], 1) for k in both]
    far_high = [shift(above_high[k], axes[k][1], -1) for k in both]
    y_second = ffn([[below_high[k], above_high[k]] for k in both], *weights)
    y_first = after(y_first, y_second)
    early_down = [shift(y_first[k][2], axes[k][1], -1) for k in both]
    early_up = [shift(y_second[k][1], axes[k][1], 1) for k in both]
    far_low, far_high = after((far_low, far_high), y_second)
    y_far = ffn([[far_low[k], far_high[k]] for k in both], *weights)
    y_far, early_down, early_up = after((y_far, early_down, early_up))
    relay_up = [shift(y_far[k][0], axes[k][1], 1) for k in both]
    relay_down = [shift(y_far[k][1], axes[k][1], -1) for k in both]
    query = after(query, y_far)
    cached, top, total = attend_cached(query, pool, more, page_table, kv_lengths)
    relay_up, relay_down = after((relay_up, relay_down), cached)
    late_up = [shift(plus(y_first[k][3], relay_up[k]), axes[k][1], 1) for k in both]
    late_down = [shift(plus(y_second[k][0], relay_down[k]), axes[k][1], -1) for k in both]
    cached = cached.reshape(row_count, HEADS * LATENT)
    late_up, late_down = after((late_up, late_down), cached)
    terms_low = [(y_first[k][0], late_up[k], early_down[k]) for k in both]
    terms_high = [(y_first[k][1], early_up[k], late_down[k]) for k in both]
    for_far = [plus(*(term[n:] for term in terms_high[k])) for k in both]
    for_below = [plus(*(term[n:] for term in terms_low[k])) for k in both]
    relayed = [shift(for_far[k], axes[k][0], 1) for k in both]
    from_above = [shift(for_below[k], axes[k][0], -1) for k in both]
    relayed, from_above = after((relayed, from_above))
    from_below = [
        shift(plus(*(term[:n] for term in terms_high[k]), relayed[k]), axes[k][0], 1) for k in both
    ]
    from_below = after(from_below)
    finished = [
        plus(*(term[:n] for term in terms_low[k]), from_below[k], from_above[k]) for k in both
    ]
    back = lax.all_to_all(
        jnp.concatenate(finished, axis=0).reshape(dp_count, slots, width),
        "dp",
        split_axis=0,
        concat_axis=0,
        tiled=True,
    ).reshape(window * CAP, width)

    half = (KVW - LATENT) // 2
    freq = 10000.0 ** (-jnp.arange(half, dtype=jnp.float32) / half)
    angle = kv_lengths.astype(jnp.float32)[:, None] * freq[None, :]
    return tuple(
        tail(
            hidden_in,
            back,
            kv_gain,
            jnp.cos(angle),
            jnp.sin(angle),
            top,
            total,
            place_weight,
            w_all,
            queries,
            cached,
        )
    )


def solution(mesh):
    return jax.shard_map(
        body,
        mesh=mesh,
        in_specs=(
            P(("dp", "expert"), None),
            P(),
            P(("dp", "expert"), None),
            P(("dp", "expert"), None),
            P("dp", None, "expert"),
            P("dp", None, "expert"),
            P("dp", "expert", None),
            P(("dp", "expert"), None),
            P(),
            P(("dp", "expert"), None),
            P(("dp", "expert"), None),
            P(("dp", "expert"), None),
            P(("dp", "expert")),
            P("dp", "expert", None, None),
        ),
        out_specs=(P(("dp", "expert"), None), P(("dp", "expert"), None)),
        check_vma=False,
    )
```

time: 301 us -> 312 us (1.037)
  Pallas kernels: 70.1 us -> 59.1 us
  other arithmetic: 15.9 us -> 22.8 us
  waiting for transfers between devices: 95.7 us -> 102 us
  starting transfers between devices: 67 us -> 72.9 us
  local copies, waits for them, and re-layouts: 33.6 us -> 36.8 us
    pallas_call x3, Pallas kernels: 36.1 us -> 28.3 us  [ffn(): pl.pallas_call(functools.partial(ffn_kernel, count, rows, parts), out_sha...]
    convert_element_type x11, other arithmetic: 11 us -> 18.3 us  [plus(): return total.astype(jnp.bfloat16)]
    all_to_all x2 -> x3, starting transfers between devices: 19.8 us -> 26.2 us  [the longest x1 15.9 us: body(): lax.all_to_all(jnp.concatenate(finished, axis=0).reshape(dp_count, slots,...]
    all_to_all x2 -> x3, waiting for transfers between devices: 19 us -> 25.3 us  [the longest x1 13.3 us: body(): lax.all_to_all(jnp.concatenate(finished, axis=0).reshape(dp_count, slots,...]
    pallas_call x1, Pallas kernels: 17.6 us -> 12.8 us  [tail(): pl.pallas_call(functools.partial(tail_kernel, parts, groups), out_shape=[...]
    unnamed x65 -> x75, local copies, waits for them, and re-layouts: 8.11 us -> 12.5 us
    optimization_barrier x2 -> x1, local copies, waits for them, and re-layouts: 5.86 us -> 2.42 us  [after(): return lax.optimization_barrier((values, others))[0]]
  transfers between devices with their start and end apart: 40 -> 41, of which waited for: 27 -> 23; matrix products, arithmetic and copies ran while one was open for 14% -> 16% of each run, Pallas kernels for 18% -> 15%
where the time goes in v2:
time: 312 us; the launch traced here: 310 us
  waiting for transfers between devices  102 us (33%)
  starting transfers between devices  72.9 us (23%)
  Pallas kernels  59.1 us (19%)
  local copies, waits for them, and re-layouts  36.8 us (12%)
  other arithmetic  22.8 us (7%)
  between operations  14.5 us (5%)
    ppermute x36, waiting for transfers between devices, shift(): return lax.ppermute(value, 'expert', pairs)  74.5 us
    ppermute x36, starting transfers between devices, shift(): return lax.ppermute(value, 'expert', pairs)  40.7 us
    pallas_call x3, Pallas kernels, ffn(): pl.pallas_call(functools.partial(ffn_kernel, count, rows, parts), out_sha...  28.3 us
    convert_element_type x11, other arithmetic, plus(): return total.astype(jnp.bfloat16)  18.3 us
    all_to_all x1, starting transfers between devices, body(): lax.all_to_all(jnp.concatenate(finished, axis=0).reshape(dp_count, slots,...  15.9 us
    all_to_all x1, waiting for transfers between devices, body(): lax.all_to_all(jnp.concatenate(finished, axis=0).reshape(dp_count, slots,...  13.3 us
    pallas_call x1, Pallas kernels, attend_cached(): pl.pallas_call(functools.partial(attend_kernel, step), out_shape=[jax.Sha...  13 us
    pallas_call x1, Pallas kernels, tail(): pl.pallas_call(functools.partial(tail_kernel, parts, groups), out_shape=[...  12.8 us
  transfers between devices with their start and end apart: 41, of which 23 were waited for; matrix products, arithmetic and copies ran while one was open for 16% of the time, Pallas kernels for 15%

profile of v2, /device:TPU:1, one launch (start us, length us, event | category | flops | bytes accessed | tf_op | source)
XLA Modules:
  0.0 310.5 jit_solution(14027735692608903499)
XLA Ops:
  10.4 2.6 fusion
  13.1 6.0 %all-to-all-start = ((bf16[8,8,7168]{2,1,0:T(8,128)(2,1)}), bf16[8,8,7168]{2,1,0:T(8,128)(2,1)S(1)}, u32[]{:S(2)}, u32[]{:S(2)}) async-start(bf16[8,8,7168]{2,1,0:T(8,128)(2,1)} %fusion), calls=%async_computation | async-start | bytes 1835008 | tf_op jit(solution)/shard_map/all_to_all | solution.py:518
  19.0 10.0 %reshape.72.q_ref = bf16[64,64,576]{2,1,0:T(8,128)(2,1)} reshape(bf16[64,36864]{1,0:T(8,128)(2,1)} %q_hbm.1) | data formatting | bytes 9437184 | tf_op jit(solution)/shard_map/reshape | solution.py:522
  39.4 7.2 %collective-permute-done.refs_1_ = bf16[32,7168]{1,0:T(8,128)(2,1)S(1)} collective-permute-done((bf16[32,7168]{1,0:T(8,128)(2,1)S(1)}, bf16[32,7168]{1,0:T(8,128)(2,1)S(1)}, u32[]{:S(2)}, u32[]{:S(2)}) %collective-permute-start) | collective-permute-done | bytes 458784 | tf_op jit(solution)/shard_map/ppermute | solution.py:37
  54.5 6.6 %all-to-all-start.1 = ((bf16[8,4,9216]{2,1,0:T(4,128)(2,1)}), bf16[8,4,9216]{2,1,0:T(4,128)(2,1)S(1)}, u32[]{:S(2)}, u32[]{:S(2)}) async-start(bf16[8,4,9216]{2,1,0:T(4,128)(2,1)} %reshape.74), calls=%async_computation.1 | async-start | bytes 1179648 | tf_op jit(solution)/shard_map/all_to_all | solution.py:533
  63.9 2.6 collective-permute-start.8
  66.5 4.9 %all-to-all-done.1 = bf16[8,4,9216]{2,1,0:T(4,128)(2,1)S(1)} async-done(((bf16[8,4,9216]{2,1,0:T(4,128)(2,1)}), bf16[8,4,9216]{2,1,0:T(4,128)(2,1)S(1)}, u32[]{:S(2)}, u32[]{:S(2)}) %all-to-all-start.1) | async-done | bytes 589856 | tf_op jit(solution)/shard_map/all_to_all | solution.py:533
  72.6 3.7 %all-to-all-start.2 = ((bf16[16,56,576]{2,1,0:T(8,128)(2,1)}), bf16[16,56,576]{2,1,0:T(8,128)(2,1)S(1)}, u32[]{:S(2)}, u32[]{:S(2)}) async-start(bf16[16,56,576]{2,1,0:T(8,128)(2,1)} %broadcast_in_dim.28), calls=%async_computation.2 | async-start | bytes 2293760 | tf_op jit(solution)/shard_map/all_to_all | solution.py:547
  76.3 2.5 collective-permute-start.9
  83.8 2.5 pack.3
  86.3 2.5 collective-permute-start.10
  92.2 7.1 %all-to-all-done.2 = bf16[16,56,576]{2,1,0:T(8,128)(2,1)S(1)} async-done(((bf16[16,56,576]{2,1,0:T(8,128)(2,1)}), bf16[16,56,576]{2,1,0:T(8,128)(2,1)S(1)}, u32[]{:S(2)}, u32[]{:S(2)}) %all-to-all-start.2) | async-done | bytes 1032224 | tf_op jit(solution)/shard_map/all_to_all | solution.py:547
  99.3 10.3 %collective-permute-done.9.refs_7_ = bf16[64,7168]{1,0:T(8,128)(2,1)} collective-permute-done((bf16[64,7168]{1,0:T(8,128)(2,1)}, bf16[64,7168]{1,0:T(8,128)(2,1)}, u32[]{:S(2)}, u32[]{:S(2)}) %collective-permute-start.9) | collective-permute-done | bytes 917536 | tf_op jit(solution)/shard_map/ppermute | solution.py:37
  109.6 11.5 %ffn.3 = (bf16[64,7168]{1,0:T(8,128)(2,1)}, bf16[64,7168]{1,0:T(8,128)(2,1)}, bf16[64,7168]{1,0:T(8,128)(2,1)}, bf16[64,7168]{1,0:T(8,128)(2,1)}, bf16[64,7168]{...) custom-call(bf16[64,7168]{1,0:T(8,128)(2,1)} %get-tuple-element.96.refs_0_, ...), custom_call_target="tpu_custom_call" | custom-call | flops 5637144576 | bytes 25690112 | tf_op jit(solution)/shard_map/ffn/pallas_call | solution.py:119
  121.1 8.2 %collective-permute-done.11.refs_3_ = bf16[64,7168]{1,0:T(8,128)(2,1)} collective-permute-done((bf16[64,7168]{1,0:T(8,128)(2,1)}, bf16[64,7168]{1,0:T(8,128)(2,1)}, u32[]{:S(2)}, u32[]{:S(2)}) %collective-permute-start.11) | collective-permute-done | bytes 917536 | tf_op jit(solution)/shard_map/ppermute | solution.py:37
  134.8 8.4 %ffn.4 = (bf16[64,7168]{1,0:T(8,128)(2,1)}, bf16[64,7168]{1,0:T(8,128)(2,1)}, bf16[64,7168]{1,0:T(8,128)(2,1)}, bf16[64,7168]{1,0:T(8,128)(2,1)}) custom-call(bf16[64,7168]{1,0:T(8,128)(2,1)} %copy-done.12, bf16[64,7168]{1,0:T(8,128)(2,1)} %collective-permute-done.10.refs_1_, bf16[64,7168]{1,0:T(8,128)(2,1)} %copy-done.13, ...), custom_call_target="tpu_custom_call" | custom-call | flops 2818572288 | bytes 18350080 | tf_op jit(solution)/shard_map/ffn/pallas_call | solution.py:119
  143.3 7.6 %collective-permute-done.14.refs_0_ = bf16[64,7168]{1,0:T(8,128)(2,1)S(1)} collective-permute-done((bf16[64,7168]{1,0:T(8,128)(2,1)}, bf16[64,7168]{1,0:T(8,128)(2,1)S(1)}, u32[]{:S(2)}, u32[]{:S(2)}) %collective-permute-start.14) | collective-permute-done | bytes 917536 | tf_op jit(solution)/shard_map/ppermute | solution.py:37
  155.6 8.4 %ffn.5 = (bf16[64,7168]{1,0:T(8,128)(2,1)}, bf16[64,7168]{1,0:T(8,128)(2,1)}, bf16[64,7168]{1,0:T(8,128)(2,1)}, bf16[64,7168]{1,0:T(8,128)(2,1)}) custom-call(bf16[64,7168]{1,0:T(8,128)(2,1)} %copy-done.14, bf16[64,7168]{1,0:T(8,128)(2,1)} %copy-done.16, bf16[64,7168]{1,0:T(8,128)(2,1)} %copy-done.15, bf16[64,7168]{1,0:T(8,128)(2,1)} %collective-permute-done.17.refs_3_, ...), custom_call_target="tpu_custom_call" | custom-call | flops 2818572288 | bytes 18350080 | tf_op jit(solution)/shard_map/ffn/pallas_call | solution.py:119
  164.1 6.4 %collective-permute-done.18 = bf16[64,7168]{1,0:T(8,128)(2,1)} collective-permute-done((bf16[64,7168]{1,0:T(8,128)(2,1)}, bf16[64,7168]{1,0:T(8,128)(2,1)}, u32[]{:S(2)}, u32[]{:S(2)}) %collective-permute-start.18) | collective-permute-done | bytes 917536 | tf_op jit(solution)/shard_map/ppermute | solution.py:37
  175.8 2.6 collective-permute-start.25
  179.2 3.5 %copy.20.pool_hbm = bf16[128,16,576]{2,1,0:T(8,128)(2,1)} copy(bf16[128,16,576]{0,2,1:T(8,128)(2,1)S(1)} %bitcast.19) | data formatting | bytes 4718592 | tf_op jit(solution)/shard_map/reshape | solution.py:554
  182.7 13.0 %attend_cached.1 = (bf16[64,64,512]{2,1,0:T(8,128)(2,1)}, f32[64,64]{1,0:T(8,128)}, f32[64,64]{1,0:T(8,128)}) custom-call(s32[384]{0:T(512)} %reshape.76.table, s32[64]{0:T(128)} %lengths.1, bf16[64,64,576]{2,1,0:T(8,128)(2,1)} %reshape.72.q_ref, bf16[128,16,576]{2,1,0:T(8,128)(2,1)} %copy.20.pool_hbm, bf16[32,16,576]{2,1,0:T(8,128)(2,1)} %reshape_reshape.3.more_hbm), custom_call_target="tpu_custom_call" | custom-call | flops 855638016 | bytes 11862016 | tf_op jit(solution)/shard_map/attend_cached/pallas_call | solution.py:205
  195.8 2.7 add_convert_fusion
  207.3 6.8 %copy.21 = bf16[8,8,64,512]{3,1,2,0:T(8,128)(2,1)} copy(bf16[8,8,64,512]{3,2,1,0:T(8,128)(2,1)} %bitcast.21) | data formatting | bytes 8388608
  215.1 3.6 %collective-permute-done.27 = bf16[64,7168]{1,0:T(8,128)(2,1)S(1)} collective-permute-done((bf16[64,7168]{1,0:T(8,128)(2,1)}, bf16[64,7168]{1,0:T(8,128)(2,1)S(1)}, u32[]{:S(2)}, u32[]{:S(2)}) %collective-permute-start.27) | collective-permute-done | bytes 917536 | tf_op jit(solution)/shard_map/ppermute | solution.py:37
  231.2 4.2 %collective-permute-done.31 = bf16[32,7168]{1,0:T(8,128)(2,1)S(1)} collective-permute-done((bf16[32,7168]{1,0:T(8,128)(2,1)S(1)}, bf16[32,7168]{1,0:T(8,128)(2,1)S(1)}, u32[]{:S(2)}, u32[]{:S(2)}) %collective-permute-start.31) | collective-permute-done | bytes 458784 | tf_op jit(solution)/shard_map/ppermute | solution.py:37
  235.4 2.6 collective-permute-done.30
  240.9 9.9 %collective-permute-done.35 = bf16[32,7168]{1,0:T(8,128)(2,1)S(1)} collective-permute-done((bf16[32,7168]{1,0:T(8,128)(2,1)S(1)}, bf16[32,7168]{1,0:T(8,128)(2,1)S(1)}, u32[]{:S(2)}, u32[]{:S(2)}) %collective-permute-start.35) | collective-permute-done | bytes 458784 | tf_op jit(solution)/shard_map/ppermute | solution.py:37
  250.8 3.1 collective-permute-done.34
  256.6 15.9 %all-to-all-start.3 = ((bf16[8,8,7168]{2,1,0:T(8,128)(2,1)}), bf16[8,8,7168]{2,1,0:T(8,128)(2,1)S(1)}, u32[]{:S(2)}, u32[]{:S(2)}) async-start(bf16[8,8,7168]{2,1,0:T(8,128)(2,1)} %maximum_bitcast_fusion), calls=%async_computation.3 | async-start | bytes 1835008 | tf_op jit(solution)/shard_map/all_to_all | solution.py:598
  272.9 13.3 %all-to-all-done.3 = bf16[8,8,7168]{2,1,0:T(8,128)(2,1)S(1)} async-done(((bf16[8,8,7168]{2,1,0:T(8,128)(2,1)}), bf16[8,8,7168]{2,1,0:T(8,128)(2,1)S(1)}, u32[]{:S(2)}, u32[]{:S(2)}) %all-to-all-start.3) | async-done | bytes 917536 | tf_op jit(solution)/shard_map/all_to_all | solution.py:598
  290.8 12.8 %tail.1 = (bf16[64,7168]{1,0:T(8,128)(2,1)}, bf16[64,32768]{1,0:T(8,128)(2,1)}) custom-call(bf16[64,7168]{1,0:T(8,128)(2,1)S(1)} %copy-done.2, bf16[64,7168]{1,0:T(8,128)(2,1)S(1)} %bitcast.17, f32[1,512]{1,0:T(1,128)S(1)} %bitcast.18, f32[64,32]{1,0:T(8,128)S(1)} %get-tuple-element.169.cos_ref, f32[64,32]{1,0:T(8,128)S(1)} %get-tuple-element.168.sin_ref, ...), custom_call_target="tpu_custom_call" | custom-call | flops 528482304 | bytes 21364736 | tf_op jit(solution)/shard_map/tail/pallas_call | solution.py:422
  (171 shorter events, 82.7 us)
Async XLA Ops:
  13.1 19.7 %all-to-all-start = ((bf16[8,8,7168]{2,1,0:T(8,128)(2,1)}), bf16[8,8,7168]{2,1,0:T(8,128)(2,1)S(1)}, u32[]{:S(2)}, u32[]{:S(2)}) async-start(bf16[8,8,7168]{2,1,0:T(8,128)(2,1)} %fusion), calls=%async_computation | async-start | bytes 1835008 | tf_op jit(solution)/shard_map/all_to_all | solution.py:518
  32.8 13.8 %collective-permute-start = (bf16[32,7168]{1,0:T(8,128)(2,1)S(1)}, bf16[32,7168]{1,0:T(8,128)(2,1)S(1)}, u32[]{:S(2)}, u32[]{:S(2)}) collective-permute-start(bf16[32,7168]{1,0:T(8,128)(2,1)S(1)} %get-tuple-element.167.refs_0_), channel_id=1, source_target_pairs={{0,1},{1,2},{2,3},{3,0},{4,5},{5,6},{6,7},{7,4},{8,9},{9,10},{10,1... | collective-permute-start | bytes 1376264 | tf_op jit(solution)/shard_map/ppermute | solution.py:37
  48.6 15.2 %collective-permute-start.4 = (bf16[32,7168]{1,0:T(8,128)(2,1)S(1)}, bf16[32,7168]{1,0:T(8,128)(2,1)}, u32[]{:S(2)}, u32[]{:S(2)}) collective-permute-start(bf16[32,7168]{1,0:T(8,128)(2,1)S(1)} %collective-permute-done.2.refs_0_), channel_id=1, source_target_pairs={{0,3},{1,0},{2,1},{3,2},{4,7},{5,4},{6,5},{7,6},{8,11},{9,8},{10,9... | collective-permute-start | bytes 1376264 | tf_op jit(solution)/shard_map/ppermute | solution.py:37
  50.1 13.8 %collective-permute-start.5 = (bf16[32,7168]{1,0:T(8,128)(2,1)}, bf16[32,7168]{1,0:T(8,128)(2,1)}, u32[]{:S(2)}, u32[]{:S(2)}) collective-permute-start(bf16[32,7168]{1,0:T(8,128)(2,1)} %collective-permute-done.3.refs_2_), channel_id=1, source_target_pairs={{0,12},{1,13},{2,14},{3,15},{4,0},{5,1},{6,2},{7,3},{8,4},{9,5},{1... | collective-permute-start | bytes 1376264 | tf_op jit(solution)/shard_map/ppermute | solution.py:37
  54.5 16.8 %all-to-all-start.1 = ((bf16[8,4,9216]{2,1,0:T(4,128)(2,1)}), bf16[8,4,9216]{2,1,0:T(4,128)(2,1)S(1)}, u32[]{:S(2)}, u32[]{:S(2)}) async-start(bf16[8,4,9216]{2,1,0:T(4,128)(2,1)} %reshape.74), calls=%async_computation.1 | async-start | bytes 1179648 | tf_op jit(solution)/shard_map/all_to_all | solution.py:533
  63.6 25.2 %collective-permute-start.6 = (bf16[64,7168]{1,0:T(8,128)(2,1)}, bf16[64,7168]{1,0:T(8,128)(2,1)}, u32[]{:S(2)}, u32[]{:S(2)}) collective-permute-start(bf16[64,7168]{1,0:T(8,128)(2,1)} %get-tuple-element.96.refs_0_), channel_id=1, source_target_pairs={{0,4},{1,5},{2,6},{3,7},{4,8},{5,9},{6,10},{7,11},{8,12},{9,13},{1... | collective-permute-start | bytes 2752520 | tf_op jit(solution)/shard_map/ppermute | solution.py:37
  63.7 27.0 %collective-permute-start.7 = (bf16[64,7168]{1,0:T(8,128)(2,1)}, bf16[64,7168]{1,0:T(8,128)(2,1)}, u32[]{:S(2)}, u32[]{:S(2)}) collective-permute-start(bf16[64,7168]{1,0:T(8,128)(2,1)} %get-tuple-element.97.refs_4_), channel_id=1, source_target_pairs={{0,1},{1,2},{2,3},{3,0},{4,5},{5,6},{6,7},{7,4},{8,9},{9,10},{10,1... | collective-permute-start | bytes 2752520 | tf_op jit(solution)/shard_map/ppermute | solution.py:37
  63.9 26.8 %collective-permute-start.8 = (bf16[64,7168]{1,0:T(8,128)(2,1)}, bf16[64,7168]{1,0:T(8,128)(2,1)}, u32[]{:S(2)}, u32[]{:S(2)}) collective-permute-start(bf16[64,7168]{1,0:T(8,128)(2,1)} %get-tuple-element.96.refs_0_), channel_id=1, source_target_pairs={{0,12},{1,13},{2,14},{3,15},{4,0},{5,1},{6,2},{7,3},{8,4},{9,5},{1... | collective-permute-start | bytes 2752520 | tf_op jit(solution)/shard_map/ppermute | solution.py:37
  72.6 26.8 %all-to-all-start.2 = ((bf16[16,56,576]{2,1,0:T(8,128)(2,1)}), bf16[16,56,576]{2,1,0:T(8,128)(2,1)S(1)}, u32[]{:S(2)}, u32[]{:S(2)}) async-start(bf16[16,56,576]{2,1,0:T(8,128)(2,1)} %broadcast_in_dim.28), calls=%async_computation.2 | async-start | bytes 2293760 | tf_op jit(solution)/shard_map/all_to_all | solution.py:547
  76.3 210.0 %all-gather.2.cloned.1.call-start = ((), (), s32[]{:S(2)}) async-start(), calls=%async_computation.4 | async-start | bytes 10321920 | tf_op jit(solution)/shard_map/all_gather | solution.py:559
  76.3 33.3 %collective-permute-start.9 = (bf16[64,7168]{1,0:T(8,128)(2,1)}, bf16[64,7168]{1,0:T(8,128)(2,1)}, u32[]{:S(2)}, u32[]{:S(2)}) collective-permute-start(bf16[64,7168]{1,0:T(8,128)(2,1)} %get-tuple-element.97.refs_4_), channel_id=1, source_target_pairs={{0,3},{1,0},{2,1},{3,2},{4,7},{5,4},{6,5},{7,6},{8,11},{9,8},{10,9... | collective-permute-start | bytes 2752520 | tf_op jit(solution)/shard_map/ppermute | solution.py:37
  86.3 34.9 %collective-permute-start.10 = (bf16[64,7168]{1,0:T(8,128)(2,1)}, bf16[64,7168]{1,0:T(8,128)(2,1)}, u32[]{:S(2)}, u32[]{:S(2)}) collective-permute-start(bf16[64,7168]{1,0:T(8,128)(2,1)} %get-tuple-element.95.refs_1_), channel_id=1, source_target_pairs={{0,12},{1,13},{2,14},{3,15},{4,0},{5,1},{6,2},{7,3},{8,4},{9,5},{1... | collective-permute-start | bytes 2752520 | tf_op jit(solution)/shard_map/ppermute | solution.py:37
  88.8 40.5 %collective-permute-start.12 = (bf16[64,7168]{1,0:T(8,128)(2,1)}, bf16[64,7168]{1,0:T(8,128)(2,1)S(1)}, u32[]{:S(2)}, u32[]{:S(2)}) collective-permute-start(bf16[64,7168]{1,0:T(8,128)(2,1)} %get-tuple-element.95.refs_1_), channel_id=1, source_target_pairs={{0,4},{1,5},{2,6},{3,7},{4,8},{5,9},{6,10},{7,11},{8,12},{9,13},{1... | collective-permute-start | bytes 2752520 | tf_op jit(solution)/shard_map/ppermute | solution.py:37
  90.7 38.6 %collective-permute-start.11 = (bf16[64,7168]{1,0:T(8,128)(2,1)}, bf16[64,7168]{1,0:T(8,128)(2,1)}, u32[]{:S(2)}, u32[]{:S(2)}) collective-permute-start(bf16[64,7168]{1,0:T(8,128)(2,1)} %get-tuple-element.101.refs_5_), channel_id=1, source_target_pairs={{0,3},{1,0},{2,1},{3,2},{4,7},{5,4},{6,5},{7,6},{8,11},{9,8},{10,9... | collective-permute-start | bytes 2752520 | tf_op jit(solution)/shard_map/ppermute | solution.py:37
  90.7 38.6 %collective-permute-start.13 = (bf16[64,7168]{1,0:T(8,128)(2,1)}, bf16[64,7168]{1,0:T(8,128)(2,1)S(1)}, u32[]{:S(2)}, u32[]{:S(2)}) collective-permute-start(bf16[64,7168]{1,0:T(8,128)(2,1)} %get-tuple-element.101.refs_5_), channel_id=1, source_target_pairs={{0,1},{1,2},{2,3},{3,0},{4,5},{5,6},{6,7},{7,4},{8,9},{9,10},{10,1... | collective-permute-start | bytes 2752520 | tf_op jit(solution)/shard_map/ppermute | solution.py:37
  129.3 21.6 %collective-permute-start.14 = (bf16[64,7168]{1,0:T(8,128)(2,1)}, bf16[64,7168]{1,0:T(8,128)(2,1)S(1)}, u32[]{:S(2)}, u32[]{:S(2)}) collective-permute-start(bf16[64,7168]{1,0:T(8,128)(2,1)} %collective-permute-done.6.refs_2_), channel_id=1, source_target_pairs={{0,4},{1,5},{2,6},{3,7},{4,8},{5,9},{6,10},{7,11},{8,12},{9,13},{1... | collective-permute-start | bytes 2752520 | tf_op jit(solution)/shard_map/ppermute | solution.py:37
  130.6 21.7 %collective-permute-start.15 = (bf16[64,7168]{1,0:T(8,128)(2,1)}, bf16[64,7168]{1,0:T(8,128)(2,1)S(1)}, u32[]{:S(2)}, u32[]{:S(2)}) collective-permute-start(bf16[64,7168]{1,0:T(8,128)(2,1)} %collective-permute-done.7.refs_6_), channel_id=1, source_target_pairs={{0,1},{1,2},{2,3},{3,0},{4,5},{5,6},{6,7},{7,4},{8,9},{9,10},{10,1... | collective-permute-start | bytes 2752520 | tf_op jit(solution)/shard_map/ppermute | solution.py:37
  132.4 22.3 %collective-permute-start.16 = (bf16[64,7168]{1,0:T(8,128)(2,1)}, bf16[64,7168]{1,0:T(8,128)(2,1)S(1)}, u32[]{:S(2)}, u32[]{:S(2)}) collective-permute-start(bf16[64,7168]{1,0:T(8,128)(2,1)} %collective-permute-done.10.refs_1_), channel_id=1, source_target_pairs={{0,12},{1,13},{2,14},{3,15},{4,0},{5,1},{6,2},{7,3},{8,4},{9,5},{1... | collective-permute-start | bytes 2752520 | tf_op jit(solution)/shard_map/ppermute | solution.py:37
  133.9 20.9 %collective-permute-start.17 = (bf16[64,7168]{1,0:T(8,128)(2,1)}, bf16[64,7168]{1,0:T(8,128)(2,1)}, u32[]{:S(2)}, u32[]{:S(2)}) collective-permute-start(bf16[64,7168]{1,0:T(8,128)(2,1)} %collective-permute-done.11.refs_3_), channel_id=1, source_target_pairs={{0,3},{1,0},{2,1},{3,2},{4,7},{5,4},{6,5},{7,6},{8,11},{9,8},{10,9... | collective-permute-start | bytes 2752520 | tf_op jit(solution)/shard_map/ppermute | solution.py:37
  143.2 28.6 %collective-permute-start.20 = (bf16[64,7168]{1,0:T(8,128)(2,1)}, bf16[64,7168]{1,0:T(8,128)(2,1)}, u32[]{:S(2)}, u32[]{:S(2)}) collective-permute-start(bf16[64,7168]{1,0:T(8,128)(2,1)} %get-tuple-element.117), channel_id=1, source_target_pairs={{0,4},{1,5},{2,6},{3,7},{4,8},{5,9},{6,10},{7,11},{8,12},{9,13},{1... | collective-permute-start | bytes 2752520 | tf_op jit(solution)/shard_map/ppermute | solution.py:37
  150.9 19.6 %collective-permute-start.18 = (bf16[64,7168]{1,0:T(8,128)(2,1)}, bf16[64,7168]{1,0:T(8,128)(2,1)}, u32[]{:S(2)}, u32[]{:S(2)}) collective-permute-start(bf16[64,7168]{1,0:T(8,128)(2,1)} %get-tuple-element.132), channel_id=1, source_target_pairs={{0,12},{1,13},{2,14},{3,15},{4,0},{5,1},{6,2},{7,3},{8,4},{9,5},{1... | collective-permute-start | bytes 2752520 | tf_op jit(solution)/shard_map/ppermute | solution.py:37
  152.3 19.6 %collective-permute-start.19 = (bf16[64,7168]{1,0:T(8,128)(2,1)}, bf16[64,7168]{1,0:T(8,128)(2,1)}, u32[]{:S(2)}, u32[]{:S(2)}) collective-permute-start(bf16[64,7168]{1,0:T(8,128)(2,1)} %get-tuple-element.133), channel_id=1, source_target_pairs={{0,3},{1,0},{2,1},{3,2},{4,7},{5,4},{6,5},{7,6},{8,11},{9,8},{10,9... | collective-permute-start | bytes 2752520 | tf_op jit(solution)/shard_map/ppermute | solution.py:37
  154.7 18.3 %collective-permute-start.21 = (bf16[64,7168]{1,0:T(8,128)(2,1)}, bf16[64,7168]{1,0:T(8,128)(2,1)}, u32[]{:S(2)}, u32[]{:S(2)}) collective-permute-start(bf16[64,7168]{1,0:T(8,128)(2,1)} %get-tuple-element.119), channel_id=1, source_target_pairs={{0,1},{1,2},{2,3},{3,0},{4,5},{5,6},{6,7},{7,4},{8,9},{9,10},{10,1... | collective-permute-start | bytes 2752520 | tf_op jit(solution)/shard_map/ppermute | solution.py:37
  173.0 22.7 %collective-permute-start.22 = (bf16[64,7168]{1,0:T(8,128)(2,1)}, bf16[64,7168]{1,0:T(8,128)(2,1)S(1)}, u32[]{:S(2)}, u32[]{:S(2)}) collective-permute-start(bf16[64,7168]{1,0:T(8,128)(2,1)} %get-tuple-element.134), channel_id=1, source_target_pairs={{0,4},{1,5},{2,6},{3,7},{4,8},{5,9},{6,10},{7,11},{8,12},{9,13},{1... | collective-permute-start | bytes 2752520 | tf_op jit(solution)/shard_map/ppermute | solution.py:37
  173.4 22.4 %collective-permute-start.23 = (bf16[64,7168]{1,0:T(8,128)(2,1)}, bf16[64,7168]{1,0:T(8,128)(2,1)}, u32[]{:S(2)}, u32[]{:S(2)}) collective-permute-start(bf16[64,7168]{1,0:T(8,128)(2,1)} %get-tuple-element.135), channel_id=1, source_target_pairs={{0,1},{1,2},{2,3},{3,0},{4,5},{5,6},{6,7},{7,4},{8,9},{9,10},{10,1... | collective-permute-start | bytes 2752520 | tf_op jit(solution)/shard_map/ppermute | solution.py:37
  173.4 22.4 %collective-permute-start.24 = (bf16[64,7168]{1,0:T(8,128)(2,1)}, bf16[64,7168]{1,0:T(8,128)(2,1)}, u32[]{:S(2)}, u32[]{:S(2)}) collective-permute-start(bf16[64,7168]{1,0:T(8,128)(2,1)} %get-tuple-element.136), channel_id=1, source_target_pairs={{0,12},{1,13},{2,14},{3,15},{4,0},{5,1},{6,2},{7,3},{8,4},{9,5},{1... | collective-permute-start | bytes 2752520 | tf_op jit(solution)/shard_map/ppermute | solution.py:37
  175.8 20.0 %collective-permute-start.25 = (bf16[64,7168]{1,0:T(8,128)(2,1)}, bf16[64,7168]{1,0:T(8,128)(2,1)}, u32[]{:S(2)}, u32[]{:S(2)}) collective-permute-start(bf16[64,7168]{1,0:T(8,128)(2,1)} %get-tuple-element.137), channel_id=1, source_target_pairs={{0,3},{1,0},{2,1},{3,2},{4,7},{5,4},{6,5},{7,6},{8,11},{9,8},{10,9... | collective-permute-start | bytes 2752520 | tf_op jit(solution)/shard_map/ppermute | solution.py:37
  198.5 15.6 %collective-permute-start.29 = (bf16[64,7168]{1,0:T(8,128)(2,1)}, bf16[64,7168]{1,0:T(8,128)(2,1)}, u32[]{:S(2)}, u32[]{:S(2)}) collective-permute-start(bf16[64,7168]{1,0:T(8,128)(2,1)} %add_convert_fusion), channel_id=1, source_target_pairs={{0,3},{1,0},{2,1},{3,2},{4,7},{5,4},{6,5},{7,6},{8,11},{9,8},{10,9... | collective-permute-start | bytes 2752520 | tf_op jit(solution)/shard_map/ppermute | solution.py:37
  201.0 14.1 %collective-permute-start.28 = (bf16[64,7168]{1,0:T(8,128)(2,1)}, bf16[64,7168]{1,0:T(8,128)(2,1)S(1)}, u32[]{:S(2)}, u32[]{:S(2)}) collective-permute-start(bf16[64,7168]{1,0:T(8,128)(2,1)} %add_convert_fusion.1), channel_id=1, source_target_pairs={{0,12},{1,13},{2,14},{3,15},{4,0},{5,1},{6,2},{7,3},{8,4},{9,5},{1... | collective-permute-start | bytes 2752520 | tf_op jit(solution)/shard_map/ppermute | solution.py:37
  203.5 15.2 %collective-permute-start.27 = (bf16[64,7168]{1,0:T(8,128)(2,1)}, bf16[64,7168]{1,0:T(8,128)(2,1)S(1)}, u32[]{:S(2)}, u32[]{:S(2)}) collective-permute-start(bf16[64,7168]{1,0:T(8,128)(2,1)} %add_convert_fusion.2), channel_id=1, source_target_pairs={{0,1},{1,2},{2,3},{3,0},{4,5},{5,6},{6,7},{7,4},{8,9},{9,10},{10,1... | collective-permute-start | bytes 2752520 | tf_op jit(solution)/shard_map/ppermute | solution.py:37
  206.0 14.7 %collective-permute-start.26 = (bf16[64,7168]{1,0:T(8,128)(2,1)}, bf16[64,7168]{1,0:T(8,128)(2,1)S(1)}, u32[]{:S(2)}, u32[]{:S(2)}) collective-permute-start(bf16[64,7168]{1,0:T(8,128)(2,1)} %add_convert_fusion.3), channel_id=1, source_target_pairs={{0,4},{1,5},{2,6},{3,7},{4,8},{5,9},{6,10},{7,11},{8,12},{9,13},{1... | collective-permute-start | bytes 2752520 | tf_op jit(solution)/shard_map/ppermute | solution.py:37
  256.6 29.6 %all-to-all-start.3 = ((bf16[8,8,7168]{2,1,0:T(8,128)(2,1)}), bf16[8,8,7168]{2,1,0:T(8,128)(2,1)S(1)}, u32[]{:S(2)}, u32[]{:S(2)}) async-start(bf16[8,8,7168]{2,1,0:T(8,128)(2,1)} %maximum_bitcast_fusion), calls=%async_computation.3 | async-start | bytes 1835008 | tf_op jit(solution)/shard_map/all_to_all | solution.py:598
  (45 other events, 548.8 us)
Sparse Core Ops, SparseCore 0:
  207.4 57.8 all-gather.1

commit v3 on v2

--- a/solution.py
+++ b/solution.py
@@ -276,8 +276,8 @@
 def tail_kernel(
     parts,
     groups,
-    hidden_ref,
-    back_ref,
+    hidden_hbm,
+    back_hbm,
     gain_ref,
     cos_ref,
     sin_ref,
@@ -292,10 +292,13 @@
     w_ref,
     q_ref,
     o_ref,
+    hidden_ref,
+    back_ref,
     hidden_buf,
     key_buf,
     own_buf,
     keep_buf,
+    in_sem,
     w_sem,
     q_sem,
     o_sem,
@@ -303,6 +306,12 @@
     out_sem,
 ):
     width = hidden_ref.shape[1]
+    loads = [
+        pltpu.make_async_copy(back_hbm, back_ref, in_sem.at[0]),
+        pltpu.make_async_copy(hidden_hbm, hidden_ref, in_sem.at[1]),
+    ]
+    for copy in loads:
+        copy.start()
     piece = width // parts
     per_group = HEADS // groups
     span, q_span = per_group * LATENT, per_group * KVW
@@ -338,6 +347,8 @@
     pick = (place != 0.0).astype(jnp.bfloat16)
     weight = jnp.sum(place, axis=1, keepdims=True)
     projected = jnp.zeros((hidden_ref.shape[0], KVW), jnp.float32)
+    for copy in loads:
+        copy.wait()
     for c in range(parts):
         cut = slice(c * piece, (c + 1) * piece)
         picked = jnp.dot(pick, back_ref[:, cut], preferred_element_type=jnp.float32)
@@ -425,23 +436,26 @@
             jax.ShapeDtypeStruct((rows, width), jnp.bfloat16),
             jax.ShapeDtypeStruct((rows, HEADS * LATENT), jnp.bfloat16),
         ],
-        in_specs=[vmem] * 8 + [hbm] * 3,
+        in_specs=[hbm] * 2 + [vmem] * 6 + [hbm] * 3,
         out_specs=[hbm] * 2,
         scratch_shapes=[
             pltpu.VMEM(w_all.shape, jnp.bfloat16),
             pltpu.VMEM(queries.shape, jnp.bfloat16),
             pltpu.VMEM(o.shape, jnp.bfloat16),
             pltpu.VMEM((rows, width), jnp.bfloat16),
+            pltpu.VMEM(back.shape, jnp.bfloat16),
+            pltpu.VMEM((rows, width), jnp.bfloat16),
             pltpu.VMEM((rows, 2 * KVW), jnp.float32),
             pltpu.VMEM((rows, HEADS), jnp.float32),
             pltpu.VMEM((rows, HEADS), jnp.float32),
+            pltpu.SemaphoreType.DMA((2,)),
             pltpu.SemaphoreType.DMA((parts,)),
             pltpu.SemaphoreType.DMA((groups,)),
             pltpu.SemaphoreType.DMA((groups,)),
             pltpu.SemaphoreType.DMA,
             pltpu.SemaphoreType.DMA((groups,)),
         ],
-        compiler_params=pltpu.CompilerParams(vmem_limit_bytes=40 * MIB),
+        compiler_params=pltpu.CompilerParams(vmem_limit_bytes=58 * MIB),
         cost_estimate=pl.CostEstimate(
             flops=2 * rows * width * KVW,
             bytes_accessed=2 * (w_all.size + queries.size + 2 * o.size),
@@ -468,6 +482,16 @@
     for term in terms[1:]:
         total = total + term.astype(jnp.float32)
     return total.astype(jnp.bfloat16)
+
+
+def round_trip(piece, axis, index):
+    rows = piece.shape[0]
+    joined = jnp.zeros((SIDE * rows, piece.shape[1]), piece.dtype)
+    for step in range(SIDE):
+        part = piece if step == 0 else shift(piece, axis, -step)
+        at = jnp.bitwise_and(index + step, SIDE - 1) * rows
+        joined = lax.dynamic_update_slice_in_dim(joined, part, at, axis=0)
+    return joined
 
 
 def after(values, *others):
@@ -530,38 +554,26 @@
 
     below = [shift(rows[k], axes[k][0], 1) for k in both]
     above = [shift(rows[k], axes[k][0], -1) for k in both]
-    incoming = lax.all_to_all(
-        after(outgoing, arrived).reshape(dp_count, MCAP, page_pool.shape[1]),
-        "dp",
-        split_axis=0,
-        concat_axis=0,
-        tiled=True,
-    ).reshape(dp_count * MCAP, page_pool.shape[1])
     below, above = after((below, above))
     beyond = [shift(above[k], axes[k][0], -1) for k in both]
     low = pack([(rows[k], below[k]) for k in both])
     below_low = [shift(low[k], axes[k][1], 1) for k in both]
     low_too, beyond = after((low, beyond))
     above_low = [shift(low_too[k], axes[k][1], -1) for k in both]
-    w_local, pool = after((w_latent, page_pool), low, incoming)
-    spread = lax.all_to_all(
-        jnp.broadcast_to(w_local[None], (ex_count,) + w_latent.shape),
-        "expert",
+    high = pack([(above[k], beyond[k]) for k in both])
+    more = lax.all_to_all(
+        after(outgoing, high).reshape(dp_count, MCAP, page_pool.shape[1]),
+        "dp",
         split_axis=0,
         concat_axis=0,
         tiled=True,
-    ).reshape(ex_count * w_latent.shape[0], KVW)
-    pool = pool.reshape(page_pool.shape[0], PAGE, KVW)
-    more = incoming.reshape(dp_count * MCAP, PAGE, KVW)
-    high = pack([(above[k], beyond[k]) for k in both])
-    high = after(high, pool, more)
-    below_low, above_low = after((below_low, above_low), spread)
-    w_all = lax.all_gather(spread, "dp", axis=0, tiled=True)
+    ).reshape(dp_count * MCAP, PAGE, KVW)
+    pool = after(page_pool, high).reshape(page_pool.shape[0], PAGE, KVW)
     below_high = [shift(high[k], axes[k][1], 1) for k in both]
     above_high = [shift(high[k], axes[k][1], -1) for k in both]
     y_first = ffn([[low[k], high[k], below_low[k], above_low[k]] for k in both], *weights)
     below_low, above_high, below_high, above_low = after(
-        (below_low, above_high, below_high, above_low), y_first
+        (below_low, above_high, below_high, above_low), y_first, pool
     )
     far_low = [shift(below_low[k], axes[k][1], 1) for k in both]
     far_high = [shift(above_high[k], axes[k][1], -1) for k in both]
@@ -569,14 +581,18 @@
     y_first = after(y_first, y_second)
     early_down = [shift(y_first[k][2], axes[k][1], -1) for k in both]
     early_up = [shift(y_second[k][1], axes[k][1], 1) for k in both]
-    far_low, far_high = after((far_low, far_high), y_second)
+    index = lax.axis_index("expert")
+    w_line = round_trip(after(w_latent, y_first), "z", jnp.bitwise_and(index, SIDE - 1))
+    far_low, far_high = after((far_low, far_high), y_second, w_line, more)
     y_far = ffn([[far_low[k], far_high[k]] for k in both], *weights)
     y_far, early_down, early_up = after((y_far, early_down, early_up))
     relay_up = [shift(y_far[k][0], axes[k][1], 1) for k in both]
     relay_down = [shift(y_far[k][1], axes[k][1], -1) for k in both]
+    w_plane = round_trip(after(w_line, y_second), "x", jnp.right_shift(index, 2))
+    w_all = lax.all_gather(w_plane, "dp", axis=0, tiled=True)
     query = after(query, y_far)
     cached, top, total = attend_cached(query, pool, more, page_table, kv_lengths)
-    relay_up, relay_down = after((relay_up, relay_down), cached)
+    relay_up, relay_down = after((relay_up, relay_down), cached, w_plane)
     late_up = [shift(plus(y_first[k][3], relay_up[k]), axes[k][1], 1) for k in both]
     late_down = [shift(plus(y_second[k][0], relay_down[k]), axes[k][1], -1) for k in both]
     cached = cached.reshape(row_count, HEADS * LATENT)

time: 312 us -> 336 us (1.077)
  waiting for transfers between devices: 102 us -> 121 us
  Pallas kernels: 59.1 us -> 62.5 us
    ppermute x36 -> x42, waiting for transfers between devices: 74.5 us -> 108 us  [shift(): return lax.ppermute(value, 'expert', pairs)]
    all_to_all x2 -> x1, waiting for transfers between devices: 12 us -> 0.01 us  [body(): lax.all_to_all(after(outgoing, high).reshape(dp_count, MCAP, page_pool.sh...]
    ppermute x36 -> x42, starting transfers between devices: 40.7 us -> 45.4 us  [shift(): return lax.ppermute(value, 'expert', pairs)]
    unnamed x75 -> x65, local copies, waits for them, and re-layouts: 12.5 us -> 10.7 us
    all_to_all x2 -> x1, starting transfers between devices: 10.3 us -> 9.42 us  [body(): lax.all_to_all(after(outgoing, high).reshape(dp_count, MCAP, page_pool.sh...]
  transfers between devices with their start and end apart: 41 -> 46, of which waited for: 23 -> 29; matrix products, arithmetic and copies ran while one was open for 16% -> 15% of each run, Pallas kernels for 15% -> 14%
where the time goes in v3:
time: 336 us; the launch traced here: 335 us
  waiting for transfers between devices  121 us (36%)
  starting transfers between devices  75.1 us (22%)
  Pallas kernels  62.5 us (19%)
  local copies, waits for them, and re-layouts  33.9 us (10%)
  other arithmetic  24.9 us (7%)
  between operations  14.5 us (4%)
    ppermute x42, waiting for transfers between devices, shift(): return lax.ppermute(value, 'expert', pairs)  108 us
    ppermute x42, starting transfers between devices, shift(): return lax.ppermute(value, 'expert', pairs)  45.4 us
    pallas_call x3, Pallas kernels, ffn(): pl.pallas_call(functools.partial(ffn_kernel, count, rows, parts), out_sha...  28.4 us
    convert_element_type x11, other arithmetic, plus(): return total.astype(jnp.bfloat16)  19.1 us
    pallas_call x1, Pallas kernels, tail(): pl.pallas_call(functools.partial(tail_kernel, parts, groups), out_shape=[...  16.2 us
    all_to_all x1, starting transfers between devices, body(): lax.all_to_all(jnp.concatenate(finished, axis=0).reshape(dp_count, slots,...  14.3 us
    pallas_call x1, Pallas kernels, attend_cached(): pl.pallas_call(functools.partial(attend_kernel, step), out_shape=[jax.Sha...  13 us
    all_to_all x1, waiting for transfers between devices, body(): lax.all_to_all(jnp.concatenate(finished, axis=0).reshape(dp_count, slots,...  12.1 us
  transfers between devices with their start and end apart: 46, of which 29 were waited for; matrix products, arithmetic and copies ran while one was open for 15% of the time, Pallas kernels for 14%

profile of v3, /device:TPU:1, one launch (start us, length us, event | category | flops | bytes accessed | tf_op | source)
XLA Modules:
  0.0 335.0 jit_solution(11558557719089229258)
XLA Ops:
  13.1 6.0 %all-to-all-start = ((bf16[8,8,7168]{2,1,0:T(8,128)(2,1)}), bf16[8,8,7168]{2,1,0:T(8,128)(2,1)S(1)}, u32[]{:S(2)}, u32[]{:S(2)}) async-start(bf16[8,8,7168]{2,1,0:T(8,128)(2,1)} %fusion), calls=%async_computation | async-start | bytes 1835008 | tf_op jit(solution)/shard_map/all_to_all | solution.py:542
  19.0 10.0 %reshape.70.q_ref = bf16[64,64,576]{2,1,0:T(8,128)(2,1)} reshape(bf16[64,36864]{1,0:T(8,128)(2,1)} %q_hbm.1) | data formatting | bytes 9437184 | tf_op jit(solution)/shard_map/reshape | solution.py:546
  39.4 7.3 %collective-permute-done.refs_1_ = bf16[32,7168]{1,0:T(8,128)(2,1)S(1)} collective-permute-done((bf16[32,7168]{1,0:T(8,128)(2,1)S(1)}, bf16[32,7168]{1,0:T(8,128)(2,1)S(1)}, u32[]{:S(2)}, u32[]{:S(2)}) %collective-permute-start) | collective-permute-done | bytes 458784 | tf_op jit(solution)/shard_map/ppermute | solution.py:37
  55.3 2.9 collective-permute-done.4.refs_1_
  59.7 2.9 collective-permute-start.7
  66.5 8.5 %collective-permute-done.6.refs_2_ = bf16[64,7168]{1,0:T(8,128)(2,1)} collective-permute-done((bf16[64,7168]{1,0:T(8,128)(2,1)}, bf16[64,7168]{1,0:T(8,128)(2,1)}, u32[]{:S(2)}, u32[]{:S(2)}) %collective-permute-start.6) | collective-permute-done | bytes 917536 | tf_op jit(solution)/shard_map/ppermute | solution.py:37
  75.1 3.6 %collective-permute-done.7.refs_3_ = bf16[64,7168]{1,0:T(8,128)(2,1)} collective-permute-done((bf16[64,7168]{1,0:T(8,128)(2,1)}, bf16[64,7168]{1,0:T(8,128)(2,1)}, u32[]{:S(2)}, u32[]{:S(2)}) %collective-permute-start.7) | collective-permute-done | bytes 917536 | tf_op jit(solution)/shard_map/ppermute | solution.py:37
  82.1 11.5 %ffn.3 = (bf16[64,7168]{1,0:T(8,128)(2,1)}, bf16[64,7168]{1,0:T(8,128)(2,1)}, bf16[64,7168]{1,0:T(8,128)(2,1)}, bf16[64,7168]{1,0:T(8,128)(2,1)}, bf16[64,7168]{...) custom-call(bf16[64,7168]{1,0:T(8,128)(2,1)} %get-tuple-element.89.refs_0_, ...), custom_call_target="tpu_custom_call" | custom-call | flops 5637144576 | bytes 25690112 | tf_op jit(solution)/shard_map/ffn/pallas_call | solution.py:119
  93.6 4.8 %collective-permute-done.10.refs_1_ = bf16[64,7168]{1,0:T(8,128)(2,1)} collective-permute-done((bf16[64,7168]{1,0:T(8,128)(2,1)}, bf16[64,7168]{1,0:T(8,128)(2,1)}, u32[]{:S(2)}, u32[]{:S(2)}) %collective-permute-start.10) | collective-permute-done | bytes 917536 | tf_op jit(solution)/shard_map/ppermute | solution.py:37
  102.2 2.7 collective-permute-start.16
  105.9 9.4 %all-to-all-start.1 = ((bf16[8,4,9216]{2,1,0:T(4,128)(2,1)}), bf16[8,4,9216]{2,1,0:T(4,128)(2,1)S(1)}, u32[]{:S(2)}, u32[]{:S(2)}) async-start(bf16[8,4,9216]{2,1,0:T(4,128)(2,1)} %reshape.72), calls=%async_computation.1 | async-start | bytes 1179648 | tf_op jit(solution)/shard_map/all_to_all | solution.py:564
  117.6 8.5 %ffn.4 = (bf16[64,7168]{1,0:T(8,128)(2,1)}, bf16[64,7168]{1,0:T(8,128)(2,1)}, bf16[64,7168]{1,0:T(8,128)(2,1)}, bf16[64,7168]{1,0:T(8,128)(2,1)}) custom-call(bf16[64,7168]{1,0:T(8,128)(2,1)} %copy-done.10, bf16[64,7168]{1,0:T(8,128)(2,1)} %collective-permute-done.10.refs_1_, bf16[64,7168]{1,0:T(8,128)(2,1)} %collective-permute-done.13.refs_2_, ...), custom_call_target="tpu_custom_call" | custom-call | flops 2818572288 | bytes 18350080 | tf_op jit(solution)/shard_map/ffn/pallas_call | solution.py:119
  126.5 12.8 %collective-permute-done.18 = bf16[56,576]{1,0:T(8,128)(2,1)S(1)} collective-permute-done((bf16[56,576]{1,0:T(8,128)(2,1)S(1)}, bf16[56,576]{1,0:T(8,128)(2,1)S(1)}, u32[]{:S(2)}, u32[]{:S(2)}) %collective-permute-start.18) | collective-permute-done | bytes 64544 | tf_op jit(solution)/shard_map/ppermute | solution.py:37
  141.4 2.7 collective-permute-done.19
  144.9 4.2 %collective-permute-done.20 = bf16[56,576]{1,0:T(8,128)(2,1)} collective-permute-done((bf16[56,576]{1,0:T(8,128)(2,1)S(1)}, bf16[56,576]{1,0:T(8,128)(2,1)}, u32[]{:S(2)}, u32[]{:S(2)}) %collective-permute-start.20) | collective-permute-done | bytes 64544 | tf_op jit(solution)/shard_map/ppermute | solution.py:37
  157.7 8.4 %ffn.5 = (bf16[64,7168]{1,0:T(8,128)(2,1)}, bf16[64,7168]{1,0:T(8,128)(2,1)}, bf16[64,7168]{1,0:T(8,128)(2,1)}, bf16[64,7168]{1,0:T(8,128)(2,1)}) custom-call(bf16[64,7168]{1,0:T(8,128)(2,1)} %copy-done.7, bf16[64,7168]{1,0:T(8,128)(2,1)} %copy-done.9, bf16[64,7168]{1,0:T(8,128)(2,1)} %copy-done.8, bf16[64,7168]{1,0:T(8,128)(2,1)} %collective-permute-done.17.refs_3_, ...), custom_call_target="tpu_custom_call" | custom-call | flops 2818572288 | bytes 18350080 | tf_op jit(solution)/shard_map/ffn/pallas_call | solution.py:119
  174.1 2.7 collective-permute-start.28
  177.6 3.5 %copy.20.pool_hbm = bf16[128,16,576]{2,1,0:T(8,128)(2,1)} copy(bf16[128,16,576]{0,2,1:T(8,128)(2,1)S(1)} %bitcast.16) | data formatting | bytes 4718592 | tf_op jit(solution)/shard_map/reshape | solution.py:571
  181.1 14.5 %collective-permute-done.30 = bf16[224,576]{1,0:T(8,128)(2,1)S(1)} collective-permute-done((bf16[224,576]{1,0:T(8,128)(2,1)S(1)}, bf16[224,576]{1,0:T(8,128)(2,1)S(1)}, u32[]{:S(2)}, u32[]{:S(2)}) %collective-permute-start.30) | collective-permute-done | bytes 258080 | tf_op jit(solution)/shard_map/ppermute | solution.py:37
  195.6 4.3 %collective-permute-start.31 = (bf16[224,576]{1,0:T(8,128)(2,1)S(1)}, bf16[224,576]{1,0:T(8,128)(2,1)S(1)}, u32[]{:S(2)}, u32[]{:S(2)}) collective-permute-start(bf16[224,576]{1,0:T(8,128)(2,1)S(1)} %constant_dynamic-update-slice_fusion.3), channel_id=1, source_target_pairs={{0,4},{1,5},{2,6},{3,7},{4,8},{5,9},{6,10},{7,11},{8,12},{9,13},{1... | collective-permute-start | bytes 774152 | tf_op jit(solution)/shard_map/ppermute | solution.py:37
  200.1 6.9 %collective-permute-done.31 = bf16[224,576]{1,0:T(8,128)(2,1)S(1)} collective-permute-done((bf16[224,576]{1,0:T(8,128)(2,1)S(1)}, bf16[224,576]{1,0:T(8,128)(2,1)S(1)}, u32[]{:S(2)}, u32[]{:S(2)}) %collective-permute-start.31) | collective-permute-done | bytes 258080 | tf_op jit(solution)/shard_map/ppermute | solution.py:37
  207.1 13.0 %attend_cached.1 = (bf16[64,64,512]{2,1,0:T(8,128)(2,1)}, f32[64,64]{1,0:T(8,128)}, f32[64,64]{1,0:T(8,128)}) custom-call(s32[384]{0:T(512)} %reshape.74.table, s32[64]{0:T(128)} %lengths.1, bf16[64,64,576]{2,1,0:T(8,128)(2,1)} %reshape.70.q_ref, bf16[128,16,576]{2,1,0:T(8,128)(2,1)} %copy.20.pool_hbm, bf16[32,16,576]{2,1,0:T(8,128)(2,1)} %reshape.73.more_hbm), custom_call_target="tpu_custom_call" | custom-call | flops 855638016 | bytes 11862016 | tf_op jit(solution)/shard_map/attend_cached/pallas_call | solution.py:205
  232.6 6.9 %copy.21 = bf16[8,8,64,512]{3,1,2,0:T(8,128)(2,1)} copy(bf16[8,8,64,512]{3,2,1,0:T(8,128)(2,1)} %bitcast.17) | data formatting | bytes 8388608
  241.9 4.3 %collective-permute-done.33 = bf16[64,7168]{1,0:T(8,128)(2,1)S(1)} collective-permute-done((bf16[64,7168]{1,0:T(8,128)(2,1)}, bf16[64,7168]{1,0:T(8,128)(2,1)S(1)}, u32[]{:S(2)}, u32[]{:S(2)}) %collective-permute-start.33) | collective-permute-done | bytes 917536 | tf_op jit(solution)/shard_map/ppermute | solution.py:37
  246.2 4.2 %collective-permute-done.32 = bf16[64,7168]{1,0:T(8,128)(2,1)S(1)} collective-permute-done((bf16[64,7168]{1,0:T(8,128)(2,1)}, bf16[64,7168]{1,0:T(8,128)(2,1)S(1)}, u32[]{:S(2)}, u32[]{:S(2)}) %collective-permute-start.32) | collective-permute-done | bytes 917536 | tf_op jit(solution)/shard_map/ppermute | solution.py:37
  261.0 3.2 collective-permute-done.37
  264.1 2.7 collective-permute-done.36
  269.6 7.6 %collective-permute-done.41 = bf16[32,7168]{1,0:T(8,128)(2,1)S(1)} collective-permute-done((bf16[32,7168]{1,0:T(8,128)(2,1)S(1)}, bf16[32,7168]{1,0:T(8,128)(2,1)S(1)}, u32[]{:S(2)}, u32[]{:S(2)}) %collective-permute-start.41) | collective-permute-done | bytes 458784 | tf_op jit(solution)/shard_map/ppermute | solution.py:37
  277.2 3.1 collective-permute-done.40
  283.0 14.3 %all-to-all-start.2 = ((bf16[8,8,7168]{2,1,0:T(8,128)(2,1)}), bf16[8,8,7168]{2,1,0:T(8,128)(2,1)S(1)}, u32[]{:S(2)}, u32[]{:S(2)}) async-start(bf16[8,8,7168]{2,1,0:T(8,128)(2,1)} %maximum_bitcast_fusion), calls=%async_computation.2 | async-start | bytes 1835008 | tf_op jit(solution)/shard_map/all_to_all | solution.py:614
  299.0 12.1 %all-to-all-done.2 = bf16[8,8,7168]{2,1,0:T(8,128)(2,1)S(1)} async-done(((bf16[8,8,7168]{2,1,0:T(8,128)(2,1)}), bf16[8,8,7168]{2,1,0:T(8,128)(2,1)S(1)}, u32[]{:S(2)}, u32[]{:S(2)}) %all-to-all-start.2) | async-done | bytes 917536 | tf_op jit(solution)/shard_map/all_to_all | solution.py:614
  312.0 16.2 %tail.1 = (bf16[64,7168]{1,0:T(8,128)(2,1)}, bf16[64,32768]{1,0:T(8,128)(2,1)}) custom-call(bf16[64,7168]{1,0:T(8,128)(2,1)} %hidden_hbm.1, bf16[64,7168]{1,0:T(8,128)(2,1)} %bitcast.18, f32[1,512]{1,0:T(1,128)} %bitcast.19, f32[64,32]{1,0:T(8,128)} %get-tuple-element.161.cos_ref, f32[64,32]{1,0:T(8,128)} %get-tuple-element.160.sin_ref, ...), custom_call_target="tpu_custom_call" | custom-call | flops 528482304 | bytes 21364736 | tf_op jit(solution)/shard_map/tail/pallas_call | solution.py:433
  (180 shorter events, 95.0 us)
Async XLA Ops:
  13.1 19.7 %all-to-all-start = ((bf16[8,8,7168]{2,1,0:T(8,128)(2,1)}), bf16[8,8,7168]{2,1,0:T(8,128)(2,1)S(1)}, u32[]{:S(2)}, u32[]{:S(2)}) async-start(bf16[8,8,7168]{2,1,0:T(8,128)(2,1)} %fusion), calls=%async_computation | async-start | bytes 1835008 | tf_op jit(solution)/shard_map/all_to_all | solution.py:542
  32.8 13.8 %collective-permute-start = (bf16[32,7168]{1,0:T(8,128)(2,1)S(1)}, bf16[32,7168]{1,0:T(8,128)(2,1)S(1)}, u32[]{:S(2)}, u32[]{:S(2)}) collective-permute-start(bf16[32,7168]{1,0:T(8,128)(2,1)S(1)} %get-tuple-element.159.refs_0_), channel_id=1, source_target_pairs={{0,1},{1,2},{2,3},{3,0},{4,5},{5,6},{6,7},{7,4},{8,9},{9,10},{10,1... | collective-permute-start | bytes 1376264 | tf_op jit(solution)/shard_map/ppermute | solution.py:37
  54.8 20.2 %collective-permute-start.6 = (bf16[64,7168]{1,0:T(8,128)(2,1)}, bf16[64,7168]{1,0:T(8,128)(2,1)}, u32[]{:S(2)}, u32[]{:S(2)}) collective-permute-start(bf16[64,7168]{1,0:T(8,128)(2,1)} %get-tuple-element.89.refs_0_), channel_id=1, source_target_pairs={{0,4},{1,5},{2,6},{3,7},{4,8},{5,9},{6,10},{7,11},{8,12},{9,13},{1... | collective-permute-start | bytes 2752520 | tf_op jit(solution)/shard_map/ppermute | solution.py:37
  54.9 20.2 %collective-permute-start.8 = (bf16[64,7168]{1,0:T(8,128)(2,1)}, bf16[64,7168]{1,0:T(8,128)(2,1)}, u32[]{:S(2)}, u32[]{:S(2)}) collective-permute-start(bf16[64,7168]{1,0:T(8,128)(2,1)} %get-tuple-element.91.refs_4_), channel_id=1, source_target_pairs={{0,1},{1,2},{2,3},{3,0},{4,5},{5,6},{6,7},{7,4},{8,9},{9,10},{10,1... | collective-permute-start | bytes 2752520 | tf_op jit(solution)/shard_map/ppermute | solution.py:37
  59.7 19.1 %collective-permute-start.7 = (bf16[64,7168]{1,0:T(8,128)(2,1)}, bf16[64,7168]{1,0:T(8,128)(2,1)}, u32[]{:S(2)}, u32[]{:S(2)}) collective-permute-start(bf16[64,7168]{1,0:T(8,128)(2,1)} %get-tuple-element.89.refs_0_), channel_id=1, source_target_pairs={{0,12},{1,13},{2,14},{3,15},{4,0},{5,1},{6,2},{7,3},{8,4},{9,5},{1... | collective-permute-start | bytes 2752520 | tf_op jit(solution)/shard_map/ppermute | solution.py:37
  62.6 19.5 %collective-permute-start.9 = (bf16[64,7168]{1,0:T(8,128)(2,1)}, bf16[64,7168]{1,0:T(8,128)(2,1)}, u32[]{:S(2)}, u32[]{:S(2)}) collective-permute-start(bf16[64,7168]{1,0:T(8,128)(2,1)} %get-tuple-element.91.refs_4_), channel_id=1, source_target_pairs={{0,3},{1,0},{2,1},{3,2},{4,7},{5,4},{6,5},{7,6},{8,11},{9,8},{10,9... | collective-permute-start | bytes 2752520 | tf_op jit(solution)/shard_map/ppermute | solution.py:37
  65.4 33.0 %collective-permute-start.10 = (bf16[64,7168]{1,0:T(8,128)(2,1)}, bf16[64,7168]{1,0:T(8,128)(2,1)}, u32[]{:S(2)}, u32[]{:S(2)}) collective-permute-start(bf16[64,7168]{1,0:T(8,128)(2,1)} %get-tuple-element.88.refs_1_), channel_id=1, source_target_pairs={{0,12},{1,13},{2,14},{3,15},{4,0},{5,1},{6,2},{7,3},{8,4},{9,5},{1... | collective-permute-start | bytes 2752520 | tf_op jit(solution)/shard_map/ppermute | solution.py:37
  75.0 25.3 %collective-permute-start.12 = (bf16[64,7168]{1,0:T(8,128)(2,1)}, bf16[64,7168]{1,0:T(8,128)(2,1)S(1)}, u32[]{:S(2)}, u32[]{:S(2)}) collective-permute-start(bf16[64,7168]{1,0:T(8,128)(2,1)} %get-tuple-element.88.refs_1_), channel_id=1, source_target_pairs={{0,4},{1,5},{2,6},{3,7},{4,8},{5,9},{6,10},{7,11},{8,12},{9,13},{1... | collective-permute-start | bytes 2752520 | tf_op jit(solution)/shard_map/ppermute | solution.py:37
  75.1 25.2 %collective-permute-start.11 = (bf16[64,7168]{1,0:T(8,128)(2,1)}, bf16[64,7168]{1,0:T(8,128)(2,1)}, u32[]{:S(2)}, u32[]{:S(2)}) collective-permute-start(bf16[64,7168]{1,0:T(8,128)(2,1)} %get-tuple-element.90.refs_5_), channel_id=1, source_target_pairs={{0,3},{1,0},{2,1},{3,2},{4,7},{5,4},{6,5},{7,6},{8,11},{9,8},{10,9... | collective-permute-start | bytes 2752520 | tf_op jit(solution)/shard_map/ppermute | solution.py:37
  78.7 21.6 %collective-permute-start.13 = (bf16[64,7168]{1,0:T(8,128)(2,1)}, bf16[64,7168]{1,0:T(8,128)(2,1)}, u32[]{:S(2)}, u32[]{:S(2)}) collective-permute-start(bf16[64,7168]{1,0:T(8,128)(2,1)} %get-tuple-element.90.refs_5_), channel_id=1, source_target_pairs={{0,1},{1,2},{2,3},{3,0},{4,5},{5,6},{6,7},{7,4},{8,9},{9,10},{10,1... | collective-permute-start | bytes 2752520 | tf_op jit(solution)/shard_map/ppermute | solution.py:37
  101.3 47.9 %collective-permute-start.14 = (bf16[64,7168]{1,0:T(8,128)(2,1)}, bf16[64,7168]{1,0:T(8,128)(2,1)S(1)}, u32[]{:S(2)}, u32[]{:S(2)}) collective-permute-start(bf16[64,7168]{1,0:T(8,128)(2,1)} %collective-permute-done.6.refs_2_), channel_id=1, source_target_pairs={{0,4},{1,5},{2,6},{3,7},{4,8},{5,9},{6,10},{7,11},{8,12},{9,13},{1... | collective-permute-start | bytes 2752520 | tf_op jit(solution)/shard_map/ppermute | solution.py:37
  101.3 49.4 %collective-permute-start.15 = (bf16[64,7168]{1,0:T(8,128)(2,1)}, bf16[64,7168]{1,0:T(8,128)(2,1)S(1)}, u32[]{:S(2)}, u32[]{:S(2)}) collective-permute-start(bf16[64,7168]{1,0:T(8,128)(2,1)} %collective-permute-done.8.refs_6_), channel_id=1, source_target_pairs={{0,1},{1,2},{2,3},{3,0},{4,5},{5,6},{6,7},{7,4},{8,9},{9,10},{10,1... | collective-permute-start | bytes 2752520 | tf_op jit(solution)/shard_map/ppermute | solution.py:37
  102.2 49.9 %collective-permute-start.16 = (bf16[64,7168]{1,0:T(8,128)(2,1)}, bf16[64,7168]{1,0:T(8,128)(2,1)S(1)}, u32[]{:S(2)}, u32[]{:S(2)}) collective-permute-start(bf16[64,7168]{1,0:T(8,128)(2,1)} %collective-permute-done.10.refs_1_), channel_id=1, source_target_pairs={{0,12},{1,13},{2,14},{3,15},{4,0},{5,1},{6,2},{7,3},{8,4},{9,5},{1... | collective-permute-start | bytes 2752520 | tf_op jit(solution)/shard_map/ppermute | solution.py:37
  105.9 46.1 %all-to-all-start.1 = ((bf16[8,4,9216]{2,1,0:T(4,128)(2,1)}), bf16[8,4,9216]{2,1,0:T(4,128)(2,1)S(1)}, u32[]{:S(2)}, u32[]{:S(2)}) async-start(bf16[8,4,9216]{2,1,0:T(4,128)(2,1)} %reshape.72), calls=%async_computation.1 | async-start | bytes 1179648 | tf_op jit(solution)/shard_map/all_to_all | solution.py:564
  115.4 195.7 %all-gather.2.cloned.1.call-start = ((), (), s32[]{:S(2)}) async-start(), calls=%async_computation.3 | async-start | bytes 10321920 | tf_op jit(solution)/shard_map/all_gather | solution.py:592
  115.4 40.9 %collective-permute-start.17 = (bf16[64,7168]{1,0:T(8,128)(2,1)}, bf16[64,7168]{1,0:T(8,128)(2,1)}, u32[]{:S(2)}, u32[]{:S(2)}) collective-permute-start(bf16[64,7168]{1,0:T(8,128)(2,1)} %collective-permute-done.11.refs_3_), channel_id=1, source_target_pairs={{0,3},{1,0},{2,1},{3,2},{4,7},{5,4},{6,5},{7,6},{8,11},{9,8},{10,9... | collective-permute-start | bytes 2752520 | tf_op jit(solution)/shard_map/ppermute | solution.py:37
  126.1 13.2 %collective-permute-start.18 = (bf16[56,576]{1,0:T(8,128)(2,1)S(1)}, bf16[56,576]{1,0:T(8,128)(2,1)S(1)}, u32[]{:S(2)}, u32[]{:S(2)}) collective-permute-start(bf16[56,576]{1,0:T(8,128)(2,1)S(1)} %copy-done.25), channel_id=1, source_target_pairs={{0,3},{1,0},{2,1},{3,2},{4,7},{5,4},{6,5},{7,6},{8,11},{9,8},{10,9... | collective-permute-start | bytes 193544 | tf_op jit(solution)/shard_map/ppermute | solution.py:37
  149.1 19.3 %collective-permute-start.21 = (bf16[64,7168]{1,0:T(8,128)(2,1)}, bf16[64,7168]{1,0:T(8,128)(2,1)}, u32[]{:S(2)}, u32[]{:S(2)}) collective-permute-start(bf16[64,7168]{1,0:T(8,128)(2,1)} %get-tuple-element.114), channel_id=1, source_target_pairs={{0,12},{1,13},{2,14},{3,15},{4,0},{5,1},{6,2},{7,3},{8,4},{9,5},{1... | collective-permute-start | bytes 2752520 | tf_op jit(solution)/shard_map/ppermute | solution.py:37
  149.1 19.3 %collective-permute-start.22 = (bf16[64,7168]{1,0:T(8,128)(2,1)}, bf16[64,7168]{1,0:T(8,128)(2,1)}, u32[]{:S(2)}, u32[]{:S(2)}) collective-permute-start(bf16[64,7168]{1,0:T(8,128)(2,1)} %get-tuple-element.117), channel_id=1, source_target_pairs={{0,3},{1,0},{2,1},{3,2},{4,7},{5,4},{6,5},{7,6},{8,11},{9,8},{10,9... | collective-permute-start | bytes 2752520 | tf_op jit(solution)/shard_map/ppermute | solution.py:37
  150.7 19.7 %collective-permute-start.23 = (bf16[64,7168]{1,0:T(8,128)(2,1)}, bf16[64,7168]{1,0:T(8,128)(2,1)}, u32[]{:S(2)}, u32[]{:S(2)}) collective-permute-start(bf16[64,7168]{1,0:T(8,128)(2,1)} %get-tuple-element.106), channel_id=1, source_target_pairs={{0,4},{1,5},{2,6},{3,7},{4,8},{5,9},{6,10},{7,11},{8,12},{9,13},{1... | collective-permute-start | bytes 2752520 | tf_op jit(solution)/shard_map/ppermute | solution.py:37
  152.1 19.4 %collective-permute-start.24 = (bf16[64,7168]{1,0:T(8,128)(2,1)}, bf16[64,7168]{1,0:T(8,128)(2,1)}, u32[]{:S(2)}, u32[]{:S(2)}) collective-permute-start(bf16[64,7168]{1,0:T(8,128)(2,1)} %get-tuple-element.108), channel_id=1, source_target_pairs={{0,1},{1,2},{2,3},{3,0},{4,5},{5,6},{6,7},{7,4},{8,9},{9,10},{10,1... | collective-permute-start | bytes 2752520 | tf_op jit(solution)/shard_map/ppermute | solution.py:37
  156.3 20.5 %collective-permute-start.29 = (bf16[224,576]{1,0:T(8,128)(2,1)S(1)}, bf16[224,576]{1,0:T(8,128)(2,1)S(1)}, u32[]{:S(2)}, u32[]{:S(2)}) collective-permute-start(bf16[224,576]{1,0:T(8,128)(2,1)S(1)} %constant_dynamic-update-slice_fusion.3), channel_id=1, source_target_pairs={{0,12},{1,13},{2,14},{3,15},{4,0},{5,1},{6,2},{7,3},{8,4},{9,5},{1... | collective-permute-start | bytes 774152 | tf_op jit(solution)/shard_map/ppermute | solution.py:37
  171.4 48.7 %collective-permute-start.25 = (bf16[64,7168]{1,0:T(8,128)(2,1)}, bf16[64,7168]{1,0:T(8,128)(2,1)}, u32[]{:S(2)}, u32[]{:S(2)}) collective-permute-start(bf16[64,7168]{1,0:T(8,128)(2,1)} %get-tuple-element.129), channel_id=1, source_target_pairs={{0,4},{1,5},{2,6},{3,7},{4,8},{5,9},{6,10},{7,11},{8,12},{9,13},{1... | collective-permute-start | bytes 2752520 | tf_op jit(solution)/shard_map/ppermute | solution.py:37
  171.8 48.3 %collective-permute-start.26 = (bf16[64,7168]{1,0:T(8,128)(2,1)}, bf16[64,7168]{1,0:T(8,128)(2,1)}, u32[]{:S(2)}, u32[]{:S(2)}) collective-permute-start(bf16[64,7168]{1,0:T(8,128)(2,1)} %get-tuple-element.130), channel_id=1, source_target_pairs={{0,1},{1,2},{2,3},{3,0},{4,5},{5,6},{6,7},{7,4},{8,9},{9,10},{10,1... | collective-permute-start | bytes 2752520 | tf_op jit(solution)/shard_map/ppermute | solution.py:37
  171.8 48.4 %collective-permute-start.27 = (bf16[64,7168]{1,0:T(8,128)(2,1)}, bf16[64,7168]{1,0:T(8,128)(2,1)}, u32[]{:S(2)}, u32[]{:S(2)}) collective-permute-start(bf16[64,7168]{1,0:T(8,128)(2,1)} %get-tuple-element.131), channel_id=1, source_target_pairs={{0,12},{1,13},{2,14},{3,15},{4,0},{5,1},{6,2},{7,3},{8,4},{9,5},{1... | collective-permute-start | bytes 2752520 | tf_op jit(solution)/shard_map/ppermute | solution.py:37
  174.1 46.1 %collective-permute-start.28 = (bf16[64,7168]{1,0:T(8,128)(2,1)}, bf16[64,7168]{1,0:T(8,128)(2,1)}, u32[]{:S(2)}, u32[]{:S(2)}) collective-permute-start(bf16[64,7168]{1,0:T(8,128)(2,1)} %get-tuple-element.132), channel_id=1, source_target_pairs={{0,3},{1,0},{2,1},{3,2},{4,7},{5,4},{6,5},{7,6},{8,11},{9,8},{10,9... | collective-permute-start | bytes 2752520 | tf_op jit(solution)/shard_map/ppermute | solution.py:37
  176.8 18.8 %collective-permute-start.30 = (bf16[224,576]{1,0:T(8,128)(2,1)S(1)}, bf16[224,576]{1,0:T(8,128)(2,1)S(1)}, u32[]{:S(2)}, u32[]{:S(2)}) collective-permute-start(bf16[224,576]{1,0:T(8,128)(2,1)S(1)} %constant_dynamic-update-slice_fusion.3), channel_id=1, source_target_pairs={{0,8},{1,9},{2,10},{3,11},{4,12},{5,13},{6,14},{7,15},{8,0},{9,1},... | collective-permute-start | bytes 774152 | tf_op jit(solution)/shard_map/ppermute | solution.py:37
  222.6 17.9 %collective-permute-start.35 = (bf16[64,7168]{1,0:T(8,128)(2,1)}, bf16[64,7168]{1,0:T(8,128)(2,1)}, u32[]{:S(2)}, u32[]{:S(2)}) collective-permute-start(bf16[64,7168]{1,0:T(8,128)(2,1)} %add_convert_fusion), channel_id=1, source_target_pairs={{0,3},{1,0},{2,1},{3,2},{4,7},{5,4},{6,5},{7,6},{8,11},{9,8},{10,9... | collective-permute-start | bytes 2752520 | tf_op jit(solution)/shard_map/ppermute | solution.py:37
  225.4 16.5 %collective-permute-start.34 = (bf16[64,7168]{1,0:T(8,128)(2,1)}, bf16[64,7168]{1,0:T(8,128)(2,1)S(1)}, u32[]{:S(2)}, u32[]{:S(2)}) collective-permute-start(bf16[64,7168]{1,0:T(8,128)(2,1)} %add_convert_fusion.1), channel_id=1, source_target_pairs={{0,12},{1,13},{2,14},{3,15},{4,0},{5,1},{6,2},{7,3},{8,4},{9,5},{1... | collective-permute-start | bytes 2752520 | tf_op jit(solution)/shard_map/ppermute | solution.py:37
  229.2 17.0 %collective-permute-start.33 = (bf16[64,7168]{1,0:T(8,128)(2,1)}, bf16[64,7168]{1,0:T(8,128)(2,1)S(1)}, u32[]{:S(2)}, u32[]{:S(2)}) collective-permute-start(bf16[64,7168]{1,0:T(8,128)(2,1)} %add_convert_fusion.2), channel_id=1, source_target_pairs={{0,1},{1,2},{2,3},{3,0},{4,5},{5,6},{6,7},{7,4},{8,9},{9,10},{10,1... | collective-permute-start | bytes 2752520 | tf_op jit(solution)/shard_map/ppermute | solution.py:37
  232.6 17.8 %collective-permute-start.32 = (bf16[64,7168]{1,0:T(8,128)(2,1)}, bf16[64,7168]{1,0:T(8,128)(2,1)S(1)}, u32[]{:S(2)}, u32[]{:S(2)}) collective-permute-start(bf16[64,7168]{1,0:T(8,128)(2,1)} %add_convert_fusion.3), channel_id=1, source_target_pairs={{0,4},{1,5},{2,6},{3,7},{4,8},{5,9},{6,10},{7,11},{8,12},{9,13},{1... | collective-permute-start | bytes 2752520 | tf_op jit(solution)/shard_map/ppermute | solution.py:37
  283.0 28.0 %all-to-all-start.2 = ((bf16[8,8,7168]{2,1,0:T(8,128)(2,1)}), bf16[8,8,7168]{2,1,0:T(8,128)(2,1)S(1)}, u32[]{:S(2)}, u32[]{:S(2)}) async-start(bf16[8,8,7168]{2,1,0:T(8,128)(2,1)} %maximum_bitcast_fusion), calls=%async_computation.2 | async-start | bytes 1835008 | tf_op jit(solution)/shard_map/all_to_all | solution.py:614
  (45 other events, 439.6 us)
Sparse Core Ops, SparseCore 0:
  232.7 59.4 all-gather.1

commit v4 on v3

--- a/solution.py
+++ b/solution.py
@@ -484,16 +484,6 @@
     return total.astype(jnp.bfloat16)
 
 
-def round_trip(piece, axis, index):
-    rows = piece.shape[0]
-    joined = jnp.zeros((SIDE * rows, piece.shape[1]), piece.dtype)
-    for step in range(SIDE):
-        part = piece if step == 0 else shift(piece, axis, -step)
-        at = jnp.bitwise_and(index + step, SIDE - 1) * rows
-        joined = lax.dynamic_update_slice_in_dim(joined, part, at, axis=0)
-    return joined
-
-
 def after(values, *others):
     return lax.optimization_barrier((values, others))[0]
 
@@ -520,6 +510,7 @@
     local_experts = w_gate.shape[0]
     window = local_experts * dp_count
     width = hidden_in.shape[1]
+    w_plane = lax.all_gather(jnp.concatenate([w_latent] * 2, axis=0), "expert", axis=0, tiled=True)
     x_wide = hidden_in.astype(jnp.float32)
     normed = rms_rows(x_wide, norm_gain).astype(jnp.bfloat16)
     in_window = expert_ids < window
@@ -554,7 +545,11 @@
 
     below = [shift(rows[k], axes[k][0], 1) for k in both]
     above = [shift(rows[k], axes[k][0], -1) for k in both]
-    below, above = after((below, above))
+    below, above, w_plane = after((below, above, w_plane))
+    w_plane = w_plane.reshape(ex_count, 2 * w_latent.shape[0], KVW)[:, : w_latent.shape[0]]
+    w_all = lax.all_gather(
+        w_plane.reshape(ex_count * w_latent.shape[0], KVW), "dp", axis=0, tiled=True
+    )
     beyond = [shift(above[k], axes[k][0], -1) for k in both]
     low = pack([(rows[k], below[k]) for k in both])
     below_low = [shift(low[k], axes[k][1], 1) for k in both]
@@ -573,7 +568,7 @@
     above_high = [shift(high[k], axes[k][1], -1) for k in both]
     y_first = ffn([[low[k], high[k], below_low[k], above_low[k]] for k in both], *weights)
     below_low, above_high, below_high, above_low = after(
-        (below_low, above_high, below_high, above_low), y_first, pool
+        (below_low, above_high, below_high, above_low), y_first, pool, more
     )
     far_low = [shift(below_low[k], axes[k][1], 1) for k in both]
     far_high = [shift(above_high[k], axes[k][1], -1) for k in both]
@@ -581,18 +576,14 @@
     y_first = after(y_first, y_second)
     early_down = [shift(y_first[k][2], axes[k][1], -1) for k in both]
     early_up = [shift(y_second[k][1], axes[k][1], 1) for k in both]
-    index = lax.axis_index("expert")
-    w_line = round_trip(after(w_latent, y_first), "z", jnp.bitwise_and(index, SIDE - 1))
-    far_low, far_high = after((far_low, far_high), y_second, w_line, more)
+    far_low, far_high = after((far_low, far_high), y_second)
     y_far = ffn([[far_low[k], far_high[k]] for k in both], *weights)
     y_far, early_down, early_up = after((y_far, early_down, early_up))
     relay_up = [shift(y_far[k][0], axes[k][1], 1) for k in both]
     relay_down = [shift(y_far[k][1], axes[k][1], -1) for k in both]
-    w_plane = round_trip(after(w_line, y_second), "x", jnp.right_shift(index, 2))
-    w_all = lax.all_gather(w_plane, "dp", axis=0, tiled=True)
     query = after(query, y_far)
     cached, top, total = attend_cached(query, pool, more, page_table, kv_lengths)
-    relay_up, relay_down = after((relay_up, relay_down), cached, w_plane)
+    relay_up, relay_down = after((relay_up, relay_down), cached)
     late_up = [shift(plus(y_first[k][3], relay_up[k]), axes[k][1], 1) for k in both]
     late_down = [shift(plus(y_second[k][0], relay_down[k]), axes[k][1], -1) for k in both]
     cached = cached.reshape(row_count, HEADS * LATENT)

time: 336 us -> 298 us (0.89)
  waiting for transfers between devices: 121 us -> 99.1 us
  starting transfers between devices: 75.1 us -> 61.2 us
    ppermute x42 -> x36, waiting for transfers between devices: 108 us -> 78.7 us  [shift(): return lax.ppermute(value, 'expert', pairs)]
    ppermute x42 -> x36, starting transfers between devices: 45.4 us -> 35.2 us  [shift(): return lax.ppermute(value, 'expert', pairs)]
    all_gather x1 -> x2, waiting for transfers between devices: 0.01 us -> 6.61 us  [the longest x1 6.61 us: body(): lax.all_gather(jnp.concatenate([w_latent] * 2, axis=0), 'expert', axis=0,...]
    all_to_all x1, starting transfers between devices: 9.42 us -> 5.49 us  [body(): lax.all_to_all(after(outgoing, high).reshape(dp_count, MCAP, page_pool.sh...]
    unnamed x65 -> x63, local copies, waits for them, and re-layouts: 10.7 us -> 8.97 us
  transfers between devices with their start and end apart: 46 -> 41, of which waited for: 29 -> 26; matrix products, arithmetic and copies ran while one was open for 15% -> 18% of each run, Pallas kernels for 14% -> 16%
where the time goes in v4:
time: 298 us; the launch traced here: 297 us
  waiting for transfers between devices  99.1 us (33%)
  Pallas kernels  62.4 us (21%)
  starting transfers between devices  61.2 us (21%)
  local copies, waits for them, and re-layouts  31.2 us (10%)
  other arithmetic  25.9 us (9%)
  between operations  14.5 us (5%)
    ppermute x36, waiting for transfers between devices, shift(): return lax.ppermute(value, 'expert', pairs)  78.7 us
    ppermute x36, starting transfers between devices, shift(): return lax.ppermute(value, 'expert', pairs)  35.2 us
    pallas_call x3, Pallas kernels, ffn(): pl.pallas_call(functools.partial(ffn_kernel, count, rows, parts), out_sha...  28.4 us
    convert_element_type x11, other arithmetic, plus(): return total.astype(jnp.bfloat16)  18.5 us
    pallas_call x1, Pallas kernels, tail(): pl.pallas_call(functools.partial(tail_kernel, parts, groups), out_shape=[...  16.2 us
    all_to_all x1, starting transfers between devices, body(): lax.all_to_all(jnp.concatenate(finished, axis=0).reshape(dp_count, slots,...  14.5 us
    pallas_call x1, Pallas kernels, attend_cached(): pl.pallas_call(functools.partial(attend_kernel, step), out_shape=[jax.Sha...  13 us
    all_to_all x1, waiting for transfers between devices, body(): lax.all_to_all(jnp.concatenate(finished, axis=0).reshape(dp_count, slots,...  12.1 us
  transfers between devices with their start and end apart: 41, of which 26 were waited for; matrix products, arithmetic and copies ran while one was open for 18% of the time, Pallas kernels for 16%

profile of v4, /device:TPU:1, one launch (start us, length us, event | category | flops | bytes accessed | tf_op | source)
XLA Modules:
  0.0 297.0 jit_solution(16453980265914054633)
XLA Ops:
  14.8 6.0 %all-to-all-start = ((bf16[8,8,7168]{2,1,0:T(8,128)(2,1)}), bf16[8,8,7168]{2,1,0:T(8,128)(2,1)S(1)}, u32[]{:S(2)}, u32[]{:S(2)}) async-start(bf16[8,8,7168]{2,1,0:T(8,128)(2,1)} %fusion), calls=%async_computation | async-start | bytes 1835008 | tf_op jit(solution)/shard_map/all_to_all | solution.py:533
  20.7 10.1 %reshape.76.q_ref = bf16[64,64,576]{2,1,0:T(8,128)(2,1)} reshape(bf16[64,36864]{1,0:T(8,128)(2,1)} %q_hbm.1) | data formatting | bytes 9437184 | tf_op jit(solution)/shard_map/reshape | solution.py:537
  41.1 8.3 %collective-permute-done.refs_1_ = bf16[32,7168]{1,0:T(8,128)(2,1)S(1)} collective-permute-done((bf16[32,7168]{1,0:T(8,128)(2,1)S(1)}, bf16[32,7168]{1,0:T(8,128)(2,1)S(1)}, u32[]{:S(2)}, u32[]{:S(2)}) %collective-permute-start) | collective-permute-done | bytes 458784 | tf_op jit(solution)/shard_map/ppermute | solution.py:37
  49.6 3.2 %collective-permute-done.2.refs_0_ = bf16[32,7168]{1,0:T(8,128)(2,1)S(1)} collective-permute-done((bf16[32,7168]{1,0:T(8,128)(2,1)S(1)}, bf16[32,7168]{1,0:T(8,128)(2,1)S(1)}, u32[]{:S(2)}, u32[]{:S(2)}) %collective-permute-start.2) | collective-permute-done | bytes 458784 | tf_op jit(solution)/shard_map/ppermute | solution.py:37
  55.1 6.6 %all-gather.3.cloned.1.call-done = bf16[1792,576]{1,0:T(8,128)(2,1)} async-done(((bf16[112,576]{1,0:T(8,128)(2,1)}), bf16[1792,576]{1,0:T(8,128)(2,1)}) %all-gather.3.cloned.1.call-update) | async-done | bytes 2064400 | tf_op jit(solution)/shard_map/all_gather | solution.py:513
  63.1 2.7 collective-permute-start.5
  68.5 4.7 %collective-permute-done.4.refs_1_ = bf16[32,7168]{1,0:T(8,128)(2,1)S(1)} collective-permute-done((bf16[32,7168]{1,0:T(8,128)(2,1)S(1)}, bf16[32,7168]{1,0:T(8,128)(2,1)S(1)}, u32[]{:S(2)}, u32[]{:S(2)}) %collective-permute-start.4) | collective-permute-done | bytes 458784 | tf_op jit(solution)/shard_map/ppermute | solution.py:37
  75.3 3.4 %collective-permute-start.7 = (bf16[64,7168]{1,0:T(8,128)(2,1)}, bf16[64,7168]{1,0:T(8,128)(2,1)}, u32[]{:S(2)}, u32[]{:S(2)}) collective-permute-start(bf16[64,7168]{1,0:T(8,128)(2,1)} %get-tuple-element.88.refs_0_), channel_id=1, source_target_pairs={{0,12},{1,13},{2,14},{3,15},{4,0},{5,1},{6,2},{7,3},{8,4},{9,5},{1... | collective-permute-start | bytes 2752520 | tf_op jit(solution)/shard_map/ppermute | solution.py:37
  82.3 5.5 %all-to-all-start.1 = ((bf16[8,4,9216]{2,1,0:T(4,128)(2,1)}), bf16[8,4,9216]{2,1,0:T(4,128)(2,1)S(1)}, u32[]{:S(2)}, u32[]{:S(2)}) async-start(bf16[8,4,9216]{2,1,0:T(4,128)(2,1)} %reshape.78), calls=%async_computation.1 | async-start | bytes 1179648 | tf_op jit(solution)/shard_map/all_to_all | solution.py:559
  87.9 2.8 collective-permute-done.6.refs_2_
  90.9 6.3 %collective-permute-done.7.refs_3_ = bf16[64,7168]{1,0:T(8,128)(2,1)} collective-permute-done((bf16[64,7168]{1,0:T(8,128)(2,1)}, bf16[64,7168]{1,0:T(8,128)(2,1)}, u32[]{:S(2)}, u32[]{:S(2)}) %collective-permute-start.7) | collective-permute-done | bytes 917536 | tf_op jit(solution)/shard_map/ppermute | solution.py:37
  101.0 11.5 %ffn.3 = (bf16[64,7168]{1,0:T(8,128)(2,1)}, bf16[64,7168]{1,0:T(8,128)(2,1)}, bf16[64,7168]{1,0:T(8,128)(2,1)}, bf16[64,7168]{1,0:T(8,128)(2,1)}, bf16[64,7168]{...) custom-call(bf16[64,7168]{1,0:T(8,128)(2,1)} %get-tuple-element.88.refs_0_, ...), custom_call_target="tpu_custom_call" | custom-call | flops 5637144576 | bytes 25690112 | tf_op jit(solution)/shard_map/ffn/pallas_call | solution.py:119
  112.5 4.3 %collective-permute-done.10.refs_1_ = bf16[64,7168]{1,0:T(8,128)(2,1)} collective-permute-done((bf16[64,7168]{1,0:T(8,128)(2,1)}, bf16[64,7168]{1,0:T(8,128)(2,1)}, u32[]{:S(2)}, u32[]{:S(2)}) %collective-permute-start.10) | collective-permute-done | bytes 917536 | tf_op jit(solution)/shard_map/ppermute | solution.py:37
  124.1 8.4 %ffn.4 = (bf16[64,7168]{1,0:T(8,128)(2,1)}, bf16[64,7168]{1,0:T(8,128)(2,1)}, bf16[64,7168]{1,0:T(8,128)(2,1)}, bf16[64,7168]{1,0:T(8,128)(2,1)}) custom-call(bf16[64,7168]{1,0:T(8,128)(2,1)} %collective-permute-done.12.refs_0_, bf16[64,7168]{1,0:T(8,128)(2,1)} %collective-permute-done.10.refs_1_, bf16[64,7168]{1,0:T(8,128)(2,1)} %collective-permute-done.13.refs_2_, ...), custom_call_target="tpu_custom_call" | custom-call | flops 2818572288 | bytes 18350080 | tf_op jit(solution)/shard_map/ffn/pallas_call | solution.py:119
  132.7 6.2 %collective-permute-done.14.refs_0_ = bf16[64,7168]{1,0:T(8,128)(2,1)S(1)} collective-permute-done((bf16[64,7168]{1,0:T(8,128)(2,1)}, bf16[64,7168]{1,0:T(8,128)(2,1)S(1)}, u32[]{:S(2)}, u32[]{:S(2)}) %collective-permute-start.14) | collective-permute-done | bytes 917536 | tf_op jit(solution)/shard_map/ppermute | solution.py:37
  141.8 8.4 %ffn.5 = (bf16[64,7168]{1,0:T(8,128)(2,1)}, bf16[64,7168]{1,0:T(8,128)(2,1)}, bf16[64,7168]{1,0:T(8,128)(2,1)}, bf16[64,7168]{1,0:T(8,128)(2,1)}) custom-call(bf16[64,7168]{1,0:T(8,128)(2,1)} %copy-done.6, bf16[64,7168]{1,0:T(8,128)(2,1)} %copy-done.8, bf16[64,7168]{1,0:T(8,128)(2,1)} %copy-done.7, bf16[64,7168]{1,0:T(8,128)(2,1)} %collective-permute-done.17.refs_3_, ...), custom_call_target="tpu_custom_call" | custom-call | flops 2818572288 | bytes 18350080 | tf_op jit(solution)/shard_map/ffn/pallas_call | solution.py:119
  150.3 3.5 %collective-permute-done.18 = bf16[64,7168]{1,0:T(8,128)(2,1)} collective-permute-done((bf16[64,7168]{1,0:T(8,128)(2,1)}, bf16[64,7168]{1,0:T(8,128)(2,1)}, u32[]{:S(2)}, u32[]{:S(2)}) %collective-permute-start.18) | collective-permute-done | bytes 917536 | tf_op jit(solution)/shard_map/ppermute | solution.py:37
  153.8 5.3 %collective-permute-done.19 = bf16[64,7168]{1,0:T(8,128)(2,1)} collective-permute-done((bf16[64,7168]{1,0:T(8,128)(2,1)}, bf16[64,7168]{1,0:T(8,128)(2,1)}, u32[]{:S(2)}, u32[]{:S(2)}) %collective-permute-start.19) | collective-permute-done | bytes 917536 | tf_op jit(solution)/shard_map/ppermute | solution.py:37
  161.8 3.4 %collective-permute-start.25 = (bf16[64,7168]{1,0:T(8,128)(2,1)}, bf16[64,7168]{1,0:T(8,128)(2,1)}, u32[]{:S(2)}, u32[]{:S(2)}) collective-permute-start(bf16[64,7168]{1,0:T(8,128)(2,1)} %get-tuple-element.126), channel_id=1, source_target_pairs={{0,3},{1,0},{2,1},{3,2},{4,7},{5,4},{6,5},{7,6},{8,11},{9,8},{10,9... | collective-permute-start | bytes 2752520 | tf_op jit(solution)/shard_map/ppermute | solution.py:37
  166.0 3.5 %copy.20.pool_hbm = bf16[128,16,576]{2,1,0:T(8,128)(2,1)} copy(bf16[128,16,576]{0,2,1:T(8,128)(2,1)S(1)} %bitcast.18) | data formatting | bytes 4718592 | tf_op jit(solution)/shard_map/reshape | solution.py:566
  169.5 13.0 %attend_cached.1 = (bf16[64,64,512]{2,1,0:T(8,128)(2,1)}, f32[64,64]{1,0:T(8,128)}, f32[64,64]{1,0:T(8,128)}) custom-call(s32[384]{0:T(512)} %reshape.80.table, s32[64]{0:T(128)} %lengths.1, bf16[64,64,576]{2,1,0:T(8,128)(2,1)} %reshape.76.q_ref, bf16[128,16,576]{2,1,0:T(8,128)(2,1)} %copy.20.pool_hbm, bf16[32,16,576]{2,1,0:T(8,128)(2,1)} %reshape.79.more_hbm), custom_call_target="tpu_custom_call" | custom-call | flops 855638016 | bytes 11862016 | tf_op jit(solution)/shard_map/attend_cached/pallas_call | solution.py:205
  182.6 2.7 add_convert_fusion
  195.3 6.8 %copy.21 = bf16[8,8,64,512]{3,1,2,0:T(8,128)(2,1)} copy(bf16[8,8,64,512]{3,2,1,0:T(8,128)(2,1)} %bitcast.20) | data formatting | bytes 8388608
  204.4 3.6 %collective-permute-done.27 = bf16[64,7168]{1,0:T(8,128)(2,1)S(1)} collective-permute-done((bf16[64,7168]{1,0:T(8,128)(2,1)}, bf16[64,7168]{1,0:T(8,128)(2,1)S(1)}, u32[]{:S(2)}, u32[]{:S(2)}) %collective-permute-start.27) | collective-permute-done | bytes 917536 | tf_op jit(solution)/shard_map/ppermute | solution.py:37
  211.6 2.9 collective-permute-start.32
  220.0 5.0 %collective-permute-done.31 = bf16[32,7168]{1,0:T(8,128)(2,1)S(1)} collective-permute-done((bf16[32,7168]{1,0:T(8,128)(2,1)S(1)}, bf16[32,7168]{1,0:T(8,128)(2,1)S(1)}, u32[]{:S(2)}, u32[]{:S(2)}) %collective-permute-start.31) | collective-permute-done | bytes 458784 | tf_op jit(solution)/shard_map/ppermute | solution.py:37
  224.9 2.7 collective-permute-done.30
  230.6 8.0 %collective-permute-done.35 = bf16[32,7168]{1,0:T(8,128)(2,1)S(1)} collective-permute-done((bf16[32,7168]{1,0:T(8,128)(2,1)S(1)}, bf16[32,7168]{1,0:T(8,128)(2,1)S(1)}, u32[]{:S(2)}, u32[]{:S(2)}) %collective-permute-start.35) | collective-permute-done | bytes 458784 | tf_op jit(solution)/shard_map/ppermute | solution.py:37
  238.6 3.4 %collective-permute-done.34 = bf16[32,7168]{1,0:T(8,128)(2,1)S(1)} collective-permute-done((bf16[32,7168]{1,0:T(8,128)(2,1)S(1)}, bf16[32,7168]{1,0:T(8,128)(2,1)S(1)}, u32[]{:S(2)}, u32[]{:S(2)}) %collective-permute-start.34) | collective-permute-done | bytes 458784 | tf_op jit(solution)/shard_map/ppermute | solution.py:37
  244.8 14.5 %all-to-all-start.2 = ((bf16[8,8,7168]{2,1,0:T(8,128)(2,1)}), bf16[8,8,7168]{2,1,0:T(8,128)(2,1)S(1)}, u32[]{:S(2)}, u32[]{:S(2)}) async-start(bf16[8,8,7168]{2,1,0:T(8,128)(2,1)} %maximum_bitcast_fusion), calls=%async_computation.2 | async-start | bytes 1835008 | tf_op jit(solution)/shard_map/all_to_all | solution.py:605
  260.9 12.1 %all-to-all-done.2 = bf16[8,8,7168]{2,1,0:T(8,128)(2,1)S(1)} async-done(((bf16[8,8,7168]{2,1,0:T(8,128)(2,1)}), bf16[8,8,7168]{2,1,0:T(8,128)(2,1)S(1)}, u32[]{:S(2)}, u32[]{:S(2)}) %all-to-all-start.2) | async-done | bytes 917536 | tf_op jit(solution)/shard_map/all_to_all | solution.py:605
  274.0 16.2 %tail.1 = (bf16[64,7168]{1,0:T(8,128)(2,1)}, bf16[64,32768]{1,0:T(8,128)(2,1)}) custom-call(bf16[64,7168]{1,0:T(8,128)(2,1)} %hidden_hbm.1, bf16[64,7168]{1,0:T(8,128)(2,1)} %bitcast.21, f32[1,512]{1,0:T(1,128)} %bitcast.23, f32[64,32]{1,0:T(8,128)} %get-tuple-element.159.cos_ref, f32[64,32]{1,0:T(8,128)} %get-tuple-element.158.sin_ref, ...), custom_call_target="tpu_custom_call" | custom-call | flops 528482304 | bytes 21364736 | tf_op jit(solution)/shard_map/tail/pallas_call | solution.py:433
  (161 shorter events, 77.3 us)
Async XLA Ops:
  7.2 54.6 %all-gather.3.cloned.1.call-start = ((), (), s32[]{:S(2)}) async-start(), calls=%async_computation.3 | async-start | bytes 2437120 | tf_op jit(solution)/shard_map/all_gather | solution.py:513
  14.8 19.7 %all-to-all-start = ((bf16[8,8,7168]{2,1,0:T(8,128)(2,1)}), bf16[8,8,7168]{2,1,0:T(8,128)(2,1)S(1)}, u32[]{:S(2)}, u32[]{:S(2)}) async-start(bf16[8,8,7168]{2,1,0:T(8,128)(2,1)} %fusion), calls=%async_computation | async-start | bytes 1835008 | tf_op jit(solution)/shard_map/all_to_all | solution.py:533
  34.5 15.0 %collective-permute-start = (bf16[32,7168]{1,0:T(8,128)(2,1)S(1)}, bf16[32,7168]{1,0:T(8,128)(2,1)S(1)}, u32[]{:S(2)}, u32[]{:S(2)}) collective-permute-start(bf16[32,7168]{1,0:T(8,128)(2,1)S(1)} %get-tuple-element.157.refs_0_), channel_id=1, source_target_pairs={{0,1},{1,2},{2,3},{3,0},{4,5},{5,6},{6,7},{7,4},{8,9},{9,10},{10,1... | collective-permute-start | bytes 1376264 | tf_op jit(solution)/shard_map/ppermute | solution.py:37
  37.4 15.3 %collective-permute-start.2 = (bf16[32,7168]{1,0:T(8,128)(2,1)S(1)}, bf16[32,7168]{1,0:T(8,128)(2,1)S(1)}, u32[]{:S(2)}, u32[]{:S(2)}) collective-permute-start(bf16[32,7168]{1,0:T(8,128)(2,1)S(1)} %get-tuple-element.157.refs_0_), channel_id=1, source_target_pairs={{0,3},{1,0},{2,1},{3,2},{4,7},{5,4},{6,5},{7,6},{8,11},{9,8},{10,9... | collective-permute-start | bytes 1376264 | tf_op jit(solution)/shard_map/ppermute | solution.py:37
  39.6 15.5 %collective-permute-start.3 = (bf16[32,7168]{1,0:T(8,128)(2,1)S(1)}, bf16[32,7168]{1,0:T(8,128)(2,1)}, u32[]{:S(2)}, u32[]{:S(2)}) collective-permute-start(bf16[32,7168]{1,0:T(8,128)(2,1)S(1)} %get-tuple-element.156.refs_2_), channel_id=1, source_target_pairs={{0,12},{1,13},{2,14},{3,15},{4,0},{5,1},{6,2},{7,3},{8,4},{9,5},{1... | collective-permute-start | bytes 1376264 | tf_op jit(solution)/shard_map/ppermute | solution.py:37
  68.3 22.4 %collective-permute-start.6 = (bf16[64,7168]{1,0:T(8,128)(2,1)}, bf16[64,7168]{1,0:T(8,128)(2,1)}, u32[]{:S(2)}, u32[]{:S(2)}) collective-permute-start(bf16[64,7168]{1,0:T(8,128)(2,1)} %get-tuple-element.88.refs_0_), channel_id=1, source_target_pairs={{0,4},{1,5},{2,6},{3,7},{4,8},{5,9},{6,10},{7,11},{8,12},{9,13},{1... | collective-permute-start | bytes 2752520 | tf_op jit(solution)/shard_map/ppermute | solution.py:37
  68.4 22.4 %collective-permute-start.8 = (bf16[64,7168]{1,0:T(8,128)(2,1)}, bf16[64,7168]{1,0:T(8,128)(2,1)}, u32[]{:S(2)}, u32[]{:S(2)}) collective-permute-start(bf16[64,7168]{1,0:T(8,128)(2,1)} %get-tuple-element.90.refs_4_), channel_id=1, source_target_pairs={{0,1},{1,2},{2,3},{3,0},{4,5},{5,6},{6,7},{7,4},{8,9},{9,10},{10,1... | collective-permute-start | bytes 2752520 | tf_op jit(solution)/shard_map/ppermute | solution.py:37
  75.3 21.9 %collective-permute-start.7 = (bf16[64,7168]{1,0:T(8,128)(2,1)}, bf16[64,7168]{1,0:T(8,128)(2,1)}, u32[]{:S(2)}, u32[]{:S(2)}) collective-permute-start(bf16[64,7168]{1,0:T(8,128)(2,1)} %get-tuple-element.88.refs_0_), channel_id=1, source_target_pairs={{0,12},{1,13},{2,14},{3,15},{4,0},{5,1},{6,2},{7,3},{8,4},{9,5},{1... | collective-permute-start | bytes 2752520 | tf_op jit(solution)/shard_map/ppermute | solution.py:37
  78.7 22.3 %collective-permute-start.9 = (bf16[64,7168]{1,0:T(8,128)(2,1)}, bf16[64,7168]{1,0:T(8,128)(2,1)}, u32[]{:S(2)}, u32[]{:S(2)}) collective-permute-start(bf16[64,7168]{1,0:T(8,128)(2,1)} %get-tuple-element.90.refs_4_), channel_id=1, source_target_pairs={{0,3},{1,0},{2,1},{3,2},{4,7},{5,4},{6,5},{7,6},{8,11},{9,8},{10,9... | collective-permute-start | bytes 2752520 | tf_op jit(solution)/shard_map/ppermute | solution.py:37
  82.3 17.3 %all-to-all-start.1 = ((bf16[8,4,9216]{2,1,0:T(4,128)(2,1)}), bf16[8,4,9216]{2,1,0:T(4,128)(2,1)S(1)}, u32[]{:S(2)}, u32[]{:S(2)}) async-start(bf16[8,4,9216]{2,1,0:T(4,128)(2,1)} %reshape.78), calls=%async_computation.1 | async-start | bytes 1179648 | tf_op jit(solution)/shard_map/all_to_all | solution.py:559
  87.8 185.2 %all-gather.5.cloned.1.call-start = ((), (), s32[]{:S(2)}) async-start(), calls=%async_computation.4 | async-start | bytes 10321920 | tf_op jit(solution)/shard_map/all_gather | solution.py:550
  87.8 29.0 %collective-permute-start.10 = (bf16[64,7168]{1,0:T(8,128)(2,1)}, bf16[64,7168]{1,0:T(8,128)(2,1)}, u32[]{:S(2)}, u32[]{:S(2)}) collective-permute-start(bf16[64,7168]{1,0:T(8,128)(2,1)} %get-tuple-element.87.refs_1_), channel_id=1, source_target_pairs={{0,12},{1,13},{2,14},{3,15},{4,0},{5,1},{6,2},{7,3},{8,4},{9,5},{1... | collective-permute-start | bytes 2752520 | tf_op jit(solution)/shard_map/ppermute | solution.py:37
  90.8 28.0 %collective-permute-start.11 = (bf16[64,7168]{1,0:T(8,128)(2,1)}, bf16[64,7168]{1,0:T(8,128)(2,1)}, u32[]{:S(2)}, u32[]{:S(2)}) collective-permute-start(bf16[64,7168]{1,0:T(8,128)(2,1)} %get-tuple-element.89.refs_5_), channel_id=1, source_target_pairs={{0,3},{1,0},{2,1},{3,2},{4,7},{5,4},{6,5},{7,6},{8,11},{9,8},{10,9... | collective-permute-start | bytes 2752520 | tf_op jit(solution)/shard_map/ppermute | solution.py:37
  90.8 27.9 %collective-permute-start.12 = (bf16[64,7168]{1,0:T(8,128)(2,1)}, bf16[64,7168]{1,0:T(8,128)(2,1)}, u32[]{:S(2)}, u32[]{:S(2)}) collective-permute-start(bf16[64,7168]{1,0:T(8,128)(2,1)} %get-tuple-element.87.refs_1_), channel_id=1, source_target_pairs={{0,4},{1,5},{2,6},{3,7},{4,8},{5,9},{6,10},{7,11},{8,12},{9,13},{1... | collective-permute-start | bytes 2752520 | tf_op jit(solution)/shard_map/ppermute | solution.py:37
  97.2 21.6 %collective-permute-start.13 = (bf16[64,7168]{1,0:T(8,128)(2,1)}, bf16[64,7168]{1,0:T(8,128)(2,1)}, u32[]{:S(2)}, u32[]{:S(2)}) collective-permute-start(bf16[64,7168]{1,0:T(8,128)(2,1)} %get-tuple-element.89.refs_5_), channel_id=1, source_target_pairs={{0,1},{1,2},{2,3},{3,0},{4,5},{5,6},{6,7},{7,4},{8,9},{9,10},{10,1... | collective-permute-start | bytes 2752520 | tf_op jit(solution)/shard_map/ppermute | solution.py:37
  118.8 20.1 %collective-permute-start.14 = (bf16[64,7168]{1,0:T(8,128)(2,1)}, bf16[64,7168]{1,0:T(8,128)(2,1)S(1)}, u32[]{:S(2)}, u32[]{:S(2)}) collective-permute-start(bf16[64,7168]{1,0:T(8,128)(2,1)} %collective-permute-done.6.refs_2_), channel_id=1, source_target_pairs={{0,4},{1,5},{2,6},{3,7},{4,8},{5,9},{6,10},{7,11},{8,12},{9,13},{1... | collective-permute-start | bytes 2752520 | tf_op jit(solution)/shard_map/ppermute | solution.py:37
  118.8 20.6 %collective-permute-start.15 = (bf16[64,7168]{1,0:T(8,128)(2,1)}, bf16[64,7168]{1,0:T(8,128)(2,1)S(1)}, u32[]{:S(2)}, u32[]{:S(2)}) collective-permute-start(bf16[64,7168]{1,0:T(8,128)(2,1)} %collective-permute-done.8.refs_6_), channel_id=1, source_target_pairs={{0,1},{1,2},{2,3},{3,0},{4,5},{5,6},{6,7},{7,4},{8,9},{9,10},{10,1... | collective-permute-start | bytes 2752520 | tf_op jit(solution)/shard_map/ppermute | solution.py:37
  118.8 22.0 %collective-permute-start.16 = (bf16[64,7168]{1,0:T(8,128)(2,1)}, bf16[64,7168]{1,0:T(8,128)(2,1)S(1)}, u32[]{:S(2)}, u32[]{:S(2)}) collective-permute-start(bf16[64,7168]{1,0:T(8,128)(2,1)} %collective-permute-done.10.refs_1_), channel_id=1, source_target_pairs={{0,12},{1,13},{2,14},{3,15},{4,0},{5,1},{6,2},{7,3},{8,4},{9,5},{1... | collective-permute-start | bytes 2752520 | tf_op jit(solution)/shard_map/ppermute | solution.py:37
  121.4 19.4 %collective-permute-start.17 = (bf16[64,7168]{1,0:T(8,128)(2,1)}, bf16[64,7168]{1,0:T(8,128)(2,1)}, u32[]{:S(2)}, u32[]{:S(2)}) collective-permute-start(bf16[64,7168]{1,0:T(8,128)(2,1)} %collective-permute-done.11.refs_3_), channel_id=1, source_target_pairs={{0,3},{1,0},{2,1},{3,2},{4,7},{5,4},{6,5},{7,6},{8,11},{9,8},{10,9... | collective-permute-start | bytes 2752520 | tf_op jit(solution)/shard_map/ppermute | solution.py:37
  132.6 26.6 %collective-permute-start.20 = (bf16[64,7168]{1,0:T(8,128)(2,1)}, bf16[64,7168]{1,0:T(8,128)(2,1)}, u32[]{:S(2)}, u32[]{:S(2)}) collective-permute-start(bf16[64,7168]{1,0:T(8,128)(2,1)} %get-tuple-element.106), channel_id=1, source_target_pairs={{0,4},{1,5},{2,6},{3,7},{4,8},{5,9},{6,10},{7,11},{8,12},{9,13},{1... | collective-permute-start | bytes 2752520 | tf_op jit(solution)/shard_map/ppermute | solution.py:37
  138.9 14.9 %collective-permute-start.18 = (bf16[64,7168]{1,0:T(8,128)(2,1)}, bf16[64,7168]{1,0:T(8,128)(2,1)}, u32[]{:S(2)}, u32[]{:S(2)}) collective-permute-start(bf16[64,7168]{1,0:T(8,128)(2,1)} %get-tuple-element.121), channel_id=1, source_target_pairs={{0,12},{1,13},{2,14},{3,15},{4,0},{5,1},{6,2},{7,3},{8,4},{9,5},{1... | collective-permute-start | bytes 2752520 | tf_op jit(solution)/shard_map/ppermute | solution.py:37
  139.4 19.7 %collective-permute-start.19 = (bf16[64,7168]{1,0:T(8,128)(2,1)}, bf16[64,7168]{1,0:T(8,128)(2,1)}, u32[]{:S(2)}, u32[]{:S(2)}) collective-permute-start(bf16[64,7168]{1,0:T(8,128)(2,1)} %get-tuple-element.122), channel_id=1, source_target_pairs={{0,3},{1,0},{2,1},{3,2},{4,7},{5,4},{6,5},{7,6},{8,11},{9,8},{10,9... | collective-permute-start | bytes 2752520 | tf_op jit(solution)/shard_map/ppermute | solution.py:37
  140.8 18.3 %collective-permute-start.21 = (bf16[64,7168]{1,0:T(8,128)(2,1)}, bf16[64,7168]{1,0:T(8,128)(2,1)}, u32[]{:S(2)}, u32[]{:S(2)}) collective-permute-start(bf16[64,7168]{1,0:T(8,128)(2,1)} %get-tuple-element.108), channel_id=1, source_target_pairs={{0,1},{1,2},{2,3},{3,0},{4,5},{5,6},{6,7},{7,4},{8,9},{9,10},{10,1... | collective-permute-start | bytes 2752520 | tf_op jit(solution)/shard_map/ppermute | solution.py:37
  159.1 23.4 %collective-permute-start.22 = (bf16[64,7168]{1,0:T(8,128)(2,1)}, bf16[64,7168]{1,0:T(8,128)(2,1)S(1)}, u32[]{:S(2)}, u32[]{:S(2)}) collective-permute-start(bf16[64,7168]{1,0:T(8,128)(2,1)} %get-tuple-element.123), channel_id=1, source_target_pairs={{0,4},{1,5},{2,6},{3,7},{4,8},{5,9},{6,10},{7,11},{8,12},{9,13},{1... | collective-permute-start | bytes 2752520 | tf_op jit(solution)/shard_map/ppermute | solution.py:37
  159.1 23.4 %collective-permute-start.23 = (bf16[64,7168]{1,0:T(8,128)(2,1)}, bf16[64,7168]{1,0:T(8,128)(2,1)}, u32[]{:S(2)}, u32[]{:S(2)}) collective-permute-start(bf16[64,7168]{1,0:T(8,128)(2,1)} %get-tuple-element.124), channel_id=1, source_target_pairs={{0,1},{1,2},{2,3},{3,0},{4,5},{5,6},{6,7},{7,4},{8,9},{9,10},{10,1... | collective-permute-start | bytes 2752520 | tf_op jit(solution)/shard_map/ppermute | solution.py:37
  159.2 23.4 %collective-permute-start.24 = (bf16[64,7168]{1,0:T(8,128)(2,1)}, bf16[64,7168]{1,0:T(8,128)(2,1)}, u32[]{:S(2)}, u32[]{:S(2)}) collective-permute-start(bf16[64,7168]{1,0:T(8,128)(2,1)} %get-tuple-element.125), channel_id=1, source_target_pairs={{0,12},{1,13},{2,14},{3,15},{4,0},{5,1},{6,2},{7,3},{8,4},{9,5},{1... | collective-permute-start | bytes 2752520 | tf_op jit(solution)/shard_map/ppermute | solution.py:37
  161.8 20.8 %collective-permute-start.25 = (bf16[64,7168]{1,0:T(8,128)(2,1)}, bf16[64,7168]{1,0:T(8,128)(2,1)}, u32[]{:S(2)}, u32[]{:S(2)}) collective-permute-start(bf16[64,7168]{1,0:T(8,128)(2,1)} %get-tuple-element.126), channel_id=1, source_target_pairs={{0,3},{1,0},{2,1},{3,2},{4,7},{5,4},{6,5},{7,6},{8,11},{9,8},{10,9... | collective-permute-start | bytes 2752520 | tf_op jit(solution)/shard_map/ppermute | solution.py:37
  185.4 16.7 %collective-permute-start.29 = (bf16[64,7168]{1,0:T(8,128)(2,1)}, bf16[64,7168]{1,0:T(8,128)(2,1)}, u32[]{:S(2)}, u32[]{:S(2)}) collective-permute-start(bf16[64,7168]{1,0:T(8,128)(2,1)} %add_convert_fusion), channel_id=1, source_target_pairs={{0,3},{1,0},{2,1},{3,2},{4,7},{5,4},{6,5},{7,6},{8,11},{9,8},{10,9... | collective-permute-start | bytes 2752520 | tf_op jit(solution)/shard_map/ppermute | solution.py:37
  189.1 15.2 %collective-permute-start.28 = (bf16[64,7168]{1,0:T(8,128)(2,1)}, bf16[64,7168]{1,0:T(8,128)(2,1)S(1)}, u32[]{:S(2)}, u32[]{:S(2)}) collective-permute-start(bf16[64,7168]{1,0:T(8,128)(2,1)} %add_convert_fusion.1), channel_id=1, source_target_pairs={{0,12},{1,13},{2,14},{3,15},{4,0},{5,1},{6,2},{7,3},{8,4},{9,5},{1... | collective-permute-start | bytes 2752520 | tf_op jit(solution)/shard_map/ppermute | solution.py:37
  191.6 16.3 %collective-permute-start.27 = (bf16[64,7168]{1,0:T(8,128)(2,1)}, bf16[64,7168]{1,0:T(8,128)(2,1)S(1)}, u32[]{:S(2)}, u32[]{:S(2)}) collective-permute-start(bf16[64,7168]{1,0:T(8,128)(2,1)} %add_convert_fusion.2), channel_id=1, source_target_pairs={{0,1},{1,2},{2,3},{3,0},{4,5},{5,6},{6,7},{7,4},{8,9},{9,10},{10,1... | collective-permute-start | bytes 2752520 | tf_op jit(solution)/shard_map/ppermute | solution.py:37
  192.8 15.9 %collective-permute-start.26 = (bf16[64,7168]{1,0:T(8,128)(2,1)}, bf16[64,7168]{1,0:T(8,128)(2,1)S(1)}, u32[]{:S(2)}, u32[]{:S(2)}) collective-permute-start(bf16[64,7168]{1,0:T(8,128)(2,1)} %add_convert_fusion.3), channel_id=1, source_target_pairs={{0,4},{1,5},{2,6},{3,7},{4,8},{5,9},{6,10},{7,11},{8,12},{9,13},{1... | collective-permute-start | bytes 2752520 | tf_op jit(solution)/shard_map/ppermute | solution.py:37
  244.8 28.2 %all-to-all-start.2 = ((bf16[8,8,7168]{2,1,0:T(8,128)(2,1)}), bf16[8,8,7168]{2,1,0:T(8,128)(2,1)S(1)}, u32[]{:S(2)}, u32[]{:S(2)}) async-start(bf16[8,8,7168]{2,1,0:T(8,128)(2,1)} %maximum_bitcast_fusion), calls=%async_computation.2 | async-start | bytes 1835008 | tf_op jit(solution)/shard_map/all_to_all | solution.py:605
  (39 other events, 406.1 us)
Sparse Core Ops, SparseCore 0:
  10.2 51.4 all-gather.2
  195.4 58.4 all-gather.4

commit v5 on v4

--- a/solution.py
+++ b/solution.py
@@ -35,6 +35,94 @@
             to_z = (z + step) % SIDE if axis == "z" else z
             pairs.append((x * SIDE + z, to_x * SIDE + to_z))
     return lax.ppermute(value, "expert", pairs)
+
+
+def dispatch_kernel(
+    window, parts, ids_ref, logits_ref, gain_ref, hidden_hbm, packed_hbm, place_ref, x_buf, out_buf, in_sem, out_sem
+):
+    rows, width = hidden_hbm.shape
+    piece = width // parts
+
+    def load(c):
+        cut = pl.ds(c * piece, piece)
+        return pltpu.make_async_copy(hidden_hbm.at[:, cut], x_buf.at[:, cut], in_sem.at[c])
+
+    def store(c):
+        cut = pl.ds(c * piece, piece)
+        return pltpu.make_async_copy(out_buf.at[:, cut], packed_hbm.at[:, cut], out_sem.at[c])
+
+    for c in range(parts):
+        load(c).start()
+    ids = ids_ref[...]
+    inside = ids < window
+    has = jnp.max(inside.astype(jnp.int32), axis=0, keepdims=True)
+    chosen = jnp.sum(jnp.where(inside, ids, 0), axis=0, keepdims=True)
+    sigma = 1.0 / (1.0 + jnp.exp(-logits_ref[...]))
+    weight = (
+        routed_scale
+        * jnp.sum(jnp.where(inside, sigma, 0.0), axis=0, keepdims=True)
+        / jnp.sum(sigma, axis=0, keepdims=True)
+    )
+    expert = lax.broadcasted_iota(jnp.int32, (window, rows), 0)
+    onehot = jnp.where((expert == chosen) & (has > 0), 1.0, 0.0)
+    earlier = lax.broadcasted_iota(jnp.int32, (rows, rows), 0) < lax.broadcasted_iota(
+        jnp.int32, (rows, rows), 1
+    )
+    rank = jnp.dot(
+        onehot.astype(jnp.bfloat16),
+        jnp.where(earlier, 1.0, 0.0).astype(jnp.bfloat16),
+        preferred_element_type=jnp.float32,
+    )
+    slot = jnp.sum(rank * onehot, axis=0, keepdims=True).astype(jnp.int32)
+    place = chosen * CAP + slot
+    pick = (lax.broadcasted_iota(jnp.int32, (window * CAP, rows), 0) == place) & (has > 0)
+    place_ref[...] = jnp.where(pick, weight, 0.0).T
+    pick = jnp.where(pick, 1.0, 0.0).astype(jnp.bfloat16)
+    square = jnp.zeros((rows, 128), jnp.float32)
+    for c in range(parts):
+        load(c).wait()
+        for i in range(c * piece, (c + 1) * piece, 128):
+            value = x_buf[:, i : i + 128].astype(jnp.float32)
+            square += value * value
+    scale = lax.rsqrt(jnp.sum(square, axis=1, keepdims=True) / width + norm_eps)
+    for c in range(parts):
+        cut = slice(c * piece, (c + 1) * piece)
+        normed = (x_buf[:, cut].astype(jnp.float32) * scale * gain_ref[:, cut]).astype(jnp.bfloat16)
+        out_buf[:, cut] = jnp.dot(pick, normed, preferred_element_type=jnp.float32).astype(
+            jnp.bfloat16
+        )
+        store(c).start()
+    for c in range(parts):
+        store(c).wait()
+
+
+def dispatch(hidden_in, norm_gain, route_logits, expert_ids, window):
+    rows, width = hidden_in.shape
+    places, parts = window * CAP, 4
+    vmem = pl.BlockSpec(memory_space=pltpu.VMEM)
+    hbm = pl.BlockSpec(memory_space=pl.ANY)
+    return pl.pallas_call(
+        functools.partial(dispatch_kernel, window, parts),
+        out_shape=[
+            jax.ShapeDtypeStruct((places, width), jnp.bfloat16),
+            jax.ShapeDtypeStruct((rows, places), jnp.float32),
+        ],
+        in_specs=[vmem] * 3 + [hbm],
+        out_specs=[hbm, vmem],
+        scratch_shapes=[
+            pltpu.VMEM((rows, width), jnp.bfloat16),
+            pltpu.VMEM((places, width), jnp.bfloat16),
+            pltpu.SemaphoreType.DMA((parts,)),
+            pltpu.SemaphoreType.DMA((parts,)),
+        ],
+        compiler_params=pltpu.CompilerParams(vmem_limit_bytes=58 * MIB),
+        cost_estimate=pl.CostEstimate(
+            flops=2 * rows * places * width,
+            bytes_accessed=4 * rows * width,
+            transcendentals=rows * 16,
+        ),
+        name="dispatch",
+    )(expert_ids.T, route_logits.T, norm_gain.reshape(1, width), hidden_in)
 
 
 def ffn_kernel(count, rows, parts, *refs):
@@ -510,26 +598,13 @@
     local_experts = w_gate.shape[0]
     window = local_experts * dp_count
     width = hidden_in.shape[1]
-    w_plane = lax.all_gather(jnp.concatenate([w_latent] * 2, axis=0), "expert", axis=0, tiled=True)
-    x_wide = hidden_in.astype(jnp.float32)
-    normed = rms_rows(x_wide, norm_gain).astype(jnp.bfloat16)
-    in_window = expert_ids < window
-    has = jnp.any(in_window, axis=1)
-    chosen = jnp.sum(jnp.where(in_window, expert_ids, 0), axis=1)
-    sigma = jax.nn.sigmoid(route_logits)
-    weight = (
-        routed_scale * jnp.sum(jnp.where(in_window, sigma, 0.0), axis=1) / jnp.sum(sigma, axis=1)
-    )
-    onehot = ((chosen[:, None] == jnp.arange(window)[None, :]) & has[:, None]).astype(jnp.int32)
-    rank = jnp.cumsum(onehot, axis=0) - onehot
-    slot = jnp.sum(rank * onehot, axis=1)
+    padded = w_latent.shape[0] + 8
+    w_padded = jnp.concatenate([w_latent, w_latent[:8]], axis=0)
+    w_plane = lax.all_gather(w_padded, "expert", axis=0, tiled=True)
     slots = local_experts * CAP
-    place = chosen * CAP + slot
-    pick = (place[:, None] == jnp.arange(window * CAP)[None, :]) & has[:, None]
-    packed = jnp.einsum(
-        "rs,rd->sd", pick.astype(jnp.bfloat16), normed, preferred_element_type=jnp.float32
-    ).astype(jnp.bfloat16)
-    place_weight = jnp.where(pick, weight[:, None], 0.0)
+    packed, place_weight = dispatch(
+        hidden_in, after(norm_gain, w_padded), route_logits, expert_ids, window
+    )
     arrived = lax.all_to_all(
         packed.reshape(dp_count, slots, width), "dp", split_axis=0, concat_axis=0, tiled=True
     )
@@ -545,11 +620,7 @@
 
     below = [shift(rows[k], axes[k][0], 1) for k in both]
     above = [shift(rows[k], axes[k][0], -1) for k in both]
-    below, above, w_plane = after((below, above, w_plane))
-    w_plane = w_plane.reshape(ex_count, 2 * w_latent.shape[0], KVW)[:, : w_latent.shape[0]]
-    w_all = lax.all_gather(
-        w_plane.reshape(ex_count * w_latent.shape[0], KVW), "dp", axis=0, tiled=True
-    )
+    below, above = after((below, above))
     beyond = [shift(above[k], axes[k][0], -1) for k in both]
     low = pack([(rows[k], below[k]) for k in both])
     below_low = [shift(low[k], axes[k][1], 1) for k in both]
@@ -563,6 +634,11 @@
         concat_axis=0,
         tiled=True,
     ).reshape(dp_count * MCAP, PAGE, KVW)
+    high, w_plane = after((high, w_plane))
+    w_plane = w_plane.reshape(ex_count, padded, KVW)[:, : w_latent.shape[0]]
+    w_all = lax.all_gather(
+        w_plane.reshape(ex_count * w_latent.shape[0], KVW), "dp", axis=0, tiled=True
+    )
     pool = after(page_pool, high).reshape(page_pool.shape[0], PAGE, KVW)
     below_high = [shift(high[k], axes[k][1], 1) for k in both]
     above_high = [shift(high[k], axes[k][1], -1) for k in both]

time: 298 us -> 293 us (0.983)
  waiting for transfers between devices: 99.1 us -> 90.1 us
  starting transfers between devices: 61.2 us -> 67.5 us
  other arithmetic: 25.9 us -> 21.4 us
  Pallas kernels: 62.4 us -> 66.5 us
    all_gather x1, waiting for transfers between devices: 6.61 us -> 0.01 us  [body(): w_plane = lax.all_gather(w_padded, 'expert', axis=0, tiled=True)]
    ppermute x36, waiting for transfers between devices: 78.7 us -> 74.5 us  [shift(): return lax.ppermute(value, 'expert', pairs)]
    pallas_call x0 -> x1, Pallas kernels: none -> 4 us  [dispatch(): pl.pallas_call(functools.partial(dispatch_kernel, window, parts), out_sha...]
    unnamed x63 -> x59, local copies, waits for them, and re-layouts: 8.97 us -> 8.84 us
  transfers between devices with their start and end apart: 41 -> 41, of which waited for: 26 -> 22; matrix products, arithmetic and copies ran while one was open for 18% -> 16% of each run, Pallas kernels for 16% -> 16%
where the time goes in v5:
time: 293 us; the launch traced here: 292 us
  waiting for transfers between devices  90.1 us (31%)
  starting transfers between devices  67.5 us (23%)
  Pallas kernels  66.5 us (23%)
  local copies, waits for them, and re-layouts  31.6 us (11%)
  other arithmetic  21.4 us (7%)
  between operations  14.5 us (5%)
    ppermute x36, waiting for transfers between devices, shift(): return lax.ppermute(value, 'expert', pairs)  74.5 us
    ppermute x36, starting transfers between devices, shift(): return lax.ppermute(value, 'expert', pairs)  36.6 us
    pallas_call x3, Pallas kernels, ffn(): pl.pallas_call(functools.partial(ffn_kernel, count, rows, parts), out_sha...  28.4 us
    convert_element_type x11, other arithmetic, plus(): return total.astype(jnp.bfloat16)  18 us
    all_to_all x1, starting transfers between devices, body(): lax.all_to_all(jnp.concatenate(finished, axis=0).reshape(dp_count, slots,...  17.4 us
    pallas_call x1, Pallas kernels, tail(): pl.pallas_call(functools.partial(tail_kernel, parts, groups), out_shape=[...  16.2 us
    pallas_call x1, Pallas kernels, attend_cached(): pl.pallas_call(functools.partial(attend_kernel, step), out_shape=[jax.Sha...  13 us
    all_to_all x1, waiting for transfers between devices, body(): lax.all_to_all(jnp.concatenate(finished, axis=0).reshape(dp_count, slots,...  12.8 us
  transfers between devices with their start and end apart: 41, of which 22 were waited for; matrix products, arithmetic and copies ran while one was open for 16% of the time, Pallas kernels for 16%

profile of v5, /device:TPU:1, one launch (start us, length us, event | category | flops | bytes accessed | tf_op | source)
XLA Modules:
  0.0 291.6 jit_solution(762719817198552260)
XLA Ops:
  9.4 4.0 %dispatch.1 = (bf16[64,7168]{1,0:T(8,128)(2,1)}, f32[64,64]{1,0:T(8,128)}) custom-call(s32[8,64]{1,0:T(8,128)} %bitcast.27, f32[8,64]{1,0:T(8,128)} %bitcast.28, f32[1,7168]{1,0:T(1,128)} %bitcast.26, bf16[64,7168]{1,0:T(8,128)(2,1)} %hidden_hbm.3), custom_call_target="tpu_custom_call" | custom-call | flops 58720256 | bytes 1835008 | tf_op jit(solution)/shard_map/dispatch/pallas_call | solution.py:104
  13.4 6.0 %all-to-all-start = ((bf16[8,8,7168]{2,1,0:T(8,128)(2,1)}), bf16[8,8,7168]{2,1,0:T(8,128)(2,1)S(1)}, u32[]{:S(2)}, u32[]{:S(2)}) async-start(bf16[8,8,7168]{2,1,0:T(8,128)(2,1)} %bitcast.25), calls=%async_computation | async-start | bytes 1835008 | tf_op jit(solution)/shard_map/all_to_all | solution.py:608
  20.1 10.0 %reshape.57.q_ref = bf16[64,64,576]{2,1,0:T(8,128)(2,1)} reshape(bf16[64,36864]{1,0:T(8,128)(2,1)} %q_hbm.1) | data formatting | bytes 9437184 | tf_op jit(solution)/shard_map/reshape | solution.py:612
  39.8 8.9 %collective-permute-done.refs_1_ = bf16[32,7168]{1,0:T(8,128)(2,1)S(1)} collective-permute-done((bf16[32,7168]{1,0:T(8,128)(2,1)S(1)}, bf16[32,7168]{1,0:T(8,128)(2,1)S(1)}, u32[]{:S(2)}, u32[]{:S(2)}) %collective-permute-start) | collective-permute-done | bytes 458784 | tf_op jit(solution)/shard_map/ppermute | solution.py:37
  56.6 7.5 %collective-permute-done.4.refs_1_ = bf16[32,7168]{1,0:T(8,128)(2,1)S(1)} collective-permute-done((bf16[32,7168]{1,0:T(8,128)(2,1)S(1)}, bf16[32,7168]{1,0:T(8,128)(2,1)S(1)}, u32[]{:S(2)}, u32[]{:S(2)}) %collective-permute-start.4) | collective-permute-done | bytes 458784 | tf_op jit(solution)/shard_map/ppermute | solution.py:37
  64.1 3.8 %collective-permute-done.5.refs_3_ = bf16[32,7168]{1,0:T(8,128)(2,1)} collective-permute-done((bf16[32,7168]{1,0:T(8,128)(2,1)S(1)}, bf16[32,7168]{1,0:T(8,128)(2,1)}, u32[]{:S(2)}, u32[]{:S(2)}) %collective-permute-start.5) | collective-permute-done | bytes 458784 | tf_op jit(solution)/shard_map/ppermute | solution.py:37
  67.9 3.5 %collective-permute-start.7 = (bf16[64,7168]{1,0:T(8,128)(2,1)}, bf16[64,7168]{1,0:T(8,128)(2,1)}, u32[]{:S(2)}, u32[]{:S(2)}) collective-permute-start(bf16[64,7168]{1,0:T(8,128)(2,1)} %get-tuple-element.97.refs_0_), channel_id=1, source_target_pairs={{0,12},{1,13},{2,14},{3,15},{4,0},{5,1},{6,2},{7,3},{8,4},{9,5},{1... | collective-permute-start | bytes 2752520 | tf_op jit(solution)/shard_map/ppermute | solution.py:37
  74.9 7.5 %all-to-all-start.1 = ((bf16[8,4,9216]{2,1,0:T(4,128)(2,1)}), bf16[8,4,9216]{2,1,0:T(4,128)(2,1)S(1)}, u32[]{:S(2)}, u32[]{:S(2)}) async-start(bf16[8,4,9216]{2,1,0:T(4,128)(2,1)} %reshape.59), calls=%async_computation.1 | async-start | bytes 1179648 | tf_op jit(solution)/shard_map/all_to_all | solution.py:630
  84.8 4.5 %collective-permute-done.7.refs_3_ = bf16[64,7168]{1,0:T(8,128)(2,1)} collective-permute-done((bf16[64,7168]{1,0:T(8,128)(2,1)}, bf16[64,7168]{1,0:T(8,128)(2,1)}, u32[]{:S(2)}, u32[]{:S(2)}) %collective-permute-start.7) | collective-permute-done | bytes 917536 | tf_op jit(solution)/shard_map/ppermute | solution.py:37
  94.1 11.5 %ffn.3 = (bf16[64,7168]{1,0:T(8,128)(2,1)}, bf16[64,7168]{1,0:T(8,128)(2,1)}, bf16[64,7168]{1,0:T(8,128)(2,1)}, bf16[64,7168]{1,0:T(8,128)(2,1)}, bf16[64,7168]{...) custom-call(bf16[64,7168]{1,0:T(8,128)(2,1)} %get-tuple-element.97.refs_0_, ...), custom_call_target="tpu_custom_call" | custom-call | flops 5637144576 | bytes 25690112 | tf_op jit(solution)/shard_map/ffn/pallas_call | solution.py:207
  105.5 3.4 %collective-permute-done.10.refs_1_ = bf16[64,7168]{1,0:T(8,128)(2,1)} collective-permute-done((bf16[64,7168]{1,0:T(8,128)(2,1)}, bf16[64,7168]{1,0:T(8,128)(2,1)}, u32[]{:S(2)}, u32[]{:S(2)}) %collective-permute-start.10) | collective-permute-done | bytes 917536 | tf_op jit(solution)/shard_map/ppermute | solution.py:37
  110.9 2.6 collective-permute-start.16
  113.5 2.7 collective-permute-start.17
  116.2 8.5 %ffn.4 = (bf16[64,7168]{1,0:T(8,128)(2,1)}, bf16[64,7168]{1,0:T(8,128)(2,1)}, bf16[64,7168]{1,0:T(8,128)(2,1)}, bf16[64,7168]{1,0:T(8,128)(2,1)}) custom-call(bf16[64,7168]{1,0:T(8,128)(2,1)} %collective-permute-done.12.refs_0_, bf16[64,7168]{1,0:T(8,128)(2,1)} %collective-permute-done.10.refs_1_, bf16[64,7168]{1,0:T(8,128)(2,1)} %collective-permute-done.13.refs_2_, ...), custom_call_target="tpu_custom_call" | custom-call | flops 2818572288 | bytes 18350080 | tf_op jit(solution)/shard_map/ffn/pallas_call | solution.py:207
  124.7 6.0 %collective-permute-done.14.refs_0_ = bf16[64,7168]{1,0:T(8,128)(2,1)S(1)} collective-permute-done((bf16[64,7168]{1,0:T(8,128)(2,1)}, bf16[64,7168]{1,0:T(8,128)(2,1)S(1)}, u32[]{:S(2)}, u32[]{:S(2)}) %collective-permute-start.14) | collective-permute-done | bytes 917536 | tf_op jit(solution)/shard_map/ppermute | solution.py:37
  132.3 8.5 %ffn.5 = (bf16[64,7168]{1,0:T(8,128)(2,1)}, bf16[64,7168]{1,0:T(8,128)(2,1)}, bf16[64,7168]{1,0:T(8,128)(2,1)}, bf16[64,7168]{1,0:T(8,128)(2,1)}) custom-call(bf16[64,7168]{1,0:T(8,128)(2,1)} %copy-done.7, bf16[64,7168]{1,0:T(8,128)(2,1)} %copy-done.9, bf16[64,7168]{1,0:T(8,128)(2,1)} %copy-done.8, bf16[64,7168]{1,0:T(8,128)(2,1)} %collective-permute-done.17.refs_3_, ...), custom_call_target="tpu_custom_call" | custom-call | flops 2818572288 | bytes 18350080 | tf_op jit(solution)/shard_map/ffn/pallas_call | solution.py:207
  140.8 5.0 %collective-permute-done.18 = bf16[64,7168]{1,0:T(8,128)(2,1)} collective-permute-done((bf16[64,7168]{1,0:T(8,128)(2,1)}, bf16[64,7168]{1,0:T(8,128)(2,1)}, u32[]{:S(2)}, u32[]{:S(2)}) %collective-permute-start.18) | collective-permute-done | bytes 917536 | tf_op jit(solution)/shard_map/ppermute | solution.py:37
  145.8 5.3 %collective-permute-done.19 = bf16[64,7168]{1,0:T(8,128)(2,1)} collective-permute-done((bf16[64,7168]{1,0:T(8,128)(2,1)}, bf16[64,7168]{1,0:T(8,128)(2,1)}, u32[]{:S(2)}, u32[]{:S(2)}) %collective-permute-start.19) | collective-permute-done | bytes 917536 | tf_op jit(solution)/shard_map/ppermute | solution.py:37
  151.2 2.6 collective-permute-start.24
  153.8 3.4 %collective-permute-start.25 = (bf16[64,7168]{1,0:T(8,128)(2,1)}, bf16[64,7168]{1,0:T(8,128)(2,1)}, u32[]{:S(2)}, u32[]{:S(2)}) collective-permute-start(bf16[64,7168]{1,0:T(8,128)(2,1)} %get-tuple-element.135), channel_id=1, source_target_pairs={{0,3},{1,0},{2,1},{3,2},{4,7},{5,4},{6,5},{7,6},{8,11},{9,8},{10,9... | collective-permute-start | bytes 2752520 | tf_op jit(solution)/shard_map/ppermute | solution.py:37
  158.1 3.5 %copy.20.pool_hbm = bf16[128,16,576]{2,1,0:T(8,128)(2,1)} copy(bf16[128,16,576]{0,2,1:T(8,128)(2,1)S(1)} %bitcast.20) | data formatting | bytes 4718592 | tf_op jit(solution)/shard_map/reshape | solution.py:642
  161.5 13.0 %attend_cached.1 = (bf16[64,64,512]{2,1,0:T(8,128)(2,1)}, f32[64,64]{1,0:T(8,128)}, f32[64,64]{1,0:T(8,128)}) custom-call(s32[384]{0:T(512)} %reshape.61.table, s32[64]{0:T(128)} %lengths.1, bf16[64,64,576]{2,1,0:T(8,128)(2,1)} %reshape.57.q_ref, bf16[128,16,576]{2,1,0:T(8,128)(2,1)} %copy.20.pool_hbm, bf16[32,16,576]{2,1,0:T(8,128)(2,1)} %reshape.60.more_hbm), custom_call_target="tpu_custom_call" | custom-call | flops 855638016 | bytes 11862016 | tf_op jit(solution)/shard_map/attend_cached/pallas_call | solution.py:293
  174.6 2.7 add_convert_fusion
  187.2 6.8 %copy.21 = bf16[8,8,64,512]{3,1,2,0:T(8,128)(2,1)} copy(bf16[8,8,64,512]{3,2,1,0:T(8,128)(2,1)} %bitcast.22) | data formatting | bytes 8388608
  196.3 3.6 %collective-permute-done.27 = bf16[64,7168]{1,0:T(8,128)(2,1)S(1)} collective-permute-done((bf16[64,7168]{1,0:T(8,128)(2,1)}, bf16[64,7168]{1,0:T(8,128)(2,1)S(1)}, u32[]{:S(2)}, u32[]{:S(2)}) %collective-permute-start.27) | collective-permute-done | bytes 917536 | tf_op jit(solution)/shard_map/ppermute | solution.py:37
  211.7 5.0 %collective-permute-done.31 = bf16[32,7168]{1,0:T(8,128)(2,1)S(1)} collective-permute-done((bf16[32,7168]{1,0:T(8,128)(2,1)S(1)}, bf16[32,7168]{1,0:T(8,128)(2,1)S(1)}, u32[]{:S(2)}, u32[]{:S(2)}) %collective-permute-start.31) | collective-permute-done | bytes 458784 | tf_op jit(solution)/shard_map/ppermute | solution.py:37
  216.7 2.7 collective-permute-done.30
  222.2 8.3 %collective-permute-done.35 = bf16[32,7168]{1,0:T(8,128)(2,1)S(1)} collective-permute-done((bf16[32,7168]{1,0:T(8,128)(2,1)S(1)}, bf16[32,7168]{1,0:T(8,128)(2,1)S(1)}, u32[]{:S(2)}, u32[]{:S(2)}) %collective-permute-start.35) | collective-permute-done | bytes 458784 | tf_op jit(solution)/shard_map/ppermute | solution.py:37
  230.5 3.3 %collective-permute-done.34 = bf16[32,7168]{1,0:T(8,128)(2,1)S(1)} collective-permute-done((bf16[32,7168]{1,0:T(8,128)(2,1)S(1)}, bf16[32,7168]{1,0:T(8,128)(2,1)S(1)}, u32[]{:S(2)}, u32[]{:S(2)}) %collective-permute-start.34) | collective-permute-done | bytes 458784 | tf_op jit(solution)/shard_map/ppermute | solution.py:37
  236.5 17.4 %all-to-all-start.2 = ((bf16[8,8,7168]{2,1,0:T(8,128)(2,1)}), bf16[8,8,7168]{2,1,0:T(8,128)(2,1)S(1)}, u32[]{:S(2)}, u32[]{:S(2)}) async-start(bf16[8,8,7168]{2,1,0:T(8,128)(2,1)} %maximum_bitcast_fusion), calls=%async_computation.2 | async-start | bytes 1835008 | tf_op jit(solution)/shard_map/all_to_all | solution.py:681
  254.8 12.8 %all-to-all-done.2 = bf16[8,8,7168]{2,1,0:T(8,128)(2,1)S(1)} async-done(((bf16[8,8,7168]{2,1,0:T(8,128)(2,1)}), bf16[8,8,7168]{2,1,0:T(8,128)(2,1)S(1)}, u32[]{:S(2)}, u32[]{:S(2)}) %all-to-all-start.2) | async-done | bytes 917536 | tf_op jit(solution)/shard_map/all_to_all | solution.py:681
  268.6 16.2 %tail.1 = (bf16[64,7168]{1,0:T(8,128)(2,1)}, bf16[64,32768]{1,0:T(8,128)(2,1)}) custom-call(bf16[64,7168]{1,0:T(8,128)(2,1)} %hidden_hbm.3, bf16[64,7168]{1,0:T(8,128)(2,1)} %bitcast.23, f32[1,512]{1,0:T(1,128)} %bitcast.29, f32[64,32]{1,0:T(8,128)} %get-tuple-element.167.cos_ref, f32[64,32]{1,0:T(8,128)} %get-tuple-element.166.sin_ref, ...), custom_call_target="tpu_custom_call" | custom-call | flops 528482304 | bytes 21364736 | tf_op jit(solution)/shard_map/tail/pallas_call | solution.py:521
  (147 shorter events, 66.9 us)
Async XLA Ops:
  13.4 19.7 %all-to-all-start = ((bf16[8,8,7168]{2,1,0:T(8,128)(2,1)}), bf16[8,8,7168]{2,1,0:T(8,128)(2,1)S(1)}, u32[]{:S(2)}, u32[]{:S(2)}) async-start(bf16[8,8,7168]{2,1,0:T(8,128)(2,1)} %bitcast.25), calls=%async_computation | async-start | bytes 1835008 | tf_op jit(solution)/shard_map/all_to_all | solution.py:608
  19.4 63.0 %all-gather.3.cloned.1.call-start = ((), (), s32[]{:S(2)}) async-start(), calls=%async_computation.3 | async-start | bytes 1392640 | tf_op jit(solution)/shard_map/all_gather | solution.py:603
  33.2 15.5 %collective-permute-start = (bf16[32,7168]{1,0:T(8,128)(2,1)S(1)}, bf16[32,7168]{1,0:T(8,128)(2,1)S(1)}, u32[]{:S(2)}, u32[]{:S(2)}) collective-permute-start(bf16[32,7168]{1,0:T(8,128)(2,1)S(1)} %get-tuple-element.165.refs_0_), channel_id=1, source_target_pairs={{0,1},{1,2},{2,3},{3,0},{4,5},{5,6},{6,7},{7,4},{8,9},{9,10},{10,1... | collective-permute-start | bytes 1376264 | tf_op jit(solution)/shard_map/ppermute | solution.py:37
  50.2 13.9 %collective-permute-start.4 = (bf16[32,7168]{1,0:T(8,128)(2,1)S(1)}, bf16[32,7168]{1,0:T(8,128)(2,1)S(1)}, u32[]{:S(2)}, u32[]{:S(2)}) collective-permute-start(bf16[32,7168]{1,0:T(8,128)(2,1)S(1)} %collective-permute-done.2.refs_0_), channel_id=1, source_target_pairs={{0,3},{1,0},{2,1},{3,2},{4,7},{5,4},{6,5},{7,6},{8,11},{9,8},{10,9... | collective-permute-start | bytes 1376264 | tf_op jit(solution)/shard_map/ppermute | solution.py:37
  52.0 15.9 %collective-permute-start.5 = (bf16[32,7168]{1,0:T(8,128)(2,1)S(1)}, bf16[32,7168]{1,0:T(8,128)(2,1)}, u32[]{:S(2)}, u32[]{:S(2)}) collective-permute-start(bf16[32,7168]{1,0:T(8,128)(2,1)S(1)} %collective-permute-done.3.refs_2_), channel_id=1, source_target_pairs={{0,12},{1,13},{2,14},{3,15},{4,0},{5,1},{6,2},{7,3},{8,4},{9,5},{1... | collective-permute-start | bytes 1376264 | tf_op jit(solution)/shard_map/ppermute | solution.py:37
  56.5 26.0 %collective-permute-start.6 = (bf16[64,7168]{1,0:T(8,128)(2,1)}, bf16[64,7168]{1,0:T(8,128)(2,1)}, u32[]{:S(2)}, u32[]{:S(2)}) collective-permute-start(bf16[64,7168]{1,0:T(8,128)(2,1)} %get-tuple-element.97.refs_0_), channel_id=1, source_target_pairs={{0,4},{1,5},{2,6},{3,7},{4,8},{5,9},{6,10},{7,11},{8,12},{9,13},{1... | collective-permute-start | bytes 2752520 | tf_op jit(solution)/shard_map/ppermute | solution.py:37
  56.5 27.4 %collective-permute-start.8 = (bf16[64,7168]{1,0:T(8,128)(2,1)}, bf16[64,7168]{1,0:T(8,128)(2,1)}, u32[]{:S(2)}, u32[]{:S(2)}) collective-permute-start(bf16[64,7168]{1,0:T(8,128)(2,1)} %get-tuple-element.99.refs_4_), channel_id=1, source_target_pairs={{0,1},{1,2},{2,3},{3,0},{4,5},{5,6},{6,7},{7,4},{8,9},{9,10},{10,1... | collective-permute-start | bytes 2752520 | tf_op jit(solution)/shard_map/ppermute | solution.py:37
  67.9 21.3 %collective-permute-start.7 = (bf16[64,7168]{1,0:T(8,128)(2,1)}, bf16[64,7168]{1,0:T(8,128)(2,1)}, u32[]{:S(2)}, u32[]{:S(2)}) collective-permute-start(bf16[64,7168]{1,0:T(8,128)(2,1)} %get-tuple-element.97.refs_0_), channel_id=1, source_target_pairs={{0,12},{1,13},{2,14},{3,15},{4,0},{5,1},{6,2},{7,3},{8,4},{9,5},{1... | collective-permute-start | bytes 2752520 | tf_op jit(solution)/shard_map/ppermute | solution.py:37
  71.4 22.7 %collective-permute-start.9 = (bf16[64,7168]{1,0:T(8,128)(2,1)}, bf16[64,7168]{1,0:T(8,128)(2,1)}, u32[]{:S(2)}, u32[]{:S(2)}) collective-permute-start(bf16[64,7168]{1,0:T(8,128)(2,1)} %get-tuple-element.99.refs_4_), channel_id=1, source_target_pairs={{0,3},{1,0},{2,1},{3,2},{4,7},{5,4},{6,5},{7,6},{8,11},{9,8},{10,9... | collective-permute-start | bytes 2752520 | tf_op jit(solution)/shard_map/ppermute | solution.py:37
  74.9 17.7 %all-to-all-start.1 = ((bf16[8,4,9216]{2,1,0:T(4,128)(2,1)}), bf16[8,4,9216]{2,1,0:T(4,128)(2,1)S(1)}, u32[]{:S(2)}, u32[]{:S(2)}) async-start(bf16[8,4,9216]{2,1,0:T(4,128)(2,1)} %reshape.59), calls=%async_computation.1 | async-start | bytes 1179648 | tf_op jit(solution)/shard_map/all_to_all | solution.py:630
  82.4 185.2 %all-gather.5.cloned.1.call-start = ((), (), s32[]{:S(2)}) async-start(), calls=%async_computation.4 | async-start | bytes 10321920 | tf_op jit(solution)/shard_map/all_gather | solution.py:639
  82.4 26.5 %collective-permute-start.10 = (bf16[64,7168]{1,0:T(8,128)(2,1)}, bf16[64,7168]{1,0:T(8,128)(2,1)}, u32[]{:S(2)}, u32[]{:S(2)}) collective-permute-start(bf16[64,7168]{1,0:T(8,128)(2,1)} %get-tuple-element.96.refs_1_), channel_id=1, source_target_pairs={{0,12},{1,13},{2,14},{3,15},{4,0},{5,1},{6,2},{7,3},{8,4},{9,5},{1... | collective-permute-start | bytes 2752520 | tf_op jit(solution)/shard_map/ppermute | solution.py:37
  82.5 28.3 %collective-permute-start.12 = (bf16[64,7168]{1,0:T(8,128)(2,1)}, bf16[64,7168]{1,0:T(8,128)(2,1)}, u32[]{:S(2)}, u32[]{:S(2)}) collective-permute-start(bf16[64,7168]{1,0:T(8,128)(2,1)} %get-tuple-element.96.refs_1_), channel_id=1, source_target_pairs={{0,4},{1,5},{2,6},{3,7},{4,8},{5,9},{6,10},{7,11},{8,12},{9,13},{1... | collective-permute-start | bytes 2752520 | tf_op jit(solution)/shard_map/ppermute | solution.py:37
  84.0 26.8 %collective-permute-start.11 = (bf16[64,7168]{1,0:T(8,128)(2,1)}, bf16[64,7168]{1,0:T(8,128)(2,1)}, u32[]{:S(2)}, u32[]{:S(2)}) collective-permute-start(bf16[64,7168]{1,0:T(8,128)(2,1)} %get-tuple-element.98.refs_5_), channel_id=1, source_target_pairs={{0,3},{1,0},{2,1},{3,2},{4,7},{5,4},{6,5},{7,6},{8,11},{9,8},{10,9... | collective-permute-start | bytes 2752520 | tf_op jit(solution)/shard_map/ppermute | solution.py:37
  89.2 21.6 %collective-permute-start.13 = (bf16[64,7168]{1,0:T(8,128)(2,1)}, bf16[64,7168]{1,0:T(8,128)(2,1)}, u32[]{:S(2)}, u32[]{:S(2)}) collective-permute-start(bf16[64,7168]{1,0:T(8,128)(2,1)} %get-tuple-element.98.refs_5_), channel_id=1, source_target_pairs={{0,1},{1,2},{2,3},{3,0},{4,5},{5,6},{6,7},{7,4},{8,9},{9,10},{10,1... | collective-permute-start | bytes 2752520 | tf_op jit(solution)/shard_map/ppermute | solution.py:37
  110.8 20.0 %collective-permute-start.14 = (bf16[64,7168]{1,0:T(8,128)(2,1)}, bf16[64,7168]{1,0:T(8,128)(2,1)S(1)}, u32[]{:S(2)}, u32[]{:S(2)}) collective-permute-start(bf16[64,7168]{1,0:T(8,128)(2,1)} %collective-permute-done.6.refs_2_), channel_id=1, source_target_pairs={{0,4},{1,5},{2,6},{3,7},{4,8},{5,9},{6,10},{7,11},{8,12},{9,13},{1... | collective-permute-start | bytes 2752520 | tf_op jit(solution)/shard_map/ppermute | solution.py:37
  110.8 20.0 %collective-permute-start.15 = (bf16[64,7168]{1,0:T(8,128)(2,1)}, bf16[64,7168]{1,0:T(8,128)(2,1)S(1)}, u32[]{:S(2)}, u32[]{:S(2)}) collective-permute-start(bf16[64,7168]{1,0:T(8,128)(2,1)} %collective-permute-done.8.refs_6_), channel_id=1, source_target_pairs={{0,1},{1,2},{2,3},{3,0},{4,5},{5,6},{6,7},{7,4},{8,9},{9,10},{10,1... | collective-permute-start | bytes 2752520 | tf_op jit(solution)/shard_map/ppermute | solution.py:37
  110.9 20.0 %collective-permute-start.16 = (bf16[64,7168]{1,0:T(8,128)(2,1)}, bf16[64,7168]{1,0:T(8,128)(2,1)S(1)}, u32[]{:S(2)}, u32[]{:S(2)}) collective-permute-start(bf16[64,7168]{1,0:T(8,128)(2,1)} %collective-permute-done.10.refs_1_), channel_id=1, source_target_pairs={{0,12},{1,13},{2,14},{3,15},{4,0},{5,1},{6,2},{7,3},{8,4},{9,5},{1... | collective-permute-start | bytes 2752520 | tf_op jit(solution)/shard_map/ppermute | solution.py:37
  113.5 18.8 %collective-permute-start.17 = (bf16[64,7168]{1,0:T(8,128)(2,1)}, bf16[64,7168]{1,0:T(8,128)(2,1)}, u32[]{:S(2)}, u32[]{:S(2)}) collective-permute-start(bf16[64,7168]{1,0:T(8,128)(2,1)} %collective-permute-done.11.refs_3_), channel_id=1, source_target_pairs={{0,3},{1,0},{2,1},{3,2},{4,7},{5,4},{6,5},{7,6},{8,11},{9,8},{10,9... | collective-permute-start | bytes 2752520 | tf_op jit(solution)/shard_map/ppermute | solution.py:37
  124.6 26.5 %collective-permute-start.20 = (bf16[64,7168]{1,0:T(8,128)(2,1)}, bf16[64,7168]{1,0:T(8,128)(2,1)}, u32[]{:S(2)}, u32[]{:S(2)}) collective-permute-start(bf16[64,7168]{1,0:T(8,128)(2,1)} %get-tuple-element.115), channel_id=1, source_target_pairs={{0,4},{1,5},{2,6},{3,7},{4,8},{5,9},{6,10},{7,11},{8,12},{9,13},{1... | collective-permute-start | bytes 2752520 | tf_op jit(solution)/shard_map/ppermute | solution.py:37
  130.8 15.1 %collective-permute-start.18 = (bf16[64,7168]{1,0:T(8,128)(2,1)}, bf16[64,7168]{1,0:T(8,128)(2,1)}, u32[]{:S(2)}, u32[]{:S(2)}) collective-permute-start(bf16[64,7168]{1,0:T(8,128)(2,1)} %get-tuple-element.130), channel_id=1, source_target_pairs={{0,12},{1,13},{2,14},{3,15},{4,0},{5,1},{6,2},{7,3},{8,4},{9,5},{1... | collective-permute-start | bytes 2752520 | tf_op jit(solution)/shard_map/ppermute | solution.py:37
  130.8 20.3 %collective-permute-start.19 = (bf16[64,7168]{1,0:T(8,128)(2,1)}, bf16[64,7168]{1,0:T(8,128)(2,1)}, u32[]{:S(2)}, u32[]{:S(2)}) collective-permute-start(bf16[64,7168]{1,0:T(8,128)(2,1)} %get-tuple-element.131), channel_id=1, source_target_pairs={{0,3},{1,0},{2,1},{3,2},{4,7},{5,4},{6,5},{7,6},{8,11},{9,8},{10,9... | collective-permute-start | bytes 2752520 | tf_op jit(solution)/shard_map/ppermute | solution.py:37
  130.9 20.2 %collective-permute-start.21 = (bf16[64,7168]{1,0:T(8,128)(2,1)}, bf16[64,7168]{1,0:T(8,128)(2,1)}, u32[]{:S(2)}, u32[]{:S(2)}) collective-permute-start(bf16[64,7168]{1,0:T(8,128)(2,1)} %get-tuple-element.117), channel_id=1, source_target_pairs={{0,1},{1,2},{2,3},{3,0},{4,5},{5,6},{6,7},{7,4},{8,9},{9,10},{10,1... | collective-permute-start | bytes 2752520 | tf_op jit(solution)/shard_map/ppermute | solution.py:37
  151.1 23.4 %collective-permute-start.22 = (bf16[64,7168]{1,0:T(8,128)(2,1)}, bf16[64,7168]{1,0:T(8,128)(2,1)S(1)}, u32[]{:S(2)}, u32[]{:S(2)}) collective-permute-start(bf16[64,7168]{1,0:T(8,128)(2,1)} %get-tuple-element.132), channel_id=1, source_target_pairs={{0,4},{1,5},{2,6},{3,7},{4,8},{5,9},{6,10},{7,11},{8,12},{9,13},{1... | collective-permute-start | bytes 2752520 | tf_op jit(solution)/shard_map/ppermute | solution.py:37
  151.1 23.4 %collective-permute-start.23 = (bf16[64,7168]{1,0:T(8,128)(2,1)}, bf16[64,7168]{1,0:T(8,128)(2,1)}, u32[]{:S(2)}, u32[]{:S(2)}) collective-permute-start(bf16[64,7168]{1,0:T(8,128)(2,1)} %get-tuple-element.133), channel_id=1, source_target_pairs={{0,1},{1,2},{2,3},{3,0},{4,5},{5,6},{6,7},{7,4},{8,9},{9,10},{10,1... | collective-permute-start | bytes 2752520 | tf_op jit(solution)/shard_map/ppermute | solution.py:37
  151.2 23.4 %collective-permute-start.24 = (bf16[64,7168]{1,0:T(8,128)(2,1)}, bf16[64,7168]{1,0:T(8,128)(2,1)}, u32[]{:S(2)}, u32[]{:S(2)}) collective-permute-start(bf16[64,7168]{1,0:T(8,128)(2,1)} %get-tuple-element.134), channel_id=1, source_target_pairs={{0,12},{1,13},{2,14},{3,15},{4,0},{5,1},{6,2},{7,3},{8,4},{9,5},{1... | collective-permute-start | bytes 2752520 | tf_op jit(solution)/shard_map/ppermute | solution.py:37
  153.8 20.8 %collective-permute-start.25 = (bf16[64,7168]{1,0:T(8,128)(2,1)}, bf16[64,7168]{1,0:T(8,128)(2,1)}, u32[]{:S(2)}, u32[]{:S(2)}) collective-permute-start(bf16[64,7168]{1,0:T(8,128)(2,1)} %get-tuple-element.135), channel_id=1, source_target_pairs={{0,3},{1,0},{2,1},{3,2},{4,7},{5,4},{6,5},{7,6},{8,11},{9,8},{10,9... | collective-permute-start | bytes 2752520 | tf_op jit(solution)/shard_map/ppermute | solution.py:37
  177.3 16.7 %collective-permute-start.29 = (bf16[64,7168]{1,0:T(8,128)(2,1)}, bf16[64,7168]{1,0:T(8,128)(2,1)}, u32[]{:S(2)}, u32[]{:S(2)}) collective-permute-start(bf16[64,7168]{1,0:T(8,128)(2,1)} %add_convert_fusion), channel_id=1, source_target_pairs={{0,3},{1,0},{2,1},{3,2},{4,7},{5,4},{6,5},{7,6},{8,11},{9,8},{10,9... | collective-permute-start | bytes 2752520 | tf_op jit(solution)/shard_map/ppermute | solution.py:37
  181.1 15.2 %collective-permute-start.28 = (bf16[64,7168]{1,0:T(8,128)(2,1)}, bf16[64,7168]{1,0:T(8,128)(2,1)S(1)}, u32[]{:S(2)}, u32[]{:S(2)}) collective-permute-start(bf16[64,7168]{1,0:T(8,128)(2,1)} %add_convert_fusion.1), channel_id=1, source_target_pairs={{0,12},{1,13},{2,14},{3,15},{4,0},{5,1},{6,2},{7,3},{8,4},{9,5},{1... | collective-permute-start | bytes 2752520 | tf_op jit(solution)/shard_map/ppermute | solution.py:37
  183.6 16.3 %collective-permute-start.27 = (bf16[64,7168]{1,0:T(8,128)(2,1)}, bf16[64,7168]{1,0:T(8,128)(2,1)S(1)}, u32[]{:S(2)}, u32[]{:S(2)}) collective-permute-start(bf16[64,7168]{1,0:T(8,128)(2,1)} %add_convert_fusion.2), channel_id=1, source_target_pairs={{0,1},{1,2},{2,3},{3,0},{4,5},{5,6},{6,7},{7,4},{8,9},{9,10},{10,1... | collective-permute-start | bytes 2752520 | tf_op jit(solution)/shard_map/ppermute | solution.py:37
  184.8 16.3 %collective-permute-start.26 = (bf16[64,7168]{1,0:T(8,128)(2,1)}, bf16[64,7168]{1,0:T(8,128)(2,1)S(1)}, u32[]{:S(2)}, u32[]{:S(2)}) collective-permute-start(bf16[64,7168]{1,0:T(8,128)(2,1)} %add_convert_fusion.3), channel_id=1, source_target_pairs={{0,4},{1,5},{2,6},{3,7},{4,8},{5,9},{6,10},{7,11},{8,12},{9,13},{1... | collective-permute-start | bytes 2752520 | tf_op jit(solution)/shard_map/ppermute | solution.py:37
  236.5 31.1 %all-to-all-start.2 = ((bf16[8,8,7168]{2,1,0:T(8,128)(2,1)}), bf16[8,8,7168]{2,1,0:T(8,128)(2,1)S(1)}, u32[]{:S(2)}, u32[]{:S(2)}) async-start(bf16[8,8,7168]{2,1,0:T(8,128)(2,1)} %maximum_bitcast_fusion), calls=%async_computation.2 | async-start | bytes 1835008 | tf_op jit(solution)/shard_map/all_to_all | solution.py:681
  (37 other events, 408.1 us)
Sparse Core Ops, SparseCore 0:
  22.4 47.5 all-gather.2
  187.3 61.8 all-gather.4

commit v6 on v5

--- a/solution.py
+++ b/solution.py
@@ -603,7 +603,7 @@
     w_plane = lax.all_gather(w_padded, "expert", axis=0, tiled=True)
     slots = local_experts * CAP
     packed, place_weight = dispatch(
-        hidden_in, after(norm_gain, w_padded), route_logits, expert_ids, window
+        hidden_in, norm_gain, route_logits, expert_ids, window
     )
     arrived = lax.all_to_all(
         packed.reshape(dp_count, slots, width), "dp", split_axis=0, concat_axis=0, tiled=True
@@ -624,11 +624,10 @@
     beyond = [shift(above[k], axes[k][0], -1) for k in both]
     low = pack([(rows[k], below[k]) for k in both])
     below_low = [shift(low[k], axes[k][1], 1) for k in both]
-    low_too, beyond = after((low, beyond))
-    above_low = [shift(low_too[k], axes[k][1], -1) for k in both]
+    above_low = [shift(low[k], axes[k][1], -1) for k in both]
     high = pack([(above[k], beyond[k]) for k in both])
     more = lax.all_to_all(
-        after(outgoing, high).reshape(dp_count, MCAP, page_pool.shape[1]),
+        after(outgoing, below_low, above_low).reshape(dp_count, MCAP, page_pool.shape[1]),
         "dp",
         split_axis=0,
         concat_axis=0,

time: 293 us -> 305 us (1.041)
  waiting for transfers between devices: 90.1 us -> 101 us
    ppermute x36, waiting for transfers between devices: 74.5 us -> 86.8 us  [shift(): return lax.ppermute(value, 'expert', pairs)]
    ppermute x36, starting transfers between devices: 36.6 us -> 44 us  [shift(): return lax.ppermute(value, 'expert', pairs)]
    all_to_all x1, starting transfers between devices: 17.4 us -> 11.8 us  [body(): lax.all_to_all(jnp.concatenate(finished, axis=0).reshape(dp_count, slots,...]
    unnamed x59 -> x63, local copies, waits for them, and re-layouts: 8.84 us -> 10.5 us
  transfers between devices with their start and end apart: 41 -> 41, of which waited for: 22 -> 19; matrix products, arithmetic and copies ran while one was open for 16% -> 15% of each run, Pallas kernels for 16% -> 15%
where the time goes in v6:
time: 305 us; the launch traced here: 304 us
  waiting for transfers between devices  101 us (33%)
  starting transfers between devices  68.7 us (23%)
  Pallas kernels  66.4 us (22%)
  local copies, waits for them, and re-layouts  32.6 us (11%)
  other arithmetic  20.6 us (7%)
  between operations  14.5 us (5%)
    ppermute x36, waiting for transfers between devices, shift(): return lax.ppermute(value, 'expert', pairs)  86.8 us
    ppermute x36, starting transfers between devices, shift(): return lax.ppermute(value, 'expert', pairs)  44 us
    pallas_call x3, Pallas kernels, ffn(): pl.pallas_call(functools.partial(ffn_kernel, count, rows, parts), out_sha...  28.3 us
    convert_element_type x11, other arithmetic, plus(): return total.astype(jnp.bfloat16)  18.1 us
    pallas_call x1, Pallas kernels, tail(): pl.pallas_call(functools.partial(tail_kernel, parts, groups), out_shape=[...  16.2 us
    pallas_call x1, Pallas kernels, attend_cached(): pl.pallas_call(functools.partial(attend_kernel, step), out_shape=[jax.Sha...  13 us
    all_to_all x1, waiting for transfers between devices, body(): lax.all_to_all(jnp.concatenate(finished, axis=0).reshape(dp_count, slots,...  12.9 us
    all_to_all x1, starting transfers between devices, body(): lax.all_to_all(jnp.concatenate(finished, axis=0).reshape(dp_count, slots,...  11.8 us
  transfers between devices with their start and end apart: 41, of which 19 were waited for; matrix products, arithmetic and copies ran while one was open for 15% of the time, Pallas kernels for 15%

profile of v6, /device:TPU:1, one launch (start us, length us, event | category | flops | bytes accessed | tf_op | source)
XLA Modules:
  0.0 303.5 jit_solution(712366752961718692)
XLA Ops:
  7.2 4.0 %dispatch.1 = (bf16[64,7168]{1,0:T(8,128)(2,1)}, f32[64,64]{1,0:T(8,128)}) custom-call(s32[8,64]{1,0:T(8,128)} %bitcast.27, f32[8,64]{1,0:T(8,128)} %bitcast.28, f32[1,7168]{1,0:T(1,128)} %bitcast.26, bf16[64,7168]{1,0:T(8,128)(2,1)} %hidden_hbm.3), custom_call_target="tpu_custom_call" | custom-call | flops 58720256 | bytes 1835008 | tf_op jit(solution)/shard_map/dispatch/pallas_call | solution.py:104
  11.2 6.0 %all-to-all-start = ((bf16[8,8,7168]{2,1,0:T(8,128)(2,1)}), bf16[8,8,7168]{2,1,0:T(8,128)(2,1)S(1)}, u32[]{:S(2)}, u32[]{:S(2)}) async-start(bf16[8,8,7168]{2,1,0:T(8,128)(2,1)} %bitcast.25), calls=%async_computation | async-start | bytes 1835008 | tf_op jit(solution)/shard_map/all_to_all | solution.py:608
  18.0 10.0 %reshape.57.q_ref = bf16[64,64,576]{2,1,0:T(8,128)(2,1)} reshape(bf16[64,36864]{1,0:T(8,128)(2,1)} %q_hbm.1) | data formatting | bytes 9437184 | tf_op jit(solution)/shard_map/reshape | solution.py:612
  37.6 8.9 %collective-permute-done.refs_1_ = bf16[32,7168]{1,0:T(8,128)(2,1)S(1)} collective-permute-done((bf16[32,7168]{1,0:T(8,128)(2,1)S(1)}, bf16[32,7168]{1,0:T(8,128)(2,1)S(1)}, u32[]{:S(2)}, u32[]{:S(2)}) %collective-permute-start) | collective-permute-done | bytes 458784 | tf_op jit(solution)/shard_map/ppermute | solution.py:37
  55.1 2.7 collective-permute-start.9
  57.7 4.3 %collective-permute-done.4.refs_1_ = bf16[32,7168]{1,0:T(8,128)(2,1)S(1)} collective-permute-done((bf16[32,7168]{1,0:T(8,128)(2,1)S(1)}, bf16[32,7168]{1,0:T(8,128)(2,1)S(1)}, u32[]{:S(2)}, u32[]{:S(2)}) %collective-permute-start.4) | collective-permute-done | bytes 458784 | tf_op jit(solution)/shard_map/ppermute | solution.py:37
  62.7 24.6 %collective-permute-done.5.refs_3_ = bf16[32,7168]{1,0:T(8,128)(2,1)S(1)} collective-permute-done((bf16[32,7168]{1,0:T(8,128)(2,1)S(1)}, bf16[32,7168]{1,0:T(8,128)(2,1)S(1)}, u32[]{:S(2)}, u32[]{:S(2)}) %collective-permute-start.5) | collective-permute-done | bytes 458784 | tf_op jit(solution)/shard_map/ppermute | solution.py:37
  90.5 3.0 collective-permute-start.10
  96.5 7.0 %all-to-all-start.1 = ((bf16[8,4,9216]{2,1,0:T(4,128)(2,1)}), bf16[8,4,9216]{2,1,0:T(4,128)(2,1)S(1)}, u32[]{:S(2)}, u32[]{:S(2)}) async-start(bf16[8,4,9216]{2,1,0:T(4,128)(2,1)} %reshape.59), calls=%async_computation.1 | async-start | bytes 1179648 | tf_op jit(solution)/shard_map/all_to_all | solution.py:629
  105.9 11.5 %ffn.3 = (bf16[64,7168]{1,0:T(8,128)(2,1)}, bf16[64,7168]{1,0:T(8,128)(2,1)}, bf16[64,7168]{1,0:T(8,128)(2,1)}, bf16[64,7168]{1,0:T(8,128)(2,1)}, bf16[64,7168]{...) custom-call(bf16[64,7168]{1,0:T(8,128)(2,1)} %get-tuple-element.82.refs_0_, ...), custom_call_target="tpu_custom_call" | custom-call | flops 5637144576 | bytes 25690112 | tf_op jit(solution)/shard_map/ffn/pallas_call | solution.py:207
  122.2 2.7 collective-permute-start.17
  124.9 8.4 %ffn.4 = (bf16[64,7168]{1,0:T(8,128)(2,1)}, bf16[64,7168]{1,0:T(8,128)(2,1)}, bf16[64,7168]{1,0:T(8,128)(2,1)}, bf16[64,7168]{1,0:T(8,128)(2,1)}) custom-call(bf16[64,7168]{1,0:T(8,128)(2,1)} %collective-permute-done.12.refs_0_, bf16[64,7168]{1,0:T(8,128)(2,1)} %collective-permute-done.10.refs_1_, bf16[64,7168]{1,0:T(8,128)(2,1)} %collective-permute-done.13.refs_2_, ...), custom_call_target="tpu_custom_call" | custom-call | flops 2818572288 | bytes 18350080 | tf_op jit(solution)/shard_map/ffn/pallas_call | solution.py:207
  133.4 8.3 %collective-permute-done.14.refs_0_ = bf16[64,7168]{1,0:T(8,128)(2,1)S(1)} collective-permute-done((bf16[64,7168]{1,0:T(8,128)(2,1)}, bf16[64,7168]{1,0:T(8,128)(2,1)S(1)}, u32[]{:S(2)}, u32[]{:S(2)}) %collective-permute-start.14) | collective-permute-done | bytes 917536 | tf_op jit(solution)/shard_map/ppermute | solution.py:37
  143.4 3.6 %collective-permute-start.19 = (bf16[64,7168]{1,0:T(8,128)(2,1)}, bf16[64,7168]{1,0:T(8,128)(2,1)}, u32[]{:S(2)}, u32[]{:S(2)}) collective-permute-start(bf16[64,7168]{1,0:T(8,128)(2,1)} %get-tuple-element.121), channel_id=1, source_target_pairs={{0,3},{1,0},{2,1},{3,2},{4,7},{5,4},{6,5},{7,6},{8,11},{9,8},{10,9... | collective-permute-start | bytes 2752520 | tf_op jit(solution)/shard_map/ppermute | solution.py:37
  147.9 8.4 %ffn.5 = (bf16[64,7168]{1,0:T(8,128)(2,1)}, bf16[64,7168]{1,0:T(8,128)(2,1)}, bf16[64,7168]{1,0:T(8,128)(2,1)}, bf16[64,7168]{1,0:T(8,128)(2,1)}) custom-call(bf16[64,7168]{1,0:T(8,128)(2,1)} %copy-done.7, bf16[64,7168]{1,0:T(8,128)(2,1)} %copy-done.9, bf16[64,7168]{1,0:T(8,128)(2,1)} %copy-done.8, bf16[64,7168]{1,0:T(8,128)(2,1)} %collective-permute-done.17.refs_3_, ...), custom_call_target="tpu_custom_call" | custom-call | flops 2818572288 | bytes 18350080 | tf_op jit(solution)/shard_map/ffn/pallas_call | solution.py:207
  156.4 4.9 %collective-permute-done.18 = bf16[64,7168]{1,0:T(8,128)(2,1)} collective-permute-done((bf16[64,7168]{1,0:T(8,128)(2,1)}, bf16[64,7168]{1,0:T(8,128)(2,1)}, u32[]{:S(2)}, u32[]{:S(2)}) %collective-permute-start.18) | collective-permute-done | bytes 917536 | tf_op jit(solution)/shard_map/ppermute | solution.py:37
  161.2 4.2 %collective-permute-done.19 = bf16[64,7168]{1,0:T(8,128)(2,1)} collective-permute-done((bf16[64,7168]{1,0:T(8,128)(2,1)}, bf16[64,7168]{1,0:T(8,128)(2,1)}, u32[]{:S(2)}, u32[]{:S(2)}) %collective-permute-start.19) | collective-permute-done | bytes 917536 | tf_op jit(solution)/shard_map/ppermute | solution.py:37
  165.5 3.1 %collective-permute-done.21 = bf16[64,7168]{1,0:T(8,128)(2,1)} collective-permute-done((bf16[64,7168]{1,0:T(8,128)(2,1)}, bf16[64,7168]{1,0:T(8,128)(2,1)}, u32[]{:S(2)}, u32[]{:S(2)}) %collective-permute-start.21) | collective-permute-done | bytes 917536 | tf_op jit(solution)/shard_map/ppermute | solution.py:37
  171.3 2.7 collective-permute-start.25
  174.8 3.5 %copy.20.pool_hbm = bf16[128,16,576]{2,1,0:T(8,128)(2,1)} copy(bf16[128,16,576]{0,2,1:T(8,128)(2,1)S(1)} %bitcast.20) | data formatting | bytes 4718592 | tf_op jit(solution)/shard_map/reshape | solution.py:641
  178.3 13.0 %attend_cached.1 = (bf16[64,64,512]{2,1,0:T(8,128)(2,1)}, f32[64,64]{1,0:T(8,128)}, f32[64,64]{1,0:T(8,128)}) custom-call(s32[384]{0:T(512)} %reshape.61.table, s32[64]{0:T(128)} %lengths.1, bf16[64,64,576]{2,1,0:T(8,128)(2,1)} %reshape.57.q_ref, bf16[128,16,576]{2,1,0:T(8,128)(2,1)} %copy.20.pool_hbm, bf16[32,16,576]{2,1,0:T(8,128)(2,1)} %reshape.60.more_hbm), custom_call_target="tpu_custom_call" | custom-call | flops 855638016 | bytes 11862016 | tf_op jit(solution)/shard_map/attend_cached/pallas_call | solution.py:293
  191.4 2.7 add_convert_fusion
  198.8 2.5 add_convert_fusion.2
  204.6 6.8 %copy.21 = bf16[8,8,64,512]{3,1,2,0:T(8,128)(2,1)} copy(bf16[8,8,64,512]{3,2,1,0:T(8,128)(2,1)} %bitcast.22) | data formatting | bytes 8388608
  212.4 3.5 %collective-permute-done.28 = bf16[64,7168]{1,0:T(8,128)(2,1)S(1)} collective-permute-done((bf16[64,7168]{1,0:T(8,128)(2,1)}, bf16[64,7168]{1,0:T(8,128)(2,1)S(1)}, u32[]{:S(2)}, u32[]{:S(2)}) %collective-permute-start.28) | collective-permute-done | bytes 917536 | tf_op jit(solution)/shard_map/ppermute | solution.py:37
  215.9 3.9 %collective-permute-done.27 = bf16[64,7168]{1,0:T(8,128)(2,1)S(1)} collective-permute-done((bf16[64,7168]{1,0:T(8,128)(2,1)}, bf16[64,7168]{1,0:T(8,128)(2,1)S(1)}, u32[]{:S(2)}, u32[]{:S(2)}) %collective-permute-start.27) | collective-permute-done | bytes 917536 | tf_op jit(solution)/shard_map/ppermute | solution.py:37
  231.7 5.0 %collective-permute-done.31 = bf16[32,7168]{1,0:T(8,128)(2,1)S(1)} collective-permute-done((bf16[32,7168]{1,0:T(8,128)(2,1)S(1)}, bf16[32,7168]{1,0:T(8,128)(2,1)S(1)}, u32[]{:S(2)}, u32[]{:S(2)}) %collective-permute-start.31) | collective-permute-done | bytes 458784 | tf_op jit(solution)/shard_map/ppermute | solution.py:37
  236.7 2.6 collective-permute-done.30
  242.1 7.6 %collective-permute-done.35 = bf16[32,7168]{1,0:T(8,128)(2,1)S(1)} collective-permute-done((bf16[32,7168]{1,0:T(8,128)(2,1)S(1)}, bf16[32,7168]{1,0:T(8,128)(2,1)S(1)}, u32[]{:S(2)}, u32[]{:S(2)}) %collective-permute-start.35) | collective-permute-done | bytes 458784 | tf_op jit(solution)/shard_map/ppermute | solution.py:37
  254.1 11.8 %all-to-all-start.2 = ((bf16[8,8,7168]{2,1,0:T(8,128)(2,1)}), bf16[8,8,7168]{2,1,0:T(8,128)(2,1)S(1)}, u32[]{:S(2)}, u32[]{:S(2)}) async-start(bf16[8,8,7168]{2,1,0:T(8,128)(2,1)} %maximum_bitcast_fusion), calls=%async_computation.2 | async-start | bytes 1835008 | tf_op jit(solution)/shard_map/all_to_all | solution.py:680
  266.7 12.9 %all-to-all-done.2 = bf16[8,8,7168]{2,1,0:T(8,128)(2,1)S(1)} async-done(((bf16[8,8,7168]{2,1,0:T(8,128)(2,1)}), bf16[8,8,7168]{2,1,0:T(8,128)(2,1)S(1)}, u32[]{:S(2)}, u32[]{:S(2)}) %all-to-all-start.2) | async-done | bytes 917536 | tf_op jit(solution)/shard_map/all_to_all | solution.py:680
  280.5 16.2 %tail.1 = (bf16[64,7168]{1,0:T(8,128)(2,1)}, bf16[64,32768]{1,0:T(8,128)(2,1)}) custom-call(bf16[64,7168]{1,0:T(8,128)(2,1)} %hidden_hbm.3, bf16[64,7168]{1,0:T(8,128)(2,1)} %bitcast.23, f32[1,512]{1,0:T(1,128)} %bitcast.29, f32[64,32]{1,0:T(8,128)} %get-tuple-element.157.cos_ref, f32[64,32]{1,0:T(8,128)} %get-tuple-element.156.sin_ref, ...), custom_call_target="tpu_custom_call" | custom-call | flops 528482304 | bytes 21364736 | tf_op jit(solution)/shard_map/tail/pallas_call | solution.py:521
  (152 shorter events, 69.0 us)
Async XLA Ops:
  11.2 19.7 %all-to-all-start = ((bf16[8,8,7168]{2,1,0:T(8,128)(2,1)}), bf16[8,8,7168]{2,1,0:T(8,128)(2,1)S(1)}, u32[]{:S(2)}, u32[]{:S(2)}) async-start(bf16[8,8,7168]{2,1,0:T(8,128)(2,1)} %bitcast.25), calls=%async_computation | async-start | bytes 1835008 | tf_op jit(solution)/shard_map/all_to_all | solution.py:608
  17.2 73.3 %all-gather.3.cloned.1.call-start = ((), (), s32[]{:S(2)}) async-start(), calls=%async_computation.3 | async-start | bytes 1392640 | tf_op jit(solution)/shard_map/all_gather | solution.py:603
  31.0 15.5 %collective-permute-start = (bf16[32,7168]{1,0:T(8,128)(2,1)S(1)}, bf16[32,7168]{1,0:T(8,128)(2,1)S(1)}, u32[]{:S(2)}, u32[]{:S(2)}) collective-permute-start(bf16[32,7168]{1,0:T(8,128)(2,1)S(1)} %get-tuple-element.155.refs_0_), channel_id=1, source_target_pairs={{0,1},{1,2},{2,3},{3,0},{4,5},{5,6},{6,7},{7,4},{8,9},{9,10},{10,1... | collective-permute-start | bytes 1376264 | tf_op jit(solution)/shard_map/ppermute | solution.py:37
  48.0 14.0 %collective-permute-start.4 = (bf16[32,7168]{1,0:T(8,128)(2,1)S(1)}, bf16[32,7168]{1,0:T(8,128)(2,1)S(1)}, u32[]{:S(2)}, u32[]{:S(2)}) collective-permute-start(bf16[32,7168]{1,0:T(8,128)(2,1)S(1)} %collective-permute-done.2.refs_0_), channel_id=1, source_target_pairs={{0,3},{1,0},{2,1},{3,2},{4,7},{5,4},{6,5},{7,6},{8,11},{9,8},{10,9... | collective-permute-start | bytes 1376264 | tf_op jit(solution)/shard_map/ppermute | solution.py:37
  52.3 41.2 %collective-permute-start.6 = (bf16[64,7168]{1,0:T(8,128)(2,1)}, bf16[64,7168]{1,0:T(8,128)(2,1)}, u32[]{:S(2)}, u32[]{:S(2)}) collective-permute-start(bf16[64,7168]{1,0:T(8,128)(2,1)} %get-tuple-element.82.refs_0_), channel_id=1, source_target_pairs={{0,4},{1,5},{2,6},{3,7},{4,8},{5,9},{6,10},{7,11},{8,12},{9,13},{1... | collective-permute-start | bytes 2752520 | tf_op jit(solution)/shard_map/ppermute | solution.py:37
  53.1 40.3 %collective-permute-start.7 = (bf16[64,7168]{1,0:T(8,128)(2,1)}, bf16[64,7168]{1,0:T(8,128)(2,1)}, u32[]{:S(2)}, u32[]{:S(2)}) collective-permute-start(bf16[64,7168]{1,0:T(8,128)(2,1)} %get-tuple-element.82.refs_0_), channel_id=1, source_target_pairs={{0,12},{1,13},{2,14},{3,15},{4,0},{5,1},{6,2},{7,3},{8,4},{9,5},{1... | collective-permute-start | bytes 2752520 | tf_op jit(solution)/shard_map/ppermute | solution.py:37
  55.0 40.4 %collective-permute-start.8 = (bf16[64,7168]{1,0:T(8,128)(2,1)}, bf16[64,7168]{1,0:T(8,128)(2,1)}, u32[]{:S(2)}, u32[]{:S(2)}) collective-permute-start(bf16[64,7168]{1,0:T(8,128)(2,1)} %get-tuple-element.88.refs_4_), channel_id=1, source_target_pairs={{0,1},{1,2},{2,3},{3,0},{4,5},{5,6},{6,7},{7,4},{8,9},{9,10},{10,1... | collective-permute-start | bytes 2752520 | tf_op jit(solution)/shard_map/ppermute | solution.py:37
  55.1 40.4 %collective-permute-start.9 = (bf16[64,7168]{1,0:T(8,128)(2,1)}, bf16[64,7168]{1,0:T(8,128)(2,1)}, u32[]{:S(2)}, u32[]{:S(2)}) collective-permute-start(bf16[64,7168]{1,0:T(8,128)(2,1)} %get-tuple-element.88.refs_4_), channel_id=1, source_target_pairs={{0,3},{1,0},{2,1},{3,2},{4,7},{5,4},{6,5},{7,6},{8,11},{9,8},{10,9... | collective-permute-start | bytes 2752520 | tf_op jit(solution)/shard_map/ppermute | solution.py:37
  62.0 25.2 %collective-permute-start.5 = (bf16[32,7168]{1,0:T(8,128)(2,1)S(1)}, bf16[32,7168]{1,0:T(8,128)(2,1)S(1)}, u32[]{:S(2)}, u32[]{:S(2)}) collective-permute-start(bf16[32,7168]{1,0:T(8,128)(2,1)S(1)} %collective-permute-done.3.refs_2_), channel_id=1, source_target_pairs={{0,12},{1,13},{2,14},{3,15},{4,0},{5,1},{6,2},{7,3},{8,4},{9,5},{1... | collective-permute-start | bytes 1376264 | tf_op jit(solution)/shard_map/ppermute | solution.py:37
  90.5 28.3 %collective-permute-start.10 = (bf16[64,7168]{1,0:T(8,128)(2,1)}, bf16[64,7168]{1,0:T(8,128)(2,1)}, u32[]{:S(2)}, u32[]{:S(2)}) collective-permute-start(bf16[64,7168]{1,0:T(8,128)(2,1)} %get-tuple-element.87.refs_1_), channel_id=1, source_target_pairs={{0,12},{1,13},{2,14},{3,15},{4,0},{5,1},{6,2},{7,3},{8,4},{9,5},{1... | collective-permute-start | bytes 2752520 | tf_op jit(solution)/shard_map/ppermute | solution.py:37
  93.5 25.4 %collective-permute-start.12 = (bf16[64,7168]{1,0:T(8,128)(2,1)}, bf16[64,7168]{1,0:T(8,128)(2,1)}, u32[]{:S(2)}, u32[]{:S(2)}) collective-permute-start(bf16[64,7168]{1,0:T(8,128)(2,1)} %get-tuple-element.87.refs_1_), channel_id=1, source_target_pairs={{0,4},{1,5},{2,6},{3,7},{4,8},{5,9},{6,10},{7,11},{8,12},{9,13},{1... | collective-permute-start | bytes 2752520 | tf_op jit(solution)/shard_map/ppermute | solution.py:37
  93.5 25.3 %collective-permute-start.11 = (bf16[64,7168]{1,0:T(8,128)(2,1)}, bf16[64,7168]{1,0:T(8,128)(2,1)}, u32[]{:S(2)}, u32[]{:S(2)}) collective-permute-start(bf16[64,7168]{1,0:T(8,128)(2,1)} %get-tuple-element.89.refs_5_), channel_id=1, source_target_pairs={{0,3},{1,0},{2,1},{3,2},{4,7},{5,4},{6,5},{7,6},{8,11},{9,8},{10,9... | collective-permute-start | bytes 2752520 | tf_op jit(solution)/shard_map/ppermute | solution.py:37
  95.5 23.3 %collective-permute-start.13 = (bf16[64,7168]{1,0:T(8,128)(2,1)}, bf16[64,7168]{1,0:T(8,128)(2,1)}, u32[]{:S(2)}, u32[]{:S(2)}) collective-permute-start(bf16[64,7168]{1,0:T(8,128)(2,1)} %get-tuple-element.89.refs_5_), channel_id=1, source_target_pairs={{0,1},{1,2},{2,3},{3,0},{4,5},{5,6},{6,7},{7,4},{8,9},{9,10},{10,1... | collective-permute-start | bytes 2752520 | tf_op jit(solution)/shard_map/ppermute | solution.py:37
  96.5 20.9 %all-to-all-start.1 = ((bf16[8,4,9216]{2,1,0:T(4,128)(2,1)}), bf16[8,4,9216]{2,1,0:T(4,128)(2,1)S(1)}, u32[]{:S(2)}, u32[]{:S(2)}) async-start(bf16[8,4,9216]{2,1,0:T(4,128)(2,1)} %reshape.59), calls=%async_computation.1 | async-start | bytes 1179648 | tf_op jit(solution)/shard_map/all_to_all | solution.py:629
  103.5 176.1 %all-gather.5.cloned.1.call-start = ((), (), s32[]{:S(2)}) async-start(), calls=%async_computation.4 | async-start | bytes 10321920 | tf_op jit(solution)/shard_map/all_gather | solution.py:638
  118.8 22.9 %collective-permute-start.14 = (bf16[64,7168]{1,0:T(8,128)(2,1)}, bf16[64,7168]{1,0:T(8,128)(2,1)S(1)}, u32[]{:S(2)}, u32[]{:S(2)}) collective-permute-start(bf16[64,7168]{1,0:T(8,128)(2,1)} %collective-permute-done.6.refs_2_), channel_id=1, source_target_pairs={{0,4},{1,5},{2,6},{3,7},{4,8},{5,9},{6,10},{7,11},{8,12},{9,13},{1... | collective-permute-start | bytes 2752520 | tf_op jit(solution)/shard_map/ppermute | solution.py:37
  119.3 24.1 %collective-permute-start.15 = (bf16[64,7168]{1,0:T(8,128)(2,1)}, bf16[64,7168]{1,0:T(8,128)(2,1)S(1)}, u32[]{:S(2)}, u32[]{:S(2)}) collective-permute-start(bf16[64,7168]{1,0:T(8,128)(2,1)} %collective-permute-done.8.refs_6_), channel_id=1, source_target_pairs={{0,1},{1,2},{2,3},{3,0},{4,5},{5,6},{6,7},{7,4},{8,9},{9,10},{10,1... | collective-permute-start | bytes 2752520 | tf_op jit(solution)/shard_map/ppermute | solution.py:37
  119.9 27.1 %collective-permute-start.16 = (bf16[64,7168]{1,0:T(8,128)(2,1)}, bf16[64,7168]{1,0:T(8,128)(2,1)S(1)}, u32[]{:S(2)}, u32[]{:S(2)}) collective-permute-start(bf16[64,7168]{1,0:T(8,128)(2,1)} %collective-permute-done.10.refs_1_), channel_id=1, source_target_pairs={{0,12},{1,13},{2,14},{3,15},{4,0},{5,1},{6,2},{7,3},{8,4},{9,5},{1... | collective-permute-start | bytes 2752520 | tf_op jit(solution)/shard_map/ppermute | solution.py:37
  122.2 24.8 %collective-permute-start.17 = (bf16[64,7168]{1,0:T(8,128)(2,1)}, bf16[64,7168]{1,0:T(8,128)(2,1)}, u32[]{:S(2)}, u32[]{:S(2)}) collective-permute-start(bf16[64,7168]{1,0:T(8,128)(2,1)} %collective-permute-done.11.refs_3_), channel_id=1, source_target_pairs={{0,3},{1,0},{2,1},{3,2},{4,7},{5,4},{6,5},{7,6},{8,11},{9,8},{10,9... | collective-permute-start | bytes 2752520 | tf_op jit(solution)/shard_map/ppermute | solution.py:37
  133.3 32.2 %collective-permute-start.20 = (bf16[64,7168]{1,0:T(8,128)(2,1)}, bf16[64,7168]{1,0:T(8,128)(2,1)}, u32[]{:S(2)}, u32[]{:S(2)}) collective-permute-start(bf16[64,7168]{1,0:T(8,128)(2,1)} %get-tuple-element.105), channel_id=1, source_target_pairs={{0,4},{1,5},{2,6},{3,7},{4,8},{5,9},{6,10},{7,11},{8,12},{9,13},{1... | collective-permute-start | bytes 2752520 | tf_op jit(solution)/shard_map/ppermute | solution.py:37
  141.8 19.5 %collective-permute-start.18 = (bf16[64,7168]{1,0:T(8,128)(2,1)}, bf16[64,7168]{1,0:T(8,128)(2,1)}, u32[]{:S(2)}, u32[]{:S(2)}) collective-permute-start(bf16[64,7168]{1,0:T(8,128)(2,1)} %get-tuple-element.120), channel_id=1, source_target_pairs={{0,12},{1,13},{2,14},{3,15},{4,0},{5,1},{6,2},{7,3},{8,4},{9,5},{1... | collective-permute-start | bytes 2752520 | tf_op jit(solution)/shard_map/ppermute | solution.py:37
  143.4 22.1 %collective-permute-start.19 = (bf16[64,7168]{1,0:T(8,128)(2,1)}, bf16[64,7168]{1,0:T(8,128)(2,1)}, u32[]{:S(2)}, u32[]{:S(2)}) collective-permute-start(bf16[64,7168]{1,0:T(8,128)(2,1)} %get-tuple-element.121), channel_id=1, source_target_pairs={{0,3},{1,0},{2,1},{3,2},{4,7},{5,4},{6,5},{7,6},{8,11},{9,8},{10,9... | collective-permute-start | bytes 2752520 | tf_op jit(solution)/shard_map/ppermute | solution.py:37
  147.0 21.6 %collective-permute-start.21 = (bf16[64,7168]{1,0:T(8,128)(2,1)}, bf16[64,7168]{1,0:T(8,128)(2,1)}, u32[]{:S(2)}, u32[]{:S(2)}) collective-permute-start(bf16[64,7168]{1,0:T(8,128)(2,1)} %get-tuple-element.107), channel_id=1, source_target_pairs={{0,1},{1,2},{2,3},{3,0},{4,5},{5,6},{6,7},{7,4},{8,9},{9,10},{10,1... | collective-permute-start | bytes 2752520 | tf_op jit(solution)/shard_map/ppermute | solution.py:37
  168.6 22.7 %collective-permute-start.22 = (bf16[64,7168]{1,0:T(8,128)(2,1)}, bf16[64,7168]{1,0:T(8,128)(2,1)S(1)}, u32[]{:S(2)}, u32[]{:S(2)}) collective-permute-start(bf16[64,7168]{1,0:T(8,128)(2,1)} %get-tuple-element.122), channel_id=1, source_target_pairs={{0,4},{1,5},{2,6},{3,7},{4,8},{5,9},{6,10},{7,11},{8,12},{9,13},{1... | collective-permute-start | bytes 2752520 | tf_op jit(solution)/shard_map/ppermute | solution.py:37
  169.0 22.3 %collective-permute-start.23 = (bf16[64,7168]{1,0:T(8,128)(2,1)}, bf16[64,7168]{1,0:T(8,128)(2,1)}, u32[]{:S(2)}, u32[]{:S(2)}) collective-permute-start(bf16[64,7168]{1,0:T(8,128)(2,1)} %get-tuple-element.123), channel_id=1, source_target_pairs={{0,1},{1,2},{2,3},{3,0},{4,5},{5,6},{6,7},{7,4},{8,9},{9,10},{10,1... | collective-permute-start | bytes 2752520 | tf_op jit(solution)/shard_map/ppermute | solution.py:37
  169.0 22.3 %collective-permute-start.24 = (bf16[64,7168]{1,0:T(8,128)(2,1)}, bf16[64,7168]{1,0:T(8,128)(2,1)}, u32[]{:S(2)}, u32[]{:S(2)}) collective-permute-start(bf16[64,7168]{1,0:T(8,128)(2,1)} %get-tuple-element.124), channel_id=1, source_target_pairs={{0,12},{1,13},{2,14},{3,15},{4,0},{5,1},{6,2},{7,3},{8,4},{9,5},{1... | collective-permute-start | bytes 2752520 | tf_op jit(solution)/shard_map/ppermute | solution.py:37
  171.3 20.1 %collective-permute-start.25 = (bf16[64,7168]{1,0:T(8,128)(2,1)}, bf16[64,7168]{1,0:T(8,128)(2,1)}, u32[]{:S(2)}, u32[]{:S(2)}) collective-permute-start(bf16[64,7168]{1,0:T(8,128)(2,1)} %get-tuple-element.125), channel_id=1, source_target_pairs={{0,3},{1,0},{2,1},{3,2},{4,7},{5,4},{6,5},{7,6},{8,11},{9,8},{10,9... | collective-permute-start | bytes 2752520 | tf_op jit(solution)/shard_map/ppermute | solution.py:37
  194.0 18.4 %collective-permute-start.29 = (bf16[64,7168]{1,0:T(8,128)(2,1)}, bf16[64,7168]{1,0:T(8,128)(2,1)}, u32[]{:S(2)}, u32[]{:S(2)}) collective-permute-start(bf16[64,7168]{1,0:T(8,128)(2,1)} %add_convert_fusion), channel_id=1, source_target_pairs={{0,3},{1,0},{2,1},{3,2},{4,7},{5,4},{6,5},{7,6},{8,11},{9,8},{10,9... | collective-permute-start | bytes 2752520 | tf_op jit(solution)/shard_map/ppermute | solution.py:37
  198.5 17.5 %collective-permute-start.28 = (bf16[64,7168]{1,0:T(8,128)(2,1)}, bf16[64,7168]{1,0:T(8,128)(2,1)S(1)}, u32[]{:S(2)}, u32[]{:S(2)}) collective-permute-start(bf16[64,7168]{1,0:T(8,128)(2,1)} %add_convert_fusion.1), channel_id=1, source_target_pairs={{0,12},{1,13},{2,14},{3,15},{4,0},{5,1},{6,2},{7,3},{8,4},{9,5},{1... | collective-permute-start | bytes 2752520 | tf_op jit(solution)/shard_map/ppermute | solution.py:37
  201.2 18.6 %collective-permute-start.27 = (bf16[64,7168]{1,0:T(8,128)(2,1)}, bf16[64,7168]{1,0:T(8,128)(2,1)S(1)}, u32[]{:S(2)}, u32[]{:S(2)}) collective-permute-start(bf16[64,7168]{1,0:T(8,128)(2,1)} %add_convert_fusion.2), channel_id=1, source_target_pairs={{0,1},{1,2},{2,3},{3,0},{4,5},{5,6},{6,7},{7,4},{8,9},{9,10},{10,1... | collective-permute-start | bytes 2752520 | tf_op jit(solution)/shard_map/ppermute | solution.py:37
  202.4 18.6 %collective-permute-start.26 = (bf16[64,7168]{1,0:T(8,128)(2,1)}, bf16[64,7168]{1,0:T(8,128)(2,1)S(1)}, u32[]{:S(2)}, u32[]{:S(2)}) collective-permute-start(bf16[64,7168]{1,0:T(8,128)(2,1)} %add_convert_fusion.3), channel_id=1, source_target_pairs={{0,4},{1,5},{2,6},{3,7},{4,8},{5,9},{6,10},{7,11},{8,12},{9,13},{1... | collective-permute-start | bytes 2752520 | tf_op jit(solution)/shard_map/ppermute | solution.py:37
  254.1 25.5 %all-to-all-start.2 = ((bf16[8,8,7168]{2,1,0:T(8,128)(2,1)}), bf16[8,8,7168]{2,1,0:T(8,128)(2,1)S(1)}, u32[]{:S(2)}, u32[]{:S(2)}) async-start(bf16[8,8,7168]{2,1,0:T(8,128)(2,1)} %maximum_bitcast_fusion), calls=%async_computation.2 | async-start | bytes 1835008 | tf_op jit(solution)/shard_map/all_to_all | solution.py:680
  (40 other events, 521.2 us)
Sparse Core Ops, SparseCore 0:
  20.2 47.6 all-gather.2
  204.7 57.1 all-gather.4

commit v7 on v5

--- a/solution.py
+++ b/solution.py
@@ -603,7 +603,7 @@
     w_plane = lax.all_gather(w_padded, "expert", axis=0, tiled=True)
     slots = local_experts * CAP
     packed, place_weight = dispatch(
-        hidden_in, after(norm_gain, w_padded), route_logits, expert_ids, window
+        hidden_in, norm_gain, route_logits, expert_ids, window
     )
     arrived = lax.all_to_all(
         packed.reshape(dp_count, slots, width), "dp", split_axis=0, concat_axis=0, tiled=True
@@ -633,7 +633,7 @@
         split_axis=0,
         concat_axis=0,
         tiled=True,
-    ).reshape(dp_count * MCAP, PAGE, KVW)
+    )
     high, w_plane = after((high, w_plane))
     w_plane = w_plane.reshape(ex_count, padded, KVW)[:, : w_latent.shape[0]]
     w_all = lax.all_gather(
@@ -642,21 +642,20 @@
     pool = after(page_pool, high).reshape(page_pool.shape[0], PAGE, KVW)
     below_high = [shift(high[k], axes[k][1], 1) for k in both]
     above_high = [shift(high[k], axes[k][1], -1) for k in both]
+    low, more = after((low, more))
     y_first = ffn([[low[k], high[k], below_low[k], above_low[k]] for k in both], *weights)
-    below_low, above_high, below_high, above_low = after(
-        (below_low, above_high, below_high, above_low), y_first, pool, more
-    )
-    far_low = [shift(below_low[k], axes[k][1], 1) for k in both]
-    far_high = [shift(above_high[k], axes[k][1], -1) for k in both]
+    far_low = [shift(after(below_low[k], y_first), axes[k][1], 1) for k in both]
+    far_high = [shift(after(above_high[k], y_first), axes[k][1], -1) for k in both]
+    more = after(more, y_first).reshape(dp_count * MCAP, PAGE, KVW)
+    below_high, above_high = after((below_high, above_high), y_first, pool, more)
     y_second = ffn([[below_high[k], above_high[k]] for k in both], *weights)
     y_first = after(y_first, y_second)
     early_down = [shift(y_first[k][2], axes[k][1], -1) for k in both]
     early_up = [shift(y_second[k][1], axes[k][1], 1) for k in both]
     far_low, far_high = after((far_low, far_high), y_second)
     y_far = ffn([[far_low[k], far_high[k]] for k in both], *weights)
-    y_far, early_down, early_up = after((y_far, early_down, early_up))
-    relay_up = [shift(y_far[k][0], axes[k][1], 1) for k in both]
-    relay_down = [shift(y_far[k][1], axes[k][1], -1) for k in both]
+    relay_up = [shift(after(y_far[k][0], early_up[k]), axes[k][1], 1) for k in both]
+    relay_down = [shift(after(y_far[k][1], early_down[k]), axes[k][1], -1) for k in both]
     query = after(query, y_far)
     cached, top, total = attend_cached(query, pool, more, page_table, kv_lengths)
     relay_up, relay_down = after((relay_up, relay_down), cached)

time: 293 us -> 290 us (0.990)
  starting transfers between devices: 67.5 us -> 56.8 us
  waiting for transfers between devices: 90.1 us -> 98.4 us
    all_to_all x1, waiting for transfers between devices: 0.97 us -> 10 us  [body(): lax.all_to_all(after(outgoing, high).reshape(dp_count, MCAP, page_pool.sh...]
    all_to_all x1, starting transfers between devices: 17.4 us -> 11.7 us  [body(): lax.all_to_all(jnp.concatenate(finished, axis=0).reshape(dp_count, slots,...]
    ppermute x36, starting transfers between devices: 36.6 us -> 31.7 us  [shift(): return lax.ppermute(value, 'expert', pairs)]
    unnamed x59 -> x55, local copies, waits for them, and re-layouts: 8.84 us -> 9.74 us
  transfers between devices with their start and end apart: 41 -> 41, of which waited for: 22 -> 21; matrix products, arithmetic and copies ran while one was open for 16% -> 16% of each run, Pallas kernels for 16% -> 16%
where the time goes in v7:
time: 290 us; the launch traced here: 288 us
  waiting for transfers between devices  98.4 us (34%)
  Pallas kernels  66.6 us (23%)
  starting transfers between devices  56.8 us (20%)
  local copies, waits for them, and re-layouts  31.9 us (11%)
  other arithmetic  20.4 us (7%)
  between operations  14.5 us (5%)
    ppermute x36, waiting for transfers between devices, shift(): return lax.ppermute(value, 'expert', pairs)  74.4 us
    ppermute x36, starting transfers between devices, shift(): return lax.ppermute(value, 'expert', pairs)  31.7 us
    pallas_call x3, Pallas kernels, ffn(): pl.pallas_call(functools.partial(ffn_kernel, count, rows, parts), out_sha...  28.4 us
    convert_element_type x11, other arithmetic, plus(): return total.astype(jnp.bfloat16)  17.9 us
    pallas_call x1, Pallas kernels, tail(): pl.pallas_call(functools.partial(tail_kernel, parts, groups), out_shape=[...  16.2 us
    pallas_call x1, Pallas kernels, attend_cached(): pl.pallas_call(functools.partial(attend_kernel, step), out_shape=[jax.Sha...  13 us
    all_to_all x1, waiting for transfers between devices, body(): lax.all_to_all(jnp.concatenate(finished, axis=0).reshape(dp_count, slots,...  12.9 us
    all_to_all x1, starting transfers between devices, body(): lax.all_to_all(jnp.concatenate(finished, axis=0).reshape(dp_count, slots,...  11.7 us
  transfers between devices with their start and end apart: 41, of which 21 were waited for; matrix products, arithmetic and copies ran while one was open for 16% of the time, Pallas kernels for 16%

profile of v7, /device:TPU:1, one launch (start us, length us, event | category | flops | bytes accessed | tf_op | source)
XLA Modules:
  0.0 288.5 jit_solution(16981378906575863132)
XLA Ops:
  7.2 4.0 %dispatch.1 = (bf16[64,7168]{1,0:T(8,128)(2,1)}, f32[64,64]{1,0:T(8,128)}) custom-call(s32[8,64]{1,0:T(8,128)} %bitcast.27, f32[8,64]{1,0:T(8,128)} %bitcast.28, f32[1,7168]{1,0:T(1,128)} %bitcast.26, bf16[64,7168]{1,0:T(8,128)(2,1)} %hidden_hbm.3), custom_call_target="tpu_custom_call" | custom-call | flops 58720256 | bytes 1835008 | tf_op jit(solution)/shard_map/dispatch/pallas_call | solution.py:104
  11.2 6.0 %all-to-all-start = ((bf16[8,8,7168]{2,1,0:T(8,128)(2,1)}), bf16[8,8,7168]{2,1,0:T(8,128)(2,1)S(1)}, u32[]{:S(2)}, u32[]{:S(2)}) async-start(bf16[8,8,7168]{2,1,0:T(8,128)(2,1)} %bitcast.25), calls=%async_computation | async-start | bytes 1835008 | tf_op jit(solution)/shard_map/all_to_all | solution.py:608
  18.0 10.0 %reshape.57.q_ref = bf16[64,64,576]{2,1,0:T(8,128)(2,1)} reshape(bf16[64,36864]{1,0:T(8,128)(2,1)} %q_hbm.1) | data formatting | bytes 9437184 | tf_op jit(solution)/shard_map/reshape | solution.py:612
  37.6 8.9 %collective-permute-done.refs_1_ = bf16[32,7168]{1,0:T(8,128)(2,1)S(1)} collective-permute-done((bf16[32,7168]{1,0:T(8,128)(2,1)S(1)}, bf16[32,7168]{1,0:T(8,128)(2,1)S(1)}, u32[]{:S(2)}, u32[]{:S(2)}) %collective-permute-start) | collective-permute-done | bytes 458784 | tf_op jit(solution)/shard_map/ppermute | solution.py:37
  51.8 2.5 pack.2
  54.5 7.6 %collective-permute-done.4.refs_1_ = bf16[32,7168]{1,0:T(8,128)(2,1)S(1)} collective-permute-done((bf16[32,7168]{1,0:T(8,128)(2,1)S(1)}, bf16[32,7168]{1,0:T(8,128)(2,1)S(1)}, u32[]{:S(2)}, u32[]{:S(2)}) %collective-permute-start.4) | collective-permute-done | bytes 458784 | tf_op jit(solution)/shard_map/ppermute | solution.py:37
  62.1 3.6 %collective-permute-done.5.refs_3_ = bf16[32,7168]{1,0:T(8,128)(2,1)} collective-permute-done((bf16[32,7168]{1,0:T(8,128)(2,1)S(1)}, bf16[32,7168]{1,0:T(8,128)(2,1)}, u32[]{:S(2)}, u32[]{:S(2)}) %collective-permute-start.5) | collective-permute-done | bytes 458784 | tf_op jit(solution)/shard_map/ppermute | solution.py:37
  65.7 3.5 %collective-permute-start.7 = (bf16[64,7168]{1,0:T(8,128)(2,1)}, bf16[64,7168]{1,0:T(8,128)(2,1)}, u32[]{:S(2)}, u32[]{:S(2)}) collective-permute-start(bf16[64,7168]{1,0:T(8,128)(2,1)} %get-tuple-element.99.refs_0_), channel_id=1, source_target_pairs={{0,12},{1,13},{2,14},{3,15},{4,0},{5,1},{6,2},{7,3},{8,4},{9,5},{1... | collective-permute-start | bytes 2752520 | tf_op jit(solution)/shard_map/ppermute | solution.py:37
  69.2 2.4 pack.3
  72.8 7.5 %all-to-all-start.1 = ((bf16[8,4,9216]{2,1,0:T(4,128)(2,1)}), bf16[8,4,9216]{2,1,0:T(4,128)(2,1)S(1)}, u32[]{:S(2)}, u32[]{:S(2)}) async-start(bf16[8,4,9216]{2,1,0:T(4,128)(2,1)} %reshape.58), calls=%async_computation.1 | async-start | bytes 1179648 | tf_op jit(solution)/shard_map/all_to_all | solution.py:630
  80.4 10.0 %all-to-all-done.1 = bf16[8,4,9216]{2,1,0:T(4,128)(2,1)S(1)} async-done(((bf16[8,4,9216]{2,1,0:T(4,128)(2,1)}), bf16[8,4,9216]{2,1,0:T(4,128)(2,1)S(1)}, u32[]{:S(2)}, u32[]{:S(2)}) %all-to-all-start.1) | async-done | bytes 589856 | tf_op jit(solution)/shard_map/all_to_all | solution.py:630
  90.8 11.4 %ffn.3 = (bf16[64,7168]{1,0:T(8,128)(2,1)}, bf16[64,7168]{1,0:T(8,128)(2,1)}, bf16[64,7168]{1,0:T(8,128)(2,1)}, bf16[64,7168]{1,0:T(8,128)(2,1)}, bf16[64,7168]{...) custom-call(bf16[64,7168]{1,0:T(8,128)(2,1)} %get-tuple-element.99.refs_0_, ...), custom_call_target="tpu_custom_call" | custom-call | flops 5637144576 | bytes 25690112 | tf_op jit(solution)/shard_map/ffn/pallas_call | solution.py:207
  102.9 5.8 %collective-permute-done.13.refs_3_ = bf16[64,7168]{1,0:T(8,128)(2,1)} collective-permute-done((bf16[64,7168]{1,0:T(8,128)(2,1)}, bf16[64,7168]{1,0:T(8,128)(2,1)}, u32[]{:S(2)}, u32[]{:S(2)}) %collective-permute-start.13) | collective-permute-done | bytes 917536 | tf_op jit(solution)/shard_map/ppermute | solution.py:37
  115.2 8.5 %ffn.4 = (bf16[64,7168]{1,0:T(8,128)(2,1)}, bf16[64,7168]{1,0:T(8,128)(2,1)}, bf16[64,7168]{1,0:T(8,128)(2,1)}, bf16[64,7168]{1,0:T(8,128)(2,1)}) custom-call(bf16[64,7168]{1,0:T(8,128)(2,1)} %collective-permute-done.10.refs_0_, bf16[64,7168]{1,0:T(8,128)(2,1)} %collective-permute-done.12.refs_1_, bf16[64,7168]{1,0:T(8,128)(2,1)} %collective-permute-done.11.refs_2_, ...), custom_call_target="tpu_custom_call" | custom-call | flops 2818572288 | bytes 18350080 | tf_op jit(solution)/shard_map/ffn/pallas_call | solution.py:207
  123.8 7.5 %collective-permute-done.15.refs_2_ = bf16[64,7168]{1,0:T(8,128)(2,1)} collective-permute-done((bf16[64,7168]{1,0:T(8,128)(2,1)}, bf16[64,7168]{1,0:T(8,128)(2,1)}, u32[]{:S(2)}, u32[]{:S(2)}) %collective-permute-start.15) | collective-permute-done | bytes 917536 | tf_op jit(solution)/shard_map/ppermute | solution.py:37
  134.1 8.4 %ffn.5 = (bf16[64,7168]{1,0:T(8,128)(2,1)}, bf16[64,7168]{1,0:T(8,128)(2,1)}, bf16[64,7168]{1,0:T(8,128)(2,1)}, bf16[64,7168]{1,0:T(8,128)(2,1)}) custom-call(bf16[64,7168]{1,0:T(8,128)(2,1)} %collective-permute-done.14.refs_0_, bf16[64,7168]{1,0:T(8,128)(2,1)} %copy-done.7, bf16[64,7168]{1,0:T(8,128)(2,1)} %collective-permute-done.15.refs_2_, ...), custom_call_target="tpu_custom_call" | custom-call | flops 2818572288 | bytes 18350080 | tf_op jit(solution)/shard_map/ffn/pallas_call | solution.py:207
  142.6 4.6 %collective-permute-done.24 = bf16[64,7168]{1,0:T(8,128)(2,1)S(1)} collective-permute-done((bf16[64,7168]{1,0:T(8,128)(2,1)}, bf16[64,7168]{1,0:T(8,128)(2,1)S(1)}, u32[]{:S(2)}, u32[]{:S(2)}) %collective-permute-start.24) | collective-permute-done | bytes 917536 | tf_op jit(solution)/shard_map/ppermute | solution.py:37
  147.8 5.4 %collective-permute-done.22 = bf16[64,7168]{1,0:T(8,128)(2,1)} collective-permute-done((bf16[64,7168]{1,0:T(8,128)(2,1)S(1)}, bf16[64,7168]{1,0:T(8,128)(2,1)}, u32[]{:S(2)}, u32[]{:S(2)}) %collective-permute-start.22) | collective-permute-done | bytes 917536 | tf_op jit(solution)/shard_map/ppermute | solution.py:37
  153.1 3.1 %collective-permute-start.23 = (bf16[64,7168]{1,0:T(8,128)(2,1)}, bf16[64,7168]{1,0:T(8,128)(2,1)}, u32[]{:S(2)}, u32[]{:S(2)}) collective-permute-start(bf16[64,7168]{1,0:T(8,128)(2,1)} %get-tuple-element.138), channel_id=1, source_target_pairs={{0,12},{1,13},{2,14},{3,15},{4,0},{5,1},{6,2},{7,3},{8,4},{9,5},{1... | collective-permute-start | bytes 2752520 | tf_op jit(solution)/shard_map/ppermute | solution.py:37
  157.2 3.5 %copy.20.pool_hbm = bf16[128,16,576]{2,1,0:T(8,128)(2,1)} copy(bf16[128,16,576]{0,2,1:T(8,128)(2,1)S(1)} %bitcast.20) | data formatting | bytes 4718592 | tf_op jit(solution)/shard_map/reshape | solution.py:642
  160.7 13.0 %attend_cached.1 = (bf16[64,64,512]{2,1,0:T(8,128)(2,1)}, f32[64,64]{1,0:T(8,128)}, f32[64,64]{1,0:T(8,128)}) custom-call(s32[384]{0:T(512)} %reshape.61.table, s32[64]{0:T(128)} %lengths.1, bf16[64,64,576]{2,1,0:T(8,128)(2,1)} %reshape.57.q_ref, bf16[128,16,576]{2,1,0:T(8,128)(2,1)} %copy.20.pool_hbm, bf16[32,16,576]{2,1,0:T(8,128)(2,1)} %reshape.60.more_hbm), custom_call_target="tpu_custom_call" | custom-call | flops 855638016 | bytes 11862016 | tf_op jit(solution)/shard_map/attend_cached/pallas_call | solution.py:293
  173.7 2.7 collective-permute-done.21
  190.9 6.8 %copy.21 = bf16[8,8,64,512]{3,1,2,0:T(8,128)(2,1)} copy(bf16[8,8,64,512]{3,2,1,0:T(8,128)(2,1)} %bitcast.22) | data formatting | bytes 8388608
  197.7 3.3 %collective-permute-done.28 = bf16[64,7168]{1,0:T(8,128)(2,1)} collective-permute-done((bf16[64,7168]{1,0:T(8,128)(2,1)}, bf16[64,7168]{1,0:T(8,128)(2,1)}, u32[]{:S(2)}, u32[]{:S(2)}) %collective-permute-start.28) | collective-permute-done | bytes 917536 | tf_op jit(solution)/shard_map/ppermute | solution.py:37
  201.0 3.9 %collective-permute-done.27 = bf16[64,7168]{1,0:T(8,128)(2,1)S(1)} collective-permute-done((bf16[64,7168]{1,0:T(8,128)(2,1)}, bf16[64,7168]{1,0:T(8,128)(2,1)S(1)}, u32[]{:S(2)}, u32[]{:S(2)}) %collective-permute-start.27) | collective-permute-done | bytes 917536 | tf_op jit(solution)/shard_map/ppermute | solution.py:37
  208.8 2.6 collective-permute-start.32
  216.9 4.9 %collective-permute-done.31 = bf16[32,7168]{1,0:T(8,128)(2,1)S(1)} collective-permute-done((bf16[32,7168]{1,0:T(8,128)(2,1)S(1)}, bf16[32,7168]{1,0:T(8,128)(2,1)S(1)}, u32[]{:S(2)}, u32[]{:S(2)}) %collective-permute-start.31) | collective-permute-done | bytes 458784 | tf_op jit(solution)/shard_map/ppermute | solution.py:37
  221.8 2.8 collective-permute-done.30
  227.6 7.4 %collective-permute-done.35 = bf16[32,7168]{1,0:T(8,128)(2,1)S(1)} collective-permute-done((bf16[32,7168]{1,0:T(8,128)(2,1)S(1)}, bf16[32,7168]{1,0:T(8,128)(2,1)S(1)}, u32[]{:S(2)}, u32[]{:S(2)}) %collective-permute-start.35) | collective-permute-done | bytes 458784 | tf_op jit(solution)/shard_map/ppermute | solution.py:37
  239.1 11.7 %all-to-all-start.2 = ((bf16[8,8,7168]{2,1,0:T(8,128)(2,1)}), bf16[8,8,7168]{2,1,0:T(8,128)(2,1)S(1)}, u32[]{:S(2)}, u32[]{:S(2)}) async-start(bf16[8,8,7168]{2,1,0:T(8,128)(2,1)} %maximum_bitcast_fusion), calls=%async_computation.2 | async-start | bytes 1835008 | tf_op jit(solution)/shard_map/all_to_all | solution.py:680
  251.6 12.9 %all-to-all-done.2 = bf16[8,8,7168]{2,1,0:T(8,128)(2,1)S(1)} async-done(((bf16[8,8,7168]{2,1,0:T(8,128)(2,1)}), bf16[8,8,7168]{2,1,0:T(8,128)(2,1)S(1)}, u32[]{:S(2)}, u32[]{:S(2)}) %all-to-all-start.2) | async-done | bytes 917536 | tf_op jit(solution)/shard_map/all_to_all | solution.py:680
  265.4 16.2 %tail.1 = (bf16[64,7168]{1,0:T(8,128)(2,1)}, bf16[64,32768]{1,0:T(8,128)(2,1)}) custom-call(bf16[64,7168]{1,0:T(8,128)(2,1)} %hidden_hbm.3, bf16[64,7168]{1,0:T(8,128)(2,1)} %bitcast.23, f32[1,512]{1,0:T(1,128)} %bitcast.29, f32[64,32]{1,0:T(8,128)} %get-tuple-element.169.cos_ref, f32[64,32]{1,0:T(8,128)} %get-tuple-element.168.sin_ref, ...), custom_call_target="tpu_custom_call" | custom-call | flops 528482304 | bytes 21364736 | tf_op jit(solution)/shard_map/tail/pallas_call | solution.py:521
  (144 shorter events, 61.5 us)
Async XLA Ops:
  11.2 19.7 %all-to-all-start = ((bf16[8,8,7168]{2,1,0:T(8,128)(2,1)}), bf16[8,8,7168]{2,1,0:T(8,128)(2,1)S(1)}, u32[]{:S(2)}, u32[]{:S(2)}) async-start(bf16[8,8,7168]{2,1,0:T(8,128)(2,1)} %bitcast.25), calls=%async_computation | async-start | bytes 1835008 | tf_op jit(solution)/shard_map/all_to_all | solution.py:608
  17.2 63.0 %all-gather.3.cloned.1.call-start = ((), (), s32[]{:S(2)}) async-start(), calls=%async_computation.3 | async-start | bytes 1392640 | tf_op jit(solution)/shard_map/all_gather | solution.py:603
  31.0 15.5 %collective-permute-start = (bf16[32,7168]{1,0:T(8,128)(2,1)S(1)}, bf16[32,7168]{1,0:T(8,128)(2,1)S(1)}, u32[]{:S(2)}, u32[]{:S(2)}) collective-permute-start(bf16[32,7168]{1,0:T(8,128)(2,1)S(1)} %get-tuple-element.167.refs_0_), channel_id=1, source_target_pairs={{0,1},{1,2},{2,3},{3,0},{4,5},{5,6},{6,7},{7,4},{8,9},{9,10},{10,1... | collective-permute-start | bytes 1376264 | tf_op jit(solution)/shard_map/ppermute | solution.py:37
  48.0 14.0 %collective-permute-start.4 = (bf16[32,7168]{1,0:T(8,128)(2,1)S(1)}, bf16[32,7168]{1,0:T(8,128)(2,1)S(1)}, u32[]{:S(2)}, u32[]{:S(2)}) collective-permute-start(bf16[32,7168]{1,0:T(8,128)(2,1)S(1)} %collective-permute-done.2.refs_0_), channel_id=1, source_target_pairs={{0,3},{1,0},{2,1},{3,2},{4,7},{5,4},{6,5},{7,6},{8,11},{9,8},{10,9... | collective-permute-start | bytes 1376264 | tf_op jit(solution)/shard_map/ppermute | solution.py:37
  49.8 15.9 %collective-permute-start.5 = (bf16[32,7168]{1,0:T(8,128)(2,1)S(1)}, bf16[32,7168]{1,0:T(8,128)(2,1)}, u32[]{:S(2)}, u32[]{:S(2)}) collective-permute-start(bf16[32,7168]{1,0:T(8,128)(2,1)S(1)} %collective-permute-done.3.refs_2_), channel_id=1, source_target_pairs={{0,12},{1,13},{2,14},{3,15},{4,0},{5,1},{6,2},{7,3},{8,4},{9,5},{1... | collective-permute-start | bytes 1376264 | tf_op jit(solution)/shard_map/ppermute | solution.py:37
  54.3 26.0 %collective-permute-start.6 = (bf16[64,7168]{1,0:T(8,128)(2,1)}, bf16[64,7168]{1,0:T(8,128)(2,1)}, u32[]{:S(2)}, u32[]{:S(2)}) collective-permute-start(bf16[64,7168]{1,0:T(8,128)(2,1)} %get-tuple-element.99.refs_0_), channel_id=1, source_target_pairs={{0,4},{1,5},{2,6},{3,7},{4,8},{5,9},{6,10},{7,11},{8,12},{9,13},{1... | collective-permute-start | bytes 2752520 | tf_op jit(solution)/shard_map/ppermute | solution.py:37
  54.4 36.0 %collective-permute-start.8 = (bf16[64,7168]{1,0:T(8,128)(2,1)}, bf16[64,7168]{1,0:T(8,128)(2,1)}, u32[]{:S(2)}, u32[]{:S(2)}) collective-permute-start(bf16[64,7168]{1,0:T(8,128)(2,1)} %get-tuple-element.102.refs_4_), channel_id=1, source_target_pairs={{0,1},{1,2},{2,3},{3,0},{4,5},{5,6},{6,7},{7,4},{8,9},{9,10},{10,1... | collective-permute-start | bytes 2752520 | tf_op jit(solution)/shard_map/ppermute | solution.py:37
  65.7 24.7 %collective-permute-start.7 = (bf16[64,7168]{1,0:T(8,128)(2,1)}, bf16[64,7168]{1,0:T(8,128)(2,1)}, u32[]{:S(2)}, u32[]{:S(2)}) collective-permute-start(bf16[64,7168]{1,0:T(8,128)(2,1)} %get-tuple-element.99.refs_0_), channel_id=1, source_target_pairs={{0,12},{1,13},{2,14},{3,15},{4,0},{5,1},{6,2},{7,3},{8,4},{9,5},{1... | collective-permute-start | bytes 2752520 | tf_op jit(solution)/shard_map/ppermute | solution.py:37
  69.2 21.6 %collective-permute-start.9 = (bf16[64,7168]{1,0:T(8,128)(2,1)}, bf16[64,7168]{1,0:T(8,128)(2,1)}, u32[]{:S(2)}, u32[]{:S(2)}) collective-permute-start(bf16[64,7168]{1,0:T(8,128)(2,1)} %get-tuple-element.102.refs_4_), channel_id=1, source_target_pairs={{0,3},{1,0},{2,1},{3,2},{4,7},{5,4},{6,5},{7,6},{8,11},{9,8},{10,9... | collective-permute-start | bytes 2752520 | tf_op jit(solution)/shard_map/ppermute | solution.py:37
  72.8 17.7 %all-to-all-start.1 = ((bf16[8,4,9216]{2,1,0:T(4,128)(2,1)}), bf16[8,4,9216]{2,1,0:T(4,128)(2,1)S(1)}, u32[]{:S(2)}, u32[]{:S(2)}) async-start(bf16[8,4,9216]{2,1,0:T(4,128)(2,1)} %reshape.58), calls=%async_computation.1 | async-start | bytes 1179648 | tf_op jit(solution)/shard_map/all_to_all | solution.py:630
  80.2 184.3 %all-gather.5.cloned.1.call-start = ((), (), s32[]{:S(2)}) async-start(), calls=%async_computation.4 | async-start | bytes 10321920 | tf_op jit(solution)/shard_map/all_gather | solution.py:639
  80.2 28.5 %collective-permute-start.13 = (bf16[64,7168]{1,0:T(8,128)(2,1)}, bf16[64,7168]{1,0:T(8,128)(2,1)}, u32[]{:S(2)}, u32[]{:S(2)}) collective-permute-start(bf16[64,7168]{1,0:T(8,128)(2,1)} %get-tuple-element.101.refs_5_), channel_id=1, source_target_pairs={{0,3},{1,0},{2,1},{3,2},{4,7},{5,4},{6,5},{7,6},{8,11},{9,8},{10,9... | collective-permute-start | bytes 2752520 | tf_op jit(solution)/shard_map/ppermute | solution.py:37
  80.3 28.4 %collective-permute-start.12 = (bf16[64,7168]{1,0:T(8,128)(2,1)}, bf16[64,7168]{1,0:T(8,128)(2,1)}, u32[]{:S(2)}, u32[]{:S(2)}) collective-permute-start(bf16[64,7168]{1,0:T(8,128)(2,1)} %get-tuple-element.98.refs_1_), channel_id=1, source_target_pairs={{0,12},{1,13},{2,14},{3,15},{4,0},{5,1},{6,2},{7,3},{8,4},{9,5},{1... | collective-permute-start | bytes 2752520 | tf_op jit(solution)/shard_map/ppermute | solution.py:37
  90.4 22.5 %collective-permute-start.10 = (bf16[64,7168]{1,0:T(8,128)(2,1)}, bf16[64,7168]{1,0:T(8,128)(2,1)}, u32[]{:S(2)}, u32[]{:S(2)}) collective-permute-start(bf16[64,7168]{1,0:T(8,128)(2,1)} %get-tuple-element.98.refs_1_), channel_id=1, source_target_pairs={{0,4},{1,5},{2,6},{3,7},{4,8},{5,9},{6,10},{7,11},{8,12},{9,13},{1... | collective-permute-start | bytes 2752520 | tf_op jit(solution)/shard_map/ppermute | solution.py:37
  90.4 24.8 %collective-permute-start.11 = (bf16[64,7168]{1,0:T(8,128)(2,1)}, bf16[64,7168]{1,0:T(8,128)(2,1)}, u32[]{:S(2)}, u32[]{:S(2)}) collective-permute-start(bf16[64,7168]{1,0:T(8,128)(2,1)} %get-tuple-element.101.refs_5_), channel_id=1, source_target_pairs={{0,1},{1,2},{2,3},{3,0},{4,5},{5,6},{6,7},{7,4},{8,9},{9,10},{10,1... | collective-permute-start | bytes 2752520 | tf_op jit(solution)/shard_map/ppermute | solution.py:37
  102.3 29.0 %collective-permute-start.15 = (bf16[64,7168]{1,0:T(8,128)(2,1)}, bf16[64,7168]{1,0:T(8,128)(2,1)}, u32[]{:S(2)}, u32[]{:S(2)}) collective-permute-start(bf16[64,7168]{1,0:T(8,128)(2,1)} %collective-permute-done.8.refs_6_), channel_id=1, source_target_pairs={{0,1},{1,2},{2,3},{3,0},{4,5},{5,6},{6,7},{7,4},{8,9},{9,10},{10,1... | collective-permute-start | bytes 2752520 | tf_op jit(solution)/shard_map/ppermute | solution.py:37
  108.7 24.4 %collective-permute-start.14 = (bf16[64,7168]{1,0:T(8,128)(2,1)}, bf16[64,7168]{1,0:T(8,128)(2,1)}, u32[]{:S(2)}, u32[]{:S(2)}) collective-permute-start(bf16[64,7168]{1,0:T(8,128)(2,1)} %collective-permute-done.6.refs_2_), channel_id=1, source_target_pairs={{0,4},{1,5},{2,6},{3,7},{4,8},{5,9},{6,10},{7,11},{8,12},{9,13},{1... | collective-permute-start | bytes 2752520 | tf_op jit(solution)/shard_map/ppermute | solution.py:37
  108.7 24.4 %collective-permute-start.17 = (bf16[64,7168]{1,0:T(8,128)(2,1)}, bf16[64,7168]{1,0:T(8,128)(2,1)}, u32[]{:S(2)}, u32[]{:S(2)}) collective-permute-start(bf16[64,7168]{1,0:T(8,128)(2,1)} %collective-permute-done.13.refs_3_), channel_id=1, source_target_pairs={{0,3},{1,0},{2,1},{3,2},{4,7},{5,4},{6,5},{7,6},{8,11},{9,8},{10,9... | collective-permute-start | bytes 2752520 | tf_op jit(solution)/shard_map/ppermute | solution.py:37
  112.9 20.3 %collective-permute-start.16 = (bf16[64,7168]{1,0:T(8,128)(2,1)}, bf16[64,7168]{1,0:T(8,128)(2,1)S(1)}, u32[]{:S(2)}, u32[]{:S(2)}) collective-permute-start(bf16[64,7168]{1,0:T(8,128)(2,1)} %collective-permute-done.12.refs_1_), channel_id=1, source_target_pairs={{0,12},{1,13},{2,14},{3,15},{4,0},{5,1},{6,2},{7,3},{8,4},{9,5},{1... | collective-permute-start | bytes 2752520 | tf_op jit(solution)/shard_map/ppermute | solution.py:37
  123.7 23.5 %collective-permute-start.24 = (bf16[64,7168]{1,0:T(8,128)(2,1)}, bf16[64,7168]{1,0:T(8,128)(2,1)S(1)}, u32[]{:S(2)}, u32[]{:S(2)}) collective-permute-start(bf16[64,7168]{1,0:T(8,128)(2,1)} %get-tuple-element.140), channel_id=1, source_target_pairs={{0,3},{1,0},{2,1},{3,2},{4,7},{5,4},{6,5},{7,6},{8,11},{9,8},{10,9... | collective-permute-start | bytes 2752520 | tf_op jit(solution)/shard_map/ppermute | solution.py:37
  131.3 21.8 %collective-permute-start.22 = (bf16[64,7168]{1,0:T(8,128)(2,1)S(1)}, bf16[64,7168]{1,0:T(8,128)(2,1)}, u32[]{:S(2)}, u32[]{:S(2)}) collective-permute-start(bf16[64,7168]{1,0:T(8,128)(2,1)S(1)} %copy-done.25), channel_id=1, source_target_pairs={{0,12},{1,13},{2,14},{3,15},{4,0},{5,1},{6,2},{7,3},{8,4},{9,5},{1... | collective-permute-start | bytes 2752520 | tf_op jit(solution)/shard_map/ppermute | solution.py:37
  133.1 23.1 %collective-permute-start.20 = (bf16[64,7168]{1,0:T(8,128)(2,1)}, bf16[64,7168]{1,0:T(8,128)(2,1)}, u32[]{:S(2)}, u32[]{:S(2)}) collective-permute-start(bf16[64,7168]{1,0:T(8,128)(2,1)} %get-tuple-element.121), channel_id=1, source_target_pairs={{0,1},{1,2},{2,3},{3,0},{4,5},{5,6},{6,7},{7,4},{8,9},{9,10},{10,1... | collective-permute-start | bytes 2752520 | tf_op jit(solution)/shard_map/ppermute | solution.py:37
  133.1 23.2 %collective-permute-start.18 = (bf16[64,7168]{1,0:T(8,128)(2,1)}, bf16[64,7168]{1,0:T(8,128)(2,1)}, u32[]{:S(2)}, u32[]{:S(2)}) collective-permute-start(bf16[64,7168]{1,0:T(8,128)(2,1)} %get-tuple-element.119), channel_id=1, source_target_pairs={{0,4},{1,5},{2,6},{3,7},{4,8},{5,9},{6,10},{7,11},{8,12},{9,13},{1... | collective-permute-start | bytes 2752520 | tf_op jit(solution)/shard_map/ppermute | solution.py:37
  147.2 26.5 %collective-permute-start.25 = (bf16[64,7168]{1,0:T(8,128)(2,1)}, bf16[64,7168]{1,0:T(8,128)(2,1)}, u32[]{:S(2)}, u32[]{:S(2)}) collective-permute-start(bf16[64,7168]{1,0:T(8,128)(2,1)} %get-tuple-element.141), channel_id=1, source_target_pairs={{0,3},{1,0},{2,1},{3,2},{4,7},{5,4},{6,5},{7,6},{8,11},{9,8},{10,9... | collective-permute-start | bytes 2752520 | tf_op jit(solution)/shard_map/ppermute | solution.py:37
  153.1 20.6 %collective-permute-start.23 = (bf16[64,7168]{1,0:T(8,128)(2,1)}, bf16[64,7168]{1,0:T(8,128)(2,1)}, u32[]{:S(2)}, u32[]{:S(2)}) collective-permute-start(bf16[64,7168]{1,0:T(8,128)(2,1)} %get-tuple-element.138), channel_id=1, source_target_pairs={{0,12},{1,13},{2,14},{3,15},{4,0},{5,1},{6,2},{7,3},{8,4},{9,5},{1... | collective-permute-start | bytes 2752520 | tf_op jit(solution)/shard_map/ppermute | solution.py:37
  156.3 20.2 %collective-permute-start.21 = (bf16[64,7168]{1,0:T(8,128)(2,1)}, bf16[64,7168]{1,0:T(8,128)(2,1)}, u32[]{:S(2)}, u32[]{:S(2)}) collective-permute-start(bf16[64,7168]{1,0:T(8,128)(2,1)} %get-tuple-element.135), channel_id=1, source_target_pairs={{0,1},{1,2},{2,3},{3,0},{4,5},{5,6},{6,7},{7,4},{8,9},{9,10},{10,1... | collective-permute-start | bytes 2752520 | tf_op jit(solution)/shard_map/ppermute | solution.py:37
  156.3 20.1 %collective-permute-start.19 = (bf16[64,7168]{1,0:T(8,128)(2,1)}, bf16[64,7168]{1,0:T(8,128)(2,1)}, u32[]{:S(2)}, u32[]{:S(2)}) collective-permute-start(bf16[64,7168]{1,0:T(8,128)(2,1)} %get-tuple-element.133), channel_id=1, source_target_pairs={{0,4},{1,5},{2,6},{3,7},{4,8},{5,9},{6,10},{7,11},{8,12},{9,13},{1... | collective-permute-start | bytes 2752520 | tf_op jit(solution)/shard_map/ppermute | solution.py:37
  178.8 19.0 %collective-permute-start.29 = (bf16[64,7168]{1,0:T(8,128)(2,1)}, bf16[64,7168]{1,0:T(8,128)(2,1)}, u32[]{:S(2)}, u32[]{:S(2)}) collective-permute-start(bf16[64,7168]{1,0:T(8,128)(2,1)} %add_convert_fusion), channel_id=1, source_target_pairs={{0,3},{1,0},{2,1},{3,2},{4,7},{5,4},{6,5},{7,6},{8,11},{9,8},{10,9... | collective-permute-start | bytes 2752520 | tf_op jit(solution)/shard_map/ppermute | solution.py:37
  183.5 17.5 %collective-permute-start.28 = (bf16[64,7168]{1,0:T(8,128)(2,1)}, bf16[64,7168]{1,0:T(8,128)(2,1)}, u32[]{:S(2)}, u32[]{:S(2)}) collective-permute-start(bf16[64,7168]{1,0:T(8,128)(2,1)} %add_convert_fusion.1), channel_id=1, source_target_pairs={{0,12},{1,13},{2,14},{3,15},{4,0},{5,1},{6,2},{7,3},{8,4},{9,5},{1... | collective-permute-start | bytes 2752520 | tf_op jit(solution)/shard_map/ppermute | solution.py:37
  186.1 18.8 %collective-permute-start.27 = (bf16[64,7168]{1,0:T(8,128)(2,1)}, bf16[64,7168]{1,0:T(8,128)(2,1)S(1)}, u32[]{:S(2)}, u32[]{:S(2)}) collective-permute-start(bf16[64,7168]{1,0:T(8,128)(2,1)} %add_convert_fusion.2), channel_id=1, source_target_pairs={{0,1},{1,2},{2,3},{3,0},{4,5},{5,6},{6,7},{7,4},{8,9},{9,10},{10,1... | collective-permute-start | bytes 2752520 | tf_op jit(solution)/shard_map/ppermute | solution.py:37
  188.6 18.5 %collective-permute-start.26 = (bf16[64,7168]{1,0:T(8,128)(2,1)}, bf16[64,7168]{1,0:T(8,128)(2,1)S(1)}, u32[]{:S(2)}, u32[]{:S(2)}) collective-permute-start(bf16[64,7168]{1,0:T(8,128)(2,1)} %add_convert_fusion.3), channel_id=1, source_target_pairs={{0,4},{1,5},{2,6},{3,7},{4,8},{5,9},{6,10},{7,11},{8,12},{9,13},{1... | collective-permute-start | bytes 2752520 | tf_op jit(solution)/shard_map/ppermute | solution.py:37
  239.1 25.4 %all-to-all-start.2 = ((bf16[8,8,7168]{2,1,0:T(8,128)(2,1)}), bf16[8,8,7168]{2,1,0:T(8,128)(2,1)S(1)}, u32[]{:S(2)}, u32[]{:S(2)}) async-start(bf16[8,8,7168]{2,1,0:T(8,128)(2,1)} %maximum_bitcast_fusion), calls=%async_computation.2 | async-start | bytes 1835008 | tf_op jit(solution)/shard_map/all_to_all | solution.py:680
  (36 other events, 436.9 us)
Sparse Core Ops, SparseCore 0:
  20.2 47.4 all-gather.2
  191.0 55.1 all-gather.4

commit v8 on v7

--- a/solution.py
+++ b/solution.py
@@ -628,7 +628,7 @@
     above_low = [shift(low_too[k], axes[k][1], -1) for k in both]
     high = pack([(above[k], beyond[k]) for k in both])
     more = lax.all_to_all(
-        after(outgoing, high).reshape(dp_count, MCAP, page_pool.shape[1]),
+        after(outgoing, below_low, above_low).reshape(dp_count, MCAP, page_pool.shape[1]),
         "dp",
         split_axis=0,
         concat_axis=0,
@@ -642,12 +642,11 @@
     pool = after(page_pool, high).reshape(page_pool.shape[0], PAGE, KVW)
     below_high = [shift(high[k], axes[k][1], 1) for k in both]
     above_high = [shift(high[k], axes[k][1], -1) for k in both]
-    low, more = after((low, more))
     y_first = ffn([[low[k], high[k], below_low[k], above_low[k]] for k in both], *weights)
-    far_low = [shift(after(below_low[k], y_first), axes[k][1], 1) for k in both]
+    more = more.reshape(dp_count * MCAP, PAGE, KVW)
+    far_low = [shift(after(below_low[k], y_first, more), axes[k][1], 1) for k in both]
     far_high = [shift(after(above_high[k], y_first), axes[k][1], -1) for k in both]
-    more = after(more, y_first).reshape(dp_count * MCAP, PAGE, KVW)
-    below_high, above_high = after((below_high, above_high), y_first, pool, more)
+    below_high, above_high = after((below_high, above_high), y_first, pool)
     y_second = ffn([[below_high[k], above_high[k]] for k in both], *weights)
     y_first = after(y_first, y_second)
     early_down = [shift(y_first[k][2], axes[k][1], -1) for k in both]

time: 290 us -> 297 us (1.024)
  starting transfers between devices: 56.8 us -> 66.1 us
    all_to_all x1, waiting for transfers between devices: 10 us -> 0.01 us  [body(): lax.all_to_all(after(outgoing, below_low, above_low).reshape(dp_count, MC...]
    ppermute x36, waiting for transfers between devices: 74.4 us -> 82.7 us  [shift(): return lax.ppermute(value, 'expert', pairs)]
    ppermute x36, starting transfers between devices: 31.7 us -> 39.4 us  [shift(): return lax.ppermute(value, 'expert', pairs)]
    unnamed x55 -> x57, local copies, waits for them, and re-layouts: 9.74 us -> 9.81 us
  transfers between devices with their start and end apart: 41 -> 41, of which waited for: 21 -> 27; matrix products, arithmetic and copies ran while one was open for 16% -> 16% of each run, Pallas kernels for 16% -> 16%
where the time goes in v8:
time: 297 us; the launch traced here: 296 us
  waiting for transfers between devices  96.6 us (33%)
  Pallas kernels  66.5 us (22%)
  starting transfers between devices  66.1 us (22%)
  local copies, waits for them, and re-layouts  32 us (11%)
  other arithmetic  20.2 us (7%)
  between operations  14.4 us (5%)
    ppermute x36, waiting for transfers between devices, shift(): return lax.ppermute(value, 'expert', pairs)  82.7 us
    ppermute x36, starting transfers between devices, shift(): return lax.ppermute(value, 'expert', pairs)  39.4 us
    pallas_call x3, Pallas kernels, ffn(): pl.pallas_call(functools.partial(ffn_kernel, count, rows, parts), out_sha...  28.3 us
    convert_element_type x11, other arithmetic, plus(): return total.astype(jnp.bfloat16)  17.7 us
    pallas_call x1, Pallas kernels, tail(): pl.pallas_call(functools.partial(tail_kernel, parts, groups), out_shape=[...  16.2 us
    pallas_call x1, Pallas kernels, attend_cached(): pl.pallas_call(functools.partial(attend_kernel, step), out_shape=[jax.Sha...  13 us
    all_to_all x1, waiting for transfers between devices, body(): lax.all_to_all(jnp.concatenate(finished, axis=0).reshape(dp_count, slots,...  12.8 us
    all_to_all x1, starting transfers between devices, body(): lax.all_to_all(jnp.concatenate(finished, axis=0).reshape(dp_count, slots,...  10.7 us
  transfers between devices with their start and end apart: 41, of which 27 were waited for; matrix products, arithmetic and copies ran while one was open for 16% of the time, Pallas kernels for 16%

profile of v8, /device:TPU:1, one launch (start us, length us, event | category | flops | bytes accessed | tf_op | source)
XLA Modules:
  0.0 295.7 jit_solution(5765364507629371372)
XLA Ops:
  7.2 4.0 %dispatch.1 = (bf16[64,7168]{1,0:T(8,128)(2,1)}, f32[64,64]{1,0:T(8,128)}) custom-call(s32[8,64]{1,0:T(8,128)} %bitcast.27, f32[8,64]{1,0:T(8,128)} %bitcast.28, f32[1,7168]{1,0:T(1,128)} %bitcast.26, bf16[64,7168]{1,0:T(8,128)(2,1)} %hidden_hbm.3), custom_call_target="tpu_custom_call" | custom-call | flops 58720256 | bytes 1835008 | tf_op jit(solution)/shard_map/dispatch/pallas_call | solution.py:104
  11.2 6.0 %all-to-all-start = ((bf16[8,8,7168]{2,1,0:T(8,128)(2,1)}), bf16[8,8,7168]{2,1,0:T(8,128)(2,1)S(1)}, u32[]{:S(2)}, u32[]{:S(2)}) async-start(bf16[8,8,7168]{2,1,0:T(8,128)(2,1)} %bitcast.25), calls=%async_computation | async-start | bytes 1835008 | tf_op jit(solution)/shard_map/all_to_all | solution.py:608
  18.0 10.0 %reshape.57.q_ref = bf16[64,64,576]{2,1,0:T(8,128)(2,1)} reshape(bf16[64,36864]{1,0:T(8,128)(2,1)} %q_hbm.1) | data formatting | bytes 9437184 | tf_op jit(solution)/shard_map/reshape | solution.py:612
  37.6 8.9 %collective-permute-done.refs_1_ = bf16[32,7168]{1,0:T(8,128)(2,1)S(1)} collective-permute-done((bf16[32,7168]{1,0:T(8,128)(2,1)S(1)}, bf16[32,7168]{1,0:T(8,128)(2,1)S(1)}, u32[]{:S(2)}, u32[]{:S(2)}) %collective-permute-start) | collective-permute-done | bytes 458784 | tf_op jit(solution)/shard_map/ppermute | solution.py:37
  54.5 7.6 %collective-permute-done.4.refs_1_ = bf16[32,7168]{1,0:T(8,128)(2,1)S(1)} collective-permute-done((bf16[32,7168]{1,0:T(8,128)(2,1)S(1)}, bf16[32,7168]{1,0:T(8,128)(2,1)S(1)}, u32[]{:S(2)}, u32[]{:S(2)}) %collective-permute-start.4) | collective-permute-done | bytes 458784 | tf_op jit(solution)/shard_map/ppermute | solution.py:37
  62.1 3.7 %collective-permute-done.5.refs_3_ = bf16[32,7168]{1,0:T(8,128)(2,1)} collective-permute-done((bf16[32,7168]{1,0:T(8,128)(2,1)S(1)}, bf16[32,7168]{1,0:T(8,128)(2,1)}, u32[]{:S(2)}, u32[]{:S(2)}) %collective-permute-start.5) | collective-permute-done | bytes 458784 | tf_op jit(solution)/shard_map/ppermute | solution.py:37
  65.7 3.5 %collective-permute-start.7 = (bf16[64,7168]{1,0:T(8,128)(2,1)}, bf16[64,7168]{1,0:T(8,128)(2,1)}, u32[]{:S(2)}, u32[]{:S(2)}) collective-permute-start(bf16[64,7168]{1,0:T(8,128)(2,1)} %get-tuple-element.93.refs_0_), channel_id=1, source_target_pairs={{0,12},{1,13},{2,14},{3,15},{4,0},{5,1},{6,2},{7,3},{8,4},{9,5},{1... | collective-permute-start | bytes 2752520 | tf_op jit(solution)/shard_map/ppermute | solution.py:37
  69.2 2.5 pack.3
  71.9 7.2 %collective-permute-done.6.refs_2_ = bf16[64,7168]{1,0:T(8,128)(2,1)} collective-permute-done((bf16[64,7168]{1,0:T(8,128)(2,1)}, bf16[64,7168]{1,0:T(8,128)(2,1)}, u32[]{:S(2)}, u32[]{:S(2)}) %collective-permute-start.6) | collective-permute-done | bytes 917536 | tf_op jit(solution)/shard_map/ppermute | solution.py:37
  80.6 6.5 %collective-permute-done.7.refs_3_ = bf16[64,7168]{1,0:T(8,128)(2,1)} collective-permute-done((bf16[64,7168]{1,0:T(8,128)(2,1)}, bf16[64,7168]{1,0:T(8,128)(2,1)}, u32[]{:S(2)}, u32[]{:S(2)}) %collective-permute-start.7) | collective-permute-done | bytes 917536 | tf_op jit(solution)/shard_map/ppermute | solution.py:37
  90.0 10.0 %all-to-all-start.1 = ((bf16[8,4,9216]{2,1,0:T(4,128)(2,1)}), bf16[8,4,9216]{2,1,0:T(4,128)(2,1)S(1)}, u32[]{:S(2)}, u32[]{:S(2)}) async-start(bf16[8,4,9216]{2,1,0:T(4,128)(2,1)} %reshape.59), calls=%async_computation.1 | async-start | bytes 1179648 | tf_op jit(solution)/shard_map/all_to_all | solution.py:630
  100.0 11.4 %ffn.3 = (bf16[64,7168]{1,0:T(8,128)(2,1)}, bf16[64,7168]{1,0:T(8,128)(2,1)}, bf16[64,7168]{1,0:T(8,128)(2,1)}, bf16[64,7168]{1,0:T(8,128)(2,1)}, bf16[64,7168]{...) custom-call(bf16[64,7168]{1,0:T(8,128)(2,1)} %get-tuple-element.93.refs_0_, ...), custom_call_target="tpu_custom_call" | custom-call | flops 5637144576 | bytes 25690112 | tf_op jit(solution)/shard_map/ffn/pallas_call | solution.py:207
  119.5 8.4 %ffn.4 = (bf16[64,7168]{1,0:T(8,128)(2,1)}, bf16[64,7168]{1,0:T(8,128)(2,1)}, bf16[64,7168]{1,0:T(8,128)(2,1)}, bf16[64,7168]{1,0:T(8,128)(2,1)}) custom-call(bf16[64,7168]{1,0:T(8,128)(2,1)} %collective-permute-done.10.refs_0_, bf16[64,7168]{1,0:T(8,128)(2,1)} %collective-permute-done.12.refs_1_, bf16[64,7168]{1,0:T(8,128)(2,1)} %collective-permute-done.11.refs_2_, ...), custom_call_target="tpu_custom_call" | custom-call | flops 2818572288 | bytes 18350080 | tf_op jit(solution)/shard_map/ffn/pallas_call | solution.py:207
  128.0 2.7 collective-permute-start.24
  130.7 3.0 collective-permute-done.17.refs_3_
  135.6 4.0 %collective-permute-done.15.refs_2_ = bf16[64,7168]{1,0:T(8,128)(2,1)S(1)} collective-permute-done((bf16[64,7168]{1,0:T(8,128)(2,1)}, bf16[64,7168]{1,0:T(8,128)(2,1)S(1)}, u32[]{:S(2)}, u32[]{:S(2)}) %collective-permute-start.15) | collective-permute-done | bytes 917536 | tf_op jit(solution)/shard_map/ppermute | solution.py:37
  139.5 2.8 collective-permute-done.14.refs_0_
  143.3 8.4 %ffn.5 = (bf16[64,7168]{1,0:T(8,128)(2,1)}, bf16[64,7168]{1,0:T(8,128)(2,1)}, bf16[64,7168]{1,0:T(8,128)(2,1)}, bf16[64,7168]{1,0:T(8,128)(2,1)}) custom-call(bf16[64,7168]{1,0:T(8,128)(2,1)} %copy-done.8, bf16[64,7168]{1,0:T(8,128)(2,1)} %collective-permute-done.16.refs_1_, bf16[64,7168]{1,0:T(8,128)(2,1)} %copy-done.7, ...), custom_call_target="tpu_custom_call" | custom-call | flops 2818572288 | bytes 18350080 | tf_op jit(solution)/shard_map/ffn/pallas_call | solution.py:207
  153.4 3.4 %collective-permute-start.25 = (bf16[64,7168]{1,0:T(8,128)(2,1)}, bf16[64,7168]{1,0:T(8,128)(2,1)S(1)}, u32[]{:S(2)}, u32[]{:S(2)}) collective-permute-start(bf16[64,7168]{1,0:T(8,128)(2,1)} %get-tuple-element.133), channel_id=1, source_target_pairs={{0,3},{1,0},{2,1},{3,2},{4,7},{5,4},{6,5},{7,6},{8,11},{9,8},{10,9... | collective-permute-start | bytes 2752520 | tf_op jit(solution)/shard_map/ppermute | solution.py:37
  162.0 3.5 %copy.20.pool_hbm = bf16[128,16,576]{2,1,0:T(8,128)(2,1)} copy(bf16[128,16,576]{0,2,1:T(8,128)(2,1)S(1)} %bitcast.20) | data formatting | bytes 4718592 | tf_op jit(solution)/shard_map/reshape | solution.py:642
  165.5 13.0 %attend_cached.1 = (bf16[64,64,512]{2,1,0:T(8,128)(2,1)}, f32[64,64]{1,0:T(8,128)}, f32[64,64]{1,0:T(8,128)}) custom-call(s32[384]{0:T(512)} %reshape.61.table, s32[64]{0:T(128)} %lengths.1, bf16[64,64,576]{2,1,0:T(8,128)(2,1)} %reshape.57.q_ref, bf16[128,16,576]{2,1,0:T(8,128)(2,1)} %copy.20.pool_hbm, bf16[32,16,576]{2,1,0:T(8,128)(2,1)} %reshape.60.more_hbm), custom_call_target="tpu_custom_call" | custom-call | flops 855638016 | bytes 11862016 | tf_op jit(solution)/shard_map/attend_cached/pallas_call | solution.py:293
  183.0 4.0 %collective-permute-start.29 = (bf16[64,7168]{1,0:T(8,128)(2,1)}, bf16[64,7168]{1,0:T(8,128)(2,1)}, u32[]{:S(2)}, u32[]{:S(2)}) collective-permute-start(bf16[64,7168]{1,0:T(8,128)(2,1)} %add_convert_fusion), channel_id=1, source_target_pairs={{0,3},{1,0},{2,1},{3,2},{4,7},{5,4},{6,5},{7,6},{8,11},{9,8},{10,9... | collective-permute-start | bytes 2752520 | tf_op jit(solution)/shard_map/ppermute | solution.py:37
  196.8 6.8 %copy.21 = bf16[8,8,64,512]{3,1,2,0:T(8,128)(2,1)} copy(bf16[8,8,64,512]{3,2,1,0:T(8,128)(2,1)} %bitcast.22) | data formatting | bytes 8388608
  204.3 4.2 %collective-permute-done.28 = bf16[64,7168]{1,0:T(8,128)(2,1)S(1)} collective-permute-done((bf16[64,7168]{1,0:T(8,128)(2,1)}, bf16[64,7168]{1,0:T(8,128)(2,1)S(1)}, u32[]{:S(2)}, u32[]{:S(2)}) %collective-permute-start.28) | collective-permute-done | bytes 917536 | tf_op jit(solution)/shard_map/ppermute | solution.py:37
  208.4 3.6 %collective-permute-done.27 = bf16[64,7168]{1,0:T(8,128)(2,1)S(1)} collective-permute-done((bf16[64,7168]{1,0:T(8,128)(2,1)}, bf16[64,7168]{1,0:T(8,128)(2,1)S(1)}, u32[]{:S(2)}, u32[]{:S(2)}) %collective-permute-start.27) | collective-permute-done | bytes 917536 | tf_op jit(solution)/shard_map/ppermute | solution.py:37
  212.0 2.5 collective-permute-done.26
  225.7 4.2 %collective-permute-done.31 = bf16[32,7168]{1,0:T(8,128)(2,1)S(1)} collective-permute-done((bf16[32,7168]{1,0:T(8,128)(2,1)S(1)}, bf16[32,7168]{1,0:T(8,128)(2,1)S(1)}, u32[]{:S(2)}, u32[]{:S(2)}) %collective-permute-start.31) | collective-permute-done | bytes 458784 | tf_op jit(solution)/shard_map/ppermute | solution.py:37
  230.0 2.8 collective-permute-done.30
  235.6 7.6 %collective-permute-done.35 = bf16[32,7168]{1,0:T(8,128)(2,1)S(1)} collective-permute-done((bf16[32,7168]{1,0:T(8,128)(2,1)S(1)}, bf16[32,7168]{1,0:T(8,128)(2,1)S(1)}, u32[]{:S(2)}, u32[]{:S(2)}) %collective-permute-start.35) | collective-permute-done | bytes 458784 | tf_op jit(solution)/shard_map/ppermute | solution.py:37
  247.3 10.7 %all-to-all-start.2 = ((bf16[8,8,7168]{2,1,0:T(8,128)(2,1)}), bf16[8,8,7168]{2,1,0:T(8,128)(2,1)S(1)}, u32[]{:S(2)}, u32[]{:S(2)}) async-start(bf16[8,8,7168]{2,1,0:T(8,128)(2,1)} %maximum_bitcast_fusion), calls=%async_computation.2 | async-start | bytes 1835008 | tf_op jit(solution)/shard_map/all_to_all | solution.py:679
  258.9 12.8 %all-to-all-done.2 = bf16[8,8,7168]{2,1,0:T(8,128)(2,1)S(1)} async-done(((bf16[8,8,7168]{2,1,0:T(8,128)(2,1)}), bf16[8,8,7168]{2,1,0:T(8,128)(2,1)S(1)}, u32[]{:S(2)}, u32[]{:S(2)}) %all-to-all-start.2) | async-done | bytes 917536 | tf_op jit(solution)/shard_map/all_to_all | solution.py:679
  272.7 16.2 %tail.1 = (bf16[64,7168]{1,0:T(8,128)(2,1)}, bf16[64,32768]{1,0:T(8,128)(2,1)}) custom-call(bf16[64,7168]{1,0:T(8,128)(2,1)} %hidden_hbm.3, bf16[64,7168]{1,0:T(8,128)(2,1)} %bitcast.23, f32[1,512]{1,0:T(1,128)} %bitcast.29, f32[64,32]{1,0:T(8,128)} %get-tuple-element.161.cos_ref, f32[64,32]{1,0:T(8,128)} %get-tuple-element.160.sin_ref, ...), custom_call_target="tpu_custom_call" | custom-call | flops 528482304 | bytes 21364736 | tf_op jit(solution)/shard_map/tail/pallas_call | solution.py:521
  (146 shorter events, 75.3 us)
Async XLA Ops:
  11.2 19.7 %all-to-all-start = ((bf16[8,8,7168]{2,1,0:T(8,128)(2,1)}), bf16[8,8,7168]{2,1,0:T(8,128)(2,1)S(1)}, u32[]{:S(2)}, u32[]{:S(2)}) async-start(bf16[8,8,7168]{2,1,0:T(8,128)(2,1)} %bitcast.25), calls=%async_computation | async-start | bytes 1835008 | tf_op jit(solution)/shard_map/all_to_all | solution.py:608
  17.2 54.6 %all-gather.3.cloned.1.call-start = ((), (), s32[]{:S(2)}) async-start(), calls=%async_computation.3 | async-start | bytes 1392640 | tf_op jit(solution)/shard_map/all_gather | solution.py:603
  31.0 15.5 %collective-permute-start = (bf16[32,7168]{1,0:T(8,128)(2,1)S(1)}, bf16[32,7168]{1,0:T(8,128)(2,1)S(1)}, u32[]{:S(2)}, u32[]{:S(2)}) collective-permute-start(bf16[32,7168]{1,0:T(8,128)(2,1)S(1)} %get-tuple-element.159.refs_0_), channel_id=1, source_target_pairs={{0,1},{1,2},{2,3},{3,0},{4,5},{5,6},{6,7},{7,4},{8,9},{9,10},{10,1... | collective-permute-start | bytes 1376264 | tf_op jit(solution)/shard_map/ppermute | solution.py:37
  48.0 14.0 %collective-permute-start.4 = (bf16[32,7168]{1,0:T(8,128)(2,1)S(1)}, bf16[32,7168]{1,0:T(8,128)(2,1)S(1)}, u32[]{:S(2)}, u32[]{:S(2)}) collective-permute-start(bf16[32,7168]{1,0:T(8,128)(2,1)S(1)} %collective-permute-done.2.refs_0_), channel_id=1, source_target_pairs={{0,3},{1,0},{2,1},{3,2},{4,7},{5,4},{6,5},{7,6},{8,11},{9,8},{10,9... | collective-permute-start | bytes 1376264 | tf_op jit(solution)/shard_map/ppermute | solution.py:37
  49.8 15.9 %collective-permute-start.5 = (bf16[32,7168]{1,0:T(8,128)(2,1)S(1)}, bf16[32,7168]{1,0:T(8,128)(2,1)}, u32[]{:S(2)}, u32[]{:S(2)}) collective-permute-start(bf16[32,7168]{1,0:T(8,128)(2,1)S(1)} %collective-permute-done.3.refs_2_), channel_id=1, source_target_pairs={{0,12},{1,13},{2,14},{3,15},{4,0},{5,1},{6,2},{7,3},{8,4},{9,5},{1... | collective-permute-start | bytes 1376264 | tf_op jit(solution)/shard_map/ppermute | solution.py:37
  54.3 24.8 %collective-permute-start.6 = (bf16[64,7168]{1,0:T(8,128)(2,1)}, bf16[64,7168]{1,0:T(8,128)(2,1)}, u32[]{:S(2)}, u32[]{:S(2)}) collective-permute-start(bf16[64,7168]{1,0:T(8,128)(2,1)} %get-tuple-element.93.refs_0_), channel_id=1, source_target_pairs={{0,4},{1,5},{2,6},{3,7},{4,8},{5,9},{6,10},{7,11},{8,12},{9,13},{1... | collective-permute-start | bytes 2752520 | tf_op jit(solution)/shard_map/ppermute | solution.py:37
  54.4 25.4 %collective-permute-start.8 = (bf16[64,7168]{1,0:T(8,128)(2,1)}, bf16[64,7168]{1,0:T(8,128)(2,1)}, u32[]{:S(2)}, u32[]{:S(2)}) collective-permute-start(bf16[64,7168]{1,0:T(8,128)(2,1)} %get-tuple-element.95.refs_4_), channel_id=1, source_target_pairs={{0,1},{1,2},{2,3},{3,0},{4,5},{5,6},{6,7},{7,4},{8,9},{9,10},{10,1... | collective-permute-start | bytes 2752520 | tf_op jit(solution)/shard_map/ppermute | solution.py:37
  65.7 21.4 %collective-permute-start.7 = (bf16[64,7168]{1,0:T(8,128)(2,1)}, bf16[64,7168]{1,0:T(8,128)(2,1)}, u32[]{:S(2)}, u32[]{:S(2)}) collective-permute-start(bf16[64,7168]{1,0:T(8,128)(2,1)} %get-tuple-element.93.refs_0_), channel_id=1, source_target_pairs={{0,12},{1,13},{2,14},{3,15},{4,0},{5,1},{6,2},{7,3},{8,4},{9,5},{1... | collective-permute-start | bytes 2752520 | tf_op jit(solution)/shard_map/ppermute | solution.py:37
  69.2 19.8 %collective-permute-start.9 = (bf16[64,7168]{1,0:T(8,128)(2,1)}, bf16[64,7168]{1,0:T(8,128)(2,1)}, u32[]{:S(2)}, u32[]{:S(2)}) collective-permute-start(bf16[64,7168]{1,0:T(8,128)(2,1)} %get-tuple-element.95.refs_4_), channel_id=1, source_target_pairs={{0,3},{1,0},{2,1},{3,2},{4,7},{5,4},{6,5},{7,6},{8,11},{9,8},{10,9... | collective-permute-start | bytes 2752520 | tf_op jit(solution)/shard_map/ppermute | solution.py:37
  71.8 39.7 %collective-permute-start.13 = (bf16[64,7168]{1,0:T(8,128)(2,1)}, bf16[64,7168]{1,0:T(8,128)(2,1)}, u32[]{:S(2)}, u32[]{:S(2)}) collective-permute-start(bf16[64,7168]{1,0:T(8,128)(2,1)} %get-tuple-element.94.refs_5_), channel_id=1, source_target_pairs={{0,3},{1,0},{2,1},{3,2},{4,7},{5,4},{6,5},{7,6},{8,11},{9,8},{10,9... | collective-permute-start | bytes 2752520 | tf_op jit(solution)/shard_map/ppermute | solution.py:37
  79.1 34.7 %collective-permute-start.12 = (bf16[64,7168]{1,0:T(8,128)(2,1)}, bf16[64,7168]{1,0:T(8,128)(2,1)}, u32[]{:S(2)}, u32[]{:S(2)}) collective-permute-start(bf16[64,7168]{1,0:T(8,128)(2,1)} %get-tuple-element.92.refs_1_), channel_id=1, source_target_pairs={{0,12},{1,13},{2,14},{3,15},{4,0},{5,1},{6,2},{7,3},{8,4},{9,5},{1... | collective-permute-start | bytes 2752520 | tf_op jit(solution)/shard_map/ppermute | solution.py:37
  79.8 39.5 %collective-permute-start.10 = (bf16[64,7168]{1,0:T(8,128)(2,1)}, bf16[64,7168]{1,0:T(8,128)(2,1)}, u32[]{:S(2)}, u32[]{:S(2)}) collective-permute-start(bf16[64,7168]{1,0:T(8,128)(2,1)} %get-tuple-element.92.refs_1_), channel_id=1, source_target_pairs={{0,4},{1,5},{2,6},{3,7},{4,8},{5,9},{6,10},{7,11},{8,12},{9,13},{1... | collective-permute-start | bytes 2752520 | tf_op jit(solution)/shard_map/ppermute | solution.py:37
  87.1 32.2 %collective-permute-start.11 = (bf16[64,7168]{1,0:T(8,128)(2,1)}, bf16[64,7168]{1,0:T(8,128)(2,1)}, u32[]{:S(2)}, u32[]{:S(2)}) collective-permute-start(bf16[64,7168]{1,0:T(8,128)(2,1)} %get-tuple-element.94.refs_5_), channel_id=1, source_target_pairs={{0,1},{1,2},{2,3},{3,0},{4,5},{5,6},{6,7},{7,4},{8,9},{9,10},{10,1... | collective-permute-start | bytes 2752520 | tf_op jit(solution)/shard_map/ppermute | solution.py:37
  90.0 25.4 %all-to-all-start.1 = ((bf16[8,4,9216]{2,1,0:T(4,128)(2,1)}), bf16[8,4,9216]{2,1,0:T(4,128)(2,1)S(1)}, u32[]{:S(2)}, u32[]{:S(2)}) async-start(bf16[8,4,9216]{2,1,0:T(4,128)(2,1)} %reshape.59), calls=%async_computation.1 | async-start | bytes 1179648 | tf_op jit(solution)/shard_map/all_to_all | solution.py:630
  100.0 171.7 %all-gather.5.cloned.1.call-start = ((), (), s32[]{:S(2)}) async-start(), calls=%async_computation.4 | async-start | bytes 10321920 | tf_op jit(solution)/shard_map/all_gather | solution.py:639
  111.5 22.2 %collective-permute-start.17 = (bf16[64,7168]{1,0:T(8,128)(2,1)}, bf16[64,7168]{1,0:T(8,128)(2,1)}, u32[]{:S(2)}, u32[]{:S(2)}) collective-permute-start(bf16[64,7168]{1,0:T(8,128)(2,1)} %collective-permute-done.13.refs_3_), channel_id=1, source_target_pairs={{0,3},{1,0},{2,1},{3,2},{4,7},{5,4},{6,5},{7,6},{8,11},{9,8},{10,9... | collective-permute-start | bytes 2752520 | tf_op jit(solution)/shard_map/ppermute | solution.py:37
  113.8 21.8 %collective-permute-start.16 = (bf16[64,7168]{1,0:T(8,128)(2,1)}, bf16[64,7168]{1,0:T(8,128)(2,1)}, u32[]{:S(2)}, u32[]{:S(2)}) collective-permute-start(bf16[64,7168]{1,0:T(8,128)(2,1)} %collective-permute-done.12.refs_1_), channel_id=1, source_target_pairs={{0,12},{1,13},{2,14},{3,15},{4,0},{5,1},{6,2},{7,3},{8,4},{9,5},{1... | collective-permute-start | bytes 2752520 | tf_op jit(solution)/shard_map/ppermute | solution.py:37
  116.8 22.7 %collective-permute-start.15 = (bf16[64,7168]{1,0:T(8,128)(2,1)}, bf16[64,7168]{1,0:T(8,128)(2,1)S(1)}, u32[]{:S(2)}, u32[]{:S(2)}) collective-permute-start(bf16[64,7168]{1,0:T(8,128)(2,1)} %collective-permute-done.8.refs_6_), channel_id=1, source_target_pairs={{0,1},{1,2},{2,3},{3,0},{4,5},{5,6},{6,7},{7,4},{8,9},{9,10},{10,1... | collective-permute-start | bytes 2752520 | tf_op jit(solution)/shard_map/ppermute | solution.py:37
  119.3 23.0 %collective-permute-start.14 = (bf16[64,7168]{1,0:T(8,128)(2,1)}, bf16[64,7168]{1,0:T(8,128)(2,1)S(1)}, u32[]{:S(2)}, u32[]{:S(2)}) collective-permute-start(bf16[64,7168]{1,0:T(8,128)(2,1)} %collective-permute-done.6.refs_2_), channel_id=1, source_target_pairs={{0,4},{1,5},{2,6},{3,7},{4,8},{5,9},{6,10},{7,11},{8,12},{9,13},{1... | collective-permute-start | bytes 2752520 | tf_op jit(solution)/shard_map/ppermute | solution.py:37
  128.0 25.3 %collective-permute-start.24 = (bf16[64,7168]{1,0:T(8,128)(2,1)}, bf16[64,7168]{1,0:T(8,128)(2,1)}, u32[]{:S(2)}, u32[]{:S(2)}) collective-permute-start(bf16[64,7168]{1,0:T(8,128)(2,1)} %get-tuple-element.132), channel_id=1, source_target_pairs={{0,3},{1,0},{2,1},{3,2},{4,7},{5,4},{6,5},{7,6},{8,11},{9,8},{10,9... | collective-permute-start | bytes 2752520 | tf_op jit(solution)/shard_map/ppermute | solution.py:37
  133.7 23.1 %collective-permute-start.22 = (bf16[64,7168]{1,0:T(8,128)(2,1)S(1)}, bf16[64,7168]{1,0:T(8,128)(2,1)}, u32[]{:S(2)}, u32[]{:S(2)}) collective-permute-start(bf16[64,7168]{1,0:T(8,128)(2,1)S(1)} %copy-done.26), channel_id=1, source_target_pairs={{0,12},{1,13},{2,14},{3,15},{4,0},{5,1},{6,2},{7,3},{8,4},{9,5},{1... | collective-permute-start | bytes 2752520 | tf_op jit(solution)/shard_map/ppermute | solution.py:37
  135.6 23.3 %collective-permute-start.20 = (bf16[64,7168]{1,0:T(8,128)(2,1)}, bf16[64,7168]{1,0:T(8,128)(2,1)}, u32[]{:S(2)}, u32[]{:S(2)}) collective-permute-start(bf16[64,7168]{1,0:T(8,128)(2,1)} %get-tuple-element.112), channel_id=1, source_target_pairs={{0,1},{1,2},{2,3},{3,0},{4,5},{5,6},{6,7},{7,4},{8,9},{9,10},{10,1... | collective-permute-start | bytes 2752520 | tf_op jit(solution)/shard_map/ppermute | solution.py:37
  139.5 21.6 %collective-permute-start.18 = (bf16[64,7168]{1,0:T(8,128)(2,1)}, bf16[64,7168]{1,0:T(8,128)(2,1)}, u32[]{:S(2)}, u32[]{:S(2)}) collective-permute-start(bf16[64,7168]{1,0:T(8,128)(2,1)} %get-tuple-element.110), channel_id=1, source_target_pairs={{0,4},{1,5},{2,6},{3,7},{4,8},{5,9},{6,10},{7,11},{8,12},{9,13},{1... | collective-permute-start | bytes 2752520 | tf_op jit(solution)/shard_map/ppermute | solution.py:37
  153.4 25.2 %collective-permute-start.25 = (bf16[64,7168]{1,0:T(8,128)(2,1)}, bf16[64,7168]{1,0:T(8,128)(2,1)S(1)}, u32[]{:S(2)}, u32[]{:S(2)}) collective-permute-start(bf16[64,7168]{1,0:T(8,128)(2,1)} %get-tuple-element.133), channel_id=1, source_target_pairs={{0,3},{1,0},{2,1},{3,2},{4,7},{5,4},{6,5},{7,6},{8,11},{9,8},{10,9... | collective-permute-start | bytes 2752520 | tf_op jit(solution)/shard_map/ppermute | solution.py:37
  156.8 21.8 %collective-permute-start.23 = (bf16[64,7168]{1,0:T(8,128)(2,1)}, bf16[64,7168]{1,0:T(8,128)(2,1)}, u32[]{:S(2)}, u32[]{:S(2)}) collective-permute-start(bf16[64,7168]{1,0:T(8,128)(2,1)} %get-tuple-element.130), channel_id=1, source_target_pairs={{0,12},{1,13},{2,14},{3,15},{4,0},{5,1},{6,2},{7,3},{8,4},{9,5},{1... | collective-permute-start | bytes 2752520 | tf_op jit(solution)/shard_map/ppermute | solution.py:37
  158.9 21.4 %collective-permute-start.21 = (bf16[64,7168]{1,0:T(8,128)(2,1)}, bf16[64,7168]{1,0:T(8,128)(2,1)}, u32[]{:S(2)}, u32[]{:S(2)}) collective-permute-start(bf16[64,7168]{1,0:T(8,128)(2,1)} %get-tuple-element.127), channel_id=1, source_target_pairs={{0,1},{1,2},{2,3},{3,0},{4,5},{5,6},{6,7},{7,4},{8,9},{9,10},{10,1... | collective-permute-start | bytes 2752520 | tf_op jit(solution)/shard_map/ppermute | solution.py:37
  161.2 20.7 %collective-permute-start.19 = (bf16[64,7168]{1,0:T(8,128)(2,1)}, bf16[64,7168]{1,0:T(8,128)(2,1)}, u32[]{:S(2)}, u32[]{:S(2)}) collective-permute-start(bf16[64,7168]{1,0:T(8,128)(2,1)} %get-tuple-element.125), channel_id=1, source_target_pairs={{0,4},{1,5},{2,6},{3,7},{4,8},{5,9},{6,10},{7,11},{8,12},{9,13},{1... | collective-permute-start | bytes 2752520 | tf_op jit(solution)/shard_map/ppermute | solution.py:37
  183.0 21.2 %collective-permute-start.29 = (bf16[64,7168]{1,0:T(8,128)(2,1)}, bf16[64,7168]{1,0:T(8,128)(2,1)}, u32[]{:S(2)}, u32[]{:S(2)}) collective-permute-start(bf16[64,7168]{1,0:T(8,128)(2,1)} %add_convert_fusion), channel_id=1, source_target_pairs={{0,3},{1,0},{2,1},{3,2},{4,7},{5,4},{6,5},{7,6},{8,11},{9,8},{10,9... | collective-permute-start | bytes 2752520 | tf_op jit(solution)/shard_map/ppermute | solution.py:37
  189.4 19.0 %collective-permute-start.28 = (bf16[64,7168]{1,0:T(8,128)(2,1)}, bf16[64,7168]{1,0:T(8,128)(2,1)S(1)}, u32[]{:S(2)}, u32[]{:S(2)}) collective-permute-start(bf16[64,7168]{1,0:T(8,128)(2,1)} %add_convert_fusion.1), channel_id=1, source_target_pairs={{0,12},{1,13},{2,14},{3,15},{4,0},{5,1},{6,2},{7,3},{8,4},{9,5},{1... | collective-permute-start | bytes 2752520 | tf_op jit(solution)/shard_map/ppermute | solution.py:37
  191.8 20.2 %collective-permute-start.27 = (bf16[64,7168]{1,0:T(8,128)(2,1)}, bf16[64,7168]{1,0:T(8,128)(2,1)S(1)}, u32[]{:S(2)}, u32[]{:S(2)}) collective-permute-start(bf16[64,7168]{1,0:T(8,128)(2,1)} %add_convert_fusion.2), channel_id=1, source_target_pairs={{0,1},{1,2},{2,3},{3,0},{4,5},{5,6},{6,7},{7,4},{8,9},{9,10},{10,1... | collective-permute-start | bytes 2752520 | tf_op jit(solution)/shard_map/ppermute | solution.py:37
  194.2 20.4 %collective-permute-start.26 = (bf16[64,7168]{1,0:T(8,128)(2,1)}, bf16[64,7168]{1,0:T(8,128)(2,1)S(1)}, u32[]{:S(2)}, u32[]{:S(2)}) collective-permute-start(bf16[64,7168]{1,0:T(8,128)(2,1)} %add_convert_fusion.3), channel_id=1, source_target_pairs={{0,4},{1,5},{2,6},{3,7},{4,8},{5,9},{6,10},{7,11},{8,12},{9,13},{1... | collective-permute-start | bytes 2752520 | tf_op jit(solution)/shard_map/ppermute | solution.py:37
  247.3 24.4 %all-to-all-start.2 = ((bf16[8,8,7168]{2,1,0:T(8,128)(2,1)}), bf16[8,8,7168]{2,1,0:T(8,128)(2,1)S(1)}, u32[]{:S(2)}, u32[]{:S(2)}) async-start(bf16[8,8,7168]{2,1,0:T(8,128)(2,1)} %maximum_bitcast_fusion), calls=%async_computation.2 | async-start | bytes 1835008 | tf_op jit(solution)/shard_map/all_to_all | solution.py:679
  (37 other events, 463.7 us)
Sparse Core Ops, SparseCore 0:
  20.2 47.4 all-gather.2
  196.9 55.7 all-gather.4
